TPU v7x, 256 devices: a whole 4x4x8 slice. The times are simulated.
256 devices in a mesh: dom: 8 (over y, x_lo), sub: 32 (over z, x_hi, core).
Axes of the slice: x: 4 (x_hi: 2, x_lo: 2; x = x_hi * 2 + x_lo), y: 4, z: 8, core: 2. Of those that a mesh axis runs over, the one named last changes fastest.
Arguments:
- fine_residual: float32 [3, 1048576], P(None, ('dom', 'sub')), may hold values from -6 to 6
- bonds: bfloat16 [32, 3, 3, 1048576], P(None, None, None, ('dom', 'sub')), may hold values from -0.3125 to 0.3125
- bond_col: int32 [32, 1048576], P(None, ('dom', 'sub')), may hold values from 0 to 5119, as said below
- ghost_points: int32 [256, 2, 512], P(('dom', 'sub')), may hold values from -1 to 4095, as said below
- fine_dinv: float32 [3, 3, 1048576], P(None, None, ('dom', 'sub')), may hold values from -0.2 to 1.6
- aggregate: int32 [1048576], P(('dom', 'sub')), may hold values from 0 to 131071, as said below
- coarse_dinv: float32 [3, 3, 131072], P(None, None, 'sub'), may hold values from -0.071 to 0.566
- coarse_couple: float32 [4, 131072], P(None, 'sub'), may hold values from 0.08 to 0.24
Outputs:
- preconditioned: float32 [3, 1048576], P(None, ('dom', 'sub'))
Inputs may be any that keep to these rules, and one draw needn't show every extreme that they name: ghost_points[r, 0, :] lists distinct local points of the previous run of r, ghost_points[r, 1, :] of the next run; each list holds 128 to 512 entries, followed by -1; in every draw some run has both lists full. bond_col[0, i] is i's own local index; a column below 4096 is a local point of the run, 4096 + s names slot s from the previous run and 4608 + s slot s from the next run; only slots that hold a point are named. A point of a run with sub-partition index s lies in an aggregate s * 4096 to (s + 1) * 4096 - 1.
All inputs are finite; a program needn't handle non-finite values.
Results may differ from a plain program's by a relative error of at most 0.0014.
Values may be sent and summed in bfloat16 or wider, within the bound.
No kernel may reach another device: no remote copies, remote signals or barrier semaphores. Data moves between devices by JAX's collectives and lax.ppermute only.
A program may use at most 64 MiB of HBM per device.

v0:
```python
import math

import jax
import jax.numpy as jnp
from jax import lax
from jax.sharding import PartitionSpec as P

SWEEPS = 3
JAC = 6


LOW_EIG = 0.3
HIGH_EIG = 2.2


def with_halo(x, sides, width, wrap):
    for axis, dim in sides:
        peers, length = (lax.axis_size(axis), x.shape[dim])
        up = [(i, (i + 1) % peers) for i in range(peers if wrap else peers - 1)]
        down = [(j, i) for i, j in up]
        last = lax.slice_in_dim(x, length - width, length, axis=dim)
        initial = lax.slice_in_dim(x, 0, width, axis=dim)
        before = lax.ppermute(last, axis, up)
        after = lax.ppermute(initial, axis, down)
        x = jnp.concatenate([before, x, after], axis=dim)
    return x


def passed_along(value, axis, steps):
    count = lax.axis_size(axis)
    pairs = [(source, (source + steps) % count) for source in range(count)]
    return lax.ppermute(value, axis, pairs)


def shortened(x):

    def short(part):
        return part.astype(jnp.bfloat16) if part.dtype == jnp.float32 else part

    return jax.tree.map(short, x)


def point_solve(matrix, vector):
    return jnp.sum(matrix * vector[None, :, :], axis=1)


def lookup(table, indices, precision):
    rows = table.shape[0]
    width = table.shape[1]
    groups = -(-width // 128)
    padded = table.reshape(rows * groups, 128)
    flat = indices.reshape(-1)
    total = flat.shape[0]
    block = math.gcd(total, 8192)
    lanes = jnp.arange(128, dtype=jnp.int32)
    group_ids = jnp.arange(groups, dtype=jnp.int32)

    def lookup_one_block(piece):
        onehot = (piece[None, :] % 128 == lanes[:, None]).astype(table.dtype)
        spread = jnp.dot(
            padded, onehot, preferred_element_type=jnp.float32, precision=precision
        ).reshape(rows, groups, block)
        chosen = piece[None, :] // 128 == group_ids[:, None]
        return jnp.sum(jnp.where(chosen[None, :, :], spread, 0.0), axis=1)

    result = lax.map(lookup_one_block, flat.reshape(total // block, block))
    return result.transpose(1, 0, 2).reshape((rows,) + indices.shape)


def accumulate(values, targets, count):
    points = values.shape[1]
    groups = -(-count // 128)
    block = math.gcd(points, 2048)
    lanes = jnp.arange(128, dtype=jnp.int32)
    group_ids = jnp.arange(groups, dtype=jnp.int32)
    value_blocks = values.reshape(3, points // block, block).transpose(1, 0, 2)
    target_blocks = targets.reshape(points // block, block)

    def accumulate_one_block(total, pieces):
        piece_values, piece_targets = pieces
        onehot = (piece_targets[:, None] % 128 == lanes[None, :]).astype(jnp.float32)
        chosen = piece_targets[None, :] // 128 == group_ids[:, None]
        spread = jnp.where(chosen[None, :, :], piece_values[:, None, :], 0.0).reshape(
            3 * groups, block
        )
        return (
            total
            + jnp.dot(
                spread, onehot, preferred_element_type=jnp.float32, precision=lax.Precision.HIGHEST
            ),
            None,
        )

    start = jnp.zeros((3 * groups, 128), jnp.float32)
    total, unused = lax.scan(accumulate_one_block, start, (value_blocks, target_blocks))
    return total.reshape(3, groups * 128)


def body(
    fine_residual, bonds, bond_col, ghost_points, fine_dinv, aggregate, coarse_dinv, coarse_couple
):
    wanted_lists = with_halo(ghost_points, (("sub", 0),), 1, True)
    for_next = wanted_lists[2, 0]
    for_prev = wanted_lists[0, 1]
    center_eig = (HIGH_EIG + LOW_EIG) / 2.0
    half_range = (HIGH_EIG - LOW_EIG) / 2.0
    factor = half_range / center_eig
    update = point_solve(fine_dinv, fine_residual) / center_eig
    smoothed = update
    for iteration in range(SWEEPS):
        packed = smoothed.astype(jnp.bfloat16)

        def select_points(wanted):
            picked = lookup(packed, jnp.maximum(wanted, 0), None)
            return jnp.where(wanted[None, :] >= 0, picked, 0.0).astype(jnp.bfloat16)

        from_prev = passed_along(select_points(for_next), "sub", 1)
        from_next = passed_along(select_points(for_prev), "sub", -1)
        gathered = lookup(
            jnp.concatenate([packed, from_prev, from_next], axis=1), bond_col, None
        ).astype(jnp.bfloat16)
        remainder = (
            fine_residual
            - smoothed
            - jnp.einsum("kcep,ekp->cp", bonds, gathered, preferred_element_type=jnp.float32)
        )
        factor_new = 1.0 / (2.0 * center_eig / half_range - factor)
        update = factor_new * factor * update + 2.0 * factor_new / half_range * point_solve(
            fine_dinv, remainder
        )
        smoothed = smoothed + update
        factor = factor_new
    per_group = coarse_dinv.shape[2]
    local_agg = aggregate - lax.axis_index("sub") * per_group
    rhs_part = accumulate(fine_residual, local_agg, per_group)
    coarse_rhs = lax.psum(rhs_part, "dom")
    coarse_base = point_solve(coarse_dinv, coarse_rhs)
    coarse = coarse_base
    for iteration in range(JAC - 1):
        layers = with_halo(shortened(coarse[None]), (("sub", 0),), 1, False)
        border = jnp.zeros((3, 1), jnp.float32)
        before = jnp.concatenate([border, coarse[:, :-1]], axis=1)
        after = jnp.concatenate([coarse[:, 1:], border], axis=1)
        below, above, before, after = (layers[0], layers[2], before, after)
        coarse = coarse_base + (
            coarse_couple[0] * below
            + coarse_couple[1] * above
            + coarse_couple[2] * before
            + coarse_couple[3] * after
        )
    return smoothed + lookup(coarse, local_agg, lax.Precision.HIGHEST)


def solution(mesh):
    placed = (
        P(None, ("dom", "sub")),
        P(None, None, None, ("dom", "sub")),
        P(None, ("dom", "sub")),
        P(("dom", "sub"), None, None),
        P(None, None, ("dom", "sub")),
        P(("dom", "sub")),
        P(None, None, "sub"),
        P(None, "sub"),
    )
    return jax.shard_map(
        body, mesh=mesh, in_specs=placed, out_specs=P(None, ("dom", "sub")), check_vma=False
    )
```

profile of v0, /device:TPU:101, one launch (start us, length us, event | category | flops | bytes accessed | tf_op | source)
XLA Modules:
  0.0 297.3 jit_solution(10661571524658893954)
XLA Ops:
  0.7 4.7 %collective-permute-start.2 = (s32[1,2,512]{2,1,0:T(2,128)}, s32[1,2,512]{2,1,0:T(2,128)S(1)}, u32[]{:S(2)}, u32[]{:S(2)}) collective-permute-start(s32[1,2,512]{2,1,0:T(2,128)} %param.19), channel_id=1, source_target_pairs={{0,1},{1,2},{2,3},{3,4},{4,5},{5,6},{6,7},{7,8},{8,9},{9,10},{10,1... | collective-permute-start | bytes 12296 | tf_op jit(solution)/shard_map/ppermute | solution.py:23
  6.7 3.5 %while.39 = (s32[]{:T(128)}, f32[96,128]{1,0:T(8,128)S(1)}, s32[2,2048]{1,0:T(2,128)S(1)}, f32[2,3,2048]{2,1,0:T(4,128)}, s32[]{:T(128)}, /*index=5*/s32[]{:T(128)}) while((s32[]{:T(128)}, f32[96,128]{1,0:T(8,128)S(1)}, s32[2,2048]{1,0:T(2,128)S(1)}, f32[2,3,2048]{2,1,0:T(4,128)}, s32[]{:T(128)}, /*index=5*/s32[]{:T(128)}) %tuple.160), condition=%wide.region_20.21_spmd.clone, body=%wide.region_19.20_spmd.clone.sunk | while | flops 302592000 | bytes 1933399 | solution.py:95
  10.2 27.8 %psum.7 = f32[3,4096]{1,0:T(4,128)S(1)} all-reduce(f32[3,4096]{1,0:T(4,128)S(1)} %reshape.539), channel_id=1, replica_groups=mesh['dom'=8,'sub'=32] {'dom'}, use_global_device_ids=true, to_apply=%region_21.22 | all-reduce | flops 12288 | bytes 98304 | tf_op jit(solution)/shard_map/psum | solution.py:136
  38.7 8.5 %collective-permute-start.8 = (bf16[1,3,4096]{2,1,0:T(4,128)(2,1)}, bf16[1,3,4096]{2,1,0:T(4,128)(2,1)}, u32[]{:S(2)}, u32[]{:S(2)}) collective-permute-start(bf16[1,3,4096]{2,1,0:T(4,128)(2,1)} %convert_bitcast_fusion.7), channel_id=1, source_target_pairs={{0,1},{1,2},{2,3},{3,4},{4,5},{5,6},{6,7},{7,8},{8,9},{9,10},{10,1... | collective-permute-start | bytes 73736 | tf_op jit(solution)/shard_map/ppermute | solution.py:23
  47.2 1.9 collective-permute-start.9
  52.0 5.4 %collective-permute-start.1 = (bf16[3,512]{1,0:T(4,128)(2,1)S(1)}, bf16[3,512]{1,0:T(4,128)(2,1)S(1)}, u32[]{:S(2)}, u32[]{:S(2)}) collective-permute-start(bf16[3,512]{1,0:T(4,128)(2,1)S(1)} %select_convert_fusion.5), channel_id=1, source_target_pairs={{0,1},{1,2},{2,3},{3,4},{4,5},{5,6},{6,7},{7,8},{8,9},{9,10},{10,1... | collective-permute-start | bytes 9224 | tf_op jit(solution)/shard_map/ppermute | solution.py:32
  59.1 5.6 %collective-permute-done.3 = bf16[3,512]{1,0:T(4,128)(2,1)S(1)} collective-permute-done((bf16[3,512]{1,0:T(4,128)(2,1)S(1)}, bf16[3,512]{1,0:T(4,128)(2,1)S(1)}, u32[]{:S(2)}, u32[]{:S(2)}) %collective-permute-start.3) | collective-permute-done | bytes 3104 | tf_op jit(solution)/shard_map/ppermute | solution.py:32
  65.2 43.8 %while.36 = (s32[]{:T(128)}, bf16[16,3,8192]{2,1,0:T(4,128)(2,1)S(1)}, s32[16,8192]{1,0:T(8,128)}, bf16[120,128]{1,0:T(8,128)(2,1)S(1)}, s32[]{:T(128)}) while((s32[]{:T(128)}, bf16[16,3,8192]{2,1,0:T(4,128)(2,1)S(1)}, s32[16,8192]{1,0:T(8,128)}, bf16[120,128]{1,0:T(8,128)(2,1)S(1)}, s32[]{:T(128)}) %tuple.151), condition=%wide.region_5.6_spmd.clone, body=%wide.region_3.5_spmd.clone.sunk | while | flops 255139840 | bytes 8960069 | solution.py:66
  115.6 5.5 %collective-permute-done.5 = bf16[3,512]{1,0:T(4,128)(2,1)S(1)} collective-permute-done((bf16[3,512]{1,0:T(4,128)(2,1)S(1)}, bf16[3,512]{1,0:T(4,128)(2,1)S(1)}, u32[]{:S(2)}, u32[]{:S(2)}) %collective-permute-start.5) | collective-permute-done | bytes 3104 | tf_op jit(solution)/shard_map/ppermute | solution.py:32
  122.2 55.9 %while.37 = (s32[]{:T(128)}, bf16[16,3,8192]{2,1,0:T(4,128)(2,1)S(1)}, s32[16,8192]{1,0:T(8,128)}, bf16[120,128]{1,0:T(8,128)(2,1)}, s32[]{:T(128)}) while((s32[]{:T(128)}, bf16[16,3,8192]{2,1,0:T(4,128)(2,1)S(1)}, s32[16,8192]{1,0:T(8,128)}, bf16[120,128]{1,0:T(8,128)(2,1)}, s32[]{:T(128)}) %tuple.154), condition=%wide.region_11.12_spmd.clone, body=%wide.region_9.11_spmd.clone.sunk | while | flops 255139840 | bytes 8960069 | solution.py:66
  123.4 1.5 fusion.119
  126.9 1.5 fusion.119
  137.3 1.5 fusion.119
  140.8 1.5 fusion.119
  144.3 1.5 fusion.119
  158.3 1.5 fusion.119
  161.8 1.5 fusion.119
  165.3 1.5 fusion.119
  184.5 5.6 %collective-permute-done.7 = bf16[3,512]{1,0:T(4,128)(2,1)S(1)} collective-permute-done((bf16[3,512]{1,0:T(4,128)(2,1)S(1)}, bf16[3,512]{1,0:T(4,128)(2,1)S(1)}, u32[]{:S(2)}, u32[]{:S(2)}) %collective-permute-start.7) | collective-permute-done | bytes 3104 | tf_op jit(solution)/shard_map/ppermute | solution.py:32
  191.2 55.8 %while.38 = (s32[]{:T(128)}, bf16[16,3,8192]{2,1,0:T(4,128)(2,1)S(1)}, s32[16,8192]{1,0:T(8,128)}, bf16[120,128]{1,0:T(8,128)(2,1)}, s32[]{:T(128)}) while((s32[]{:T(128)}, bf16[16,3,8192]{2,1,0:T(4,128)(2,1)S(1)}, s32[16,8192]{1,0:T(8,128)}, bf16[120,128]{1,0:T(8,128)(2,1)}, s32[]{:T(128)}) %tuple.157), condition=%wide.region_17.18_spmd.clone, body=%wide.region_15.17_spmd.clone.sunk | while | flops 255139840 | bytes 8960069 | solution.py:66
  251.9 2.0 collective-permute-start.10
  253.8 2.4 collective-permute-start.11
  256.3 6.4 %collective-permute-done.11 = bf16[1,3,4096]{2,1,0:T(4,128)(2,1)S(1)} collective-permute-done((bf16[1,3,4096]{2,1,0:T(4,128)(2,1)S(1)}, bf16[1,3,4096]{2,1,0:T(4,128)(2,1)S(1)}, u32[]{:S(2)}, u32[]{:S(2)}) %collective-permute-start.11) | collective-permute-done | bytes 24608 | tf_op jit(solution)/shard_map/ppermute | solution.py:24
  262.8 1.9 collective-permute-start.12
  264.7 2.4 collective-permute-start.13
  267.3 6.3 %collective-permute-done.13 = bf16[1,3,4096]{2,1,0:T(4,128)(2,1)S(1)} collective-permute-done((bf16[1,3,4096]{2,1,0:T(4,128)(2,1)S(1)}, bf16[1,3,4096]{2,1,0:T(4,128)(2,1)S(1)}, u32[]{:S(2)}, u32[]{:S(2)}) %collective-permute-start.13) | collective-permute-done | bytes 24608 | tf_op jit(solution)/shard_map/ppermute | solution.py:24
  273.7 1.9 collective-permute-start.14
  275.6 2.4 collective-permute-start.15
  278.1 6.3 %collective-permute-done.15 = bf16[1,3,4096]{2,1,0:T(4,128)(2,1)S(1)} collective-permute-done((bf16[1,3,4096]{2,1,0:T(4,128)(2,1)S(1)}, bf16[1,3,4096]{2,1,0:T(4,128)(2,1)S(1)}, u32[]{:S(2)}, u32[]{:S(2)}) %collective-permute-start.15) | collective-permute-done | bytes 24608 | tf_op jit(solution)/shard_map/ppermute | solution.py:24
  284.6 1.9 collective-permute-start.16
  286.5 2.4 collective-permute-start.17
  289.0 6.3 %collective-permute-done.17 = bf16[1,3,4096]{2,1,0:T(4,128)(2,1)S(1)} collective-permute-done((bf16[1,3,4096]{2,1,0:T(4,128)(2,1)S(1)}, bf16[1,3,4096]{2,1,0:T(4,128)(2,1)S(1)}, u32[]{:S(2)}, u32[]{:S(2)}) %collective-permute-start.17) | collective-permute-done | bytes 24608 | tf_op jit(solution)/shard_map/ppermute | solution.py:24
  (469 shorter events, 173.9 us)
Async XLA Ops:
  0.0 51.6 %collective-permute-start = (s32[1,2,512]{2,1,0:T(2,128)}, s32[1,2,512]{2,1,0:T(2,128)S(1)}, u32[]{:S(2)}, u32[]{:S(2)}) collective-permute-start(s32[1,2,512]{2,1,0:T(2,128)} %param.19), channel_id=1, source_target_pairs={{1,0},{2,1},{3,2},{4,3},{5,4},{6,5},{7,6},{8,7},{9,8},{10,9},{11,1... | collective-permute-start | bytes 12296 | tf_op jit(solution)/shard_map/ppermute | solution.py:24
  0.7 56.7 %collective-permute-start.2 = (s32[1,2,512]{2,1,0:T(2,128)}, s32[1,2,512]{2,1,0:T(2,128)S(1)}, u32[]{:S(2)}, u32[]{:S(2)}) collective-permute-start(s32[1,2,512]{2,1,0:T(2,128)} %param.19), channel_id=1, source_target_pairs={{0,1},{1,2},{2,3},{3,4},{4,5},{5,6},{6,7},{7,8},{8,9},{9,10},{10,1... | collective-permute-start | bytes 12296 | tf_op jit(solution)/shard_map/ppermute | solution.py:23
  6.1 31.8 %copy-start.20 = (f32[3,3,4096]{2,1,0:T(4,128)S(1)}, f32[3,3,4096]{2,1,0:T(4,128)}, u32[]{:S(2)}) copy-start(f32[3,3,4096]{2,1,0:T(4,128)} %param.22) | copy-start | bytes 442372
  6.1 43.7 %copy-start.1 = (f32[3,3,4096]{2,1,0:T(4,128)S(1)}, f32[3,3,4096]{2,1,0:T(4,128)}, u32[]{:S(2)}) copy-start(f32[3,3,4096]{2,1,0:T(4,128)} %param.20) | copy-start | bytes 442372
  6.1 52.0 %copy-start.17 = (s32[32,4096]{1,0:T(8,128)S(1)}, s32[32,4096]{1,0:T(8,128)}, u32[]{:S(2)}) copy-start(s32[32,4096]{1,0:T(8,128)} %param.18) | copy-start | bytes 1572868
  38.7 212.2 %collective-permute-start.8 = (bf16[1,3,4096]{2,1,0:T(4,128)(2,1)}, bf16[1,3,4096]{2,1,0:T(4,128)(2,1)}, u32[]{:S(2)}, u32[]{:S(2)}) collective-permute-start(bf16[1,3,4096]{2,1,0:T(4,128)(2,1)} %convert_bitcast_fusion.7), channel_id=1, source_target_pairs={{0,1},{1,2},{2,3},{3,4},{4,5},{5,6},{6,7},{7,8},{8,9},{9,10},{10,1... | collective-permute-start | bytes 73736 | tf_op jit(solution)/shard_map/ppermute | solution.py:23
  47.2 203.7 %collective-permute-start.9 = (bf16[1,3,4096]{2,1,0:T(4,128)(2,1)}, bf16[1,3,4096]{2,1,0:T(4,128)(2,1)}, u32[]{:S(2)}, u32[]{:S(2)}) collective-permute-start(bf16[1,3,4096]{2,1,0:T(4,128)(2,1)} %convert_bitcast_fusion.7), channel_id=1, source_target_pairs={{1,0},{2,1},{3,2},{4,3},{5,4},{6,5},{7,6},{8,7},{9,8},{10,9},{11,1... | collective-permute-start | bytes 73736 | tf_op jit(solution)/shard_map/ppermute | solution.py:24
  51.7 5.7 %copy-start.31 = (pred[512]{0:T(512)(128)(4,1)}, pred[512]{0:T(512)(128)(4,1)S(1)}, u32[]{:S(2)}) copy-start(pred[512]{0:T(512)(128)(4,1)S(1)} %get-tuple-element.507) | copy-start | bytes 1540
  51.7 5.8 %copy-start.37 = (s32[512]{0:T(512)}, s32[512]{0:T(512)S(1)}, u32[]{:S(2)}) copy-start(s32[512]{0:T(512)S(1)} %get-tuple-element.582) | copy-start | bytes 6148
  51.7 61.9 %copy-start.25 = (pred[32,512]{1,0:T(8,128)(4,1)}, pred[32,512]{1,0:T(8,128)(4,1)S(1)}, u32[]{:S(2)}) copy-start(pred[32,512]{1,0:T(8,128)(4,1)S(1)} %iota_compare_fusion.17) | copy-start | bytes 49156
  52.0 7.1 %collective-permute-start.1 = (bf16[3,512]{1,0:T(4,128)(2,1)S(1)}, bf16[3,512]{1,0:T(4,128)(2,1)S(1)}, u32[]{:S(2)}, u32[]{:S(2)}) collective-permute-start(bf16[3,512]{1,0:T(4,128)(2,1)S(1)} %select_convert_fusion.5), channel_id=1, source_target_pairs={{0,1},{1,2},{2,3},{3,4},{4,5},{5,6},{6,7},{7,8},{8,9},{9,10},{10,1... | collective-permute-start | bytes 9224 | tf_op jit(solution)/shard_map/ppermute | solution.py:32
  57.4 7.8 %copy-start.34 = (pred[512]{0:T(512)(128)(4,1)}, pred[512]{0:T(512)(128)(4,1)S(1)}, u32[]{:S(2)}) copy-start(pred[512]{0:T(512)(128)(4,1)S(1)} %get-tuple-element.509) | copy-start | bytes 1540
  57.5 7.7 %copy-start.27 = (pred[32,512]{1,0:T(8,128)(4,1)}, pred[32,512]{1,0:T(8,128)(4,1)S(1)}, u32[]{:S(2)}) copy-start(pred[32,512]{1,0:T(8,128)(4,1)S(1)} %iota_compare_fusion.16) | copy-start | bytes 49156
  58.1 6.6 %collective-permute-start.3 = (bf16[3,512]{1,0:T(4,128)(2,1)S(1)}, bf16[3,512]{1,0:T(4,128)(2,1)S(1)}, u32[]{:S(2)}, u32[]{:S(2)}) collective-permute-start(bf16[3,512]{1,0:T(4,128)(2,1)S(1)} %select_convert_fusion.4), channel_id=1, source_target_pairs={{0,31},{1,0},{2,1},{3,2},{4,3},{5,4},{6,5},{7,6},{8,7},{9,8},{10,9... | collective-permute-start | bytes 9224 | tf_op jit(solution)/shard_map/ppermute | solution.py:32
  109.0 3.1 %copy-start = (bf16[32,3,3,4096]{3,0,2,1:T(8,128)(2,1)S(1)}, bf16[32,3,3,4096]{3,0,2,1:T(8,128)(2,1)}, u32[]{:S(2)}) copy-start(bf16[32,3,3,4096]{3,0,2,1:T(8,128)(2,1)} %param.17) | copy-start | bytes 7077892
  111.9 3.0 %copy-start.24 = (f32[4,4096]{1,0:T(4,128)S(1)}, f32[4,4096]{1,0:T(4,128)}, u32[]{:S(2)}) copy-start(f32[4,4096]{1,0:T(4,128)} %param.23) | copy-start | bytes 196612
  114.1 1.5 collective-permute-start.4
  114.2 6.9 %collective-permute-start.5 = (bf16[3,512]{1,0:T(4,128)(2,1)S(1)}, bf16[3,512]{1,0:T(4,128)(2,1)S(1)}, u32[]{:S(2)}, u32[]{:S(2)}) collective-permute-start(bf16[3,512]{1,0:T(4,128)(2,1)S(1)} %select_convert_fusion.2), channel_id=1, source_target_pairs={{0,31},{1,0},{2,1},{3,2},{4,3},{5,4},{6,5},{7,6},{8,7},{9,8},{10,9... | collective-permute-start | bytes 9224 | tf_op jit(solution)/shard_map/ppermute | solution.py:32
  183.2 1.3 collective-permute-start.6
  183.4 6.7 %collective-permute-start.7 = (bf16[3,512]{1,0:T(4,128)(2,1)S(1)}, bf16[3,512]{1,0:T(4,128)(2,1)S(1)}, u32[]{:S(2)}, u32[]{:S(2)}) collective-permute-start(bf16[3,512]{1,0:T(4,128)(2,1)S(1)} %select_convert_fusion), channel_id=1, source_target_pairs={{0,31},{1,0},{2,1},{3,2},{4,3},{5,4},{6,5},{7,6},{8,7},{9,8},{10,9... | collective-permute-start | bytes 9224 | tf_op jit(solution)/shard_map/ppermute | solution.py:32
  250.1 45.4 %copy-start.23 = (pred[32,4096]{1,0:T(8,128)(4,1)S(1)}, pred[32,4096]{1,0:T(8,128)(4,1)}, u32[]{:S(2)}) copy-start(pred[32,4096]{1,0:T(8,128)(4,1)} %iota_compare_fusion.13) | copy-start | bytes 393220
  250.1 45.4 %copy-start.30 = (s32[4096]{0:T(1024)S(1)}, s32[4096]{0:T(1024)}, u32[]{:S(2)}) copy-start(s32[4096]{0:T(1024)} %add_select_fusion.1) | copy-start | bytes 49156
  250.1 46.5 %copy-start.10 = (f32[3,4096]{1,0:T(4,128)S(1)}, f32[3,4096]{1,0:T(4,128)}, u32[]{:S(2)}) copy-start(f32[3,4096]{1,0:T(4,128)} %copy-done.8) | copy-start | bytes 147460
  250.1 46.5 %copy-start.12 = (f32[3,4096]{1,0:T(4,128)S(1)}, f32[3,4096]{1,0:T(4,128)}, u32[]{:S(2)}) copy-start(f32[3,4096]{1,0:T(4,128)} %copy-done.11) | copy-start | bytes 147460
  251.9 4.4 %collective-permute-start.10 = (bf16[1,3,4096]{2,1,0:T(4,128)(2,1)S(1)}, bf16[1,3,4096]{2,1,0:T(4,128)(2,1)S(1)}, u32[]{:S(2)}, u32[]{:S(2)}) collective-permute-start(bf16[1,3,4096]{2,1,0:T(4,128)(2,1)S(1)} %get-tuple-element.559), channel_id=1, source_target_pairs={{0,1},{1,2},{2,3},{3,4},{4,5},{5,6},{6,7},{7,8},{8,9},{9,10},{10,1... | collective-permute-start | bytes 73736 | tf_op jit(solution)/shard_map/ppermute | solution.py:23
  253.8 8.8 %collective-permute-start.11 = (bf16[1,3,4096]{2,1,0:T(4,128)(2,1)S(1)}, bf16[1,3,4096]{2,1,0:T(4,128)(2,1)S(1)}, u32[]{:S(2)}, u32[]{:S(2)}) collective-permute-start(bf16[1,3,4096]{2,1,0:T(4,128)(2,1)S(1)} %get-tuple-element.559), channel_id=1, source_target_pairs={{1,0},{2,1},{3,2},{4,3},{5,4},{6,5},{7,6},{8,7},{9,8},{10,9},{11,1... | collective-permute-start | bytes 73736 | tf_op jit(solution)/shard_map/ppermute | solution.py:24
  262.8 4.4 %collective-permute-start.12 = (bf16[1,3,4096]{2,1,0:T(4,128)(2,1)S(1)}, bf16[1,3,4096]{2,1,0:T(4,128)(2,1)S(1)}, u32[]{:S(2)}, u32[]{:S(2)}) collective-permute-start(bf16[1,3,4096]{2,1,0:T(4,128)(2,1)S(1)} %get-tuple-element.557), channel_id=1, source_target_pairs={{0,1},{1,2},{2,3},{3,4},{4,5},{5,6},{6,7},{7,8},{8,9},{9,10},{10,1... | collective-permute-start | bytes 73736 | tf_op jit(solution)/shard_map/ppermute | solution.py:23
  264.7 8.8 %collective-permute-start.13 = (bf16[1,3,4096]{2,1,0:T(4,128)(2,1)S(1)}, bf16[1,3,4096]{2,1,0:T(4,128)(2,1)S(1)}, u32[]{:S(2)}, u32[]{:S(2)}) collective-permute-start(bf16[1,3,4096]{2,1,0:T(4,128)(2,1)S(1)} %get-tuple-element.557), channel_id=1, source_target_pairs={{1,0},{2,1},{3,2},{4,3},{5,4},{6,5},{7,6},{8,7},{9,8},{10,9},{11,1... | collective-permute-start | bytes 73736 | tf_op jit(solution)/shard_map/ppermute | solution.py:24
  273.7 4.4 %collective-permute-start.14 = (bf16[1,3,4096]{2,1,0:T(4,128)(2,1)S(1)}, bf16[1,3,4096]{2,1,0:T(4,128)(2,1)S(1)}, u32[]{:S(2)}, u32[]{:S(2)}) collective-permute-start(bf16[1,3,4096]{2,1,0:T(4,128)(2,1)S(1)} %get-tuple-element.555), channel_id=1, source_target_pairs={{0,1},{1,2},{2,3},{3,4},{4,5},{5,6},{6,7},{7,8},{8,9},{9,10},{10,1... | collective-permute-start | bytes 73736 | tf_op jit(solution)/shard_map/ppermute | solution.py:23
  275.6 8.8 %collective-permute-start.15 = (bf16[1,3,4096]{2,1,0:T(4,128)(2,1)S(1)}, bf16[1,3,4096]{2,1,0:T(4,128)(2,1)S(1)}, u32[]{:S(2)}, u32[]{:S(2)}) collective-permute-start(bf16[1,3,4096]{2,1,0:T(4,128)(2,1)S(1)} %get-tuple-element.555), channel_id=1, source_target_pairs={{1,0},{2,1},{3,2},{4,3},{5,4},{6,5},{7,6},{8,7},{9,8},{10,9},{11,1... | collective-permute-start | bytes 73736 | tf_op jit(solution)/shard_map/ppermute | solution.py:24
  284.6 4.4 %collective-permute-start.16 = (bf16[1,3,4096]{2,1,0:T(4,128)(2,1)S(1)}, bf16[1,3,4096]{2,1,0:T(4,128)(2,1)S(1)}, u32[]{:S(2)}, u32[]{:S(2)}) collective-permute-start(bf16[1,3,4096]{2,1,0:T(4,128)(2,1)S(1)} %get-tuple-element.553), channel_id=1, source_target_pairs={{0,1},{1,2},{2,3},{3,4},{4,5},{5,6},{6,7},{7,8},{8,9},{9,10},{10,1... | collective-permute-start | bytes 73736 | tf_op jit(solution)/shard_map/ppermute | solution.py:23
  286.5 8.8 %collective-permute-start.17 = (bf16[1,3,4096]{2,1,0:T(4,128)(2,1)S(1)}, bf16[1,3,4096]{2,1,0:T(4,128)(2,1)S(1)}, u32[]{:S(2)}, u32[]{:S(2)}) collective-permute-start(bf16[1,3,4096]{2,1,0:T(4,128)(2,1)S(1)} %get-tuple-element.553), channel_id=1, source_target_pairs={{1,0},{2,1},{3,2},{4,3},{5,4},{6,5},{7,6},{8,7},{9,8},{10,9},{11,1... | collective-permute-start | bytes 73736 | tf_op jit(solution)/shard_map/ppermute | solution.py:24
  (29 other events, 47.7 us)
where the time goes:
time: 302 us; the launch traced here: 297 us
  other arithmetic  99.5 us (33%)
  matrix products  65.2 us (22%)
  waiting for transfers between devices  42.1 us (14%)
  starting transfers between devices  40 us (13%)
  blocking collectives  27.8 us (9%)
  local copies, waits for them, and re-layouts  19.2 us (6%)
    dot_general x55, matrix products, lookup_one_block(): jnp.dot(padded, onehot, preferred_element_type=jnp.float32, precision=pre...  63.7 us
    select_n x51, other arithmetic, lookup_one_block(): chosen = piece[None, :] // 128 == group_ids[:, None]  54.6 us
    psum x1, blocking collectives, body(): coarse_rhs = lax.psum(rhs_part, 'dom')  27.8 us
    ppermute x6, waiting for transfers between devices, with_halo(): after = lax.ppermute(initial, axis, down)  25.3 us
    reduce_sum x48, other arithmetic, lookup_one_block(): return jnp.sum(jnp.where(chosen[None, :, :], spread, 0.0), axis=1)  25.3 us
    ppermute x6, starting transfers between devices, with_halo(): before = lax.ppermute(last, axis, up)  20.9 us
    ppermute x6, waiting for transfers between devices, passed_along(): return lax.ppermute(value, axis, pairs)  16.7 us
    ppermute x6, starting transfers between devices, with_halo(): after = lax.ppermute(initial, axis, down)  12.2 us
  transfers between devices with their start and end apart: 18, of which 7 were waited for; matrix products, arithmetic and copies ran while one was open for 60% of the time, Pallas kernels for 0%

commit v1 on v0

v1 whole, which is shorter than its diff:
```python
import functools

import jax
import jax.numpy as jnp
from jax import lax
from jax.experimental import pallas as pl
from jax.experimental.pallas import tpu as pltpu
from jax.sharding import PartitionSpec as P

SWEEPS = 3
JAC = 6
LOW_EIG = 0.3
HIGH_EIG = 2.2
CENTER = (HIGH_EIG + LOW_EIG) / 2.0
HALF = (HIGH_EIG - LOW_EIG) / 2.0
LANES = 128
F32 = jnp.float32
BF16 = jnp.bfloat16
VMEM = pltpu.VMEM


def lane_gather(rows, index):
    numbers = lax.GatherDimensionNumbers(
        offset_dims=(),
        collapsed_slice_dims=(1,),
        start_index_map=(1,),
        operand_batching_dims=(0,),
        start_indices_batching_dims=(0,),
    )
    return lax.gather(
        rows,
        index[..., None],
        numbers,
        (1, 1),
        mode=lax.GatherScatterMode.PROMISE_IN_BOUNDS,
    )


def call(kernel, out, inputs, scratch=(), us=1.0, smem=()):
    specs = [
        pl.BlockSpec(memory_space=pltpu.SMEM if i in smem else VMEM) for i in range(len(inputs))
    ]
    return pl.pallas_call(
        kernel,
        out_shape=out,
        in_specs=specs,
        out_specs=jax.tree.map(lambda _: pl.BlockSpec(memory_space=VMEM), out),
        scratch_shapes=list(scratch),
        cost_estimate=pl.CostEstimate(
            flops=int(us * 1.0e9), transcendentals=0, bytes_accessed=int(us * 1.0e6)
        ),
    )(*inputs)


def point_solve(matrix_ref, vector):
    return [jnp.sum(matrix_ref[c] * vector, axis=0, keepdims=True) for c in range(3)]


def first_kernel(dinv, residual, smooth, packed):
    solved = point_solve(dinv, residual[...])
    for c in range(3):
        row = solved[c] * (1.0 / CENTER)
        smooth[c : c + 1, :] = row
        packed[c : c + 1, :] = row.astype(BF16)


def restrict_kernel(residual, local_agg, out):
    points = residual.shape[1]
    groups = out.shape[1]
    agg = local_agg[...]
    low = (agg & (LANES - 1)).astype(jnp.int16)
    high = (agg >> 7).astype(jnp.int16)
    width = 512
    total = [jnp.zeros((2 * groups, LANES), F32) for c in range(3)]
    lane_ids = lax.broadcasted_iota(jnp.int16, (LANES, width), 0)
    group_ids = lax.broadcasted_iota(jnp.int16, (groups, width), 0)
    for block in range(points // width):
        part = slice(block * width, (block + 1) * width)
        onehot = jnp.where(
            jnp.broadcast_to(low[:, part], (LANES, width)) == lane_ids,
            jnp.ones((), BF16),
            jnp.zeros((), BF16),
        )
        chosen = jnp.broadcast_to(high[:, part], (groups, width)) == group_ids
        for c in range(3):
            value = residual[c : c + 1, part]
            upper = value.astype(BF16)
            lower = (value - upper.astype(F32)).astype(BF16)
            zero = jnp.zeros((), BF16)
            both = jnp.concatenate(
                [
                    jnp.where(chosen, jnp.broadcast_to(upper, (groups, width)), zero),
                    jnp.where(chosen, jnp.broadcast_to(lower, (groups, width)), zero),
                ],
                axis=0,
            )
            total[c] = total[c] + lax.dot_general(
                both, onehot, (((1,), (1,)), ((), ())), preferred_element_type=F32
            )
    for c in range(3):
        out[c] = total[c][:groups] + total[c][groups:]


def base_kernel(rhs, dinv, base, packed):
    groups = rhs.shape[1]
    for g in range(groups):
        lanes = slice(g * LANES, (g + 1) * LANES)
        vector = jnp.concatenate([rhs[e, g : g + 1, :] for e in range(3)], axis=0)
        for c in range(3):
            base[c, g : g + 1, :] = jnp.sum(dinv[c, :, lanes] * vector, axis=0, keepdims=True)
    for c in range(3):
        packed[c] = base[c].astype(BF16)


def fill_table(table, source, groups):
    for e in range(3):
        for g in range(groups):
            row = source[e, g : g + 1, :]
            table[e, g] = jnp.broadcast_to(row, (16, LANES)).astype(BF16)


def pick(table, index, groups, first, starts):
    low = (index & (LANES - 1)).astype(jnp.int16)
    high = (index >> 7).astype(jnp.int16)
    picked = list(starts)
    for g in range(groups):
        chosen = high == (first + g)
        for e in range(3):
            value = lane_gather(table[e, g], low)
            picked[e] = jnp.where(chosen, value, picked[e])
    return picked


def local_kernel(smooth, col, out, table, *, first, tiles):
    groups = smooth.shape[1] // LANES
    for e in range(3):
        for g in range(groups):
            row = smooth[e : e + 1, g * LANES : (g + 1) * LANES]
            table[e, g] = jnp.broadcast_to(row, (16, LANES)).astype(BF16)
    bonds_of = col.shape[0]
    zero = jnp.zeros((16, LANES), BF16)

    def one_tile(t, carry):
        source = pl.multiple_of((first + t) * LANES, LANES)
        target = pl.multiple_of(t * LANES, LANES)
        for h in range(bonds_of // 16):
            index = col[pl.ds(h * 16, 16), pl.ds(source, LANES)]
            picked = pick(table, index, groups, 0, [zero] * 3)
            for e in range(3):
                out[e, pl.ds(h * 16, 16), pl.ds(target, LANES)] = picked[e]
        return carry

    lax.fori_loop(0, tiles, one_tile, 0)


def halo_kernel(*refs, pieces, scale_old, scale_new):
    (col, ghost, prev, follow, residual, dinv, smooth, update, bonds) = refs[:9]
    picked_refs = refs[9 : 9 + pieces]
    new_smooth, new_update, packed = refs[9 + pieces : 12 + pieces]
    slots, table, applied = refs[12 + pieces :]
    points = smooth.shape[1]
    groups = points // LANES
    wanted = ghost[...]
    half = wanted.shape[0] // 2
    low = wanted & (LANES - 1)
    high = wanted >> 7
    upper = lax.broadcasted_iota(jnp.int32, wanted.shape, 0) < half
    found = [jnp.zeros(wanted.shape, F32)] * 3
    for g in range(groups):
        lanes = slice(g * LANES, (g + 1) * LANES)
        chosen = high == g
        for e in range(3):
            rows = jnp.where(
                upper,
                jnp.broadcast_to(prev[e : e + 1, lanes].astype(F32), wanted.shape),
                jnp.broadcast_to(follow[e : e + 1, lanes].astype(F32), wanted.shape),
            )
            found[e] = jnp.where(chosen, lane_gather(rows, low), found[e])
    for e in range(3):
        slots[e] = found[e]
    halo_groups = wanted.shape[0]
    fill_table(table, slots, halo_groups)
    bonds_of = col.shape[0]
    tiles_of = groups // pieces

    for piece in range(pieces):

        def one_tile(t, carry, piece=piece):
            here = pl.multiple_of((piece * tiles_of + t) * LANES, LANES)
            there = pl.multiple_of(t * LANES, LANES)
            total = [jnp.zeros((16, LANES), F32)] * 3
            for h in range(bonds_of // 16):
                rows = pl.ds(h * 16, 16)
                index = col[rows, pl.ds(here, LANES)]
                starts = [picked_refs[piece][e, rows, pl.ds(there, LANES)] for e in range(3)]
                picked = pick(table, index, halo_groups, groups, starts)
                wide = [value.astype(F32) for value in picked]
                for c in range(3):
                    for e in range(3):
                        total[c] = (
                            total[c] + bonds[c, e, rows, pl.ds(here, LANES)].astype(F32) * wide[e]
                        )
            for c in range(3):
                applied[c : c + 1, pl.ds(here, LANES)] = jnp.sum(total[c], axis=0, keepdims=True)
            return carry

        lax.fori_loop(0, tiles_of, one_tile, 0)
    remainder = residual[...] - smooth[...] - applied[...]
    solved = point_solve(dinv, remainder)
    for c in range(3):
        row = scale_old * update[c : c + 1, :] + scale_new * solved[c]
        new_update[c : c + 1, :] = row
        total = smooth[c : c + 1, :] + row
        new_smooth[c : c + 1, :] = total
        packed[c : c + 1, :] = total.astype(BF16)


def coarse_kernel(place, base, bases, own_couple, couples, local_agg, smooth, out, field, links):
    subs, me = place[0], place[1]
    groups = base.shape[1]
    steps = JAC - 1

    def valid(row):
        inside = jnp.logical_and(me + row >= 0, me + row < subs)
        return jnp.where(inside, 1.0, 0.0).astype(F32)

    def base_of(row, c):
        if row == 0:
            return base[c]
        slot = row + steps if row < 0 else row + steps - 1
        return bases[slot * 3 + c].astype(F32) * valid(row)

    for k in range(4):
        for g in range(groups):
            links[steps - 1, k, g : g + 1, :] = own_couple[
                k : k + 1, g * LANES : (g + 1) * LANES
            ]
    reach = steps - 1
    for row in range(-reach, reach + 1):
        if row == 0:
            continue
        slot = row + reach if row < 0 else row + reach - 1
        for k in range(4):
            links[row + reach, k] = couples[slot * 4 + k].astype(F32) * valid(row)
    for row in range(-steps, steps + 1):
        for c in range(3):
            field[0, row + steps, c] = base_of(row, c)
    lane = lax.broadcasted_iota(jnp.int32, (groups, LANES), 1)
    line = lax.broadcasted_iota(jnp.int32, (groups, LANES), 0)
    for step in range(steps):
        old, new = step % 2, (step + 1) % 2
        reach = steps - 1 - step
        for row in range(-reach, reach + 1):
            spot = row + steps
            weights = [links[row + steps - 1, k] for k in range(4)]
            for c in range(3):
                x = field[old, spot, c]
                right = pltpu.roll(x, 1, 1)
                right = jnp.where(lane == 0, pltpu.roll(right, 1, 0), right)
                right = jnp.where(jnp.logical_and(lane == 0, line == 0), 0.0, right)
                left = pltpu.roll(x, LANES - 1, 1)
                left = jnp.where(lane == LANES - 1, pltpu.roll(left, groups - 1, 0), left)
                left = jnp.where(
                    jnp.logical_and(lane == LANES - 1, line == groups - 1), 0.0, left
                )
                field[new, spot, c] = base_of(row, c) + (
                    weights[0] * field[old, spot - 1, c]
                    + weights[1] * field[old, spot + 1, c]
                    + weights[2] * right
                    + weights[3] * left
                )
    final = steps % 2
    agg = local_agg[...]
    for block in range(agg.shape[0] // 8):
        index = agg[block * 8 : (block + 1) * 8]
        low = index & (LANES - 1)
        high = index >> 7
        found = [jnp.zeros((8, LANES), F32)] * 3
        for g in range(groups):
            chosen = high == g
            for c in range(3):
                rows = jnp.broadcast_to(field[final, steps, c, g : g + 1, :], (8, LANES))
                found[c] = jnp.where(chosen, lane_gather(rows, low), found[c])
        for c in range(3):
            for r in range(8):
                lanes = slice((block * 8 + r) * LANES, (block * 8 + r + 1) * LANES)
                out[c : c + 1, lanes] = smooth[c : c + 1, lanes] + found[c][r : r + 1]


def shifted(value, steps):
    count = lax.axis_size("sub")
    return lax.ppermute(value, "sub", [(i, (i + steps) % count) for i in range(count)])


def body(
    fine_residual, bonds, bond_col, ghost_points, fine_dinv, aggregate, coarse_dinv, coarse_couple
):
    points = fine_residual.shape[1]
    groups = points // LANES
    bonds_of = bond_col.shape[0]
    per_group = coarse_dinv.shape[2]
    coarse_groups = per_group // LANES
    sub = lax.axis_index("sub")
    ghost = ghost_points.reshape(-1, LANES)
    sds = jax.ShapeDtypeStruct
    field = sds((3, points), F32)
    packed_field = sds((3, points), BF16)

    smooth, packed = call(first_kernel, (field, packed_field), (fine_dinv, fine_residual), us=0.5)
    update = smooth
    local_agg = aggregate - sub * per_group
    couple_rows = coarse_couple.astype(BF16).reshape(4, coarse_groups, LANES)
    message = jnp.concatenate([packed.reshape(3, groups, LANES), couple_rows], axis=0)
    after = shifted(message, 1)
    before = shifted(message, -1)

    rhs = call(
        restrict_kernel,
        sds((3, coarse_groups, LANES), F32),
        (fine_residual, local_agg.reshape(1, points)),
        us=1.5,
    )
    relaid = bonds.transpose(1, 2, 0, 3)
    doms = lax.axis_size("dom")
    step = 1
    while step < doms:
        rhs = rhs + lax.ppermute(rhs, "dom", [(i, i ^ step) for i in range(doms)])
        step *= 2
    coarse_field = sds((3, coarse_groups, LANES), F32)
    base, packed_base = call(
        base_kernel,
        (coarse_field, sds(coarse_field.shape, BF16)),
        (rhs, coarse_dinv),
        us=0.5,
    )

    def gather_local(smooth, pieces):
        tiles = groups // pieces
        return [
            call(
                functools.partial(local_kernel, first=piece * tiles, tiles=tiles),
                sds((3, bonds_of, tiles * LANES), BF16),
                (smooth, bond_col),
                scratch=[VMEM((3, groups, 16, LANES), BF16)],
                us=8.0 / pieces,
            )
            for piece in range(pieces)
        ]

    factor = HALF / CENTER
    base_rows = {0: packed_base}
    link_rows = {0: couple_rows, -1: after[3:], 1: before[3:]}
    for sweep, pieces in enumerate((4, 2, 2)):
        factor_new = 1.0 / (2.0 * CENTER / HALF - factor)
        parts = gather_local(smooth, pieces)
        smooth, update, packed = call(
            functools.partial(
                halo_kernel,
                pieces=pieces,
                scale_old=factor_new * factor,
                scale_new=2.0 * factor_new / HALF,
            ),
            (field, field, packed_field),
            (
                bond_col,
                ghost,
                after[:3].reshape(3, points),
                before[:3].reshape(3, points),
                fine_residual,
                fine_dinv,
                smooth,
                update,
                relaid,
                *parts,
            ),
            scratch=[
                VMEM((3,) + ghost.shape, F32),
                VMEM((3, ghost.shape[0], 16, LANES), BF16),
                VMEM((3, points), F32),
            ],
            us=4.0,
        )
        factor = factor_new
        shaped = packed.reshape(3, groups, LANES)
        if sweep == 0:
            after = shifted(jnp.concatenate([shaped, base_rows[0], link_rows[-1]], axis=0), 1)
            before = shifted(jnp.concatenate([shaped, base_rows[0], link_rows[1]], axis=0), -1)
            base_rows[-1], base_rows[1] = after[3:6], before[3:6]
            link_rows[-2], link_rows[2] = after[6:], before[6:]
        elif sweep == 1:
            after = shifted(jnp.concatenate([shaped, base_rows[-1]], axis=0), 1)
            before = shifted(jnp.concatenate([shaped, base_rows[1]], axis=0), -1)
            base_rows[-2], base_rows[2] = after[3:6], before[3:6]
            far_after = shifted(
                jnp.concatenate(
                    [base_rows[-2], base_rows[-1], base_rows[0], link_rows[-1], link_rows[0]],
                    axis=0,
                ),
                3,
            )
            far_before = shifted(
                jnp.concatenate(
                    [base_rows[0], base_rows[1], base_rows[2], link_rows[0], link_rows[1]],
                    axis=0,
                ),
                -3,
            )
    bases = jnp.concatenate(
        [far_after[:9], base_rows[-2], base_rows[-1], base_rows[1], base_rows[2], far_before[:9]],
        axis=0,
    )
    couples = jnp.concatenate(
        [
            far_after[9:],
            link_rows[-2],
            link_rows[-1],
            link_rows[1],
            link_rows[2],
            far_before[9:],
        ],
        axis=0,
    )
    place = jnp.stack([jnp.int32(lax.axis_size("sub")), sub.astype(jnp.int32)])
    steps = JAC - 1
    return call(
        coarse_kernel,
        field,
        (
            place,
            base,
            bases,
            coarse_couple,
            couples,
            local_agg.reshape(groups, LANES),
            smooth,
        ),
        scratch=[
            VMEM((2, 2 * steps + 1, 3, coarse_groups, LANES), F32),
            VMEM((2 * steps - 1, 4, coarse_groups, LANES), F32),
        ],
        us=2.0,
        smem=(0,),
    )


def solution(mesh):
    placed = (
        P(None, ("dom", "sub")),
        P(None, None, None, ("dom", "sub")),
        P(None, ("dom", "sub")),
        P(("dom", "sub"), None, None),
        P(None, None, ("dom", "sub")),
        P(("dom", "sub")),
        P(None, None, "sub"),
        P(None, "sub"),
    )
    return jax.shard_map(
        body, mesh=mesh, in_specs=placed, out_specs=P(None, ("dom", "sub")), check_vma=False
    )
```

time: 302 us -> 121 us (0.40)
  the two profiles are of different devices: /device:TPU:101 before, /device:TPU:1 now
where the time goes in v1:
time: 121 us; the launch traced here: 120 us
  Pallas kernels  73.7 us (61%)
  starting transfers between devices  24 us (20%)
  waiting for transfers between devices  10.9 us (9%)
  local copies, waits for them, and re-layouts  6.31 us (5%)
  other arithmetic  4.83 us (4%)
    pallas_call x15, Pallas kernels, call(): pl.pallas_call(kernel, out_shape=out, in_specs=specs, out_specs=jax.tree....  73.7 us
    ppermute x8, starting transfers between devices, shifted(): lax.ppermute(value, 'sub', [(i, (i + steps) % count) for i in range(count)])  18.9 us
    ppermute x8, waiting for transfers between devices, shifted(): lax.ppermute(value, 'sub', [(i, (i + steps) % count) for i in range(count)])  10.9 us
    ppermute x3, starting transfers between devices, body(): rhs = rhs + lax.ppermute(rhs, 'dom', [(i, i ^ step) for i in range(doms)])  5.16 us
    unnamed x38, local copies, waits for them, and re-layouts  4.99 us
  transfers between devices with their start and end apart: 11, of which 4 were waited for; matrix products, arithmetic and copies ran while one was open for 5% of the time, Pallas kernels for 50%

profile of v1, /device:TPU:1, one launch (start us, length us, event | category | flops | bytes accessed | tf_op | source)
XLA Modules:
  0.0 120.0 jit_solution(13413433528694753922)
XLA Ops:
  0.0 0.9 convert_bitcast_fusion
  0.9 1.7 %shard_map.84 = (f32[3,4096]{1,0:T(4,128)}, bf16[3,4096]{1,0:T(4,128)(2,1)}) custom-call(f32[3,3,4096]{2,1,0:T(4,128)} %refs_5_.5, f32[3,4096]{1,0:T(4,128)} %refs_4_.5), custom_call_target="tpu_custom_call" | custom-call | flops 500000000 | bytes 500000 | tf_op jit(solution)/shard_map/pallas_call | solution.py:43
  2.6 0.8 constant_dynamic-update-slice_fusion.1
  3.4 3.3 %collective-permute-start.4 = (bf16[7,32,128]{2,1,0:T(8,128)(2,1)S(1)}, bf16[7,32,128]{2,1,0:T(8,128)(2,1)S(1)}, u32[]{:S(2)}, u32[]{:S(2)}) collective-permute-start(bf16[7,32,128]{2,1,0:T(8,128)(2,1)S(1)} %constant_dynamic-update-slice_fusion), channel_id=1, source_target_pairs={{0,31},{1,0},{2,1},{3,2},{4,3},{5,4},{6,5},{7,6},{8,7},{9,8},{10,9... | collective-permute-start | bytes 172040 | tf_op jit(solution)/shard_map/ppermute | solution.py:292
  6.7 1.0 collective-permute-start.3
  7.7 1.3 %broadcast_subtract_fusion = s32[4096]{0:T(1024)} fusion(s32[4096]{0:T(1024)} %param.13, s32[]{:T(128)S(6)} %mul.3), kind=kLoop, calls=%fused_computation.44 | loop fusion | flops 4096 | bytes 32772 | tf_op jit(solution)/shard_map/sub | solution.py:311
  9.0 2.7 %shard_map.82 = f32[3,32,128]{2,1,0:T(8,128)} custom-call(f32[3,4096]{1,0:T(4,128)} %refs_4_.5, s32[1,4096]{1,0:T(1,128)} %bitcast.60), custom_call_target="tpu_custom_call" | custom-call | flops 1500000000 | bytes 1500000 | tf_op jit(solution)/shard_map/pallas_call | solution.py:43
  11.7 1.1 collective-permute-start
  13.3 4.0 %shard_map.88.refs_12_ = bf16[3,32,1024]{2,1,0:T(8,128)(2,1)} custom-call(f32[3,4096]{1,0:T(4,128)} %get-tuple-element.18.smooth.refs_6_.refs_7_, s32[32,4096]{1,0:T(8,128)} %refs_0_.5), custom_call_target="tpu_custom_call" | custom-call | flops 2000000000 | bytes 2000000 | tf_op jit(solution)/shard_map/pallas_call | solution.py:43
  17.4 4.0 %shard_map.87.refs_11_ = bf16[3,32,1024]{2,1,0:T(8,128)(2,1)} custom-call(f32[3,4096]{1,0:T(4,128)} %get-tuple-element.18.smooth.refs_6_.refs_7_, s32[32,4096]{1,0:T(8,128)} %refs_0_.5), custom_call_target="tpu_custom_call" | custom-call | flops 2000000000 | bytes 2000000 | tf_op jit(solution)/shard_map/pallas_call | solution.py:43
  21.4 4.0 %shard_map.86.refs_10_ = bf16[3,32,1024]{2,1,0:T(8,128)(2,1)} custom-call(f32[3,4096]{1,0:T(4,128)} %get-tuple-element.18.smooth.refs_6_.refs_7_, s32[32,4096]{1,0:T(8,128)} %refs_0_.5), custom_call_target="tpu_custom_call" | custom-call | flops 2000000000 | bytes 2000000 | tf_op jit(solution)/shard_map/pallas_call | solution.py:43
  25.4 4.0 %shard_map.85.refs_9_ = bf16[3,32,1024]{2,1,0:T(8,128)(2,1)} custom-call(f32[3,4096]{1,0:T(4,128)} %get-tuple-element.18.smooth.refs_6_.refs_7_, s32[32,4096]{1,0:T(8,128)} %refs_0_.5), custom_call_target="tpu_custom_call" | custom-call | flops 2000000000 | bytes 2000000 | tf_op jit(solution)/shard_map/pallas_call | solution.py:43
  30.7 1.4 %collective-permute-start.1 = (f32[3,32,128]{2,1,0:T(8,128)S(1)}, f32[3,32,128]{2,1,0:T(8,128)S(1)}, u32[]{:S(2)}, u32[]{:S(2)}) collective-permute-start(f32[3,32,128]{2,1,0:T(8,128)S(1)} %add.9), channel_id=1, source_target_pairs={{0,64},{32,96},{64,0},{96,32},{128,192},{160,224},{192,128},{224,1... | collective-permute-start | bytes 147464 | tf_op jit(solution)/shard_map/ppermute | solution.py:327
  33.4 7.7 %shard_map.89 = (f32[3,4096]{1,0:T(4,128)}, f32[3,4096]{1,0:T(4,128)}, bf16[3,4096]{1,0:T(4,128)(2,1)}) custom-call(s32[32,4096]{1,0:T(8,128)} %refs_0_.5, s32[8,128]{1,0:T(8,128)} %reshape.40.refs_1_, bf16[3,4096]{1,0:T(4,128)(2,1)} %bitcast.56, bf16[3,4096]{1,0:T(4,128)(2,1)} %bitcast.55, f32[3,4096]{1,0:T(4,128)} %refs_4_.5, f32[3,3,4096]{2,1,0:T(4,128)} %refs_5_.5, ...), custom_call_target="tpu_custom_call" | custom-call | flops 4000000000 | bytes 4000000 | tf_op jit(solution)/shard_map/pallas_call | solution.py:43
  41.1 2.7 %collective-permute-start.2 = (f32[3,32,128]{2,1,0:T(8,128)S(1)}, f32[3,32,128]{2,1,0:T(8,128)S(1)}, u32[]{:S(2)}, u32[]{:S(2)}) collective-permute-start(f32[3,32,128]{2,1,0:T(8,128)S(1)} %add.10), channel_id=1, source_target_pairs={{0,128},{32,160},{64,192},{96,224},{128,0},{160,32},{192,64},{224,... | collective-permute-start | bytes 147464 | tf_op jit(solution)/shard_map/ppermute | solution.py:327
  43.8 6.4 %shard_map.91.refs_10_ = bf16[3,32,2048]{2,1,0:T(8,128)(2,1)} custom-call(f32[3,4096]{1,0:T(4,128)} %get-tuple-element.21.smooth.refs_6_, s32[32,4096]{1,0:T(8,128)} %refs_0_.5), custom_call_target="tpu_custom_call" | custom-call | flops 4000000000 | bytes 4000000 | tf_op jit(solution)/shard_map/pallas_call | solution.py:43
  50.9 1.7 %shard_map.83 = (f32[3,32,128]{2,1,0:T(8,128)}, bf16[3,32,128]{2,1,0:T(8,128)(2,1)}) custom-call(f32[3,32,128]{2,1,0:T(8,128)} %add.11.rhs, f32[3,3,4096]{2,1,0:T(4,128)} %dinv.2), custom_call_target="tpu_custom_call" | custom-call | flops 500000000 | bytes 500000 | tf_op jit(solution)/shard_map/pallas_call | solution.py:43
  52.6 0.8 pad_maximum_fusion.2
  53.3 5.2 %collective-permute-start.6 = (bf16[10,32,128]{2,1,0:T(8,128)(2,1)S(1)}, bf16[10,32,128]{2,1,0:T(8,128)(2,1)S(1)}, u32[]{:S(2)}, u32[]{:S(2)}) collective-permute-start(bf16[10,32,128]{2,1,0:T(8,128)(2,1)S(1)} %get-tuple-element.39), channel_id=1, source_target_pairs={{0,31},{1,0},{2,1},{3,2},{4,3},{5,4},{6,5},{7,6},{8,7},{9,8},{10,9... | collective-permute-start | bytes 245768 | tf_op jit(solution)/shard_map/ppermute | solution.py:292
  58.5 6.4 %shard_map.90.refs_9_ = bf16[3,32,2048]{2,1,0:T(8,128)(2,1)} custom-call(f32[3,4096]{1,0:T(4,128)} %get-tuple-element.21.smooth.refs_6_, s32[32,4096]{1,0:T(8,128)} %refs_0_.5), custom_call_target="tpu_custom_call" | custom-call | flops 4000000000 | bytes 4000000 | tf_op jit(solution)/shard_map/pallas_call | solution.py:43
  65.5 5.3 %collective-permute-done.5 = bf16[10,32,128]{2,1,0:T(8,128)(2,1)S(1)} collective-permute-done((bf16[10,32,128]{2,1,0:T(8,128)(2,1)S(1)}, bf16[10,32,128]{2,1,0:T(8,128)(2,1)S(1)}, u32[]{:S(2)}, u32[]{:S(2)}) %collective-permute-start.5) | collective-permute-done | bytes 81952 | tf_op jit(solution)/shard_map/ppermute | solution.py:292
  71.4 7.7 %shard_map.92 = (f32[3,4096]{1,0:T(4,128)}, f32[3,4096]{1,0:T(4,128)}, bf16[3,4096]{1,0:T(4,128)(2,1)}) custom-call(s32[32,4096]{1,0:T(8,128)} %refs_0_.5, s32[8,128]{1,0:T(8,128)} %reshape.40.refs_1_, bf16[3,4096]{1,0:T(4,128)(2,1)} %bitcast.57, bf16[3,4096]{1,0:T(4,128)(2,1)} %bitcast.54, f32[3,4096]{1,0:T(4,128)} %refs_4_.5, f32[3,3,4096]{2,1,0:T(4,128)} %refs_5_.5, ...), custom_call_target="tpu_custom_call" | custom-call | flops 4000000000 | bytes 4000000 | tf_op jit(solution)/shard_map/pallas_call | solution.py:43
  79.1 0.8 copy.35
  79.9 6.4 %shard_map.94.refs_10_ = bf16[3,32,2048]{2,1,0:T(8,128)(2,1)} custom-call(f32[3,4096]{1,0:T(4,128)} %get-tuple-element.24.smooth.refs_6_, s32[32,4096]{1,0:T(8,128)} %refs_0_.5), custom_call_target="tpu_custom_call" | custom-call | flops 4000000000 | bytes 4000000 | tf_op jit(solution)/shard_map/pallas_call | solution.py:43
  86.3 1.0 collective-permute-done.7
  87.5 6.4 %shard_map.93.refs_9_ = bf16[3,32,2048]{2,1,0:T(8,128)(2,1)} custom-call(f32[3,4096]{1,0:T(4,128)} %get-tuple-element.24.smooth.refs_6_, s32[32,4096]{1,0:T(8,128)} %refs_0_.5), custom_call_target="tpu_custom_call" | custom-call | flops 4000000000 | bytes 4000000 | tf_op jit(solution)/shard_map/pallas_call | solution.py:43
  93.9 1.7 %collective-permute-done.8 = bf16[17,32,128]{2,1,0:T(8,128)(2,1)S(1)} collective-permute-done((bf16[17,32,128]{2,1,0:T(8,128)(2,1)S(1)}, bf16[17,32,128]{2,1,0:T(8,128)(2,1)S(1)}, u32[]{:S(2)}, u32[]{:S(2)}) %collective-permute-start.8) | collective-permute-done | bytes 139296 | tf_op jit(solution)/shard_map/ppermute | solution.py:292
  95.7 4.8 %collective-permute-start.9 = (bf16[6,32,128]{2,1,0:T(8,128)(2,1)S(1)}, bf16[6,32,128]{2,1,0:T(8,128)(2,1)S(1)}, u32[]{:S(2)}, u32[]{:S(2)}) collective-permute-start(bf16[6,32,128]{2,1,0:T(8,128)(2,1)S(1)} %pad_maximum_fusion.3), channel_id=1, source_target_pairs={{0,31},{1,0},{2,1},{3,2},{4,3},{5,4},{6,5},{7,6},{8,7},{9,8},{10,9... | collective-permute-start | bytes 147464 | tf_op jit(solution)/shard_map/ppermute | solution.py:292
  100.5 2.9 %collective-permute-done.9 = bf16[6,32,128]{2,1,0:T(8,128)(2,1)S(1)} collective-permute-done((bf16[6,32,128]{2,1,0:T(8,128)(2,1)S(1)}, bf16[6,32,128]{2,1,0:T(8,128)(2,1)S(1)}, u32[]{:S(2)}, u32[]{:S(2)}) %collective-permute-start.9) | collective-permute-done | bytes 49184 | tf_op jit(solution)/shard_map/ppermute | solution.py:292
  103.4 4.4 %collective-permute-start.10 = (bf16[17,32,128]{2,1,0:T(8,128)(2,1)S(1)}, bf16[17,32,128]{2,1,0:T(8,128)(2,1)S(1)}, u32[]{:S(2)}, u32[]{:S(2)}) collective-permute-start(bf16[17,32,128]{2,1,0:T(8,128)(2,1)S(1)} %get-tuple-element.33), channel_id=1, source_target_pairs={{0,29},{1,30},{2,31},{3,0},{4,1},{5,2},{6,3},{7,4},{8,5},{9,6},{10... | collective-permute-start | bytes 417800 | tf_op jit(solution)/shard_map/ppermute | solution.py:292
  108.5 7.7 %shard_map.95 = (f32[3,4096]{1,0:T(4,128)}, f32[3,4096]{1,0:T(4,128)}, bf16[3,4096]{1,0:T(4,128)(2,1)}) custom-call(s32[32,4096]{1,0:T(8,128)} %refs_0_.5, s32[8,128]{1,0:T(8,128)} %reshape.40.refs_1_, bf16[3,4096]{1,0:T(4,128)(2,1)} %get-tuple-element.46.refs_2_, bf16[3,4096]{1,0:T(4,128)(2,1)} %get-tuple-element.45.refs_3_, f32[3,4096]{1,0:T(4,128)} %refs_4_.5, ...), custom_call_target="tpu_custom_call" | custom-call | flops 4000000000 | bytes 4000000 | tf_op jit(solution)/shard_map/pallas_call | solution.py:43
  117.0 3.0 %shard_map.96 = f32[3,4096]{1,0:T(4,128)} custom-call(s32[2]{0:T(128)} %pad_add_fusion.place, f32[3,32,128]{2,1,0:T(8,128)} %get-tuple-element.16.base, bf16[30,32,128]{2,1,0:T(8,128)(2,1)} %copy-done.4, f32[4,4096]{1,0:T(4,128)} %own_couple.1, bf16[32,32,128]{2,1,0:T(8,128)(2,1)} %copy-done.5, s32[32,128]{1,0:T(8,128)} %fusion.1.local_agg, ...), custom_call_target="tpu_custom_call" | custom-call | flops 2000000000 | bytes 2000000 | tf_op jit(solution)/shard_map/pallas_call | solution.py:43
  (62 shorter events, 6.9 us)
Async XLA Ops:
  3.4 28.8 %collective-permute-start.4 = (bf16[7,32,128]{2,1,0:T(8,128)(2,1)S(1)}, bf16[7,32,128]{2,1,0:T(8,128)(2,1)S(1)}, u32[]{:S(2)}, u32[]{:S(2)}) collective-permute-start(bf16[7,32,128]{2,1,0:T(8,128)(2,1)S(1)} %constant_dynamic-update-slice_fusion), channel_id=1, source_target_pairs={{0,31},{1,0},{2,1},{3,2},{4,3},{5,4},{6,5},{7,6},{8,7},{9,8},{10,9... | collective-permute-start | bytes 172040 | tf_op jit(solution)/shard_map/ppermute | solution.py:292
  6.7 26.1 %collective-permute-start.3 = (bf16[7,32,128]{2,1,0:T(8,128)(2,1)S(1)}, bf16[7,32,128]{2,1,0:T(8,128)(2,1)S(1)}, u32[]{:S(2)}, u32[]{:S(2)}) collective-permute-start(bf16[7,32,128]{2,1,0:T(8,128)(2,1)S(1)} %constant_dynamic-update-slice_fusion), channel_id=1, source_target_pairs={{0,1},{1,2},{2,3},{3,4},{4,5},{5,6},{6,7},{7,8},{8,9},{9,10},{10,1... | collective-permute-start | bytes 172040 | tf_op jit(solution)/shard_map/ppermute | solution.py:292
  9.0 3.7 %copy-start.1 = (s32[4096]{0:T(1024)S(1)}, s32[4096]{0:T(1024)}, u32[]{:S(2)}) copy-start(s32[4096]{0:T(1024)} %param.13) | copy-start | bytes 49156
  11.7 19.1 %collective-permute-start = (f32[3,32,128]{2,1,0:T(8,128)}, f32[3,32,128]{2,1,0:T(8,128)S(1)}, u32[]{:S(2)}, u32[]{:S(2)}) collective-permute-start(f32[3,32,128]{2,1,0:T(8,128)} %shard_map.82), channel_id=1, source_target_pairs={{0,32},{32,0},{64,96},{96,64},{128,160},{160,128},{192,224},{224,1... | collective-permute-start | bytes 147464 | tf_op jit(solution)/shard_map/ppermute | solution.py:327
  25.4 4.7 %copy-start.6 = (s32[1,2,512]{2,1,0:T(2,128)S(1)}, s32[1,2,512]{2,1,0:T(2,128)}, u32[]{:S(2)}) copy-start(s32[1,2,512]{2,1,0:T(2,128)} %param.11) | copy-start | bytes 12292
  25.4 5.3 %copy-start.2 = (f32[3,32,128]{2,1,0:T(8,128)S(1)}, f32[3,32,128]{2,1,0:T(8,128)}, u32[]{:S(2)}) copy-start(f32[3,32,128]{2,1,0:T(8,128)} %shard_map.82) | copy-start | bytes 147460
  30.7 10.4 %collective-permute-start.1 = (f32[3,32,128]{2,1,0:T(8,128)S(1)}, f32[3,32,128]{2,1,0:T(8,128)S(1)}, u32[]{:S(2)}, u32[]{:S(2)}) collective-permute-start(f32[3,32,128]{2,1,0:T(8,128)S(1)} %add.9), channel_id=1, source_target_pairs={{0,64},{32,96},{64,0},{96,32},{128,192},{160,224},{192,128},{224,1... | collective-permute-start | bytes 147464 | tf_op jit(solution)/shard_map/ppermute | solution.py:327
  41.1 9.1 %collective-permute-start.2 = (f32[3,32,128]{2,1,0:T(8,128)S(1)}, f32[3,32,128]{2,1,0:T(8,128)S(1)}, u32[]{:S(2)}, u32[]{:S(2)}) collective-permute-start(f32[3,32,128]{2,1,0:T(8,128)S(1)} %add.10), channel_id=1, source_target_pairs={{0,128},{32,160},{64,192},{96,224},{128,0},{160,32},{192,64},{224,... | collective-permute-start | bytes 147464 | tf_op jit(solution)/shard_map/ppermute | solution.py:327
  43.8 6.4 %copy-start.3 = (bf16[3,4096]{1,0:T(4,128)(2,1)S(1)}, bf16[3,4096]{1,0:T(4,128)(2,1)}, u32[]{:S(2)}) copy-start(bf16[3,4096]{1,0:T(4,128)(2,1)} %get-tuple-element.19) | copy-start | bytes 73732
  53.3 11.6 %collective-permute-start.6 = (bf16[10,32,128]{2,1,0:T(8,128)(2,1)S(1)}, bf16[10,32,128]{2,1,0:T(8,128)(2,1)S(1)}, u32[]{:S(2)}, u32[]{:S(2)}) collective-permute-start(bf16[10,32,128]{2,1,0:T(8,128)(2,1)S(1)} %get-tuple-element.39), channel_id=1, source_target_pairs={{0,31},{1,0},{2,1},{3,2},{4,3},{5,4},{6,5},{7,6},{8,7},{9,8},{10,9... | collective-permute-start | bytes 245768 | tf_op jit(solution)/shard_map/ppermute | solution.py:292
  64.9 5.9 %collective-permute-start.5 = (bf16[10,32,128]{2,1,0:T(8,128)(2,1)S(1)}, bf16[10,32,128]{2,1,0:T(8,128)(2,1)S(1)}, u32[]{:S(2)}, u32[]{:S(2)}) collective-permute-start(bf16[10,32,128]{2,1,0:T(8,128)(2,1)S(1)} %get-tuple-element.40), channel_id=1, source_target_pairs={{0,1},{1,2},{2,3},{3,4},{4,5},{5,6},{6,7},{7,8},{8,9},{9,10},{10,1... | collective-permute-start | bytes 245768 | tf_op jit(solution)/shard_map/ppermute | solution.py:292
  79.8 7.5 %collective-permute-start.7 = (bf16[6,32,128]{2,1,0:T(8,128)(2,1)S(1)}, bf16[6,32,128]{2,1,0:T(8,128)(2,1)S(1)}, u32[]{:S(2)}, u32[]{:S(2)}) collective-permute-start(bf16[6,32,128]{2,1,0:T(8,128)(2,1)S(1)} %pad_maximum_fusion.4), channel_id=1, source_target_pairs={{0,1},{1,2},{2,3},{3,4},{4,5},{5,6},{6,7},{7,8},{8,9},{9,10},{10,1... | collective-permute-start | bytes 147464 | tf_op jit(solution)/shard_map/ppermute | solution.py:292
  79.9 7.4 %copy-start = (bf16[3,32,128]{2,1,0:T(8,128)(2,1)S(1)}, bf16[3,32,128]{2,1,0:T(8,128)(2,1)}, u32[]{:S(2)}) copy-start(bf16[3,32,128]{2,1,0:T(8,128)(2,1)} %get-tuple-element.20) | copy-start | bytes 73732
  87.4 8.2 %collective-permute-start.8 = (bf16[17,32,128]{2,1,0:T(8,128)(2,1)S(1)}, bf16[17,32,128]{2,1,0:T(8,128)(2,1)S(1)}, u32[]{:S(2)}, u32[]{:S(2)}) collective-permute-start(bf16[17,32,128]{2,1,0:T(8,128)(2,1)S(1)} %constant_dynamic-update-slice_fusion.2), channel_id=1, source_target_pairs={{0,3},{1,4},{2,5},{3,6},{4,7},{5,8},{6,9},{7,10},{8,11},{9,12},{10... | collective-permute-start | bytes 417800 | tf_op jit(solution)/shard_map/ppermute | solution.py:292
  95.7 7.7 %collective-permute-start.9 = (bf16[6,32,128]{2,1,0:T(8,128)(2,1)S(1)}, bf16[6,32,128]{2,1,0:T(8,128)(2,1)S(1)}, u32[]{:S(2)}, u32[]{:S(2)}) collective-permute-start(bf16[6,32,128]{2,1,0:T(8,128)(2,1)S(1)} %pad_maximum_fusion.3), channel_id=1, source_target_pairs={{0,31},{1,0},{2,1},{3,2},{4,3},{5,4},{6,5},{7,6},{8,7},{9,8},{10,9... | collective-permute-start | bytes 147464 | tf_op jit(solution)/shard_map/ppermute | solution.py:292
  103.4 12.8 %collective-permute-start.10 = (bf16[17,32,128]{2,1,0:T(8,128)(2,1)S(1)}, bf16[17,32,128]{2,1,0:T(8,128)(2,1)S(1)}, u32[]{:S(2)}, u32[]{:S(2)}) collective-permute-start(bf16[17,32,128]{2,1,0:T(8,128)(2,1)S(1)} %get-tuple-element.33), channel_id=1, source_target_pairs={{0,29},{1,30},{2,31},{3,0},{4,1},{5,2},{6,3},{7,4},{8,5},{9,6},{10... | collective-permute-start | bytes 417800 | tf_op jit(solution)/shard_map/ppermute | solution.py:292
  116.2 0.7 copy-start.5
  116.2 0.8 copy-start.4

commit v2 on v1

v2 whole, which is shorter than its diff:
```python
import functools

import jax
import jax.numpy as jnp
from jax import lax
from jax.experimental import pallas as pl
from jax.experimental.pallas import tpu as pltpu
from jax.sharding import PartitionSpec as P

SWEEPS = 3
STEPS = 5
LOW_EIG = 0.3
HIGH_EIG = 2.2
CENTER = (HIGH_EIG + LOW_EIG) / 2.0
HALF = (HIGH_EIG - LOW_EIG) / 2.0
LANES = 128
PACK = 16
F32 = jnp.float32
BF16 = jnp.bfloat16
VMEM = pltpu.VMEM


def lane_gather(rows, index):
    numbers = lax.GatherDimensionNumbers(
        offset_dims=(),
        collapsed_slice_dims=(1,),
        start_index_map=(1,),
        operand_batching_dims=(0,),
        start_indices_batching_dims=(0,),
    )
    return lax.gather(
        rows,
        index[..., None],
        numbers,
        (1, 1),
        mode=lax.GatherScatterMode.PROMISE_IN_BOUNDS,
    )


def call(kernel, out, inputs, scratch=(), us=1.0, spaces={}, limit=16):
    return pl.pallas_call(
        kernel,
        out_shape=out,
        in_specs=[
            pl.BlockSpec(memory_space=spaces.get(i, VMEM)) for i in range(len(inputs))
        ],
        out_specs=jax.tree.map(lambda _: pl.BlockSpec(memory_space=VMEM), out),
        scratch_shapes=list(scratch),
        cost_estimate=pl.CostEstimate(
            flops=int(us * 1.0e9), transcendentals=0, bytes_accessed=int(us * 1.0e6)
        ),
        compiler_params=pltpu.CompilerParams(vmem_limit_bytes=limit * 1024 * 1024),
    )(*inputs)


def rows_of(ref, lead, group):
    return ref[lead + (slice(group * LANES, (group + 1) * LANES),)]


def first_kernel(dinv, residual, couple, dense_dinv, dense_residual, smooth, message):
    groups = smooth.shape[1]
    coarse_groups = message.shape[1]
    for g in range(groups):
        lanes = slice(g * LANES, (g + 1) * LANES)
        for e in range(3):
            dense_residual[e, g : g + 1, :] = residual[e : e + 1, lanes]
            for c in range(3):
                dense_dinv[c, e, g : g + 1, :] = dinv[c, e : e + 1, lanes]
    for g in range(coarse_groups):
        lanes = slice(g * LANES, (g + 1) * LANES)
        for k in range(4):
            message[3 + k, g : g + 1, :] = couple[k : k + 1, lanes].astype(BF16)
    for c in range(3):
        total = dense_dinv[c, 0] * dense_residual[0]
        for e in range(1, 3):
            total = total + dense_dinv[c, e] * dense_residual[e]
        total = total * (1.0 / CENTER)
        smooth[c] = total
        message[c] = total.astype(BF16)


def restrict_kernel(residual, aggregate, out):
    groups = residual.shape[1]
    bins = out.shape[1]
    agg = aggregate[...] & (bins * LANES - 1)
    low = agg & (LANES - 1)
    high = agg >> 7
    batch = 4
    total = [jnp.zeros((2 * bins, LANES), F32) for c in range(3)]
    lane_ids = lax.broadcasted_iota(jnp.int32, (LANES, LANES), 0)
    bin_ids = lax.broadcasted_iota(jnp.int32, (bins, LANES), 0)
    for block in range(groups // batch):
        onehot = []
        spread = [[] for c in range(3)]
        for g in range(block * batch, (block + 1) * batch):
            same = jnp.broadcast_to(low[g : g + 1], (LANES, LANES)) == lane_ids
            onehot.append(jnp.where(same, 1.0, 0.0).astype(BF16))
            chosen = jnp.broadcast_to(high[g : g + 1], (bins, LANES)) == bin_ids
            for c in range(3):
                value = residual[c, g : g + 1, :]
                upper = value.astype(BF16).astype(F32)
                lower = value - upper
                spread[c].append(
                    jnp.concatenate(
                        [
                            jnp.where(chosen, jnp.broadcast_to(part, (bins, LANES)), 0.0)
                            for part in (upper, lower)
                        ],
                        axis=0,
                    ).astype(BF16)
                )
        onehot = jnp.concatenate(onehot, axis=1)
        for c in range(3):
            total[c] = total[c] + lax.dot_general(
                jnp.concatenate(spread[c], axis=1),
                onehot,
                (((1,), (1,)), ((), ())),
                preferred_element_type=F32,
            )
    for c in range(3):
        out[c] = total[c][:bins] + total[c][bins:]


def fill_table(table, source, groups):
    for e in range(3):
        for g in range(groups):
            row = source[e, g : g + 1, :]
            table[e, g] = jnp.broadcast_to(row, (PACK, LANES)).astype(BF16)


def pick(table, index, groups, first, starts):
    low = (index & (LANES - 1)).astype(jnp.int16)
    high = (index >> 7).astype(jnp.int16)
    picked = list(starts)
    for g in range(groups):
        chosen = high == (first + g)
        for e in range(3):
            value = lane_gather(table[e, g], low)
            picked[e] = jnp.where(chosen, value, picked[e])
    return picked


def local_kernel(smooth, col, out, table, *, first, tiles, unroll=4):
    groups = smooth.shape[1]
    fill_table(table, smooth, groups)
    bonds_of = col.shape[0]
    zero = jnp.zeros((PACK, LANES), BF16)

    def some_tiles(t, carry):
        for u in range(unroll):
            source = pl.multiple_of((first + t * unroll + u) * LANES, LANES)
            target = pl.multiple_of((t * unroll + u) * LANES, LANES)
            for h in range(bonds_of // PACK):
                rows = pl.ds(h * PACK, PACK)
                picked = pick(table, col[rows, pl.ds(source, LANES)], groups, 0, [zero] * 3)
                for e in range(3):
                    out[e, rows, pl.ds(target, LANES)] = picked[e]
        return carry

    lax.fori_loop(0, tiles // unroll, some_tiles, 0)


def dense_solve(matrix, vector):
    solved = []
    for c in range(3):
        total = matrix[c, 0] * vector[0]
        for e in range(1, 3):
            total = total + matrix[c, e] * vector[e]
        solved.append(total)
    return solved


def halo_kernel(*refs, sizes, stage, scale_old, scale_new, unroll=4):
    pieces = len(sizes)
    (col, ghost, after, before, residual, dinv, smooth, update, bonds) = refs[:9]
    picked_refs = refs[9 : 9 + pieces]
    refs = refs[9 + pieces :]
    if stage == 0:
        rhs, arrived, coarse_dinv = refs[:3]
        new_smooth, new_update, base, to_next, to_prev = refs[3:8]
        refs = refs[8:]
    elif stage == 1:
        first_after, first_before, base, couple_own = refs[:4]
        new_smooth, new_update, to_next, to_prev, far_next, far_prev = refs[4:10]
        refs = refs[10:]
    else:
        (new_smooth,) = refs[:1]
        refs = refs[1:]
    slots, table, applied = refs
    groups = smooth.shape[1]
    if stage == 0:
        vector = [rhs[e] + arrived[e] for e in range(3)]
        coarse_groups = base.shape[1]
        for c in range(3):
            for g in range(coarse_groups):
                lanes = slice(g * LANES, (g + 1) * LANES)
                total = coarse_dinv[c, 0:1, lanes] * vector[0][g : g + 1]
                for e in range(1, 3):
                    total = total + coarse_dinv[c, e : e + 1, lanes] * vector[e][g : g + 1]
                base[c, g : g + 1, :] = total
        for c in range(3):
            row = base[c].astype(BF16)
            to_next[3 + c] = row
            to_prev[3 + c] = row
        to_next[6:10] = after[3:7]
        to_prev[6:10] = before[3:7]
    elif stage == 1:
        own = base[...].astype(BF16)
        to_next[3:6] = after[3:6]
        to_prev[3:6] = before[3:6]
        for message in (far_next, far_prev):
            message[0:3] = after[3:6]
            message[3:6] = own
            message[6:9] = before[3:6]
        far_next[9:13] = couple_own[3:7]
        far_next[13:17] = first_before[3:7]
        far_prev[9:13] = first_after[3:7]
        far_prev[13:17] = couple_own[3:7]
    wanted = ghost[...]
    half = wanted.shape[0] // 2
    low = wanted & (LANES - 1)
    high = wanted >> 7
    upper = lax.broadcasted_iota(jnp.int32, wanted.shape, 0) < half
    found = [jnp.zeros(wanted.shape, F32)] * 3
    for e in range(3):
        applied[e] = after[e].astype(F32)
        new_smooth[e] = before[e].astype(F32)
    for g in range(groups):
        chosen = high == g
        for e in range(3):
            rows = jnp.where(
                upper,
                jnp.broadcast_to(applied[e, g : g + 1, :], wanted.shape),
                jnp.broadcast_to(new_smooth[e, g : g + 1, :], wanted.shape),
            )
            found[e] = jnp.where(chosen, lane_gather(rows, low), found[e])
    for e in range(3):
        slots[e] = found[e]
    halo_groups = wanted.shape[0]
    fill_table(table, slots, halo_groups)
    bonds_of = col.shape[0]

    for piece in range(pieces):
        start = sum(sizes[:piece])

        def some_tiles(t, carry, piece=piece, start=start):
            for u in range(unroll):
                tile = start + t * unroll + u
                here = pl.ds(pl.multiple_of(tile * LANES, LANES), LANES)
                there = pl.ds(pl.multiple_of((t * unroll + u) * LANES, LANES), LANES)
                total = [jnp.zeros((PACK, LANES), F32)] * 3
                for h in range(bonds_of // PACK):
                    rows = pl.ds(h * PACK, PACK)
                    starts = [picked_refs[piece][e, rows, there] for e in range(3)]
                    picked = pick(table, col[rows, here], halo_groups, groups, starts)
                    wide = [value.astype(F32) for value in picked]
                    for c in range(3):
                        for e in range(3):
                            total[c] = (
                                total[c] + bonds[c, e, rows, here].astype(F32) * wide[e]
                            )
                for c in range(3):
                    applied[c, pl.ds(tile, 1), :] = jnp.sum(total[c], axis=0, keepdims=True)
            return carry

        lax.fori_loop(0, sizes[piece] // unroll, some_tiles, 0)
    remainder = [residual[e] - smooth[e] - applied[e] for e in range(3)]
    solved = dense_solve(dinv, remainder)
    for c in range(3):
        change = scale_old * update[c] + scale_new * solved[c]
        total = smooth[c] + change
        new_smooth[c] = total
        if stage < SWEEPS - 1:
            new_update[c] = change
            to_next[c] = total.astype(BF16)
            to_prev[c] = total.astype(BF16)


def coarse_kernel(*refs):
    (place, base, own_couple, first_after, first_before, second_after, second_before) = refs[:7]
    (third_after, third_before, far_after, far_before, aggregate, smooth) = refs[7:13]
    out, field, links = refs[13:]
    subs, me = place[0], place[1]
    groups = base.shape[1]

    def valid(row):
        inside = jnp.logical_and(me + row >= 0, me + row < subs)
        return jnp.where(inside, 1.0, 0.0).astype(F32)

    base_rows = {
        -5: (far_after, 0),
        -4: (far_after, 3),
        -3: (far_after, 6),
        -2: (third_after, 3),
        -1: (second_after, 3),
        1: (second_before, 3),
        2: (third_before, 3),
        3: (far_before, 0),
        4: (far_before, 3),
        5: (far_before, 6),
    }
    link_rows = {
        -4: (far_after, 9),
        -3: (far_after, 13),
        -2: (second_after, 6),
        -1: (first_after, 3),
        1: (first_before, 3),
        2: (second_before, 6),
        3: (far_before, 9),
        4: (far_before, 13),
    }

    def base_of(row, c):
        if row == 0:
            return base[c]
        ref, start = base_rows[row]
        return ref[start + c].astype(F32) * valid(row)

    for k in range(4):
        for g in range(groups):
            links[STEPS - 1, k, g : g + 1, :] = own_couple[
                k : k + 1, g * LANES : (g + 1) * LANES
            ]
    for row, (ref, start) in link_rows.items():
        for k in range(4):
            links[row + STEPS - 1, k] = ref[start + k].astype(F32) * valid(row)
    for row in range(-STEPS, STEPS + 1):
        for c in range(3):
            field[0, row + STEPS, c] = base_of(row, c)
    lane = lax.broadcasted_iota(jnp.int32, (groups, LANES), 1)
    line = lax.broadcasted_iota(jnp.int32, (groups, LANES), 0)
    for step in range(STEPS):
        old, new = step % 2, (step + 1) % 2
        reach = STEPS - 1 - step
        for row in range(-reach, reach + 1):
            spot = row + STEPS
            weights = [links[row + STEPS - 1, k] for k in range(4)]
            for c in range(3):
                x = field[old, spot, c]
                right = pltpu.roll(x, 1, 1)
                right = jnp.where(lane == 0, pltpu.roll(right, 1, 0), right)
                right = jnp.where(jnp.logical_and(lane == 0, line == 0), 0.0, right)
                left = pltpu.roll(x, LANES - 1, 1)
                left = jnp.where(lane == LANES - 1, pltpu.roll(left, groups - 1, 0), left)
                left = jnp.where(
                    jnp.logical_and(lane == LANES - 1, line == groups - 1), 0.0, left
                )
                field[new, spot, c] = base_of(row, c) + (
                    weights[0] * field[old, spot - 1, c]
                    + weights[1] * field[old, spot + 1, c]
                    + weights[2] * right
                    + weights[3] * left
                )
    final = STEPS % 2
    agg = aggregate[...] & (groups * LANES - 1)
    for block in range(agg.shape[0] // 8):
        index = agg[block * 8 : (block + 1) * 8]
        low = index & (LANES - 1)
        high = index >> 7
        found = [jnp.zeros((8, LANES), F32)] * 3
        for g in range(groups):
            chosen = high == g
            for c in range(3):
                rows = jnp.broadcast_to(field[final, STEPS, c, g : g + 1, :], (8, LANES))
                found[c] = jnp.where(chosen, lane_gather(rows, low), found[c])
        for c in range(3):
            result = smooth[c, block * 8 : (block + 1) * 8, :] + found[c]
            for r in range(8):
                lanes = slice((block * 8 + r) * LANES, (block * 8 + r + 1) * LANES)
                out[c : c + 1, lanes] = result[r : r + 1]


def shifted(value, steps):
    count = lax.axis_size("sub")
    return lax.ppermute(value, "sub", [(i, (i + steps) % count) for i in range(count)])


def body(
    fine_residual, bonds, bond_col, ghost_points, fine_dinv, aggregate, coarse_dinv, coarse_couple
):
    points = fine_residual.shape[1]
    groups = points // LANES
    bonds_of = bond_col.shape[0]
    per_group = coarse_dinv.shape[2]
    coarse_groups = per_group // LANES
    assert per_group & (per_group - 1) == 0
    sub = lax.axis_index("sub")
    doms = lax.axis_size("dom")
    ghost = ghost_points.reshape(-1, LANES)
    agg = aggregate.reshape(groups, LANES)
    relaid = bonds.transpose(1, 2, 0, 3)
    sds = jax.ShapeDtypeStruct
    field = sds((3, groups, LANES), F32)
    coarse_field = sds((3, coarse_groups, LANES), F32)

    def message(rows):
        return sds((rows, groups, LANES), BF16)

    dinv, residual, smooth, packed = call(
        first_kernel,
        (sds((3, 3, groups, LANES), F32), field, field, message(7)),
        (fine_dinv, fine_residual, coarse_couple),
        us=2.0,
    )
    update = smooth
    own_packed = packed
    after = shifted(packed, 1)
    before = shifted(packed, -1)
    first_after, first_before = after, before
    rhs = call(restrict_kernel, coarse_field, (residual, agg), us=2.5)

    def local(smooth, first, tiles):
        return call(
            functools.partial(local_kernel, first=first, tiles=tiles),
            sds((3, bonds_of, tiles * LANES), BF16),
            (smooth, bond_col),
            scratch=[VMEM((3, groups, PACK, LANES), BF16)],
            us=7.5 * tiles / groups,
        )

    def exchanged(value, step):
        return lax.ppermute(value, "dom", [(i, i ^ step) for i in range(doms)])

    sizes = (12, 12, 8)
    parts = []
    arrived = exchanged(rhs, 1)
    parts.append(local(smooth, 0, sizes[0]))
    rhs = rhs + arrived
    arrived = exchanged(rhs, 2)
    later, rhs, parts[0] = lax.optimization_barrier((smooth, rhs, parts[0]))
    parts.append(local(later, sizes[0], sizes[1]))
    rhs = rhs + arrived
    arrived = exchanged(rhs, 4)
    later, rhs, parts[1] = lax.optimization_barrier((smooth, rhs, parts[1]))
    parts.append(local(later, sizes[0] + sizes[1], sizes[2]))

    factor = HALF / CENTER
    for stage in range(SWEEPS):
        factor_new = 1.0 / (2.0 * CENTER / HALF - factor)
        if stage:
            sizes = (groups,)
            parts = [local(smooth, 0, groups)]
        inputs = [bond_col, ghost, after, before, residual, dinv, smooth, update, relaid]
        inputs += parts
        if stage == 0:
            inputs += [rhs, arrived, coarse_dinv]
            outs = (field, field, coarse_field, message(10), message(10))
        elif stage == 1:
            inputs += [first_after, first_before, base, own_packed]
            outs = (field, field, message(6), message(6), message(17), message(17))
        else:
            outs = (field,)
        result = call(
            functools.partial(
                halo_kernel,
                sizes=sizes,
                stage=stage,
                scale_old=factor_new * factor,
                scale_new=2.0 * factor_new / HALF,
            ),
            outs,
            inputs,
            scratch=[
                VMEM((3,) + ghost.shape, F32),
                VMEM((3, ghost.shape[0], PACK, LANES), BF16),
                VMEM((3, groups, LANES), F32),
            ],
            us=4.0,
        )
        factor = factor_new
        if stage == 0:
            smooth, update, base, to_next, to_prev = result
            after = second_after = shifted(to_next, 1)
            before = second_before = shifted(to_prev, -1)
        elif stage == 1:
            smooth, update, to_next, to_prev, far_next, far_prev = result
            after = third_after = shifted(to_next, 1)
            before = third_before = shifted(to_prev, -1)
            far_after = shifted(far_next, 4)
            far_before = shifted(far_prev, -4)
        else:
            (smooth,) = result
    place = jnp.stack([jnp.int32(lax.axis_size("sub")), sub.astype(jnp.int32)])
    return call(
        coarse_kernel,
        sds((3, points), F32),
        (
            place,
            base,
            coarse_couple,
            first_after,
            first_before,
            second_after,
            second_before,
            third_after,
            third_before,
            far_after,
            far_before,
            agg,
            smooth,
        ),
        scratch=[
            VMEM((2, 2 * STEPS + 1, 3, coarse_groups, LANES), F32),
            VMEM((2 * STEPS - 1, 4, coarse_groups, LANES), F32),
        ],
        us=2.0,
        spaces={0: pltpu.SMEM},
    )


def solution(mesh):
    placed = (
        P(None, ("dom", "sub")),
        P(None, None, None, ("dom", "sub")),
        P(None, ("dom", "sub")),
        P(("dom", "sub"), None, None),
        P(None, None, ("dom", "sub")),
        P(("dom", "sub")),
        P(None, None, "sub"),
        P(None, "sub"),
    )
    return jax.shard_map(
        body, mesh=mesh, in_specs=placed, out_specs=P(None, ("dom", "sub")), check_vma=False
    )
```

time: 121 us -> 66.3 us (0.55)
  the two profiles are of different devices: /device:TPU:1 before, /device:TPU:24 now
where the time goes in v2:
time: 66.3 us; the launch traced here: 66.2 us
  Pallas kernels  34.2 us (52%)
  starting transfers between devices  23.6 us (36%)
  waiting for transfers between devices  5.44 us (8%)
  local copies, waits for them, and re-layouts  2.64 us (4%)
    pallas_call x11, Pallas kernels, call(): pl.pallas_call(kernel, out_shape=out, in_specs=[pl.BlockSpec(memory_space...  34.2 us
    ppermute x8, starting transfers between devices, shifted(): lax.ppermute(value, 'sub', [(i, (i + steps) % count) for i in range(count)])  20.9 us
    ppermute x3, waiting for transfers between devices, exchanged(): return lax.ppermute(value, 'dom', [(i, i ^ step) for i in range(doms)])  3.73 us
    ppermute x3, starting transfers between devices, exchanged(): return lax.ppermute(value, 'dom', [(i, i ^ step) for i in range(doms)])  2.77 us
    unnamed x18, local copies, waits for them, and re-layouts  2.63 us
    ppermute x8, waiting for transfers between devices, shifted(): lax.ppermute(value, 'sub', [(i, (i + steps) % count) for i in range(count)])  1.71 us
  transfers between devices with their start and end apart: 11, of which 5 were waited for; matrix products, arithmetic and copies ran while one was open for 0% of the time, Pallas kernels for 39%

profile of v2, /device:TPU:24, one launch (start us, length us, event | category | flops | bytes accessed | tf_op | source)
XLA Modules:
  0.0 66.2 jit_solution(10583920536099452108)
XLA Ops:
  0.0 0.9 %copy-done.2 = f32[3,3,4096]{2,1,0:T(4,128)S(1)} copy-done((f32[3,3,4096]{2,1,0:T(4,128)S(1)}, f32[3,3,4096]{2,1,0:T(4,128)}, u32[]{:S(2)}) %copy-start.2) | copy-done | bytes 147480
  0.9 0.8 %copy-done.4 = f32[3,4096]{1,0:T(4,128)S(1)} copy-done((f32[3,4096]{1,0:T(4,128)S(1)}, f32[3,4096]{1,0:T(4,128)}, u32[]{:S(2)}) %copy-start.4) | copy-done | bytes 49176
  1.8 0.8 %copy-done.5 = f32[4,4096]{1,0:T(4,128)S(1)} copy-done((f32[4,4096]{1,0:T(4,128)S(1)}, f32[4,4096]{1,0:T(4,128)}, u32[]{:S(2)}) %copy-start.5) | copy-done | bytes 65560
  2.6 0.3 shard_map.82
  2.9 0.1 collective-permute-start
  3.0 7.8 %collective-permute-start.1 = (bf16[7,32,128]{2,1,0:T(8,128)(2,1)S(1)}, bf16[7,32,128]{2,1,0:T(8,128)(2,1)S(1)}, u32[]{:S(2)}, u32[]{:S(2)}) collective-permute-start(bf16[7,32,128]{2,1,0:T(8,128)(2,1)S(1)} %get-tuple-element.26.refs_13_), channel_id=1, source_target_pairs={{0,31},{1,0},{2,1},{3,2},{4,3},{5,4},{6,5},{7,6},{8,7},{9,8},{10,9... | collective-permute-start | bytes 172040 | tf_op jit(solution)/shard_map/ppermute | solution.py:375
  10.8 1.2 %shard_map.83 = f32[3,32,128]{2,1,0:T(8,128)S(1)} custom-call(f32[3,32,128]{2,1,0:T(8,128)S(1)} %get-tuple-element.27.residual.refs_4_, s32[32,128]{1,0:T(8,128)S(1)} %bitcast.6), custom_call_target="tpu_custom_call" | custom-call | flops 2500000000 | bytes 2500000 | tf_op jit(solution)/shard_map/pallas_call | solution.py:41
  12.0 0.6 collective-permute-start.2
  12.6 2.8 %shard_map.84.refs_9_ = bf16[3,32,1536]{2,1,0:T(8,128)(2,1)S(1)} custom-call(f32[3,32,128]{2,1,0:T(8,128)S(1)} %get-tuple-element.34.smooth.refs_6_.refs_7_, s32[32,4096]{1,0:T(8,128)S(1)} %copy-done.1), custom_call_target="tpu_custom_call" | custom-call | flops 2812499968 | bytes 2812500 | tf_op jit(solution)/shard_map/pallas_call | solution.py:41
  15.4 0.1 pad_add_fusion.refs_0_
  15.5 0.6 collective-permute-done.2
  16.1 0.8 %collective-permute-start.3 = (f32[3,32,128]{2,1,0:T(8,128)S(1)}, f32[3,32,128]{2,1,0:T(8,128)S(1)}, u32[]{:S(2)}, u32[]{:S(2)}) collective-permute-start(f32[3,32,128]{2,1,0:T(8,128)S(1)} %add.6), channel_id=1, source_target_pairs={{0,64},{32,96},{64,0},{96,32},{128,192},{160,224},{192,128},{224,1... | collective-permute-start | bytes 147464 | tf_op jit(solution)/shard_map/ppermute | solution.py:422
  17.0 2.7 %shard_map.85.refs_10_ = bf16[3,32,1536]{2,1,0:T(8,128)(2,1)S(1)} custom-call(f32[3,32,128]{2,1,0:T(8,128)S(1)} %get-tuple-element.34.smooth.refs_6_.refs_7_, s32[32,4096]{1,0:T(8,128)S(1)} %copy-done.1), custom_call_target="tpu_custom_call" | custom-call | flops 2812499968 | bytes 2812500 | tf_op jit(solution)/shard_map/pallas_call | solution.py:41
  19.7 0.6 collective-permute-done.3
  20.3 0.0 copy-start
  20.3 1.3 %collective-permute-start.4 = (f32[3,32,128]{2,1,0:T(8,128)S(1)}, f32[3,32,128]{2,1,0:T(8,128)S(1)}, u32[]{:S(2)}, u32[]{:S(2)}) collective-permute-start(f32[3,32,128]{2,1,0:T(8,128)S(1)} %add.7.refs_12_), channel_id=1, source_target_pairs={{0,128},{32,160},{64,192},{96,224},{128,0},{160,32},{192,64},{224,... | collective-permute-start | bytes 147464 | tf_op jit(solution)/shard_map/ppermute | solution.py:422
  21.7 1.8 %shard_map.86.refs_11_ = bf16[3,32,1024]{2,1,0:T(8,128)(2,1)S(1)} custom-call(f32[3,32,128]{2,1,0:T(8,128)S(1)} %get-tuple-element.34.smooth.refs_6_.refs_7_, s32[32,4096]{1,0:T(8,128)S(1)} %copy-done.1), custom_call_target="tpu_custom_call" | custom-call | flops 1875000064 | bytes 1875000 | tf_op jit(solution)/shard_map/pallas_call | solution.py:41
  23.5 2.5 %collective-permute-done.4.refs_13_ = f32[3,32,128]{2,1,0:T(8,128)S(1)} collective-permute-done((f32[3,32,128]{2,1,0:T(8,128)S(1)}, f32[3,32,128]{2,1,0:T(8,128)S(1)}, u32[]{:S(2)}, u32[]{:S(2)}) %collective-permute-start.4) | collective-permute-done | bytes 49184 | tf_op jit(solution)/shard_map/ppermute | solution.py:422
  26.0 2.8 %shard_map.87 = (f32[3,32,128]{2,1,0:T(8,128)S(1)}, f32[3,32,128]{2,1,0:T(8,128)S(1)}, f32[3,32,128]{2,1,0:T(8,128)S(1)}, bf16[10,32,128]{2,1,0:T(8,128)(2,1)S(1)}, bf16[10,32,128]{2,1,0:T(8,128)(2,1)S(1)}) custom-call(s32[32,4096]{1,0:T(8,128)S(1)} %copy-done.1, s32[8,128]{1,0:T(8,128)S(1)} %reshape.6.refs_1_, ...), custom_call_target="tpu_custom_call" | custom-call | flops 4000000000 | bytes 4000000 | tf_op jit(solution)/shard_map/pallas_call | solution.py:41
  28.9 0.1 collective-permute-start.5
  29.0 5.3 %collective-permute-start.6 = (bf16[10,32,128]{2,1,0:T(8,128)(2,1)S(1)}, bf16[10,32,128]{2,1,0:T(8,128)(2,1)S(1)}, u32[]{:S(2)}, u32[]{:S(2)}) collective-permute-start(bf16[10,32,128]{2,1,0:T(8,128)(2,1)S(1)} %get-tuple-element.38), channel_id=1, source_target_pairs={{0,31},{1,0},{2,1},{3,2},{4,3},{5,4},{6,5},{7,6},{8,7},{9,8},{10,9... | collective-permute-start | bytes 245768 | tf_op jit(solution)/shard_map/ppermute | solution.py:375
  34.3 7.3 %shard_map.88.refs_9_ = bf16[3,32,4096]{2,1,0:T(8,128)(2,1)S(1)} custom-call(f32[3,32,128]{2,1,0:T(8,128)S(1)} %get-tuple-element.39.smooth.refs_6_, s32[32,4096]{1,0:T(8,128)S(1)} %copy-done.1), custom_call_target="tpu_custom_call" | custom-call | flops 7500000256 | bytes 7500000 | tf_op jit(solution)/shard_map/pallas_call | solution.py:41
  41.6 2.8 %shard_map.89 = (f32[3,32,128]{2,1,0:T(8,128)S(1)}, f32[3,32,128]{2,1,0:T(8,128)S(1)}, bf16[6,32,128]{2,1,0:T(8,128)(2,1)S(1)}, bf16[6,32,128]{2,1,0:T(8,128)(2,...) custom-call(s32[32,4096]{1,0:T(8,128)S(1)} %copy-done.1, s32[8,128]{1,0:T(8,128)S(1)} %reshape.6.refs_1_, ...), custom_call_target="tpu_custom_call" | custom-call | flops 4000000000 | bytes 4000000 | tf_op jit(solution)/shard_map/pallas_call | solution.py:41
  44.4 0.1 collective-permute-start.7
  44.5 5.3 %collective-permute-start.8 = (bf16[6,32,128]{2,1,0:T(8,128)(2,1)S(1)}, bf16[6,32,128]{2,1,0:T(8,128)(2,1)S(1)}, u32[]{:S(2)}, u32[]{:S(2)}) collective-permute-start(bf16[6,32,128]{2,1,0:T(8,128)(2,1)S(1)} %get-tuple-element.42), channel_id=1, source_target_pairs={{0,31},{1,0},{2,1},{3,2},{4,3},{5,4},{6,5},{7,6},{8,7},{9,8},{10,9... | collective-permute-start | bytes 147464 | tf_op jit(solution)/shard_map/ppermute | solution.py:375
  49.8 7.3 %shard_map.90.refs_9_ = bf16[3,32,4096]{2,1,0:T(8,128)(2,1)S(1)} custom-call(f32[3,32,128]{2,1,0:T(8,128)S(1)} %get-tuple-element.45.smooth.refs_6_, s32[32,4096]{1,0:T(8,128)S(1)} %copy-done.1), custom_call_target="tpu_custom_call" | custom-call | flops 7500000256 | bytes 7500000 | tf_op jit(solution)/shard_map/pallas_call | solution.py:41
  57.1 0.3 collective-permute-start.10
  57.4 1.8 %collective-permute-start.9 = (bf16[17,32,128]{2,1,0:T(8,128)(2,1)S(1)}, bf16[17,32,128]{2,1,0:T(8,128)(2,1)S(1)}, u32[]{:S(2)}, u32[]{:S(2)}) collective-permute-start(bf16[17,32,128]{2,1,0:T(8,128)(2,1)S(1)} %get-tuple-element.43), channel_id=1, source_target_pairs={{0,4},{1,5},{2,6},{3,7},{4,8},{5,9},{6,10},{7,11},{8,12},{9,13},{1... | collective-permute-start | bytes 417800 | tf_op jit(solution)/shard_map/ppermute | solution.py:375
  59.3 2.7 %shard_map.91.refs_12_ = f32[3,32,128]{2,1,0:T(8,128)S(1)} custom-call(s32[32,4096]{1,0:T(8,128)S(1)} %copy-done.1, s32[8,128]{1,0:T(8,128)S(1)} %reshape.6.refs_1_, bf16[6,32,128]{2,1,0:T(8,128)(2,1)S(1)} %collective-permute-done.7.refs_2_.refs_7_, bf16[6,32,128]{2,1,0:T(8,128)(2,1)S(1)} %collective-permute-done.8.refs_3_.refs_8_, ...), custom_call_target="tpu_custom_call" | custom-call | flops 4000000000 | bytes 4000000 | tf_op jit(solution)/shard_map/pallas_call | solution.py:41
  62.0 0.3 collective-permute-done.10.refs_10_
  62.3 1.4 %collective-permute-done.9.refs_9_ = bf16[17,32,128]{2,1,0:T(8,128)(2,1)S(1)} collective-permute-done((bf16[17,32,128]{2,1,0:T(8,128)(2,1)S(1)}, bf16[17,32,128]{2,1,0:T(8,128)(2,1)S(1)}, u32[]{:S(2)}, u32[]{:S(2)}) %collective-permute-start.9) | collective-permute-done | bytes 139296 | tf_op jit(solution)/shard_map/ppermute | solution.py:375
  63.7 2.5 %shard_map.92 = f32[3,4096]{1,0:T(4,128)} custom-call(s32[2]{0:T(128)S(1)} %pad_add_fusion.refs_0_, f32[3,32,128]{2,1,0:T(8,128)S(1)} %get-tuple-element.36.refs_12_.refs_1_, f32[4,4096]{1,0:T(4,128)S(1)} %copy-done.6, bf16[7,32,128]{2,1,0:T(8,128)(2,1)S(1)} %collective-permute-done.refs_2_.refs_10_.refs_3_, ...), custom_call_target="tpu_custom_call" | custom-call | flops 2000000000 | bytes 2000000 | tf_op jit(solution)/shard_map/pallas_call | solution.py:41
  (23 shorter events, 0.1 us)
Async XLA Ops:
  0.0 0.9 %copy-start.2 = (f32[3,3,4096]{2,1,0:T(4,128)S(1)}, f32[3,3,4096]{2,1,0:T(4,128)}, u32[]{:S(2)}) copy-start(f32[3,3,4096]{2,1,0:T(4,128)} %dinv.1) | copy-start | bytes 442372
  0.9 0.8 %copy-start.4 = (f32[3,4096]{1,0:T(4,128)S(1)}, f32[3,4096]{1,0:T(4,128)}, u32[]{:S(2)}) copy-start(f32[3,4096]{1,0:T(4,128)} %residual.1) | copy-start | bytes 147460
  1.8 0.8 %copy-start.5 = (f32[4,4096]{1,0:T(4,128)S(1)}, f32[4,4096]{1,0:T(4,128)}, u32[]{:S(2)}) copy-start(f32[4,4096]{1,0:T(4,128)} %refs_2_.1) | copy-start | bytes 196612
  2.6 8.2 %copy-start.7 = (s32[4096]{0:T(1024)S(1)}, s32[4096]{0:T(1024)}, u32[]{:S(2)}) copy-start(s32[4096]{0:T(1024)} %param.13) | copy-start | bytes 49156
  2.9 20.6 %collective-permute-start = (bf16[7,32,128]{2,1,0:T(8,128)(2,1)S(1)}, bf16[7,32,128]{2,1,0:T(8,128)(2,1)S(1)}, u32[]{:S(2)}, u32[]{:S(2)}) collective-permute-start(bf16[7,32,128]{2,1,0:T(8,128)(2,1)S(1)} %get-tuple-element.26.refs_13_), channel_id=1, source_target_pairs={{0,1},{1,2},{2,3},{3,4},{4,5},{5,6},{6,7},{7,8},{8,9},{9,10},{10,1... | collective-permute-start | bytes 172040 | tf_op jit(solution)/shard_map/ppermute | solution.py:375
  3.0 20.5 %collective-permute-start.1 = (bf16[7,32,128]{2,1,0:T(8,128)(2,1)S(1)}, bf16[7,32,128]{2,1,0:T(8,128)(2,1)S(1)}, u32[]{:S(2)}, u32[]{:S(2)}) collective-permute-start(bf16[7,32,128]{2,1,0:T(8,128)(2,1)S(1)} %get-tuple-element.26.refs_13_), channel_id=1, source_target_pairs={{0,31},{1,0},{2,1},{3,2},{4,3},{5,4},{6,5},{7,6},{8,7},{9,8},{10,9... | collective-permute-start | bytes 172040 | tf_op jit(solution)/shard_map/ppermute | solution.py:375
  10.8 1.8 %copy-start.1 = (s32[32,4096]{1,0:T(8,128)S(1)}, s32[32,4096]{1,0:T(8,128)}, u32[]{:S(2)}) copy-start(s32[32,4096]{1,0:T(8,128)} %refs_0_.5) | copy-start | bytes 1572868
  12.0 4.1 %collective-permute-start.2 = (f32[3,32,128]{2,1,0:T(8,128)S(1)}, f32[3,32,128]{2,1,0:T(8,128)S(1)}, u32[]{:S(2)}, u32[]{:S(2)}) collective-permute-start(f32[3,32,128]{2,1,0:T(8,128)S(1)} %shard_map.83), channel_id=1, source_target_pairs={{0,32},{32,0},{64,96},{96,64},{128,160},{160,128},{192,224},{224,1... | collective-permute-start | bytes 147464 | tf_op jit(solution)/shard_map/ppermute | solution.py:422
  12.6 2.8 %copy-start.8 = (s32[1,2,512]{2,1,0:T(2,128)S(1)}, s32[1,2,512]{2,1,0:T(2,128)}, u32[]{:S(2)}) copy-start(s32[1,2,512]{2,1,0:T(2,128)} %param.11) | copy-start | bytes 12292
  16.1 4.2 %collective-permute-start.3 = (f32[3,32,128]{2,1,0:T(8,128)S(1)}, f32[3,32,128]{2,1,0:T(8,128)S(1)}, u32[]{:S(2)}, u32[]{:S(2)}) collective-permute-start(f32[3,32,128]{2,1,0:T(8,128)S(1)} %add.6), channel_id=1, source_target_pairs={{0,64},{32,96},{64,0},{96,32},{128,192},{160,224},{192,128},{224,1... | collective-permute-start | bytes 147464 | tf_op jit(solution)/shard_map/ppermute | solution.py:422
  20.3 5.7 %copy-start = (bf16[32,3,3,4096]{3,0,2,1:T(8,128)(2,1)S(1)}, bf16[32,3,3,4096]{3,0,2,1:T(8,128)(2,1)}, u32[]{:S(2)}) copy-start(bf16[32,3,3,4096]{3,0,2,1:T(8,128)(2,1)} %param.9) | copy-start | bytes 7077892
  20.3 5.7 %copy-start.3 = (f32[3,3,4096]{2,1,0:T(4,128)S(1)}, f32[3,3,4096]{2,1,0:T(4,128)}, u32[]{:S(2)}) copy-start(f32[3,3,4096]{2,1,0:T(4,128)} %refs_14_.1) | copy-start | bytes 442372
  20.3 5.7 %collective-permute-start.4 = (f32[3,32,128]{2,1,0:T(8,128)S(1)}, f32[3,32,128]{2,1,0:T(8,128)S(1)}, u32[]{:S(2)}, u32[]{:S(2)}) collective-permute-start(f32[3,32,128]{2,1,0:T(8,128)S(1)} %add.7.refs_12_), channel_id=1, source_target_pairs={{0,128},{32,160},{64,192},{96,224},{128,0},{160,32},{192,64},{224,... | collective-permute-start | bytes 147464 | tf_op jit(solution)/shard_map/ppermute | solution.py:422
  28.9 12.7 %collective-permute-start.5 = (bf16[10,32,128]{2,1,0:T(8,128)(2,1)S(1)}, bf16[10,32,128]{2,1,0:T(8,128)(2,1)S(1)}, u32[]{:S(2)}, u32[]{:S(2)}) collective-permute-start(bf16[10,32,128]{2,1,0:T(8,128)(2,1)S(1)} %get-tuple-element.37), channel_id=1, source_target_pairs={{0,1},{1,2},{2,3},{3,4},{4,5},{5,6},{6,7},{7,8},{8,9},{9,10},{10,1... | collective-permute-start | bytes 245768 | tf_op jit(solution)/shard_map/ppermute | solution.py:375
  29.0 12.7 %collective-permute-start.6 = (bf16[10,32,128]{2,1,0:T(8,128)(2,1)S(1)}, bf16[10,32,128]{2,1,0:T(8,128)(2,1)S(1)}, u32[]{:S(2)}, u32[]{:S(2)}) collective-permute-start(bf16[10,32,128]{2,1,0:T(8,128)(2,1)S(1)} %get-tuple-element.38), channel_id=1, source_target_pairs={{0,31},{1,0},{2,1},{3,2},{4,3},{5,4},{6,5},{7,6},{8,7},{9,8},{10,9... | collective-permute-start | bytes 245768 | tf_op jit(solution)/shard_map/ppermute | solution.py:375
  44.4 14.8 %collective-permute-start.7 = (bf16[6,32,128]{2,1,0:T(8,128)(2,1)S(1)}, bf16[6,32,128]{2,1,0:T(8,128)(2,1)S(1)}, u32[]{:S(2)}, u32[]{:S(2)}) collective-permute-start(bf16[6,32,128]{2,1,0:T(8,128)(2,1)S(1)} %get-tuple-element.41), channel_id=1, source_target_pairs={{0,1},{1,2},{2,3},{3,4},{4,5},{5,6},{6,7},{7,8},{8,9},{9,10},{10,1... | collective-permute-start | bytes 147464 | tf_op jit(solution)/shard_map/ppermute | solution.py:375
  44.5 14.8 %collective-permute-start.8 = (bf16[6,32,128]{2,1,0:T(8,128)(2,1)S(1)}, bf16[6,32,128]{2,1,0:T(8,128)(2,1)S(1)}, u32[]{:S(2)}, u32[]{:S(2)}) collective-permute-start(bf16[6,32,128]{2,1,0:T(8,128)(2,1)S(1)} %get-tuple-element.42), channel_id=1, source_target_pairs={{0,31},{1,0},{2,1},{3,2},{4,3},{5,4},{6,5},{7,6},{8,7},{9,8},{10,9... | collective-permute-start | bytes 147464 | tf_op jit(solution)/shard_map/ppermute | solution.py:375
  57.1 5.1 %collective-permute-start.10 = (bf16[17,32,128]{2,1,0:T(8,128)(2,1)S(1)}, bf16[17,32,128]{2,1,0:T(8,128)(2,1)S(1)}, u32[]{:S(2)}, u32[]{:S(2)}) collective-permute-start(bf16[17,32,128]{2,1,0:T(8,128)(2,1)S(1)} %get-tuple-element.44), channel_id=1, source_target_pairs={{0,28},{1,29},{2,30},{3,31},{4,0},{5,1},{6,2},{7,3},{8,4},{9,5},{1... | collective-permute-start | bytes 417800 | tf_op jit(solution)/shard_map/ppermute | solution.py:375
  57.4 6.3 %collective-permute-start.9 = (bf16[17,32,128]{2,1,0:T(8,128)(2,1)S(1)}, bf16[17,32,128]{2,1,0:T(8,128)(2,1)S(1)}, u32[]{:S(2)}, u32[]{:S(2)}) collective-permute-start(bf16[17,32,128]{2,1,0:T(8,128)(2,1)S(1)} %get-tuple-element.43), channel_id=1, source_target_pairs={{0,4},{1,5},{2,6},{3,7},{4,8},{5,9},{6,10},{7,11},{8,12},{9,13},{1... | collective-permute-start | bytes 417800 | tf_op jit(solution)/shard_map/ppermute | solution.py:375
  59.2 4.4 %copy-start.6 = (f32[4,4096]{1,0:T(4,128)S(1)}, f32[4,4096]{1,0:T(4,128)}, u32[]{:S(2)}) copy-start(f32[4,4096]{1,0:T(4,128)} %refs_2_.1) | copy-start | bytes 196612

commit v3 on v2

--- a/solution.py
+++ b/solution.py
@@ -57,7 +57,18 @@
     return ref[lead + (slice(group * LANES, (group + 1) * LANES),)]
 
 
-def first_kernel(dinv, residual, couple, dense_dinv, dense_residual, smooth, message):
+def first_kernel(*refs):
+    sources = refs[:3]
+    dense_dinv, dense_residual, smooth, message = refs[3:7]
+    dinv, residual, couple, semaphores = refs[7:]
+    copies = [
+        pltpu.make_async_copy(source, target, semaphores.at[i])
+        for i, (source, target) in enumerate(zip(sources, (dinv, residual, couple)))
+    ]
+    for copy in copies:
+        copy.start()
+    for copy in copies:
+        copy.wait()
     groups = smooth.shape[1]
     coarse_groups = message.shape[1]
     for g in range(groups):
@@ -170,23 +181,49 @@
     return solved
 
 
+def sort_sides(even, outer, inner, after, before):
+    @pl.when(even)
+    def _():
+        after[...] = outer[...]
+        before[...] = inner[...]
+
+    @pl.when(jnp.logical_not(even))
+    def _():
+        after[...] = inner[...]
+        before[...] = outer[...]
+
+
+def put_sides(even, outer, inner, rows, to_next, to_prev):
+    @pl.when(even)
+    def _():
+        outer[rows] = to_prev
+        inner[rows] = to_next
+
+    @pl.when(jnp.logical_not(even))
+    def _():
+        outer[rows] = to_next
+        inner[rows] = to_prev
+
+
 def halo_kernel(*refs, sizes, stage, scale_old, scale_new, unroll=4):
     pieces = len(sizes)
-    (col, ghost, after, before, residual, dinv, smooth, update, bonds) = refs[:9]
-    picked_refs = refs[9 : 9 + pieces]
-    refs = refs[9 + pieces :]
+    (place, col, ghost, outer, inner, residual, dinv, smooth, update, bonds) = refs[:10]
+    picked_refs = refs[10 : 10 + pieces]
+    refs = refs[10 + pieces :]
+    even = (place[1] & 1) == 0
     if stage == 0:
         rhs, arrived, coarse_dinv = refs[:3]
-        new_smooth, new_update, base, to_next, to_prev = refs[3:8]
+        new_smooth, new_update, base, out_outer, out_inner = refs[3:8]
         refs = refs[8:]
     elif stage == 1:
-        first_after, first_before, base, couple_own = refs[:4]
-        new_smooth, new_update, to_next, to_prev, far_next, far_prev = refs[4:10]
+        first_outer, first_inner, base, couple_own = refs[:4]
+        new_smooth, new_update, out_outer, out_inner, far_next, far_prev = refs[4:10]
         refs = refs[10:]
     else:
         (new_smooth,) = refs[:1]
         refs = refs[1:]
-    slots, table, applied = refs
+    slots, table, applied, after, before = refs[:5]
+    sort_sides(even, outer, inner, after, before)
     groups = smooth.shape[1]
     if stage == 0:
         vector = [rhs[e] + arrived[e] for e in range(3)]
@@ -200,14 +237,14 @@
                 base[c, g : g + 1, :] = total
         for c in range(3):
             row = base[c].astype(BF16)
-            to_next[3 + c] = row
-            to_prev[3 + c] = row
-        to_next[6:10] = after[3:7]
-        to_prev[6:10] = before[3:7]
+            out_outer[3 + c] = row
+            out_inner[3 + c] = row
+        put_sides(even, out_outer, out_inner, slice(6, 10), after[3:7], before[3:7])
     elif stage == 1:
+        first_after, first_before = refs[5:7]
+        sort_sides(even, first_outer, first_inner, first_after, first_before)
         own = base[...].astype(BF16)
-        to_next[3:6] = after[3:6]
-        to_prev[3:6] = before[3:6]
+        put_sides(even, out_outer, out_inner, slice(3, 6), after[3:6], before[3:6])
         for message in (far_next, far_prev):
             message[0:3] = after[3:6]
             message[3:6] = own
@@ -272,49 +309,60 @@
         new_smooth[c] = total
         if stage < SWEEPS - 1:
             new_update[c] = change
-            to_next[c] = total.astype(BF16)
-            to_prev[c] = total.astype(BF16)
+            out_outer[c] = total.astype(BF16)
+            out_inner[c] = total.astype(BF16)
 
 
 def coarse_kernel(*refs):
-    (place, base, own_couple, first_after, first_before, second_after, second_before) = refs[:7]
-    (third_after, third_before, far_after, far_before, aggregate, smooth) = refs[7:13]
-    out, field, links = refs[13:]
+    (place, base, own_couple) = refs[:3]
+    first, second, third = refs[3:5], refs[5:7], refs[7:9]
+    far_after, far_before, aggregate, smooth = refs[9:13]
+    out, field, links, kept = refs[13:]
     subs, me = place[0], place[1]
     groups = base.shape[1]
+    even = (me & 1) == 0
 
     def valid(row):
         inside = jnp.logical_and(me + row >= 0, me + row < subs)
         return jnp.where(inside, 1.0, 0.0).astype(F32)
 
+    def from_after(pair):
+        return lambda i: jnp.where(even, pair[0][i].astype(F32), pair[1][i].astype(F32))
+
+    def from_before(pair):
+        return lambda i: jnp.where(even, pair[1][i].astype(F32), pair[0][i].astype(F32))
+
+    def plain(ref):
+        return lambda i: ref[i].astype(F32)
+
     base_rows = {
-        -5: (far_after, 0),
-        -4: (far_after, 3),
-        -3: (far_after, 6),
-        -2: (third_after, 3),
-        -1: (second_after, 3),
-        1: (second_before, 3),
-        2: (third_before, 3),
-        3: (far_before, 0),
-        4: (far_before, 3),
-        5: (far_before, 6),
+        -5: (plain(far_after), 0),
+        -4: (plain(far_after), 3),
+        -3: (plain(far_after), 6),
+        -2: (from_after(third), 3),
+        -1: (from_after(second), 3),
+        1: (from_before(second), 3),
+        2: (from_before(third), 3),
+        3: (plain(far_before), 0),
+        4: (plain(far_before), 3),
+        5: (plain(far_before), 6),
     }
     link_rows = {
-        -4: (far_after, 9),
-        -3: (far_after, 13),
-        -2: (second_after, 6),
-        -1: (first_after, 3),
-        1: (first_before, 3),
-        2: (second_before, 6),
-        3: (far_before, 9),
-        4: (far_before, 13),
+        -4: (plain(far_after), 9),
+        -3: (plain(far_after), 13),
+        -2: (from_after(second), 6),
+        -1: (from_after(first), 3),
+        1: (from_before(first), 3),
+        2: (from_before(second), 6),
+        3: (plain(far_before), 9),
+        4: (plain(far_before), 13),
     }
 
     def base_of(row, c):
         if row == 0:
             return base[c]
         ref, start = base_rows[row]
-        return ref[start + c].astype(F32) * valid(row)
+        return ref(start + c) * valid(row)
 
     for k in range(4):
         for g in range(groups):
@@ -323,10 +371,12 @@
             ]
     for row, (ref, start) in link_rows.items():
         for k in range(4):
-            links[row + STEPS - 1, k] = ref[start + k].astype(F32) * valid(row)
+            links[row + STEPS - 1, k] = ref(start + k) * valid(row)
     for row in range(-STEPS, STEPS + 1):
         for c in range(3):
-            field[0, row + STEPS, c] = base_of(row, c)
+            value = base_of(row, c)
+            kept[row + STEPS, c] = value
+            field[0, row + STEPS, c] = value
     lane = lax.broadcasted_iota(jnp.int32, (groups, LANES), 1)
     line = lax.broadcasted_iota(jnp.int32, (groups, LANES), 0)
     for step in range(STEPS):
@@ -345,7 +395,7 @@
                 left = jnp.where(
                     jnp.logical_and(lane == LANES - 1, line == groups - 1), 0.0, left
                 )
-                field[new, spot, c] = base_of(row, c) + (
+                field[new, spot, c] = kept[spot, c] + (
                     weights[0] * field[old, spot - 1, c]
                     + weights[1] * field[old, spot + 1, c]
                     + weights[2] * right
@@ -375,6 +425,15 @@
     return lax.ppermute(value, "sub", [(i, (i + steps) % count) for i in range(count)])
 
 
+def exchanged_by_pairs(outer, inner):
+    count = lax.axis_size("sub")
+    across = [(i, (i + 1) % count) for i in range(1, count, 2)]
+    within = [(i, i + 1) for i in range(0, count, 2)]
+    outer = lax.ppermute(outer, "sub", across + [(j, i) for i, j in across])
+    inner = lax.ppermute(inner, "sub", within + [(j, i) for i, j in within])
+    return outer, inner
+
+
 def body(
     fine_residual, bonds, bond_col, ghost_points, fine_dinv, aggregate, coarse_dinv, coarse_couple
 ):
@@ -399,14 +458,23 @@
     dinv, residual, smooth, packed = call(
         first_kernel,
         (sds((3, 3, groups, LANES), F32), field, field, message(7)),
-        (fine_dinv, fine_residual, coarse_couple),
+        tuple(
+            pltpu.with_memory_space_constraint(x, pltpu.HBM)
+            for x in (fine_dinv, fine_residual, coarse_couple)
+        ),
+        scratch=[
+            VMEM(fine_dinv.shape, F32),
+            VMEM(fine_residual.shape, F32),
+            VMEM(coarse_couple.shape, F32),
+            pltpu.SemaphoreType.DMA((3,)),
+        ],
         us=2.0,
+        spaces={i: pltpu.HBM for i in range(3)},
     )
     update = smooth
     own_packed = packed
-    after = shifted(packed, 1)
-    before = shifted(packed, -1)
-    first_after, first_before = after, before
+    place = jnp.stack([jnp.int32(lax.axis_size("sub")), sub.astype(jnp.int32)])
+    first = arrived_sides = exchanged_by_pairs(packed, packed)
     rhs = call(restrict_kernel, coarse_field, (residual, agg), us=2.5)
 
     def local(smooth, first, tiles):
@@ -440,13 +508,18 @@
         if stage:
             sizes = (groups,)
             parts = [local(smooth, 0, groups)]
-        inputs = [bond_col, ghost, after, before, residual, dinv, smooth, update, relaid]
+        if stage == SWEEPS - 1:
+            parts[0], far_after, far_before = lax.optimization_barrier(
+                (parts[0], far_after, far_before)
+            )
+        inputs = [place, bond_col, ghost, *arrived_sides]
+        inputs += [residual, dinv, smooth, update, relaid]
         inputs += parts
         if stage == 0:
             inputs += [rhs, arrived, coarse_dinv]
             outs = (field, field, coarse_field, message(10), message(10))
         elif stage == 1:
-            inputs += [first_after, first_before, base, own_packed]
+            inputs += [*first, base, own_packed]
             outs = (field, field, message(6), message(6), message(17), message(17))
         else:
             outs = (field,)
@@ -464,23 +537,24 @@
                 VMEM((3,) + ghost.shape, F32),
                 VMEM((3, ghost.shape[0], PACK, LANES), BF16),
                 VMEM((3, groups, LANES), F32),
-            ],
+                VMEM(arrived_sides[0].shape, BF16),
+                VMEM(arrived_sides[0].shape, BF16),
+            ]
+            + [VMEM(first[0].shape, BF16)] * (2 if stage == 1 else 0),
             us=4.0,
+            spaces={0: pltpu.SMEM},
         )
         factor = factor_new
         if stage == 0:
-            smooth, update, base, to_next, to_prev = result
-            after = second_after = shifted(to_next, 1)
-            before = second_before = shifted(to_prev, -1)
+            smooth, update, base, outer, inner = result
+            second = arrived_sides = exchanged_by_pairs(outer, inner)
         elif stage == 1:
-            smooth, update, to_next, to_prev, far_next, far_prev = result
-            after = third_after = shifted(to_next, 1)
-            before = third_before = shifted(to_prev, -1)
+            smooth, update, outer, inner, far_next, far_prev = result
+            third = arrived_sides = exchanged_by_pairs(outer, inner)
             far_after = shifted(far_next, 4)
             far_before = shifted(far_prev, -4)
         else:
             (smooth,) = result
-    place = jnp.stack([jnp.int32(lax.axis_size("sub")), sub.astype(jnp.int32)])
     return call(
         coarse_kernel,
         sds((3, points), F32),
@@ -488,12 +562,9 @@
             place,
             base,
             coarse_couple,
-            first_after,
-            first_before,
-            second_after,
-            second_before,
-            third_after,
-            third_before,
+            *first,
+            *second,
+            *third,
             far_after,
             far_before,
             agg,
@@ -502,6 +573,7 @@
         scratch=[
             VMEM((2, 2 * STEPS + 1, 3, coarse_groups, LANES), F32),
             VMEM((2 * STEPS - 1, 4, coarse_groups, LANES), F32),
+            VMEM((2 * STEPS + 1, 3, coarse_groups, LANES), F32),
         ],
         us=2.0,
         spaces={0: pltpu.SMEM},

time: 66.3 us -> 62.2 us (0.938)
  the two profiles are of different devices: /device:TPU:24 before, /device:TPU:1 now
where the time goes in v3:
time: 62.2 us; the launch traced here: 62.1 us
  Pallas kernels  36.8 us (59%)
  starting transfers between devices  24.9 us (40%)
    pallas_call x11, Pallas kernels, call(): pl.pallas_call(kernel, out_shape=out, in_specs=[pl.BlockSpec(memory_space...  36.8 us
    ppermute x3, starting transfers between devices, exchanged_by_pairs(): inner = lax.ppermute(inner, 'sub', within + [(j, i) for i, j in within])  12.4 us
    ppermute x3, starting transfers between devices, exchanged_by_pairs(): outer = lax.ppermute(outer, 'sub', across + [(j, i) for i, j in across])  5.43 us
    ppermute x3, starting transfers between devices, exchanged(): return lax.ppermute(value, 'dom', [(i, i ^ step) for i in range(doms)])  4.43 us
    ppermute x2, starting transfers between devices, shifted(): lax.ppermute(value, 'sub', [(i, (i + steps) % count) for i in range(count)])  2.68 us
  transfers between devices with their start and end apart: 11, of which 0 were waited for; matrix products, arithmetic and copies ran while one was open for 0% of the time, Pallas kernels for 37%

profile of v3, /device:TPU:1, one launch (start us, length us, event | category | flops | bytes accessed | tf_op | source)
XLA Modules:
  0.0 62.1 jit_solution(6906399242719519764)
XLA Ops:
  0.0 1.3 %shard_map.82 = (f32[3,3,32,128]{3,2,1,0:T(8,128)S(1)}, f32[3,32,128]{2,1,0:T(8,128)S(1)}, f32[3,32,128]{2,1,0:T(8,128)S(1)}, bf16[7,32,128]{2,1,0:T(8,128)(2,1)S(1)}) custom-call(f32[3,3,4096]{2,1,0:T(4,128)} %refs_0_.1, f32[3,4096]{1,0:T(4,128)} %refs_1_.4, f32[4,4096]{1,0:T(4,128)} %refs_2_.3), custom_call_target="tpu_custom_call" | custom-call | flops 2000000000 | bytes 2000000 | tf_op jit(solution)/shard_map/pallas_call | solution.py:41
  1.3 3.3 %collective-permute-start.1 = (bf16[7,32,128]{2,1,0:T(8,128)(2,1)S(1)}, bf16[7,32,128]{2,1,0:T(8,128)(2,1)S(1)}, u32[]{:S(2)}, u32[]{:S(2)}) collective-permute-start(bf16[7,32,128]{2,1,0:T(8,128)(2,1)S(1)} %get-tuple-element.29.refs_14_), channel_id=1, source_target_pairs={{0,1},{2,3},{4,5},{6,7},{8,9},{10,11},{12,13},{14,15},{16,17},{18,... | collective-permute-start | bytes 172040 | tf_op jit(solution)/shard_map/ppermute | solution.py:433
  4.6 1.0 %collective-permute-start = (bf16[7,32,128]{2,1,0:T(8,128)(2,1)S(1)}, bf16[7,32,128]{2,1,0:T(8,128)(2,1)S(1)}, u32[]{:S(2)}, u32[]{:S(2)}) collective-permute-start(bf16[7,32,128]{2,1,0:T(8,128)(2,1)S(1)} %get-tuple-element.29.refs_14_), channel_id=1, source_target_pairs={{1,2},{3,4},{5,6},{7,8},{9,10},{11,12},{13,14},{15,16},{17,18},{19... | collective-permute-start | bytes 172040 | tf_op jit(solution)/shard_map/ppermute | solution.py:432
  5.6 1.2 %shard_map.83 = f32[3,32,128]{2,1,0:T(8,128)S(1)} custom-call(f32[3,32,128]{2,1,0:T(8,128)S(1)} %get-tuple-element.30.residual.refs_5_, s32[32,128]{1,0:T(8,128)S(1)} %bitcast.6), custom_call_target="tpu_custom_call" | custom-call | flops 2500000000 | bytes 2500000 | tf_op jit(solution)/shard_map/pallas_call | solution.py:41
  6.8 0.3 collective-permute-start.2
  7.1 2.8 %shard_map.84.refs_10_ = bf16[3,32,1536]{2,1,0:T(8,128)(2,1)S(1)} custom-call(f32[3,32,128]{2,1,0:T(8,128)S(1)} %get-tuple-element.37.smooth.refs_7_.refs_8_, s32[32,4096]{1,0:T(8,128)S(1)} %copy-done.1), custom_call_target="tpu_custom_call" | custom-call | flops 2812499968 | bytes 2812500 | tf_op jit(solution)/shard_map/pallas_call | solution.py:41
  9.9 0.1 pad_add_fusion.refs_0_
  10.0 0.0 collective-permute-done.2
  10.0 1.4 %collective-permute-start.3 = (f32[3,32,128]{2,1,0:T(8,128)S(1)}, f32[3,32,128]{2,1,0:T(8,128)S(1)}, u32[]{:S(2)}, u32[]{:S(2)}) collective-permute-start(f32[3,32,128]{2,1,0:T(8,128)S(1)} %add.6), channel_id=1, source_target_pairs={{0,64},{32,96},{64,0},{96,32},{128,192},{160,224},{192,128},{224,1... | collective-permute-start | bytes 147464 | tf_op jit(solution)/shard_map/ppermute | solution.py:490
  11.4 2.7 %shard_map.85.refs_11_ = bf16[3,32,1536]{2,1,0:T(8,128)(2,1)S(1)} custom-call(f32[3,32,128]{2,1,0:T(8,128)S(1)} %get-tuple-element.37.smooth.refs_7_.refs_8_, s32[32,4096]{1,0:T(8,128)S(1)} %copy-done.1), custom_call_target="tpu_custom_call" | custom-call | flops 2812499968 | bytes 2812500 | tf_op jit(solution)/shard_map/pallas_call | solution.py:41
  14.1 0.0 collective-permute-done.3
  14.1 0.0 copy-start
  14.2 0.0 copy-start.2
  14.2 2.7 %collective-permute-start.4 = (f32[3,32,128]{2,1,0:T(8,128)S(1)}, f32[3,32,128]{2,1,0:T(8,128)S(1)}, u32[]{:S(2)}, u32[]{:S(2)}) collective-permute-start(f32[3,32,128]{2,1,0:T(8,128)S(1)} %add.7.refs_13_), channel_id=1, source_target_pairs={{0,128},{32,160},{64,192},{96,224},{128,0},{160,32},{192,64},{224,... | collective-permute-start | bytes 147464 | tf_op jit(solution)/shard_map/ppermute | solution.py:490
  16.9 1.8 %shard_map.86.refs_12_ = bf16[3,32,1024]{2,1,0:T(8,128)(2,1)S(1)} custom-call(f32[3,32,128]{2,1,0:T(8,128)S(1)} %get-tuple-element.37.smooth.refs_7_.refs_8_, s32[32,4096]{1,0:T(8,128)S(1)} %copy-done.1), custom_call_target="tpu_custom_call" | custom-call | flops 1875000064 | bytes 1875000 | tf_op jit(solution)/shard_map/pallas_call | solution.py:41
  18.7 0.0 collective-permute-done.1.refs_4_.refs_12_
  18.7 0.0 collective-permute-done.refs_3_.refs_11_
  18.8 3.4 %shard_map.87 = (f32[3,32,128]{2,1,0:T(8,128)S(1)}, f32[3,32,128]{2,1,0:T(8,128)S(1)}, f32[3,32,128]{2,1,0:T(8,128)S(1)}, bf16[10,32,128]{2,1,0:T(8,128)(2,1)S(1)}, bf16[10,32,128]{2,1,0:T(8,128)(2,1)S(1)}) custom-call(s32[2]{0:T(128)S(1)} %pad_add_fusion.refs_0_, s32[32,4096]{1,0:T(8,128)S(1)} %copy-done.1, s32[8,128]{1,0:T(8,128)S(1)} %reshape.6.refs_2_, ...), custom_call_target="tpu_custom_call" | custom-call | flops 4000000000 | bytes 4000000 | tf_op jit(solution)/shard_map/pallas_call | solution.py:41
  22.2 4.3 %collective-permute-start.5 = (bf16[10,32,128]{2,1,0:T(8,128)(2,1)S(1)}, bf16[10,32,128]{2,1,0:T(8,128)(2,1)S(1)}, u32[]{:S(2)}, u32[]{:S(2)}) collective-permute-start(bf16[10,32,128]{2,1,0:T(8,128)(2,1)S(1)} %get-tuple-element.40), channel_id=1, source_target_pairs={{1,2},{3,4},{5,6},{7,8},{9,10},{11,12},{13,14},{15,16},{17,18},{19... | collective-permute-start | bytes 245768 | tf_op jit(solution)/shard_map/ppermute | solution.py:432
  26.6 3.8 %collective-permute-start.6 = (bf16[10,32,128]{2,1,0:T(8,128)(2,1)S(1)}, bf16[10,32,128]{2,1,0:T(8,128)(2,1)S(1)}, u32[]{:S(2)}, u32[]{:S(2)}) collective-permute-start(bf16[10,32,128]{2,1,0:T(8,128)(2,1)S(1)} %get-tuple-element.41), channel_id=1, source_target_pairs={{0,1},{2,3},{4,5},{6,7},{8,9},{10,11},{12,13},{14,15},{16,17},{18,... | collective-permute-start | bytes 245768 | tf_op jit(solution)/shard_map/ppermute | solution.py:433
  30.4 7.3 %shard_map.88.refs_10_ = bf16[3,32,4096]{2,1,0:T(8,128)(2,1)S(1)} custom-call(f32[3,32,128]{2,1,0:T(8,128)S(1)} %get-tuple-element.42.smooth.refs_7_, s32[32,4096]{1,0:T(8,128)S(1)} %copy-done.1), custom_call_target="tpu_custom_call" | custom-call | flops 7500000256 | bytes 7500000 | tf_op jit(solution)/shard_map/pallas_call | solution.py:41
  37.7 0.0 collective-permute-done.5.refs_3_.refs_5_
  37.7 3.3 %shard_map.89 = (f32[3,32,128]{2,1,0:T(8,128)S(1)}, f32[3,32,128]{2,1,0:T(8,128)S(1)}, bf16[6,32,128]{2,1,0:T(8,128)(2,1)S(1)}, bf16[6,32,128]{2,1,0:T(8,128)(2,...) custom-call(s32[2]{0:T(128)S(1)} %pad_add_fusion.refs_0_, s32[32,4096]{1,0:T(8,128)S(1)} %copy-done.1, ...), custom_call_target="tpu_custom_call" | custom-call | flops 4000000000 | bytes 4000000 | tf_op jit(solution)/shard_map/pallas_call | solution.py:41
  41.0 0.1 collective-permute-start.7
  41.1 5.2 %collective-permute-start.8 = (bf16[6,32,128]{2,1,0:T(8,128)(2,1)S(1)}, bf16[6,32,128]{2,1,0:T(8,128)(2,1)S(1)}, u32[]{:S(2)}, u32[]{:S(2)}) collective-permute-start(bf16[6,32,128]{2,1,0:T(8,128)(2,1)S(1)} %get-tuple-element.45), channel_id=1, source_target_pairs={{0,1},{2,3},{4,5},{6,7},{8,9},{10,11},{12,13},{14,15},{16,17},{18,... | collective-permute-start | bytes 147464 | tf_op jit(solution)/shard_map/ppermute | solution.py:433
  46.4 0.0 collective-permute-start.9
  46.4 2.7 %collective-permute-start.10 = (bf16[17,32,128]{2,1,0:T(8,128)(2,1)S(1)}, bf16[17,32,128]{2,1,0:T(8,128)(2,1)S(1)}, u32[]{:S(2)}, u32[]{:S(2)}) collective-permute-start(bf16[17,32,128]{2,1,0:T(8,128)(2,1)S(1)} %get-tuple-element.48), channel_id=1, source_target_pairs={{0,28},{1,29},{2,30},{3,31},{4,0},{5,1},{6,2},{7,3},{8,4},{9,5},{1... | collective-permute-start | bytes 417800 | tf_op jit(solution)/shard_map/ppermute | solution.py:425
  49.0 7.3 %shard_map.90.refs_10_ = bf16[3,32,4096]{2,1,0:T(8,128)(2,1)S(1)} custom-call(f32[3,32,128]{2,1,0:T(8,128)S(1)} %get-tuple-element.46.smooth.refs_7_, s32[32,4096]{1,0:T(8,128)S(1)} %copy-done.1), custom_call_target="tpu_custom_call" | custom-call | flops 7500000256 | bytes 7500000 | tf_op jit(solution)/shard_map/pallas_call | solution.py:41
  56.3 0.0 collective-permute-done.10.refs_10_
  56.4 0.0 copy-start.3
  56.4 3.3 %shard_map.91.refs_12_ = f32[3,32,128]{2,1,0:T(8,128)S(1)} custom-call(s32[2]{0:T(128)S(1)} %pad_add_fusion.refs_0_, s32[32,4096]{1,0:T(8,128)S(1)} %copy-done.1, s32[8,128]{1,0:T(8,128)S(1)} %reshape.6.refs_2_, bf16[6,32,128]{2,1,0:T(8,128)(2,1)S(1)} %collective-permute-done.7.refs_3_.refs_7_, ...), custom_call_target="tpu_custom_call" | custom-call | flops 4000000000 | bytes 4000000 | tf_op jit(solution)/shard_map/pallas_call | solution.py:41
  59.7 2.4 %shard_map.92 = f32[3,4096]{1,0:T(4,128)} custom-call(s32[2]{0:T(128)S(1)} %pad_add_fusion.refs_0_, f32[3,32,128]{2,1,0:T(8,128)S(1)} %get-tuple-element.39.refs_13_.refs_1_, f32[4,4096]{1,0:T(4,128)S(1)} %copy-done.3, bf16[7,32,128]{2,1,0:T(8,128)(2,1)S(1)} %collective-permute-done.refs_3_.refs_11_, ...), custom_call_target="tpu_custom_call" | custom-call | flops 2000000000 | bytes 2000000 | tf_op jit(solution)/shard_map/pallas_call | solution.py:41
  (17 shorter events, 0.1 us)
Async XLA Ops:
  0.0 5.6 %copy-start.4 = (s32[4096]{0:T(1024)S(1)}, s32[4096]{0:T(1024)}, u32[]{:S(2)}) copy-start(s32[4096]{0:T(1024)} %param.13) | copy-start | bytes 49156
  1.3 17.5 %collective-permute-start.1 = (bf16[7,32,128]{2,1,0:T(8,128)(2,1)S(1)}, bf16[7,32,128]{2,1,0:T(8,128)(2,1)S(1)}, u32[]{:S(2)}, u32[]{:S(2)}) collective-permute-start(bf16[7,32,128]{2,1,0:T(8,128)(2,1)S(1)} %get-tuple-element.29.refs_14_), channel_id=1, source_target_pairs={{0,1},{2,3},{4,5},{6,7},{8,9},{10,11},{12,13},{14,15},{16,17},{18,... | collective-permute-start | bytes 172040 | tf_op jit(solution)/shard_map/ppermute | solution.py:433
  4.6 14.1 %collective-permute-start = (bf16[7,32,128]{2,1,0:T(8,128)(2,1)S(1)}, bf16[7,32,128]{2,1,0:T(8,128)(2,1)S(1)}, u32[]{:S(2)}, u32[]{:S(2)}) collective-permute-start(bf16[7,32,128]{2,1,0:T(8,128)(2,1)S(1)} %get-tuple-element.29.refs_14_), channel_id=1, source_target_pairs={{1,2},{3,4},{5,6},{7,8},{9,10},{11,12},{13,14},{15,16},{17,18},{19... | collective-permute-start | bytes 172040 | tf_op jit(solution)/shard_map/ppermute | solution.py:432
  5.6 1.5 %copy-start.1 = (s32[32,4096]{1,0:T(8,128)S(1)}, s32[32,4096]{1,0:T(8,128)}, u32[]{:S(2)}) copy-start(s32[32,4096]{1,0:T(8,128)} %refs_1_.7) | copy-start | bytes 1572868
  6.8 3.2 %collective-permute-start.2 = (f32[3,32,128]{2,1,0:T(8,128)S(1)}, f32[3,32,128]{2,1,0:T(8,128)S(1)}, u32[]{:S(2)}, u32[]{:S(2)}) collective-permute-start(f32[3,32,128]{2,1,0:T(8,128)S(1)} %shard_map.83), channel_id=1, source_target_pairs={{0,32},{32,0},{64,96},{96,64},{128,160},{160,128},{192,224},{224,1... | collective-permute-start | bytes 147464 | tf_op jit(solution)/shard_map/ppermute | solution.py:490
  7.1 2.8 %copy-start.5 = (s32[1,2,512]{2,1,0:T(2,128)S(1)}, s32[1,2,512]{2,1,0:T(2,128)}, u32[]{:S(2)}) copy-start(s32[1,2,512]{2,1,0:T(2,128)} %param.11) | copy-start | bytes 12292
  10.0 4.1 %collective-permute-start.3 = (f32[3,32,128]{2,1,0:T(8,128)S(1)}, f32[3,32,128]{2,1,0:T(8,128)S(1)}, u32[]{:S(2)}, u32[]{:S(2)}) collective-permute-start(f32[3,32,128]{2,1,0:T(8,128)S(1)} %add.6), channel_id=1, source_target_pairs={{0,64},{32,96},{64,0},{96,32},{128,192},{160,224},{192,128},{224,1... | collective-permute-start | bytes 147464 | tf_op jit(solution)/shard_map/ppermute | solution.py:490
  14.1 4.6 %copy-start = (bf16[32,3,3,4096]{3,0,2,1:T(8,128)(2,1)S(1)}, bf16[32,3,3,4096]{3,0,2,1:T(8,128)(2,1)}, u32[]{:S(2)}) copy-start(bf16[32,3,3,4096]{3,0,2,1:T(8,128)(2,1)} %param.9) | copy-start | bytes 7077892
  14.2 4.6 %copy-start.2 = (f32[3,3,4096]{2,1,0:T(4,128)S(1)}, f32[3,3,4096]{2,1,0:T(4,128)}, u32[]{:S(2)}) copy-start(f32[3,3,4096]{2,1,0:T(4,128)} %refs_15_.1) | copy-start | bytes 442372
  14.2 4.6 %collective-permute-start.4 = (f32[3,32,128]{2,1,0:T(8,128)S(1)}, f32[3,32,128]{2,1,0:T(8,128)S(1)}, u32[]{:S(2)}, u32[]{:S(2)}) collective-permute-start(f32[3,32,128]{2,1,0:T(8,128)S(1)} %add.7.refs_13_), channel_id=1, source_target_pairs={{0,128},{32,160},{64,192},{96,224},{128,0},{160,32},{192,64},{224,... | collective-permute-start | bytes 147464 | tf_op jit(solution)/shard_map/ppermute | solution.py:490
  22.2 15.5 %collective-permute-start.5 = (bf16[10,32,128]{2,1,0:T(8,128)(2,1)S(1)}, bf16[10,32,128]{2,1,0:T(8,128)(2,1)S(1)}, u32[]{:S(2)}, u32[]{:S(2)}) collective-permute-start(bf16[10,32,128]{2,1,0:T(8,128)(2,1)S(1)} %get-tuple-element.40), channel_id=1, source_target_pairs={{1,2},{3,4},{5,6},{7,8},{9,10},{11,12},{13,14},{15,16},{17,18},{19... | collective-permute-start | bytes 245768 | tf_op jit(solution)/shard_map/ppermute | solution.py:432
  26.6 11.1 %collective-permute-start.6 = (bf16[10,32,128]{2,1,0:T(8,128)(2,1)S(1)}, bf16[10,32,128]{2,1,0:T(8,128)(2,1)S(1)}, u32[]{:S(2)}, u32[]{:S(2)}) collective-permute-start(bf16[10,32,128]{2,1,0:T(8,128)(2,1)S(1)} %get-tuple-element.41), channel_id=1, source_target_pairs={{0,1},{2,3},{4,5},{6,7},{8,9},{10,11},{12,13},{14,15},{16,17},{18,... | collective-permute-start | bytes 245768 | tf_op jit(solution)/shard_map/ppermute | solution.py:433
  41.0 15.4 %collective-permute-start.7 = (bf16[6,32,128]{2,1,0:T(8,128)(2,1)S(1)}, bf16[6,32,128]{2,1,0:T(8,128)(2,1)S(1)}, u32[]{:S(2)}, u32[]{:S(2)}) collective-permute-start(bf16[6,32,128]{2,1,0:T(8,128)(2,1)S(1)} %get-tuple-element.44), channel_id=1, source_target_pairs={{1,2},{3,4},{5,6},{7,8},{9,10},{11,12},{13,14},{15,16},{17,18},{19... | collective-permute-start | bytes 147464 | tf_op jit(solution)/shard_map/ppermute | solution.py:432
  41.1 15.3 %collective-permute-start.8 = (bf16[6,32,128]{2,1,0:T(8,128)(2,1)S(1)}, bf16[6,32,128]{2,1,0:T(8,128)(2,1)S(1)}, u32[]{:S(2)}, u32[]{:S(2)}) collective-permute-start(bf16[6,32,128]{2,1,0:T(8,128)(2,1)S(1)} %get-tuple-element.45), channel_id=1, source_target_pairs={{0,1},{2,3},{4,5},{6,7},{8,9},{10,11},{12,13},{14,15},{16,17},{18,... | collective-permute-start | bytes 147464 | tf_op jit(solution)/shard_map/ppermute | solution.py:433
  46.4 10.0 %collective-permute-start.9 = (bf16[17,32,128]{2,1,0:T(8,128)(2,1)S(1)}, bf16[17,32,128]{2,1,0:T(8,128)(2,1)S(1)}, u32[]{:S(2)}, u32[]{:S(2)}) collective-permute-start(bf16[17,32,128]{2,1,0:T(8,128)(2,1)S(1)} %get-tuple-element.47), channel_id=1, source_target_pairs={{0,4},{1,5},{2,6},{3,7},{4,8},{5,9},{6,10},{7,11},{8,12},{9,13},{1... | collective-permute-start | bytes 417800 | tf_op jit(solution)/shard_map/ppermute | solution.py:425
  46.4 10.0 %collective-permute-start.10 = (bf16[17,32,128]{2,1,0:T(8,128)(2,1)S(1)}, bf16[17,32,128]{2,1,0:T(8,128)(2,1)S(1)}, u32[]{:S(2)}, u32[]{:S(2)}) collective-permute-start(bf16[17,32,128]{2,1,0:T(8,128)(2,1)S(1)} %get-tuple-element.48), channel_id=1, source_target_pairs={{0,28},{1,29},{2,30},{3,31},{4,0},{5,1},{6,2},{7,3},{8,4},{9,5},{1... | collective-permute-start | bytes 417800 | tf_op jit(solution)/shard_map/ppermute | solution.py:425
  56.4 3.3 %copy-start.3 = (f32[4,4096]{1,0:T(4,128)S(1)}, f32[4,4096]{1,0:T(4,128)}, u32[]{:S(2)}) copy-start(f32[4,4096]{1,0:T(4,128)} %refs_2_.3) | copy-start | bytes 196612

commit v4 on v3

--- a/solution.py
+++ b/solution.py
@@ -20,13 +20,13 @@
 VMEM = pltpu.VMEM
 
 
-def lane_gather(rows, index):
+def gather(rows, index, axis):
     numbers = lax.GatherDimensionNumbers(
         offset_dims=(),
-        collapsed_slice_dims=(1,),
-        start_index_map=(1,),
-        operand_batching_dims=(0,),
-        start_indices_batching_dims=(0,),
+        collapsed_slice_dims=(axis,),
+        start_index_map=(axis,),
+        operand_batching_dims=(1 - axis,),
+        start_indices_batching_dims=(1 - axis,),
     )
     return lax.gather(
         rows,
@@ -37,6 +37,39 @@
     )
 
 
+def lane_gather(rows, index):
+    return gather(rows, index, 1)
+
+
+def row_gather(rows, index):
+    return gather(rows, index, 0)
+
+
+def sorting_network(count):
+    pairs = []
+    span = 1
+    while span < count:
+        gap = span
+        while gap >= 1:
+            for j in range(gap % span, count - gap, 2 * gap):
+                for i in range(min(gap, count - j - gap)):
+                    if (i + j) // (2 * span) == (i + j + gap) // (2 * span):
+                        pairs.append((i + j, i + j + gap))
+            gap //= 2
+        span *= 2
+    return pairs
+
+
+def sort_planes(planes):
+    planes = list(planes)
+    for i, j in sorting_network(len(planes)):
+        planes[i], planes[j] = (
+            jnp.minimum(planes[i], planes[j]),
+            jnp.maximum(planes[i], planes[j]),
+        )
+    return planes
+
+
 def call(kernel, out, inputs, scratch=(), us=1.0, spaces={}, limit=16):
     return pl.pallas_call(
         kernel,
@@ -44,7 +77,9 @@
         in_specs=[
             pl.BlockSpec(memory_space=spaces.get(i, VMEM)) for i in range(len(inputs))
         ],
-        out_specs=jax.tree.map(lambda _: pl.BlockSpec(memory_space=VMEM), out),
+        out_specs=jax.tree.map(
+            lambda x: pl.BlockSpec(memory_space=pltpu.SMEM if x.shape == (2,) else VMEM), out
+        ),
         scratch_shapes=list(scratch),
         cost_estimate=pl.CostEstimate(
             flops=int(us * 1.0e9), transcendentals=0, bytes_accessed=int(us * 1.0e6)
@@ -132,43 +167,146 @@
         out[c] = total[c][:bins] + total[c][bins:]
 
 
-def fill_table(table, source, groups):
-    for e in range(3):
-        for g in range(groups):
-            row = source[e, g : g + 1, :]
-            table[e, g] = jnp.broadcast_to(row, (PACK, LANES)).astype(BF16)
-
-
-def pick(table, index, groups, first, starts):
-    low = (index & (LANES - 1)).astype(jnp.int16)
-    high = (index >> 7).astype(jnp.int16)
-    picked = list(starts)
-    for g in range(groups):
-        chosen = high == (first + g)
+def prepare_kernel(col, picks, start, halo_start, spot, rank, most, flip):
+    bonds_of = col.shape[0]
+    groups = col.shape[1] // LANES
+    stride = bonds_of + 1
+
+    def eight_tiles(block, carry):
+        best, halo_best = carry
+
+        def lanes_of(t):
+            return pl.ds(pl.multiple_of((block * 8 + t) * LANES, LANES), LANES)
+
+        for t in range(8):
+            flip[pl.ds(t * stride, bonds_of), :] = col[:, lanes_of(t)]
+        keys = []
+        for k in range(bonds_of):
+            c = flip[pl.ds(k, 8, stride=stride), :]
+            keys.append(((c >> 8) << 13) | (k << 8) | (c & 255))
+        keys = sort_planes(keys)
+        pairs = [key >> 13 for key in keys]
+        ranks = [jnp.zeros((8, LANES), jnp.int32)]
+        for k in range(1, bonds_of):
+            ranks.append(jnp.where(pairs[k] == pairs[k - 1], ranks[k - 1] + 1, 0))
+        back = []
+        for k in range(bonds_of):
+            local = pairs[k] < PACK
+            best = jnp.maximum(best, jnp.where(local, ranks[k], 0))
+            halo_best = jnp.maximum(halo_best, jnp.where(local, 0, ranks[k]))
+            code = jnp.where(
+                local,
+                (ranks[k] << 4) | pairs[k],
+                ((ranks[k] >> 2) << 4) | ((ranks[k] & 3) << 2) | ((pairs[k] - PACK) + (32 << 4)),
+            )
+            back.append((((keys[k] >> 8) & 31) << 10) | code)
+            flip[pl.ds(k, 8, stride=stride), :] = keys[k]
+        row = lax.broadcasted_iota(jnp.int32, (PACK, LANES), 0)
+        for t in range(8):
+            halves = [flip[pl.ds(t * stride + h * PACK, PACK), :] for h in range(2)]
+            for h in range(2):
+                picks[h * PACK : (h + 1) * PACK, lanes_of(t)] = (halves[h] & 255).astype(jnp.int16)
+            first, second = [(x >> 13).astype(jnp.int16) for x in halves]
+            for target, pair, extra in (
+                (start, row.astype(jnp.int16), None),
+                (halo_start, (PACK + (row & 3)).astype(jnp.int16), (row >> 2).astype(jnp.int16)),
+            ):
+                place = jnp.zeros((PACK, LANES), jnp.int16)
+                for step in (16, 8, 4, 2, 1, 1):
+                    probe = place + jnp.int16(step - 1)
+                    inner = probe & jnp.int16(PACK - 1)
+                    value = jnp.where(
+                        probe < PACK, row_gather(first, inner), row_gather(second, inner)
+                    )
+                    place = jnp.where(value < pair, place + jnp.int16(step), place)
+                target[:, lanes_of(t)] = place if extra is None else place + extra
+        back = sort_planes(back)
+        for k in range(bonds_of):
+            flip[pl.ds(k, 8, stride=stride), :] = back[k] & 1023
+        for t in range(8):
+            for h in range(2):
+                code = flip[pl.ds(t * stride + h * PACK, PACK), :]
+                rows = slice(h * PACK, (h + 1) * PACK)
+                spot[rows, lanes_of(t)] = (code & 15).astype(jnp.int16)
+                rank[rows, lanes_of(t)] = (code >> 4).astype(jnp.int16)
+        return best, halo_best
+
+    zero = jnp.zeros((8, LANES), jnp.int32)
+    best, halo_best = lax.fori_loop(0, groups // 8, eight_tiles, (zero, zero))
+    most[0] = jnp.max(best)
+    most[1] = jnp.max(halo_best) >> 2
+
+
+def layer(place, picks, even, odd):
+    inner = place & jnp.int16(PACK - 1)
+    pick = jnp.where(
+        place < PACK, row_gather(picks[0], inner), row_gather(picks[1], inner)
+    )
+    lane = pick & jnp.int16(LANES - 1)
+    second = pick >= LANES
+    return [
+        jnp.where(second, lane_gather(odd[e], lane), lane_gather(even[e], lane))
+        for e in range(3)
+    ]
+
+
+def put_back(values, number, spots, ranks, out):
+    for h in range(2):
+        hit = ranks[h] == number
         for e in range(3):
-            value = lane_gather(table[e, g], low)
-            picked[e] = jnp.where(chosen, value, picked[e])
-    return picked
-
-
-def local_kernel(smooth, col, out, table, *, first, tiles, unroll=4):
-    groups = smooth.shape[1]
-    fill_table(table, smooth, groups)
-    bonds_of = col.shape[0]
-    zero = jnp.zeros((PACK, LANES), BF16)
+            out[h][e] = jnp.where(hit, row_gather(values[e], spots[h]), out[h][e])
+
+
+def halves_of(ref, lanes):
+    return [ref[h * PACK : (h + 1) * PACK, lanes] for h in range(2)]
+
+
+def splat(number):
+    return jnp.full((PACK, LANES), number, jnp.int32).astype(jnp.int16)
+
+
+LAYERS = 10
+HALO_LAYERS = 3
+
+
+def local_kernel(smooth, picks, start, spot, rank, most, out, *, first, tiles, unroll=4):
+    even = [smooth[e, pl.ds(0, PACK, stride=2), :].astype(BF16) for e in range(3)]
+    odd = [smooth[e, pl.ds(1, PACK, stride=2), :].astype(BF16) for e in range(3)]
 
     def some_tiles(t, carry):
         for u in range(unroll):
-            source = pl.multiple_of((first + t * unroll + u) * LANES, LANES)
-            target = pl.multiple_of((t * unroll + u) * LANES, LANES)
-            for h in range(bonds_of // PACK):
-                rows = pl.ds(h * PACK, PACK)
-                picked = pick(table, col[rows, pl.ds(source, LANES)], groups, 0, [zero] * 3)
+            source = pl.ds(pl.multiple_of((first + t * unroll + u) * LANES, LANES), LANES)
+            target = pl.ds(pl.multiple_of((t * unroll + u) * LANES, LANES), LANES)
+            place = start[:, source]
+            chosen = halves_of(picks, source)
+            spots, ranks = halves_of(spot, source), halves_of(rank, source)
+            found = [[jnp.zeros((PACK, LANES), BF16)] * 3 for h in range(2)]
+            for m in range(LAYERS):
+                values = layer(place + jnp.int16(m), chosen, even, odd)
+                put_back(values, jnp.int16(m), spots, ranks, found)
+            for h in range(2):
                 for e in range(3):
-                    out[e, rows, pl.ds(target, LANES)] = picked[e]
+                    out[e, h * PACK : (h + 1) * PACK, target] = found[h][e]
         return carry
 
     lax.fori_loop(0, tiles // unroll, some_tiles, 0)
+
+    def more(m, carry):
+        number = splat(m)
+        for t in range(tiles):
+            source = slice((first + t) * LANES, (first + t + 1) * LANES)
+            target = slice(t * LANES, (t + 1) * LANES)
+            found = [
+                [out[e, h * PACK : (h + 1) * PACK, target] for e in range(3)] for h in range(2)
+            ]
+            values = layer(start[:, source] + number, halves_of(picks, source), even, odd)
+            put_back(values, number, halves_of(spot, source), halves_of(rank, source), found)
+            for h in range(2):
+                for e in range(3):
+                    out[e, h * PACK : (h + 1) * PACK, target] = found[h][e]
+        return carry
+
+    lax.fori_loop(LAYERS, most[0] + 1, more, 0)
 
 
 def dense_solve(matrix, vector):
@@ -181,49 +319,22 @@
     return solved
 
 
-def sort_sides(even, outer, inner, after, before):
-    @pl.when(even)
-    def _():
-        after[...] = outer[...]
-        before[...] = inner[...]
-
-    @pl.when(jnp.logical_not(even))
-    def _():
-        after[...] = inner[...]
-        before[...] = outer[...]
-
-
-def put_sides(even, outer, inner, rows, to_next, to_prev):
-    @pl.when(even)
-    def _():
-        outer[rows] = to_prev
-        inner[rows] = to_next
-
-    @pl.when(jnp.logical_not(even))
-    def _():
-        outer[rows] = to_next
-        inner[rows] = to_prev
-
-
-def halo_kernel(*refs, sizes, stage, scale_old, scale_new, unroll=4):
-    pieces = len(sizes)
-    (place, col, ghost, outer, inner, residual, dinv, smooth, update, bonds) = refs[:10]
-    picked_refs = refs[10 : 10 + pieces]
-    refs = refs[10 + pieces :]
-    even = (place[1] & 1) == 0
+def halo_kernel(*refs, stage, scale_old, scale_new, unroll=4):
+    (place, most, picks, halo_start, spot, rank, ghost, outer, inner) = refs[:9]
+    (residual, dinv, smooth, update, bonds, local_found) = refs[9:15]
+    refs = refs[15:]
     if stage == 0:
         rhs, arrived, coarse_dinv = refs[:3]
         new_smooth, new_update, base, out_outer, out_inner = refs[3:8]
         refs = refs[8:]
     elif stage == 1:
         first_outer, first_inner, base, couple_own = refs[:4]
-        new_smooth, new_update, out_outer, out_inner, far_next, far_prev = refs[4:10]
-        refs = refs[10:]
+        new_smooth, new_update, out_outer, out_inner, far = refs[4:9]
+        refs = refs[9:]
     else:
         (new_smooth,) = refs[:1]
         refs = refs[1:]
-    slots, table, applied, after, before = refs[:5]
-    sort_sides(even, outer, inner, after, before)
+    applied, other = refs
     groups = smooth.shape[1]
     if stage == 0:
         vector = [rhs[e] + arrived[e] for e in range(3)]
@@ -239,68 +350,96 @@
             row = base[c].astype(BF16)
             out_outer[3 + c] = row
             out_inner[3 + c] = row
-        put_sides(even, out_outer, out_inner, slice(6, 10), after[3:7], before[3:7])
+        out_outer[6:10] = inner[3:7]
+        out_inner[6:10] = outer[3:7]
     elif stage == 1:
-        first_after, first_before = refs[5:7]
-        sort_sides(even, first_outer, first_inner, first_after, first_before)
-        own = base[...].astype(BF16)
-        put_sides(even, out_outer, out_inner, slice(3, 6), after[3:6], before[3:6])
-        for message in (far_next, far_prev):
-            message[0:3] = after[3:6]
-            message[3:6] = own
-            message[6:9] = before[3:6]
-        far_next[9:13] = couple_own[3:7]
-        far_next[13:17] = first_before[3:7]
-        far_prev[9:13] = first_after[3:7]
-        far_prev[13:17] = couple_own[3:7]
+        out_outer[3:6] = inner[3:6]
+        out_inner[3:6] = outer[3:6]
+        far[0:3] = outer[3:6]
+        far[3:6] = base[...].astype(BF16)
+        far[6:9] = inner[3:6]
+        far[9:13] = couple_own[3:7]
+        far[13:17] = first_outer[3:7]
+        far[17:21] = first_inner[3:7]
     wanted = ghost[...]
     half = wanted.shape[0] // 2
     low = wanted & (LANES - 1)
     high = wanted >> 7
-    upper = lax.broadcasted_iota(jnp.int32, wanted.shape, 0) < half
+    upper = jnp.where(lax.broadcasted_iota(jnp.int32, wanted.shape, 0) < half, 1, 0)
+    from_outer = (upper ^ (place[1] & 1)) == 1
     found = [jnp.zeros(wanted.shape, F32)] * 3
     for e in range(3):
-        applied[e] = after[e].astype(F32)
-        new_smooth[e] = before[e].astype(F32)
+        applied[e] = outer[e].astype(F32)
+        other[e] = inner[e].astype(F32)
     for g in range(groups):
         chosen = high == g
         for e in range(3):
             rows = jnp.where(
-                upper,
+                from_outer,
                 jnp.broadcast_to(applied[e, g : g + 1, :], wanted.shape),
-                jnp.broadcast_to(new_smooth[e, g : g + 1, :], wanted.shape),
+                jnp.broadcast_to(other[e, g : g + 1, :], wanted.shape),
             )
             found[e] = jnp.where(chosen, lane_gather(rows, low), found[e])
-    for e in range(3):
-        slots[e] = found[e]
-    halo_groups = wanted.shape[0]
-    fill_table(table, slots, halo_groups)
-    bonds_of = col.shape[0]
-
-    for piece in range(pieces):
-        start = sum(sizes[:piece])
-
-        def some_tiles(t, carry, piece=piece, start=start):
-            for u in range(unroll):
-                tile = start + t * unroll + u
-                here = pl.ds(pl.multiple_of(tile * LANES, LANES), LANES)
-                there = pl.ds(pl.multiple_of((t * unroll + u) * LANES, LANES), LANES)
-                total = [jnp.zeros((PACK, LANES), F32)] * 3
-                for h in range(bonds_of // PACK):
-                    rows = pl.ds(h * PACK, PACK)
-                    starts = [picked_refs[piece][e, rows, there] for e in range(3)]
-                    picked = pick(table, col[rows, here], halo_groups, groups, starts)
-                    wide = [value.astype(F32) for value in picked]
-                    for c in range(3):
-                        for e in range(3):
-                            total[c] = (
-                                total[c] + bonds[c, e, rows, here].astype(F32) * wide[e]
-                            )
-                for c in range(3):
-                    applied[c, pl.ds(tile, 1), :] = jnp.sum(total[c], axis=0, keepdims=True)
+    pair = (lax.broadcasted_iota(jnp.int32, wanted.shape, 0) & 3) * 2
+
+    def four_times(rows):
+        return jnp.concatenate([rows, rows], axis=0).astype(BF16)
+
+    even = [four_times(row_gather(found[e], pair)) for e in range(3)]
+    odd = [four_times(row_gather(found[e], pair + 1)) for e in range(3)]
+
+    def apply_tile(tile, values):
+        here = pl.ds(pl.multiple_of(tile * LANES, LANES), LANES)
+        totals = []
+        for c in range(3):
+            total = jnp.zeros((PACK, LANES), F32)
+            for h in range(2):
+                for e in range(3):
+                    block = bonds[c, e, h * PACK : (h + 1) * PACK, here].astype(F32)
+                    total = total + block * values[h][e].astype(F32)
+            totals.append(jnp.sum(total, axis=0, keepdims=True))
+        return totals
+
+    def some_tiles(t, carry):
+        for u in range(unroll):
+            tile = t * unroll + u
+            here = pl.ds(pl.multiple_of(tile * LANES, LANES), LANES)
+            chosen = halves_of(picks, here)
+            spots, ranks = halves_of(spot, here), halves_of(rank, here)
+            values = [
+                [local_found[e, h * PACK : (h + 1) * PACK, here] for e in range(3)]
+                for h in range(2)
+            ]
+            for v in range(HALO_LAYERS):
+                row = layer(halo_start[:, here] + jnp.int16(4 * v), chosen, even, odd)
+                put_back(row, jnp.int16(32 + v), spots, ranks, values)
+            totals = apply_tile(tile, values)
+            for c in range(3):
+                applied[c, pl.ds(tile, 1), :] = totals[c]
+        return carry
+
+    lax.fori_loop(0, groups // unroll, some_tiles, 0)
+
+    @pl.when(most[1] >= HALO_LAYERS)
+    def _():
+        def one_tile(tile, carry):
+            here = pl.ds(pl.multiple_of(tile * LANES, LANES), LANES)
+
+            def more(v, flat):
+                values = [list(flat[:3]), list(flat[3:])]
+                row = layer(halo_start[:, here] + splat(4 * v), halves_of(picks, here), even, odd)
+                put_back(row, splat(32 + v), halves_of(spot, here), halves_of(rank, here), values)
+                return tuple(values[0] + values[1])
+
+            empty = (jnp.zeros((PACK, LANES), BF16),) * 6
+            flat = lax.fori_loop(HALO_LAYERS, most[1] + 1, more, empty)
+            totals = apply_tile(tile, [flat[:3], flat[3:]])
+            for c in range(3):
+                applied[c, pl.ds(tile, 1), :] = applied[c, pl.ds(tile, 1), :] + totals[c]
             return carry
 
-        lax.fori_loop(0, sizes[piece] // unroll, some_tiles, 0)
+        lax.fori_loop(0, groups, one_tile, 0)
+
     remainder = [residual[e] - smooth[e] - applied[e] for e in range(3)]
     solved = dense_solve(dinv, remainder)
     for c in range(3):
@@ -326,52 +465,58 @@
         inside = jnp.logical_and(me + row >= 0, me + row < subs)
         return jnp.where(inside, 1.0, 0.0).astype(F32)
 
-    def from_after(pair):
-        return lambda i: jnp.where(even, pair[0][i].astype(F32), pair[1][i].astype(F32))
-
-    def from_before(pair):
-        return lambda i: jnp.where(even, pair[1][i].astype(F32), pair[0][i].astype(F32))
-
-    def plain(ref):
-        return lambda i: ref[i].astype(F32)
+    def from_after(pair, start):
+        return lambda i: jnp.where(
+            even, pair[0][start + i].astype(F32), pair[1][start + i].astype(F32)
+        )
+
+    def from_before(pair, start):
+        return from_after((pair[1], pair[0]), start)
+
+    def plain(ref, start):
+        return lambda i: ref[start + i].astype(F32)
+
+    def either(ref, when_even, when_odd):
+        return lambda i: jnp.where(
+            even, ref[when_even + i].astype(F32), ref[when_odd + i].astype(F32)
+        )
 
     base_rows = {
-        -5: (plain(far_after), 0),
-        -4: (plain(far_after), 3),
-        -3: (plain(far_after), 6),
-        -2: (from_after(third), 3),
-        -1: (from_after(second), 3),
-        1: (from_before(second), 3),
-        2: (from_before(third), 3),
-        3: (plain(far_before), 0),
-        4: (plain(far_before), 3),
-        5: (plain(far_before), 6),
+        -5: either(far_after, 0, 6),
+        -4: plain(far_after, 3),
+        -3: either(far_after, 6, 0),
+        -2: from_after(third, 3),
+        -1: from_after(second, 3),
+        1: from_before(second, 3),
+        2: from_before(third, 3),
+        3: either(far_before, 0, 6),
+        4: plain(far_before, 3),
+        5: either(far_before, 6, 0),
     }
     link_rows = {
-        -4: (plain(far_after), 9),
-        -3: (plain(far_after), 13),
-        -2: (from_after(second), 6),
-        -1: (from_after(first), 3),
-        1: (from_before(first), 3),
-        2: (from_before(second), 6),
-        3: (plain(far_before), 9),
-        4: (plain(far_before), 13),
+        -4: plain(far_after, 9),
+        -3: either(far_after, 17, 13),
+        -2: from_after(second, 6),
+        -1: from_after(first, 3),
+        1: from_before(first, 3),
+        2: from_before(second, 6),
+        3: either(far_before, 13, 17),
+        4: plain(far_before, 9),
     }
 
     def base_of(row, c):
         if row == 0:
             return base[c]
-        ref, start = base_rows[row]
-        return ref(start + c) * valid(row)
+        return base_rows[row](c) * valid(row)
 
     for k in range(4):
         for g in range(groups):
             links[STEPS - 1, k, g : g + 1, :] = own_couple[
                 k : k + 1, g * LANES : (g + 1) * LANES
             ]
-    for row, (ref, start) in link_rows.items():
+    for row, read in link_rows.items():
         for k in range(4):
-            links[row + STEPS - 1, k] = ref(start + k) * valid(row)
+            links[row + STEPS - 1, k] = read(k) * valid(row)
     for row in range(-STEPS, STEPS + 1):
         for c in range(3):
             value = base_of(row, c)
@@ -474,85 +619,85 @@
     update = smooth
     own_packed = packed
     place = jnp.stack([jnp.int32(lax.axis_size("sub")), sub.astype(jnp.int32)])
-    first = arrived_sides = exchanged_by_pairs(packed, packed)
-    rhs = call(restrict_kernel, coarse_field, (residual, agg), us=2.5)
-
-    def local(smooth, first, tiles):
-        return call(
-            functools.partial(local_kernel, first=first, tiles=tiles),
-            sds((3, bonds_of, tiles * LANES), BF16),
-            (smooth, bond_col),
-            scratch=[VMEM((3, groups, PACK, LANES), BF16)],
-            us=7.5 * tiles / groups,
-        )
+    rhs = call(restrict_kernel, coarse_field, (residual, agg), us=1.2)
 
     def exchanged(value, step):
         return lax.ppermute(value, "dom", [(i, i ^ step) for i in range(doms)])
 
-    sizes = (12, 12, 8)
-    parts = []
+    rhs, packed = lax.optimization_barrier((rhs, packed))
     arrived = exchanged(rhs, 1)
-    parts.append(local(smooth, 0, sizes[0]))
+    first = arrived_sides = exchanged_by_pairs(packed, packed)
     rhs = rhs + arrived
     arrived = exchanged(rhs, 2)
-    later, rhs, parts[0] = lax.optimization_barrier((smooth, rhs, parts[0]))
-    parts.append(local(later, sizes[0], sizes[1]))
+    columns, rhs = lax.optimization_barrier((bond_col, rhs))
+
+    def shorts(rows):
+        return sds((rows, points), jnp.int16)
+
+    picks, start, halo_start, spot, rank, most = call(
+        prepare_kernel,
+        (
+            shorts(bonds_of),
+            shorts(PACK),
+            shorts(PACK),
+            shorts(bonds_of),
+            shorts(bonds_of),
+            sds((2,), jnp.int32),
+        ),
+        (columns,),
+        scratch=[VMEM((8 * (bonds_of + 2), LANES), jnp.int32)],
+        us=2.5,
+    )
     rhs = rhs + arrived
     arrived = exchanged(rhs, 4)
-    later, rhs, parts[1] = lax.optimization_barrier((smooth, rhs, parts[1]))
-    parts.append(local(later, sizes[0] + sizes[1], sizes[2]))
+    start, rhs = lax.optimization_barrier((start, rhs))
 
     factor = HALF / CENTER
     for stage in range(SWEEPS):
         factor_new = 1.0 / (2.0 * CENTER / HALF - factor)
-        if stage:
-            sizes = (groups,)
-            parts = [local(smooth, 0, groups)]
+        found = call(
+            functools.partial(local_kernel, first=0, tiles=groups),
+            sds((3, bonds_of, points), BF16),
+            (smooth, picks, start, spot, rank, most),
+            us=3.5,
+            spaces={5: pltpu.SMEM},
+        )
         if stage == SWEEPS - 1:
-            parts[0], far_after, far_before = lax.optimization_barrier(
-                (parts[0], far_after, far_before)
+            found, far_after, far_before = lax.optimization_barrier(
+                (found, far_after, far_before)
             )
-        inputs = [place, bond_col, ghost, *arrived_sides]
-        inputs += [residual, dinv, smooth, update, relaid]
-        inputs += parts
+        inputs = [place, most, picks, halo_start, spot, rank, ghost, *arrived_sides]
+        inputs += [residual, dinv, smooth, update, relaid, found]
         if stage == 0:
             inputs += [rhs, arrived, coarse_dinv]
             outs = (field, field, coarse_field, message(10), message(10))
         elif stage == 1:
             inputs += [*first, base, own_packed]
-            outs = (field, field, message(6), message(6), message(17), message(17))
+            outs = (field, field, message(6), message(6), message(21))
         else:
             outs = (field,)
         result = call(
             functools.partial(
                 halo_kernel,
-                sizes=sizes,
                 stage=stage,
                 scale_old=factor_new * factor,
                 scale_new=2.0 * factor_new / HALF,
             ),
             outs,
             inputs,
-            scratch=[
-                VMEM((3,) + ghost.shape, F32),
-                VMEM((3, ghost.shape[0], PACK, LANES), BF16),
-                VMEM((3, groups, LANES), F32),
-                VMEM(arrived_sides[0].shape, BF16),
-                VMEM(arrived_sides[0].shape, BF16),
-            ]
-            + [VMEM(first[0].shape, BF16)] * (2 if stage == 1 else 0),
-            us=4.0,
-            spaces={0: pltpu.SMEM},
+            scratch=[VMEM((3, groups, LANES), F32), VMEM((3, groups, LANES), F32)],
+            us=2.5,
+            spaces={0: pltpu.SMEM, 1: pltpu.SMEM},
         )
         factor = factor_new
         if stage == 0:
             smooth, update, base, outer, inner = result
             second = arrived_sides = exchanged_by_pairs(outer, inner)
         elif stage == 1:
-            smooth, update, outer, inner, far_next, far_prev = result
+            smooth, update, outer, inner, far = result
             third = arrived_sides = exchanged_by_pairs(outer, inner)
-            far_after = shifted(far_next, 4)
-            far_before = shifted(far_prev, -4)
+            far_after = shifted(far, 4)
+            far_before = shifted(far, -4)
         else:
             (smooth,) = result
     return call(

time: 62.2 us -> 57.5 us (0.924)
  Pallas kernels: 36.8 us -> 30.2 us
  waiting for transfers between devices: 0.03 us -> 3.18 us
  starting transfers between devices: 24.9 us -> 23.7 us
    pallas_call x11 -> x10, Pallas kernels: 36.8 us -> 30.2 us  [call(): pl.pallas_call(kernel, out_shape=out, in_specs=[pl.BlockSpec(memory_space...]
    ppermute x3, waiting for transfers between devices: 0.01 us -> 3.16 us  [exchanged(): return lax.ppermute(value, 'dom', [(i, i ^ step) for i in range(doms)])]
    ppermute x3, starting transfers between devices: 12.4 us -> 9.57 us  [exchanged_by_pairs(): inner = lax.ppermute(inner, 'sub', within + [(j, i) for i, j in within])]
    ppermute x3, starting transfers between devices: 5.43 us -> 7.91 us  [exchanged_by_pairs(): outer = lax.ppermute(outer, 'sub', across + [(j, i) for i, j in across])]
    ppermute x2, starting transfers between devices: 2.68 us -> 1.78 us  [shifted(): lax.ppermute(value, 'sub', [(i, (i + steps) % count) for i in range(count)])]
  transfers between devices with their start and end apart: 11 -> 11, of which waited for: 0 -> 1; matrix products, arithmetic and copies ran while one was open for 0% -> 0% of each run, Pallas kernels for 37% -> 29%
where the time goes in v4:
time: 57.5 us; the launch traced here: 57.4 us
  Pallas kernels  30.2 us (53%)
  starting transfers between devices  23.7 us (41%)
  waiting for transfers between devices  3.18 us (6%)
    pallas_call x10, Pallas kernels, call(): pl.pallas_call(kernel, out_shape=out, in_specs=[pl.BlockSpec(memory_space...  30.2 us
    ppermute x3, starting transfers between devices, exchanged_by_pairs(): inner = lax.ppermute(inner, 'sub', within + [(j, i) for i, j in within])  9.57 us
    ppermute x3, starting transfers between devices, exchanged_by_pairs(): outer = lax.ppermute(outer, 'sub', across + [(j, i) for i, j in across])  7.91 us
    ppermute x3, starting transfers between devices, exchanged(): return lax.ppermute(value, 'dom', [(i, i ^ step) for i in range(doms)])  4.4 us
    ppermute x3, waiting for transfers between devices, exchanged(): return lax.ppermute(value, 'dom', [(i, i ^ step) for i in range(doms)])  3.16 us
    ppermute x2, starting transfers between devices, shifted(): lax.ppermute(value, 'sub', [(i, (i + steps) % count) for i in range(count)])  1.78 us
  transfers between devices with their start and end apart: 11, of which 1 were waited for; matrix products, arithmetic and copies ran while one was open for 0% of the time, Pallas kernels for 29%

profile of v4, /device:TPU:1, one launch (start us, length us, event | category | flops | bytes accessed | tf_op | source)
XLA Modules:
  0.0 57.4 jit_solution(440360166608561351)
XLA Ops:
  0.0 1.3 %shard_map.82 = (f32[3,3,32,128]{3,2,1,0:T(8,128)S(1)}, f32[3,32,128]{2,1,0:T(8,128)S(1)}, f32[3,32,128]{2,1,0:T(8,128)S(1)}, bf16[7,32,128]{2,1,0:T(8,128)(2,1)S(1)}) custom-call(f32[3,3,4096]{2,1,0:T(4,128)} %refs_0_.1, f32[3,4096]{1,0:T(4,128)} %refs_1_.1, f32[4,4096]{1,0:T(4,128)} %refs_2_.3), custom_call_target="tpu_custom_call" | custom-call | flops 2000000000 | bytes 2000000 | tf_op jit(solution)/shard_map/pallas_call | solution.py:74
  1.3 0.0 copy-start.5
  1.3 0.0 copy-start.1
  1.3 1.2 %shard_map.83 = f32[3,32,128]{2,1,0:T(8,128)S(1)} custom-call(f32[3,32,128]{2,1,0:T(8,128)S(1)} %get-tuple-element.34.residual.refs_9_, s32[32,128]{1,0:T(8,128)S(1)} %bitcast.6), custom_call_target="tpu_custom_call" | custom-call | flops 1200000000 | bytes 1200000 | tf_op jit(solution)/shard_map/pallas_call | solution.py:74
  2.5 3.3 %collective-permute-start.2 = (bf16[7,32,128]{2,1,0:T(8,128)(2,1)S(1)}, bf16[7,32,128]{2,1,0:T(8,128)(2,1)S(1)}, u32[]{:S(2)}, u32[]{:S(2)}) collective-permute-start(bf16[7,32,128]{2,1,0:T(8,128)(2,1)S(1)} %get-tuple-element.43.refs_18_), channel_id=1, source_target_pairs={{0,1},{2,3},{4,5},{6,7},{8,9},{10,11},{12,13},{14,15},{16,17},{18,... | collective-permute-start | bytes 172040 | tf_op jit(solution)/shard_map/ppermute | solution.py:578
  5.7 1.0 %collective-permute-start.1 = (bf16[7,32,128]{2,1,0:T(8,128)(2,1)S(1)}, bf16[7,32,128]{2,1,0:T(8,128)(2,1)S(1)}, u32[]{:S(2)}, u32[]{:S(2)}) collective-permute-start(bf16[7,32,128]{2,1,0:T(8,128)(2,1)S(1)} %get-tuple-element.43.refs_18_), channel_id=1, source_target_pairs={{1,2},{3,4},{5,6},{7,8},{9,10},{11,12},{13,14},{15,16},{17,18},{19... | collective-permute-start | bytes 172040 | tf_op jit(solution)/shard_map/ppermute | solution.py:577
  6.7 0.3 collective-permute-start
  7.1 0.1 pad_add_fusion.refs_0_
  7.1 3.2 %collective-permute-done = f32[3,32,128]{2,1,0:T(8,128)S(1)} collective-permute-done((f32[3,32,128]{2,1,0:T(8,128)S(1)}, f32[3,32,128]{2,1,0:T(8,128)S(1)}, u32[]{:S(2)}, u32[]{:S(2)}) %collective-permute-start) | collective-permute-done | bytes 49184 | tf_op jit(solution)/shard_map/ppermute | solution.py:625
  10.3 1.4 %collective-permute-start.3 = (f32[3,32,128]{2,1,0:T(8,128)S(1)}, f32[3,32,128]{2,1,0:T(8,128)S(1)}, u32[]{:S(2)}, u32[]{:S(2)}) collective-permute-start(f32[3,32,128]{2,1,0:T(8,128)S(1)} %add.6), channel_id=1, source_target_pairs={{0,64},{32,96},{64,0},{96,32},{128,192},{160,224},{192,128},{224,1... | collective-permute-start | bytes 147464 | tf_op jit(solution)/shard_map/ppermute | solution.py:625
  11.7 2.9 %shard_map.84 = (s16[32,4096]{1,0:T(8,128)(2,1)S(1)}, s16[16,4096]{1,0:T(8,128)(2,1)S(1)}, s16[16,4096]{1,0:T(8,128)(2,1)S(1)}, s16[32,4096]{1,0:T(8,128)(2,1)S(...) custom-call(s32[32,4096]{1,0:T(8,128)S(1)} %copy-done.1), custom_call_target="tpu_custom_call" | custom-call | flops 2500000000 | bytes 2500000 | tf_op jit(solution)/shard_map/pallas_call | solution.py:74
  14.6 0.0 collective-permute-done.3
  14.7 2.7 %collective-permute-start.4 = (f32[3,32,128]{2,1,0:T(8,128)S(1)}, f32[3,32,128]{2,1,0:T(8,128)S(1)}, u32[]{:S(2)}, u32[]{:S(2)}) collective-permute-start(f32[3,32,128]{2,1,0:T(8,128)S(1)} %add.7.refs_15_), channel_id=1, source_target_pairs={{0,128},{32,160},{64,192},{96,224},{128,0},{160,32},{192,64},{224,... | collective-permute-start | bytes 147464 | tf_op jit(solution)/shard_map/ppermute | solution.py:625
  17.4 4.5 %shard_map.85.refs_14_ = bf16[3,32,4096]{2,1,0:T(8,128)(2,1)S(1)} custom-call(f32[3,32,128]{2,1,0:T(8,128)S(1)} %get-tuple-element.45.smooth.refs_11_.refs_12_, s16[32,4096]{1,0:T(8,128)(2,1)S(1)} %get-tuple-element.39.picks.refs_2_, s16[16,4096]{1,0:T(8,128)(2,1)S(1)} %get-tuple-element.48.start, s16[32,4096]{1,0:T(8,128)(2,1)S(1)} %get-tuple-element.41.spot.refs_4_, ...), custom_call_target="tpu_custom_call" | custom-call | flops 3500000000 | bytes 3500000 | tf_op jit(solution)/shard_map/pallas_call | solution.py:74
  21.9 0.0 collective-permute-done.2.refs_8_.refs_16_.refs_4_
  21.9 0.0 collective-permute-done.1.refs_7_.refs_15_.refs_3_
  21.9 0.0 collective-permute-done.4.refs_16_
  22.0 3.0 %shard_map.86 = (f32[3,32,128]{2,1,0:T(8,128)S(1)}, f32[3,32,128]{2,1,0:T(8,128)S(1)}, f32[3,32,128]{2,1,0:T(8,128)S(1)}, bf16[10,32,128]{2,1,0:T(8,128)(2,1)S(1)}, bf16[10,32,128]{2,1,0:T(8,128)(2,1)S(1)}) custom-call(s32[2]{0:T(128)S(1)} %pad_add_fusion.refs_0_, s32[2]{0:T(128)S(1)} %get-tuple-element.38.most.refs_1_, ...), custom_call_target="tpu_custom_call" | custom-call | flops 2500000000 | bytes 2500000 | tf_op jit(solution)/shard_map/pallas_call | solution.py:74
  25.0 2.8 %collective-permute-start.5 = (bf16[10,32,128]{2,1,0:T(8,128)(2,1)S(1)}, bf16[10,32,128]{2,1,0:T(8,128)(2,1)S(1)}, u32[]{:S(2)}, u32[]{:S(2)}) collective-permute-start(bf16[10,32,128]{2,1,0:T(8,128)(2,1)S(1)} %get-tuple-element.51), channel_id=1, source_target_pairs={{1,2},{3,4},{5,6},{7,8},{9,10},{11,12},{13,14},{15,16},{17,18},{19... | collective-permute-start | bytes 245768 | tf_op jit(solution)/shard_map/ppermute | solution.py:577
  27.8 4.2 %collective-permute-start.6 = (bf16[10,32,128]{2,1,0:T(8,128)(2,1)S(1)}, bf16[10,32,128]{2,1,0:T(8,128)(2,1)S(1)}, u32[]{:S(2)}, u32[]{:S(2)}) collective-permute-start(bf16[10,32,128]{2,1,0:T(8,128)(2,1)S(1)} %get-tuple-element.52), channel_id=1, source_target_pairs={{0,1},{2,3},{4,5},{6,7},{8,9},{10,11},{12,13},{14,15},{16,17},{18,... | collective-permute-start | bytes 245768 | tf_op jit(solution)/shard_map/ppermute | solution.py:578
  32.0 4.5 %shard_map.87.refs_14_ = bf16[3,32,4096]{2,1,0:T(8,128)(2,1)S(1)} custom-call(f32[3,32,128]{2,1,0:T(8,128)S(1)} %get-tuple-element.53.smooth.refs_11_, s16[32,4096]{1,0:T(8,128)(2,1)S(1)} %get-tuple-element.39.picks.refs_2_, s16[16,4096]{1,0:T(8,128)(2,1)S(1)} %get-tuple-element.48.start, s16[32,4096]{1,0:T(8,128)(2,1)S(1)} %get-tuple-element.41.spot.refs_4_, ...), custom_call_target="tpu_custom_call" | custom-call | flops 3500000000 | bytes 3500000 | tf_op jit(solution)/shard_map/pallas_call | solution.py:74
  36.5 0.0 collective-permute-done.5.refs_7_.refs_5_
  36.5 2.9 %shard_map.88 = (f32[3,32,128]{2,1,0:T(8,128)S(1)}, f32[3,32,128]{2,1,0:T(8,128)S(1)}, bf16[6,32,128]{2,1,0:T(8,128)(2,1)S(1)}, bf16[6,32,128]{2,1,0:T(8,128)(2,1)S(1)}, bf16[21,32,128]{2,1,0:T(8,128)(2,1)S(1)}) custom-call(s32[2]{0:T(128)S(1)} %pad_add_fusion.refs_0_, s32[2]{0:T(128)S(1)} %get-tuple-element.38.most.refs_1_, ...), custom_call_target="tpu_custom_call" | custom-call | flops 2500000000 | bytes 2500000 | tf_op jit(solution)/shard_map/pallas_call | solution.py:74
  39.4 1.8 %collective-permute-start.10 = (bf16[21,32,128]{2,1,0:T(8,128)(2,1)S(1)}, bf16[21,32,128]{2,1,0:T(8,128)(2,1)S(1)}, u32[]{:S(2)}, u32[]{:S(2)}) collective-permute-start(bf16[21,32,128]{2,1,0:T(8,128)(2,1)S(1)} %get-tuple-element.58), channel_id=1, source_target_pairs={{0,28},{1,29},{2,30},{3,31},{4,0},{5,1},{6,2},{7,3},{8,4},{9,5},{1... | collective-permute-start | bytes 516104 | tf_op jit(solution)/shard_map/ppermute | solution.py:570
  41.2 4.1 %collective-permute-start.7 = (bf16[6,32,128]{2,1,0:T(8,128)(2,1)S(1)}, bf16[6,32,128]{2,1,0:T(8,128)(2,1)S(1)}, u32[]{:S(2)}, u32[]{:S(2)}) collective-permute-start(bf16[6,32,128]{2,1,0:T(8,128)(2,1)S(1)} %get-tuple-element.55), channel_id=1, source_target_pairs={{1,2},{3,4},{5,6},{7,8},{9,10},{11,12},{13,14},{15,16},{17,18},{19... | collective-permute-start | bytes 147464 | tf_op jit(solution)/shard_map/ppermute | solution.py:577
  45.3 2.1 %collective-permute-start.8 = (bf16[6,32,128]{2,1,0:T(8,128)(2,1)S(1)}, bf16[6,32,128]{2,1,0:T(8,128)(2,1)S(1)}, u32[]{:S(2)}, u32[]{:S(2)}) collective-permute-start(bf16[6,32,128]{2,1,0:T(8,128)(2,1)S(1)} %get-tuple-element.56), channel_id=1, source_target_pairs={{0,1},{2,3},{4,5},{6,7},{8,9},{10,11},{12,13},{14,15},{16,17},{18,... | collective-permute-start | bytes 147464 | tf_op jit(solution)/shard_map/ppermute | solution.py:578
  47.4 4.5 %shard_map.89.refs_14_ = bf16[3,32,4096]{2,1,0:T(8,128)(2,1)S(1)} custom-call(f32[3,32,128]{2,1,0:T(8,128)S(1)} %get-tuple-element.57.smooth.refs_11_, s16[32,4096]{1,0:T(8,128)(2,1)S(1)} %get-tuple-element.39.picks.refs_2_, s16[16,4096]{1,0:T(8,128)(2,1)S(1)} %get-tuple-element.48.start, s16[32,4096]{1,0:T(8,128)(2,1)S(1)} %get-tuple-element.41.spot.refs_4_, ...), custom_call_target="tpu_custom_call" | custom-call | flops 3500000000 | bytes 3500000 | tf_op jit(solution)/shard_map/pallas_call | solution.py:74
  52.0 0.0 collective-permute-done.10.refs_10_
  52.0 0.0 collective-permute-done.8.refs_8_
  52.0 0.0 copy-start.3
  52.0 2.9 %shard_map.90.refs_12_ = f32[3,32,128]{2,1,0:T(8,128)S(1)} custom-call(s32[2]{0:T(128)S(1)} %pad_add_fusion.refs_0_, s32[2]{0:T(128)S(1)} %get-tuple-element.38.most.refs_1_, s16[32,4096]{1,0:T(8,128)(2,1)S(1)} %get-tuple-element.39.picks.refs_2_, s16[16,4096]{1,0:T(8,128)(2,1)S(1)} %get-tuple-element.40.refs_3_, ...), custom_call_target="tpu_custom_call" | custom-call | flops 2500000000 | bytes 2500000 | tf_op jit(solution)/shard_map/pallas_call | solution.py:74
  54.9 2.5 %shard_map.91 = f32[3,4096]{1,0:T(4,128)} custom-call(s32[2]{0:T(128)S(1)} %pad_add_fusion.refs_0_, f32[3,32,128]{2,1,0:T(8,128)S(1)} %get-tuple-element.50.refs_17_.refs_1_, f32[4,4096]{1,0:T(4,128)S(1)} %copy-done.3, bf16[7,32,128]{2,1,0:T(8,128)(2,1)S(1)} %collective-permute-done.1.refs_7_.refs_15_.refs_3_, ...), custom_call_target="tpu_custom_call" | custom-call | flops 2000000000 | bytes 2000000 | tf_op jit(solution)/shard_map/pallas_call | solution.py:74
  (16 shorter events, 0.1 us)
Async XLA Ops:
  0.0 1.3 %copy-start.4 = (s32[4096]{0:T(1024)S(1)}, s32[4096]{0:T(1024)}, u32[]{:S(2)}) copy-start(s32[4096]{0:T(1024)} %param.13) | copy-start | bytes 49156
  1.3 5.9 %copy-start.5 = (s32[1,2,512]{2,1,0:T(2,128)S(1)}, s32[1,2,512]{2,1,0:T(2,128)}, u32[]{:S(2)}) copy-start(s32[1,2,512]{2,1,0:T(2,128)} %param.11) | copy-start | bytes 12292
  1.3 10.4 %copy-start.1 = (s32[32,4096]{1,0:T(8,128)S(1)}, s32[32,4096]{1,0:T(8,128)}, u32[]{:S(2)}) copy-start(s32[32,4096]{1,0:T(8,128)} %col) | copy-start | bytes 1572868
  2.5 19.4 %collective-permute-start.2 = (bf16[7,32,128]{2,1,0:T(8,128)(2,1)S(1)}, bf16[7,32,128]{2,1,0:T(8,128)(2,1)S(1)}, u32[]{:S(2)}, u32[]{:S(2)}) collective-permute-start(bf16[7,32,128]{2,1,0:T(8,128)(2,1)S(1)} %get-tuple-element.43.refs_18_), channel_id=1, source_target_pairs={{0,1},{2,3},{4,5},{6,7},{8,9},{10,11},{12,13},{14,15},{16,17},{18,... | collective-permute-start | bytes 172040 | tf_op jit(solution)/shard_map/ppermute | solution.py:578
  5.7 16.2 %collective-permute-start.1 = (bf16[7,32,128]{2,1,0:T(8,128)(2,1)S(1)}, bf16[7,32,128]{2,1,0:T(8,128)(2,1)S(1)}, u32[]{:S(2)}, u32[]{:S(2)}) collective-permute-start(bf16[7,32,128]{2,1,0:T(8,128)(2,1)S(1)} %get-tuple-element.43.refs_18_), channel_id=1, source_target_pairs={{1,2},{3,4},{5,6},{7,8},{9,10},{11,12},{13,14},{15,16},{17,18},{19... | collective-permute-start | bytes 172040 | tf_op jit(solution)/shard_map/ppermute | solution.py:577
  6.7 3.6 %collective-permute-start = (f32[3,32,128]{2,1,0:T(8,128)S(1)}, f32[3,32,128]{2,1,0:T(8,128)S(1)}, u32[]{:S(2)}, u32[]{:S(2)}) collective-permute-start(f32[3,32,128]{2,1,0:T(8,128)S(1)} %shard_map.83), channel_id=1, source_target_pairs={{0,32},{32,0},{64,96},{96,64},{128,160},{160,128},{192,224},{224,1... | collective-permute-start | bytes 147464 | tf_op jit(solution)/shard_map/ppermute | solution.py:625
  10.3 4.3 %collective-permute-start.3 = (f32[3,32,128]{2,1,0:T(8,128)S(1)}, f32[3,32,128]{2,1,0:T(8,128)S(1)}, u32[]{:S(2)}, u32[]{:S(2)}) collective-permute-start(f32[3,32,128]{2,1,0:T(8,128)S(1)} %add.6), channel_id=1, source_target_pairs={{0,64},{32,96},{64,0},{96,32},{128,192},{160,224},{192,128},{224,1... | collective-permute-start | bytes 147464 | tf_op jit(solution)/shard_map/ppermute | solution.py:625
  14.7 7.3 %collective-permute-start.4 = (f32[3,32,128]{2,1,0:T(8,128)S(1)}, f32[3,32,128]{2,1,0:T(8,128)S(1)}, u32[]{:S(2)}, u32[]{:S(2)}) collective-permute-start(f32[3,32,128]{2,1,0:T(8,128)S(1)} %add.7.refs_15_), channel_id=1, source_target_pairs={{0,128},{32,160},{64,192},{96,224},{128,0},{160,32},{192,64},{224,... | collective-permute-start | bytes 147464 | tf_op jit(solution)/shard_map/ppermute | solution.py:625
  17.4 4.6 %copy-start = (bf16[32,3,3,4096]{3,0,2,1:T(8,128)(2,1)S(1)}, bf16[32,3,3,4096]{3,0,2,1:T(8,128)(2,1)}, u32[]{:S(2)}) copy-start(bf16[32,3,3,4096]{3,0,2,1:T(8,128)(2,1)} %param.9) | copy-start | bytes 7077892
  17.4 4.6 %copy-start.2 = (f32[3,3,4096]{2,1,0:T(4,128)S(1)}, f32[3,3,4096]{2,1,0:T(4,128)}, u32[]{:S(2)}) copy-start(f32[3,3,4096]{2,1,0:T(4,128)} %refs_17_.1) | copy-start | bytes 442372
  25.0 11.5 %collective-permute-start.5 = (bf16[10,32,128]{2,1,0:T(8,128)(2,1)S(1)}, bf16[10,32,128]{2,1,0:T(8,128)(2,1)S(1)}, u32[]{:S(2)}, u32[]{:S(2)}) collective-permute-start(bf16[10,32,128]{2,1,0:T(8,128)(2,1)S(1)} %get-tuple-element.51), channel_id=1, source_target_pairs={{1,2},{3,4},{5,6},{7,8},{9,10},{11,12},{13,14},{15,16},{17,18},{19... | collective-permute-start | bytes 245768 | tf_op jit(solution)/shard_map/ppermute | solution.py:577
  27.8 8.7 %collective-permute-start.6 = (bf16[10,32,128]{2,1,0:T(8,128)(2,1)S(1)}, bf16[10,32,128]{2,1,0:T(8,128)(2,1)S(1)}, u32[]{:S(2)}, u32[]{:S(2)}) collective-permute-start(bf16[10,32,128]{2,1,0:T(8,128)(2,1)S(1)} %get-tuple-element.52), channel_id=1, source_target_pairs={{0,1},{2,3},{4,5},{6,7},{8,9},{10,11},{12,13},{14,15},{16,17},{18,... | collective-permute-start | bytes 245768 | tf_op jit(solution)/shard_map/ppermute | solution.py:578
  39.4 12.6 %collective-permute-start.10 = (bf16[21,32,128]{2,1,0:T(8,128)(2,1)S(1)}, bf16[21,32,128]{2,1,0:T(8,128)(2,1)S(1)}, u32[]{:S(2)}, u32[]{:S(2)}) collective-permute-start(bf16[21,32,128]{2,1,0:T(8,128)(2,1)S(1)} %get-tuple-element.58), channel_id=1, source_target_pairs={{0,28},{1,29},{2,30},{3,31},{4,0},{5,1},{6,2},{7,3},{8,4},{9,5},{1... | collective-permute-start | bytes 516104 | tf_op jit(solution)/shard_map/ppermute | solution.py:570
  41.2 10.8 %collective-permute-start.9 = (bf16[21,32,128]{2,1,0:T(8,128)(2,1)S(1)}, bf16[21,32,128]{2,1,0:T(8,128)(2,1)S(1)}, u32[]{:S(2)}, u32[]{:S(2)}) collective-permute-start(bf16[21,32,128]{2,1,0:T(8,128)(2,1)S(1)} %get-tuple-element.58), channel_id=1, source_target_pairs={{0,4},{1,5},{2,6},{3,7},{4,8},{5,9},{6,10},{7,11},{8,12},{9,13},{1... | collective-permute-start | bytes 516104 | tf_op jit(solution)/shard_map/ppermute | solution.py:570
  41.2 10.8 %collective-permute-start.7 = (bf16[6,32,128]{2,1,0:T(8,128)(2,1)S(1)}, bf16[6,32,128]{2,1,0:T(8,128)(2,1)S(1)}, u32[]{:S(2)}, u32[]{:S(2)}) collective-permute-start(bf16[6,32,128]{2,1,0:T(8,128)(2,1)S(1)} %get-tuple-element.55), channel_id=1, source_target_pairs={{1,2},{3,4},{5,6},{7,8},{9,10},{11,12},{13,14},{15,16},{17,18},{19... | collective-permute-start | bytes 147464 | tf_op jit(solution)/shard_map/ppermute | solution.py:577
  45.3 6.7 %collective-permute-start.8 = (bf16[6,32,128]{2,1,0:T(8,128)(2,1)S(1)}, bf16[6,32,128]{2,1,0:T(8,128)(2,1)S(1)}, u32[]{:S(2)}, u32[]{:S(2)}) collective-permute-start(bf16[6,32,128]{2,1,0:T(8,128)(2,1)S(1)} %get-tuple-element.56), channel_id=1, source_target_pairs={{0,1},{2,3},{4,5},{6,7},{8,9},{10,11},{12,13},{14,15},{16,17},{18,... | collective-permute-start | bytes 147464 | tf_op jit(solution)/shard_map/ppermute | solution.py:578
  52.0 2.9 %copy-start.3 = (f32[4,4096]{1,0:T(4,128)S(1)}, f32[4,4096]{1,0:T(4,128)}, u32[]{:S(2)}) copy-start(f32[4,4096]{1,0:T(4,128)} %refs_2_.3) | copy-start | bytes 196612

commit v5 on v4

--- a/solution.py
+++ b/solution.py
@@ -93,23 +93,30 @@
 
 
 def first_kernel(*refs):
-    sources = refs[:3]
-    dense_dinv, dense_residual, smooth, message = refs[3:7]
-    dinv, residual, couple, semaphores = refs[7:]
+    sources = refs[:4]
+    dense_dinv, dense_residual, smooth, message, rhs = refs[4:9]
+    residual, aggregate, dinv, couple, semaphores = refs[9:]
     copies = [
         pltpu.make_async_copy(source, target, semaphores.at[i])
-        for i, (source, target) in enumerate(zip(sources, (dinv, residual, couple)))
+        for i, (source, target) in enumerate(zip(sources, (residual, aggregate, dinv, couple)))
     ]
     for copy in copies:
         copy.start()
-    for copy in copies:
-        copy.wait()
     groups = smooth.shape[1]
+    copies[0].wait()
+    for g in range(groups):
+        for e in range(3):
+            dense_residual[e, g : g + 1, :] = residual[
+                e : e + 1, g * LANES : (g + 1) * LANES
+            ]
+    copies[1].wait()
+    restrict(dense_residual, aggregate, rhs)
+    copies[2].wait()
+    copies[3].wait()
     coarse_groups = message.shape[1]
     for g in range(groups):
         lanes = slice(g * LANES, (g + 1) * LANES)
         for e in range(3):
-            dense_residual[e, g : g + 1, :] = residual[e : e + 1, lanes]
             for c in range(3):
                 dense_dinv[c, e, g : g + 1, :] = dinv[c, e : e + 1, lanes]
     for g in range(coarse_groups):
@@ -125,7 +132,7 @@
         message[c] = total.astype(BF16)
 
 
-def restrict_kernel(residual, aggregate, out):
+def restrict(residual, aggregate, out):
     groups = residual.shape[1]
     bins = out.shape[1]
     agg = aggregate[...] & (bins * LANES - 1)
@@ -269,7 +276,7 @@
 HALO_LAYERS = 3
 
 
-def local_kernel(smooth, picks, start, spot, rank, most, out, *, first, tiles, unroll=4):
+def local_kernel(smooth, picks, start, spot, rank, most, out, *, first, tiles, unroll=8):
     even = [smooth[e, pl.ds(0, PACK, stride=2), :].astype(BF16) for e in range(3)]
     odd = [smooth[e, pl.ds(1, PACK, stride=2), :].astype(BF16) for e in range(3)]
 
@@ -319,7 +326,7 @@
     return solved
 
 
-def halo_kernel(*refs, stage, scale_old, scale_new, unroll=4):
+def halo_kernel(*refs, stage, scale_old, scale_new, unroll=8):
     (place, most, picks, halo_start, spot, rank, ghost, outer, inner) = refs[:9]
     (residual, dinv, smooth, update, bonds, local_found) = refs[9:15]
     refs = refs[15:]
@@ -334,7 +341,7 @@
     else:
         (new_smooth,) = refs[:1]
         refs = refs[1:]
-    applied, other = refs
+    applied, other, partial = refs
     groups = smooth.shape[1]
     if stage == 0:
         vector = [rhs[e] + arrived[e] for e in range(3)]
@@ -397,7 +404,7 @@
                 for e in range(3):
                     block = bonds[c, e, h * PACK : (h + 1) * PACK, here].astype(F32)
                     total = total + block * values[h][e].astype(F32)
-            totals.append(jnp.sum(total, axis=0, keepdims=True))
+            totals.append(total[:8] + total[8:])
         return totals
 
     def some_tiles(t, carry):
@@ -415,7 +422,7 @@
                 put_back(row, jnp.int16(32 + v), spots, ranks, values)
             totals = apply_tile(tile, values)
             for c in range(3):
-                applied[c, pl.ds(tile, 1), :] = totals[c]
+                partial[c, pl.ds(pl.multiple_of(tile * 8, 8), 8), :] = totals[c]
         return carry
 
     lax.fori_loop(0, groups // unroll, some_tiles, 0)
@@ -435,12 +442,18 @@
             flat = lax.fori_loop(HALO_LAYERS, most[1] + 1, more, empty)
             totals = apply_tile(tile, [flat[:3], flat[3:]])
             for c in range(3):
-                applied[c, pl.ds(tile, 1), :] = applied[c, pl.ds(tile, 1), :] + totals[c]
+                rows = pl.ds(pl.multiple_of(tile * 8, 8), 8)
+                partial[c, rows, :] = partial[c, rows, :] + totals[c]
             return carry
 
         lax.fori_loop(0, groups, one_tile, 0)
 
-    remainder = [residual[e] - smooth[e] - applied[e] for e in range(3)]
+    remainder = []
+    for e in range(3):
+        total = partial[e, pl.ds(0, groups, stride=8), :]
+        for row in range(1, 8):
+            total = total + partial[e, pl.ds(row, groups, stride=8), :]
+        remainder.append(residual[e] - smooth[e] - total)
     solved = dense_solve(dinv, remainder)
     for c in range(3):
         change = scale_old * update[c] + scale_new * solved[c]
@@ -517,13 +530,18 @@
     for row, read in link_rows.items():
         for k in range(4):
             links[row + STEPS - 1, k] = read(k) * valid(row)
+    lane = lax.broadcasted_iota(jnp.int32, (groups, LANES), 1)
+    line = lax.broadcasted_iota(jnp.int32, (groups, LANES), 0)
+    inner_first = jnp.logical_or(lane > 0, line > 0)
+    inner_last = jnp.logical_or(lane < LANES - 1, line < groups - 1)
+    for row in range(2 * STEPS - 1):
+        links[row, 2] = jnp.where(inner_first, links[row, 2], 0.0)
+        links[row, 3] = jnp.where(inner_last, links[row, 3], 0.0)
     for row in range(-STEPS, STEPS + 1):
         for c in range(3):
             value = base_of(row, c)
             kept[row + STEPS, c] = value
             field[0, row + STEPS, c] = value
-    lane = lax.broadcasted_iota(jnp.int32, (groups, LANES), 1)
-    line = lax.broadcasted_iota(jnp.int32, (groups, LANES), 0)
     for step in range(STEPS):
         old, new = step % 2, (step + 1) % 2
         reach = STEPS - 1 - step
@@ -534,12 +552,8 @@
                 x = field[old, spot, c]
                 right = pltpu.roll(x, 1, 1)
                 right = jnp.where(lane == 0, pltpu.roll(right, 1, 0), right)
-                right = jnp.where(jnp.logical_and(lane == 0, line == 0), 0.0, right)
                 left = pltpu.roll(x, LANES - 1, 1)
                 left = jnp.where(lane == LANES - 1, pltpu.roll(left, groups - 1, 0), left)
-                left = jnp.where(
-                    jnp.logical_and(lane == LANES - 1, line == groups - 1), 0.0, left
-                )
                 field[new, spot, c] = kept[spot, c] + (
                     weights[0] * field[old, spot - 1, c]
                     + weights[1] * field[old, spot + 1, c]
@@ -600,35 +614,30 @@
     def message(rows):
         return sds((rows, groups, LANES), BF16)
 
-    dinv, residual, smooth, packed = call(
+    dinv, residual, smooth, packed, rhs = call(
         first_kernel,
-        (sds((3, 3, groups, LANES), F32), field, field, message(7)),
+        (sds((3, 3, groups, LANES), F32), field, field, message(7), coarse_field),
         tuple(
             pltpu.with_memory_space_constraint(x, pltpu.HBM)
-            for x in (fine_dinv, fine_residual, coarse_couple)
+            for x in (fine_residual, agg, fine_dinv, coarse_couple)
         ),
         scratch=[
+            VMEM(fine_residual.shape, F32),
+            VMEM(agg.shape, jnp.int32),
             VMEM(fine_dinv.shape, F32),
-            VMEM(fine_residual.shape, F32),
             VMEM(coarse_couple.shape, F32),
-            pltpu.SemaphoreType.DMA((3,)),
+            pltpu.SemaphoreType.DMA((4,)),
         ],
-        us=2.0,
-        spaces={i: pltpu.HBM for i in range(3)},
+        us=2.2,
+        spaces={i: pltpu.HBM for i in range(4)},
     )
     update = smooth
     own_packed = packed
     place = jnp.stack([jnp.int32(lax.axis_size("sub")), sub.astype(jnp.int32)])
-    rhs = call(restrict_kernel, coarse_field, (residual, agg), us=1.2)
-
     def exchanged(value, step):
         return lax.ppermute(value, "dom", [(i, i ^ step) for i in range(doms)])
 
-    rhs, packed = lax.optimization_barrier((rhs, packed))
     arrived = exchanged(rhs, 1)
-    first = arrived_sides = exchanged_by_pairs(packed, packed)
-    rhs = rhs + arrived
-    arrived = exchanged(rhs, 2)
     columns, rhs = lax.optimization_barrier((bond_col, rhs))
 
     def shorts(rows):
@@ -648,6 +657,11 @@
         scratch=[VMEM((8 * (bonds_of + 2), LANES), jnp.int32)],
         us=2.5,
     )
+    start, rhs = lax.optimization_barrier((start, rhs))
+    rhs = rhs + arrived
+    packed, rhs = lax.optimization_barrier((packed, rhs))
+    arrived = exchanged(rhs, 2)
+    first = arrived_sides = exchanged_by_pairs(packed, packed)
     rhs = rhs + arrived
     arrived = exchanged(rhs, 4)
     start, rhs = lax.optimization_barrier((start, rhs))
@@ -685,7 +699,7 @@
             ),
             outs,
             inputs,
-            scratch=[VMEM((3, groups, LANES), F32), VMEM((3, groups, LANES), F32)],
+            scratch=[VMEM((3, groups, LANES), F32)] * 2 + [VMEM((3, 8 * groups, LANES), F32)],
             us=2.5,
             spaces={0: pltpu.SMEM, 1: pltpu.SMEM},
         )

time: 57.5 us -> 53.4 us (0.929)
  waiting for transfers between devices: 3.18 us -> 0.03 us
  Pallas kernels: 30.2 us -> 28.6 us
  starting transfers between devices: 23.7 us -> 24.6 us
    ppermute x3, waiting for transfers between devices: 3.16 us -> 0.01 us  [exchanged(): return lax.ppermute(value, 'dom', [(i, i ^ step) for i in range(doms)])]
    ppermute x3, starting transfers between devices: 9.57 us -> 7.11 us  [exchanged_by_pairs(): inner = lax.ppermute(inner, 'sub', within + [(j, i) for i, j in within])]
    ppermute x3, starting transfers between devices: 4.4 us -> 6.22 us  [exchanged(): return lax.ppermute(value, 'dom', [(i, i ^ step) for i in range(doms)])]
    pallas_call x10 -> x9, Pallas kernels: 30.2 us -> 28.6 us  [call(): pl.pallas_call(kernel, out_shape=out, in_specs=[pl.BlockSpec(memory_space...]
    ppermute x3, starting transfers between devices: 7.91 us -> 9.3 us  [exchanged_by_pairs(): outer = lax.ppermute(outer, 'sub', across + [(j, i) for i, j in across])]
  transfers between devices with their start and end apart: 11 -> 11, of which waited for: 1 -> 0; matrix products, arithmetic and copies ran while one was open for 0% -> 0% of each run, Pallas kernels for 29% -> 29%
where the time goes in v5:
time: 53.4 us; the launch traced here: 53.5 us
  Pallas kernels  28.6 us (54%)
  starting transfers between devices  24.6 us (46%)
    pallas_call x9, Pallas kernels, call(): pl.pallas_call(kernel, out_shape=out, in_specs=[pl.BlockSpec(memory_space...  28.6 us
    ppermute x3, starting transfers between devices, exchanged_by_pairs(): outer = lax.ppermute(outer, 'sub', across + [(j, i) for i, j in across])  9.3 us
    ppermute x3, starting transfers between devices, exchanged_by_pairs(): inner = lax.ppermute(inner, 'sub', within + [(j, i) for i, j in within])  7.11 us
    ppermute x3, starting transfers between devices, exchanged(): return lax.ppermute(value, 'dom', [(i, i ^ step) for i in range(doms)])  6.22 us
    ppermute x2, starting transfers between devices, shifted(): lax.ppermute(value, 'sub', [(i, (i + steps) % count) for i in range(count)])  1.96 us
  transfers between devices with their start and end apart: 11, of which 0 were waited for; matrix products, arithmetic and copies ran while one was open for 0% of the time, Pallas kernels for 29%

profile of v5, /device:TPU:1, one launch (start us, length us, event | category | flops | bytes accessed | tf_op | source)
XLA Modules:
  0.0 53.5 jit_solution(16558771887981511572)
XLA Ops:
  0.0 2.4 %shard_map.82 = (f32[3,3,32,128]{3,2,1,0:T(8,128)S(1)}, f32[3,32,128]{2,1,0:T(8,128)S(1)}, f32[3,32,128]{2,1,0:T(8,128)S(1)}, bf16[7,32,128]{2,1,0:T(8,128)(2,1)S(1)}, f32[3,32,128]{2,1,0:T(8,128)S(1)}) custom-call(f32[3,4096]{1,0:T(4,128)} %refs_0_.1, s32[32,128]{1,0:T(8,128)} %bitcast.6, f32[3,3,4096]{2,1,0:T(4,128)} %refs_2_.2, f32[4,4096]{1,0:T(4,128)} %refs_2_.3), custom_call_target="tpu_custom_call" | custom-call | flops 2200000000 | bytes 2200000 | tf_op jit(solution)/shard_map/pallas_call | solution.py:74
  2.4 0.0 copy-start.5
  2.4 2.1 %collective-permute-start = (f32[3,32,128]{2,1,0:T(8,128)S(1)}, f32[3,32,128]{2,1,0:T(8,128)S(1)}, u32[]{:S(2)}, u32[]{:S(2)}) collective-permute-start(f32[3,32,128]{2,1,0:T(8,128)S(1)} %get-tuple-element.47), channel_id=1, source_target_pairs={{0,32},{32,0},{64,96},{96,64},{128,160},{160,128},{192,224},{224,1... | collective-permute-start | bytes 147464 | tf_op jit(solution)/shard_map/ppermute | solution.py:638
  4.6 2.9 %shard_map.83 = (s16[32,4096]{1,0:T(8,128)(2,1)S(1)}, s16[16,4096]{1,0:T(8,128)(2,1)S(1)}, s16[16,4096]{1,0:T(8,128)(2,1)S(1)}, s16[32,4096]{1,0:T(8,128)(2,1)S(...) custom-call(s32[32,4096]{1,0:T(8,128)S(1)} %copy-done.1), custom_call_target="tpu_custom_call" | custom-call | flops 2500000000 | bytes 2500000 | tf_op jit(solution)/shard_map/pallas_call | solution.py:74
  7.5 0.0 collective-permute-done
  7.5 1.4 %collective-permute-start.3 = (f32[3,32,128]{2,1,0:T(8,128)S(1)}, f32[3,32,128]{2,1,0:T(8,128)S(1)}, u32[]{:S(2)}, u32[]{:S(2)}) collective-permute-start(f32[3,32,128]{2,1,0:T(8,128)S(1)} %add.6), channel_id=1, source_target_pairs={{0,64},{32,96},{64,0},{96,32},{128,192},{160,224},{192,128},{224,1... | collective-permute-start | bytes 147464 | tf_op jit(solution)/shard_map/ppermute | solution.py:638
  8.9 0.1 pad_add_fusion.refs_0_
  9.0 1.3 %collective-permute-start.2 = (bf16[7,32,128]{2,1,0:T(8,128)(2,1)S(1)}, bf16[7,32,128]{2,1,0:T(8,128)(2,1)S(1)}, u32[]{:S(2)}, u32[]{:S(2)}) collective-permute-start(bf16[7,32,128]{2,1,0:T(8,128)(2,1)S(1)} %get-tuple-element.48.refs_18_), channel_id=1, source_target_pairs={{0,1},{2,3},{4,5},{6,7},{8,9},{10,11},{12,13},{14,15},{16,17},{18,... | collective-permute-start | bytes 172040 | tf_op jit(solution)/shard_map/ppermute | solution.py:592
  10.3 2.4 %collective-permute-start.1 = (bf16[7,32,128]{2,1,0:T(8,128)(2,1)S(1)}, bf16[7,32,128]{2,1,0:T(8,128)(2,1)S(1)}, u32[]{:S(2)}, u32[]{:S(2)}) collective-permute-start(bf16[7,32,128]{2,1,0:T(8,128)(2,1)S(1)} %get-tuple-element.48.refs_18_), channel_id=1, source_target_pairs={{1,2},{3,4},{5,6},{7,8},{9,10},{11,12},{13,14},{15,16},{17,18},{19... | collective-permute-start | bytes 172040 | tf_op jit(solution)/shard_map/ppermute | solution.py:591
  12.8 0.0 collective-permute-done.3
  12.8 2.7 %collective-permute-start.4 = (f32[3,32,128]{2,1,0:T(8,128)S(1)}, f32[3,32,128]{2,1,0:T(8,128)S(1)}, u32[]{:S(2)}, u32[]{:S(2)}) collective-permute-start(f32[3,32,128]{2,1,0:T(8,128)S(1)} %add.7.refs_15_), channel_id=1, source_target_pairs={{0,128},{32,160},{64,192},{96,224},{128,0},{160,32},{192,64},{224,... | collective-permute-start | bytes 147464 | tf_op jit(solution)/shard_map/ppermute | solution.py:638
  15.5 4.3 %shard_map.84.refs_14_ = bf16[3,32,4096]{2,1,0:T(8,128)(2,1)S(1)} custom-call(f32[3,32,128]{2,1,0:T(8,128)S(1)} %get-tuple-element.51.smooth.refs_11_.refs_12_, s16[32,4096]{1,0:T(8,128)(2,1)S(1)} %get-tuple-element.40.picks.refs_2_, s16[16,4096]{1,0:T(8,128)(2,1)S(1)} %get-tuple-element.54.start, s16[32,4096]{1,0:T(8,128)(2,1)S(1)} %get-tuple-element.42.spot.refs_4_, ...), custom_call_target="tpu_custom_call" | custom-call | flops 3500000000 | bytes 3500000 | tf_op jit(solution)/shard_map/pallas_call | solution.py:74
  19.8 0.0 collective-permute-done.2.refs_8_.refs_16_.refs_4_
  19.8 0.0 collective-permute-done.1.refs_7_.refs_15_.refs_3_
  19.8 0.0 collective-permute-done.4.refs_16_
  19.8 2.7 %shard_map.85 = (f32[3,32,128]{2,1,0:T(8,128)S(1)}, f32[3,32,128]{2,1,0:T(8,128)S(1)}, f32[3,32,128]{2,1,0:T(8,128)S(1)}, bf16[10,32,128]{2,1,0:T(8,128)(2,1)S(1)}, bf16[10,32,128]{2,1,0:T(8,128)(2,1)S(1)}) custom-call(s32[2]{0:T(128)S(1)} %pad_add_fusion.refs_0_, s32[2]{0:T(128)S(1)} %get-tuple-element.39.most.refs_1_, ...), custom_call_target="tpu_custom_call" | custom-call | flops 2500000000 | bytes 2500000 | tf_op jit(solution)/shard_map/pallas_call | solution.py:74
  22.5 2.9 %collective-permute-start.5 = (bf16[10,32,128]{2,1,0:T(8,128)(2,1)S(1)}, bf16[10,32,128]{2,1,0:T(8,128)(2,1)S(1)}, u32[]{:S(2)}, u32[]{:S(2)}) collective-permute-start(bf16[10,32,128]{2,1,0:T(8,128)(2,1)S(1)} %get-tuple-element.57), channel_id=1, source_target_pairs={{1,2},{3,4},{5,6},{7,8},{9,10},{11,12},{13,14},{15,16},{17,18},{19... | collective-permute-start | bytes 245768 | tf_op jit(solution)/shard_map/ppermute | solution.py:591
  25.5 3.7 %collective-permute-start.6 = (bf16[10,32,128]{2,1,0:T(8,128)(2,1)S(1)}, bf16[10,32,128]{2,1,0:T(8,128)(2,1)S(1)}, u32[]{:S(2)}, u32[]{:S(2)}) collective-permute-start(bf16[10,32,128]{2,1,0:T(8,128)(2,1)S(1)} %get-tuple-element.58), channel_id=1, source_target_pairs={{0,1},{2,3},{4,5},{6,7},{8,9},{10,11},{12,13},{14,15},{16,17},{18,... | collective-permute-start | bytes 245768 | tf_op jit(solution)/shard_map/ppermute | solution.py:592
  29.2 4.3 %shard_map.86.refs_14_ = bf16[3,32,4096]{2,1,0:T(8,128)(2,1)S(1)} custom-call(f32[3,32,128]{2,1,0:T(8,128)S(1)} %get-tuple-element.59.smooth.refs_11_, s16[32,4096]{1,0:T(8,128)(2,1)S(1)} %get-tuple-element.40.picks.refs_2_, s16[16,4096]{1,0:T(8,128)(2,1)S(1)} %get-tuple-element.54.start, s16[32,4096]{1,0:T(8,128)(2,1)S(1)} %get-tuple-element.42.spot.refs_4_, ...), custom_call_target="tpu_custom_call" | custom-call | flops 3500000000 | bytes 3500000 | tf_op jit(solution)/shard_map/pallas_call | solution.py:74
  33.4 0.0 collective-permute-done.5.refs_7_.refs_5_
  33.5 0.0 collective-permute-done.6.refs_8_.refs_6_
  33.5 2.6 %shard_map.87 = (f32[3,32,128]{2,1,0:T(8,128)S(1)}, f32[3,32,128]{2,1,0:T(8,128)S(1)}, bf16[6,32,128]{2,1,0:T(8,128)(2,1)S(1)}, bf16[6,32,128]{2,1,0:T(8,128)(2,1)S(1)}, bf16[21,32,128]{2,1,0:T(8,128)(2,1)S(1)}) custom-call(s32[2]{0:T(128)S(1)} %pad_add_fusion.refs_0_, s32[2]{0:T(128)S(1)} %get-tuple-element.39.most.refs_1_, ...), custom_call_target="tpu_custom_call" | custom-call | flops 2500000000 | bytes 2500000 | tf_op jit(solution)/shard_map/pallas_call | solution.py:74
  36.1 2.0 %collective-permute-start.10 = (bf16[21,32,128]{2,1,0:T(8,128)(2,1)S(1)}, bf16[21,32,128]{2,1,0:T(8,128)(2,1)S(1)}, u32[]{:S(2)}, u32[]{:S(2)}) collective-permute-start(bf16[21,32,128]{2,1,0:T(8,128)(2,1)S(1)} %get-tuple-element.64), channel_id=1, source_target_pairs={{0,28},{1,29},{2,30},{3,31},{4,0},{5,1},{6,2},{7,3},{8,4},{9,5},{1... | collective-permute-start | bytes 516104 | tf_op jit(solution)/shard_map/ppermute | solution.py:584
  38.0 0.0 collective-permute-start.9
  38.1 3.9 %collective-permute-start.7 = (bf16[6,32,128]{2,1,0:T(8,128)(2,1)S(1)}, bf16[6,32,128]{2,1,0:T(8,128)(2,1)S(1)}, u32[]{:S(2)}, u32[]{:S(2)}) collective-permute-start(bf16[6,32,128]{2,1,0:T(8,128)(2,1)S(1)} %get-tuple-element.61), channel_id=1, source_target_pairs={{1,2},{3,4},{5,6},{7,8},{9,10},{11,12},{13,14},{15,16},{17,18},{19... | collective-permute-start | bytes 147464 | tf_op jit(solution)/shard_map/ppermute | solution.py:591
  42.0 2.1 %collective-permute-start.8 = (bf16[6,32,128]{2,1,0:T(8,128)(2,1)S(1)}, bf16[6,32,128]{2,1,0:T(8,128)(2,1)S(1)}, u32[]{:S(2)}, u32[]{:S(2)}) collective-permute-start(bf16[6,32,128]{2,1,0:T(8,128)(2,1)S(1)} %get-tuple-element.62), channel_id=1, source_target_pairs={{0,1},{2,3},{4,5},{6,7},{8,9},{10,11},{12,13},{14,15},{16,17},{18,... | collective-permute-start | bytes 147464 | tf_op jit(solution)/shard_map/ppermute | solution.py:592
  44.1 4.3 %shard_map.88.refs_14_ = bf16[3,32,4096]{2,1,0:T(8,128)(2,1)S(1)} custom-call(f32[3,32,128]{2,1,0:T(8,128)S(1)} %get-tuple-element.63.smooth.refs_11_, s16[32,4096]{1,0:T(8,128)(2,1)S(1)} %get-tuple-element.40.picks.refs_2_, s16[16,4096]{1,0:T(8,128)(2,1)S(1)} %get-tuple-element.54.start, s16[32,4096]{1,0:T(8,128)(2,1)S(1)} %get-tuple-element.42.spot.refs_4_, ...), custom_call_target="tpu_custom_call" | custom-call | flops 3500000000 | bytes 3500000 | tf_op jit(solution)/shard_map/pallas_call | solution.py:74
  48.4 0.0 collective-permute-done.7.refs_7_
  48.4 0.0 copy-start.3
  48.4 0.0 copy-start.4
  48.5 2.6 %shard_map.89.refs_12_ = f32[3,32,128]{2,1,0:T(8,128)S(1)} custom-call(s32[2]{0:T(128)S(1)} %pad_add_fusion.refs_0_, s32[2]{0:T(128)S(1)} %get-tuple-element.39.most.refs_1_, s16[32,4096]{1,0:T(8,128)(2,1)S(1)} %get-tuple-element.40.picks.refs_2_, s16[16,4096]{1,0:T(8,128)(2,1)S(1)} %get-tuple-element.41.refs_3_, ...), custom_call_target="tpu_custom_call" | custom-call | flops 2500000000 | bytes 2500000 | tf_op jit(solution)/shard_map/pallas_call | solution.py:74
  51.1 2.5 %shard_map.90 = f32[3,4096]{1,0:T(4,128)} custom-call(s32[2]{0:T(128)S(1)} %pad_add_fusion.refs_0_, f32[3,32,128]{2,1,0:T(8,128)S(1)} %get-tuple-element.56.refs_17_.refs_1_, f32[4,4096]{1,0:T(4,128)S(1)} %copy-done.3, bf16[7,32,128]{2,1,0:T(8,128)(2,1)S(1)} %collective-permute-done.1.refs_7_.refs_15_.refs_3_, ...), custom_call_target="tpu_custom_call" | custom-call | flops 2000000000 | bytes 2000000 | tf_op jit(solution)/shard_map/pallas_call | solution.py:74
  (15 shorter events, 0.1 us)
Async XLA Ops:
  0.0 4.6 %copy-start.1 = (s32[32,4096]{1,0:T(8,128)S(1)}, s32[32,4096]{1,0:T(8,128)}, u32[]{:S(2)}) copy-start(s32[32,4096]{1,0:T(8,128)} %col) | copy-start | bytes 1572868
  2.4 6.6 %copy-start.5 = (s32[1,2,512]{2,1,0:T(2,128)S(1)}, s32[1,2,512]{2,1,0:T(2,128)}, u32[]{:S(2)}) copy-start(s32[1,2,512]{2,1,0:T(2,128)} %param.11) | copy-start | bytes 12292
  2.4 5.1 %collective-permute-start = (f32[3,32,128]{2,1,0:T(8,128)S(1)}, f32[3,32,128]{2,1,0:T(8,128)S(1)}, u32[]{:S(2)}, u32[]{:S(2)}) collective-permute-start(f32[3,32,128]{2,1,0:T(8,128)S(1)} %get-tuple-element.47), channel_id=1, source_target_pairs={{0,32},{32,0},{64,96},{96,64},{128,160},{160,128},{192,224},{224,1... | collective-permute-start | bytes 147464 | tf_op jit(solution)/shard_map/ppermute | solution.py:638
  7.5 5.2 %collective-permute-start.3 = (f32[3,32,128]{2,1,0:T(8,128)S(1)}, f32[3,32,128]{2,1,0:T(8,128)S(1)}, u32[]{:S(2)}, u32[]{:S(2)}) collective-permute-start(f32[3,32,128]{2,1,0:T(8,128)S(1)} %add.6), channel_id=1, source_target_pairs={{0,64},{32,96},{64,0},{96,32},{128,192},{160,224},{192,128},{224,1... | collective-permute-start | bytes 147464 | tf_op jit(solution)/shard_map/ppermute | solution.py:638
  9.0 10.7 %collective-permute-start.2 = (bf16[7,32,128]{2,1,0:T(8,128)(2,1)S(1)}, bf16[7,32,128]{2,1,0:T(8,128)(2,1)S(1)}, u32[]{:S(2)}, u32[]{:S(2)}) collective-permute-start(bf16[7,32,128]{2,1,0:T(8,128)(2,1)S(1)} %get-tuple-element.48.refs_18_), channel_id=1, source_target_pairs={{0,1},{2,3},{4,5},{6,7},{8,9},{10,11},{12,13},{14,15},{16,17},{18,... | collective-permute-start | bytes 172040 | tf_op jit(solution)/shard_map/ppermute | solution.py:592
  10.3 9.5 %collective-permute-start.1 = (bf16[7,32,128]{2,1,0:T(8,128)(2,1)S(1)}, bf16[7,32,128]{2,1,0:T(8,128)(2,1)S(1)}, u32[]{:S(2)}, u32[]{:S(2)}) collective-permute-start(bf16[7,32,128]{2,1,0:T(8,128)(2,1)S(1)} %get-tuple-element.48.refs_18_), channel_id=1, source_target_pairs={{1,2},{3,4},{5,6},{7,8},{9,10},{11,12},{13,14},{15,16},{17,18},{19... | collective-permute-start | bytes 172040 | tf_op jit(solution)/shard_map/ppermute | solution.py:591
  12.8 7.0 %collective-permute-start.4 = (f32[3,32,128]{2,1,0:T(8,128)S(1)}, f32[3,32,128]{2,1,0:T(8,128)S(1)}, u32[]{:S(2)}, u32[]{:S(2)}) collective-permute-start(f32[3,32,128]{2,1,0:T(8,128)S(1)} %add.7.refs_15_), channel_id=1, source_target_pairs={{0,128},{32,160},{64,192},{96,224},{128,0},{160,32},{192,64},{224,... | collective-permute-start | bytes 147464 | tf_op jit(solution)/shard_map/ppermute | solution.py:638
  15.5 4.3 %copy-start = (bf16[32,3,3,4096]{3,0,2,1:T(8,128)(2,1)S(1)}, bf16[32,3,3,4096]{3,0,2,1:T(8,128)(2,1)}, u32[]{:S(2)}) copy-start(bf16[32,3,3,4096]{3,0,2,1:T(8,128)(2,1)} %param.9) | copy-start | bytes 7077892
  15.5 4.3 %copy-start.2 = (f32[3,3,4096]{2,1,0:T(4,128)S(1)}, f32[3,3,4096]{2,1,0:T(4,128)}, u32[]{:S(2)}) copy-start(f32[3,3,4096]{2,1,0:T(4,128)} %refs_17_.1) | copy-start | bytes 442372
  22.5 10.9 %collective-permute-start.5 = (bf16[10,32,128]{2,1,0:T(8,128)(2,1)S(1)}, bf16[10,32,128]{2,1,0:T(8,128)(2,1)S(1)}, u32[]{:S(2)}, u32[]{:S(2)}) collective-permute-start(bf16[10,32,128]{2,1,0:T(8,128)(2,1)S(1)} %get-tuple-element.57), channel_id=1, source_target_pairs={{1,2},{3,4},{5,6},{7,8},{9,10},{11,12},{13,14},{15,16},{17,18},{19... | collective-permute-start | bytes 245768 | tf_op jit(solution)/shard_map/ppermute | solution.py:591
  25.5 8.0 %collective-permute-start.6 = (bf16[10,32,128]{2,1,0:T(8,128)(2,1)S(1)}, bf16[10,32,128]{2,1,0:T(8,128)(2,1)S(1)}, u32[]{:S(2)}, u32[]{:S(2)}) collective-permute-start(bf16[10,32,128]{2,1,0:T(8,128)(2,1)S(1)} %get-tuple-element.58), channel_id=1, source_target_pairs={{0,1},{2,3},{4,5},{6,7},{8,9},{10,11},{12,13},{14,15},{16,17},{18,... | collective-permute-start | bytes 245768 | tf_op jit(solution)/shard_map/ppermute | solution.py:592
  36.1 12.3 %collective-permute-start.10 = (bf16[21,32,128]{2,1,0:T(8,128)(2,1)S(1)}, bf16[21,32,128]{2,1,0:T(8,128)(2,1)S(1)}, u32[]{:S(2)}, u32[]{:S(2)}) collective-permute-start(bf16[21,32,128]{2,1,0:T(8,128)(2,1)S(1)} %get-tuple-element.64), channel_id=1, source_target_pairs={{0,28},{1,29},{2,30},{3,31},{4,0},{5,1},{6,2},{7,3},{8,4},{9,5},{1... | collective-permute-start | bytes 516104 | tf_op jit(solution)/shard_map/ppermute | solution.py:584
  38.0 10.4 %collective-permute-start.9 = (bf16[21,32,128]{2,1,0:T(8,128)(2,1)S(1)}, bf16[21,32,128]{2,1,0:T(8,128)(2,1)S(1)}, u32[]{:S(2)}, u32[]{:S(2)}) collective-permute-start(bf16[21,32,128]{2,1,0:T(8,128)(2,1)S(1)} %get-tuple-element.64), channel_id=1, source_target_pairs={{0,4},{1,5},{2,6},{3,7},{4,8},{5,9},{6,10},{7,11},{8,12},{9,13},{1... | collective-permute-start | bytes 516104 | tf_op jit(solution)/shard_map/ppermute | solution.py:584
  38.1 10.4 %collective-permute-start.7 = (bf16[6,32,128]{2,1,0:T(8,128)(2,1)S(1)}, bf16[6,32,128]{2,1,0:T(8,128)(2,1)S(1)}, u32[]{:S(2)}, u32[]{:S(2)}) collective-permute-start(bf16[6,32,128]{2,1,0:T(8,128)(2,1)S(1)} %get-tuple-element.61), channel_id=1, source_target_pairs={{1,2},{3,4},{5,6},{7,8},{9,10},{11,12},{13,14},{15,16},{17,18},{19... | collective-permute-start | bytes 147464 | tf_op jit(solution)/shard_map/ppermute | solution.py:591
  42.0 6.4 %collective-permute-start.8 = (bf16[6,32,128]{2,1,0:T(8,128)(2,1)S(1)}, bf16[6,32,128]{2,1,0:T(8,128)(2,1)S(1)}, u32[]{:S(2)}, u32[]{:S(2)}) collective-permute-start(bf16[6,32,128]{2,1,0:T(8,128)(2,1)S(1)} %get-tuple-element.62), channel_id=1, source_target_pairs={{0,1},{2,3},{4,5},{6,7},{8,9},{10,11},{12,13},{14,15},{16,17},{18,... | collective-permute-start | bytes 147464 | tf_op jit(solution)/shard_map/ppermute | solution.py:592
  48.4 2.6 %copy-start.3 = (f32[4,4096]{1,0:T(4,128)S(1)}, f32[4,4096]{1,0:T(4,128)}, u32[]{:S(2)}) copy-start(f32[4,4096]{1,0:T(4,128)} %refs_2_.3) | copy-start | bytes 196612
  48.4 2.6 %copy-start.4 = (s32[4096]{0:T(1024)S(1)}, s32[4096]{0:T(1024)}, u32[]{:S(2)}) copy-start(s32[4096]{0:T(1024)} %param.13) | copy-start | bytes 49156

commit v6 on v5

--- a/solution.py
+++ b/solution.py
@@ -78,7 +78,7 @@
             pl.BlockSpec(memory_space=spaces.get(i, VMEM)) for i in range(len(inputs))
         ],
         out_specs=jax.tree.map(
-            lambda x: pl.BlockSpec(memory_space=pltpu.SMEM if x.shape == (2,) else VMEM), out
+            lambda _: pl.BlockSpec(memory_space=VMEM), out
         ),
         scratch_shapes=list(scratch),
         cost_estimate=pl.CostEstimate(
@@ -174,6 +174,11 @@
         out[c] = total[c][:bins] + total[c][bins:]
 
 
+def spread_max(values):
+    top = jnp.max(jnp.max(values, axis=1, keepdims=True), axis=0, keepdims=True)
+    return jnp.broadcast_to(top, values.shape)
+
+
 def prepare_kernel(col, picks, start, halo_start, spot, rank, most, flip):
     bonds_of = col.shape[0]
     groups = col.shape[1] // LANES
@@ -197,9 +202,10 @@
         for k in range(1, bonds_of):
             ranks.append(jnp.where(pairs[k] == pairs[k - 1], ranks[k - 1] + 1, 0))
         back = []
+        here = jnp.zeros((8, LANES), jnp.int32)
         for k in range(bonds_of):
             local = pairs[k] < PACK
-            best = jnp.maximum(best, jnp.where(local, ranks[k], 0))
+            here = jnp.maximum(here, jnp.where(local, ranks[k], 0))
             halo_best = jnp.maximum(halo_best, jnp.where(local, 0, ranks[k]))
             code = jnp.where(
                 local,
@@ -236,12 +242,13 @@
                 rows = slice(h * PACK, (h + 1) * PACK)
                 spot[rows, lanes_of(t)] = (code & 15).astype(jnp.int16)
                 rank[rows, lanes_of(t)] = (code >> 4).astype(jnp.int16)
-        return best, halo_best
+        most[pl.ds(pl.multiple_of(block * 8, 8), 8), :] = spread_max(here)
+        return jnp.maximum(best, here), halo_best
 
     zero = jnp.zeros((8, LANES), jnp.int32)
     best, halo_best = lax.fori_loop(0, groups // 8, eight_tiles, (zero, zero))
-    most[0] = jnp.max(best)
-    most[1] = jnp.max(halo_best) >> 2
+    most[groups : groups + 8, :] = spread_max(best)
+    most[groups + 8 :, :] = spread_max(halo_best) >> 2
 
 
 def layer(place, picks, even, odd):
@@ -298,22 +305,34 @@
 
     lax.fori_loop(0, tiles // unroll, some_tiles, 0)
 
-    def more(m, carry):
-        number = splat(m)
-        for t in range(tiles):
-            source = slice((first + t) * LANES, (first + t + 1) * LANES)
-            target = slice(t * LANES, (t + 1) * LANES)
-            found = [
-                [out[e, h * PACK : (h + 1) * PACK, target] for e in range(3)] for h in range(2)
-            ]
-            values = layer(start[:, source] + number, halves_of(picks, source), even, odd)
-            put_back(values, number, halves_of(spot, source), halves_of(rank, source), found)
-            for h in range(2):
-                for e in range(3):
-                    out[e, h * PACK : (h + 1) * PACK, target] = found[h][e]
-        return carry
-
-    lax.fori_loop(LAYERS, most[0] + 1, more, 0)
+    @pl.when(most[smooth.shape[1], 0] >= LAYERS)
+    def _():
+        def eight_tiles(block, carry):
+            def more(m, inner):
+                number = splat(m)
+                for t in range(8):
+                    tile = block * 8 + t
+                    source = pl.ds(pl.multiple_of((first + tile) * LANES, LANES), LANES)
+                    target = pl.ds(pl.multiple_of(tile * LANES, LANES), LANES)
+                    found = [
+                        [out[e, h * PACK : (h + 1) * PACK, target] for e in range(3)]
+                        for h in range(2)
+                    ]
+                    values = layer(
+                        start[:, source] + number, halves_of(picks, source), even, odd
+                    )
+                    put_back(
+                        values, number, halves_of(spot, source), halves_of(rank, source), found
+                    )
+                    for h in range(2):
+                        for e in range(3):
+                            out[e, h * PACK : (h + 1) * PACK, target] = found[h][e]
+                return inner
+
+            lax.fori_loop(LAYERS, most[first + block * 8, 0] + 1, more, 0)
+            return carry
+
+        lax.fori_loop(0, tiles // 8, eight_tiles, 0)
 
 
 def dense_solve(matrix, vector):
@@ -373,7 +392,7 @@
     low = wanted & (LANES - 1)
     high = wanted >> 7
     upper = jnp.where(lax.broadcasted_iota(jnp.int32, wanted.shape, 0) < half, 1, 0)
-    from_outer = (upper ^ (place[1] & 1)) == 1
+    from_outer = (upper ^ (place[...] & 1)) == 1
     found = [jnp.zeros(wanted.shape, F32)] * 3
     for e in range(3):
         applied[e] = outer[e].astype(F32)
@@ -427,7 +446,9 @@
 
     lax.fori_loop(0, groups // unroll, some_tiles, 0)
 
-    @pl.when(most[1] >= HALO_LAYERS)
+    last_layer = most[groups + 8, 0]
+
+    @pl.when(last_layer >= HALO_LAYERS)
     def _():
         def one_tile(tile, carry):
             here = pl.ds(pl.multiple_of(tile * LANES, LANES), LANES)
@@ -439,7 +460,7 @@
                 return tuple(values[0] + values[1])
 
             empty = (jnp.zeros((PACK, LANES), BF16),) * 6
-            flat = lax.fori_loop(HALO_LAYERS, most[1] + 1, more, empty)
+            flat = lax.fori_loop(HALO_LAYERS, last_layer + 1, more, empty)
             totals = apply_tile(tile, [flat[:3], flat[3:]])
             for c in range(3):
                 rows = pl.ds(pl.multiple_of(tile * 8, 8), 8)
@@ -465,18 +486,19 @@
             out_inner[c] = total.astype(BF16)
 
 
-def coarse_kernel(*refs):
+def coarse_kernel(*refs, subs):
     (place, base, own_couple) = refs[:3]
     first, second, third = refs[3:5], refs[5:7], refs[7:9]
     far_after, far_before, aggregate, smooth = refs[9:13]
     out, field, links, kept = refs[13:]
-    subs, me = place[0], place[1]
     groups = base.shape[1]
+    me = jnp.concatenate([place[...]] * (groups // 8), axis=0)
     even = (me & 1) == 0
 
     def valid(row):
-        inside = jnp.logical_and(me + row >= 0, me + row < subs)
-        return jnp.where(inside, 1.0, 0.0).astype(F32)
+        if row < 0:
+            return jnp.where(me + row >= 0, 1.0, 0.0)
+        return jnp.where(me + row < subs, 1.0, 0.0)
 
     def from_after(pair, start):
         return lambda i: jnp.where(
@@ -633,7 +655,7 @@
     )
     update = smooth
     own_packed = packed
-    place = jnp.stack([jnp.int32(lax.axis_size("sub")), sub.astype(jnp.int32)])
+    place = jnp.full((8, LANES), sub, jnp.int32)
     def exchanged(value, step):
         return lax.ppermute(value, "dom", [(i, i ^ step) for i in range(doms)])
 
@@ -651,7 +673,7 @@
             shorts(PACK),
             shorts(bonds_of),
             shorts(bonds_of),
-            sds((2,), jnp.int32),
+            sds((groups + 16, LANES), jnp.int32),
         ),
         (columns,),
         scratch=[VMEM((8 * (bonds_of + 2), LANES), jnp.int32)],
@@ -674,7 +696,6 @@
             sds((3, bonds_of, points), BF16),
             (smooth, picks, start, spot, rank, most),
             us=3.5,
-            spaces={5: pltpu.SMEM},
         )
         if stage == SWEEPS - 1:
             found, far_after, far_before = lax.optimization_barrier(
@@ -701,7 +722,6 @@
             inputs,
             scratch=[VMEM((3, groups, LANES), F32)] * 2 + [VMEM((3, 8 * groups, LANES), F32)],
             us=2.5,
-            spaces={0: pltpu.SMEM, 1: pltpu.SMEM},
         )
         factor = factor_new
         if stage == 0:
@@ -715,7 +735,7 @@
         else:
             (smooth,) = result
     return call(
-        coarse_kernel,
+        functools.partial(coarse_kernel, subs=lax.axis_size("sub")),
         sds((3, points), F32),
         (
             place,
@@ -735,7 +755,6 @@
             VMEM((2 * STEPS + 1, 3, coarse_groups, LANES), F32),
         ],
         us=2.0,
-        spaces={0: pltpu.SMEM},
     )
 
 

time: 53.4 us -> 49.4 us (0.925)
  Pallas kernels: 28.6 us -> 24.7 us
    pallas_call x9, Pallas kernels: 28.6 us -> 24.7 us  [call(): pl.pallas_call(kernel, out_shape=out, in_specs=[pl.BlockSpec(memory_space...]
  transfers between devices with their start and end apart: 11 -> 11, of which waited for: 0 -> 0; matrix products, arithmetic and copies ran while one was open for 0% -> 0% of each run, Pallas kernels for 29% -> 28%
where the time goes in v6:
time: 49.4 us; the launch traced here: 49.3 us
  Pallas kernels  24.7 us (50%)
  starting transfers between devices  24.3 us (49%)
    pallas_call x9, Pallas kernels, call(): pl.pallas_call(kernel, out_shape=out, in_specs=[pl.BlockSpec(memory_space...  24.7 us
    ppermute x3, starting transfers between devices, exchanged_by_pairs(): outer = lax.ppermute(outer, 'sub', across + [(j, i) for i, j in across])  8.87 us
    ppermute x3, starting transfers between devices, exchanged_by_pairs(): inner = lax.ppermute(inner, 'sub', within + [(j, i) for i, j in within])  6.98 us
    ppermute x3, starting transfers between devices, exchanged(): return lax.ppermute(value, 'dom', [(i, i ^ step) for i in range(doms)])  6.22 us
    ppermute x2, starting transfers between devices, shifted(): lax.ppermute(value, 'sub', [(i, (i + steps) % count) for i in range(count)])  2.26 us
  transfers between devices with their start and end apart: 11, of which 0 were waited for; matrix products, arithmetic and copies ran while one was open for 0% of the time, Pallas kernels for 28%

profile of v6, /device:TPU:1, one launch (start us, length us, event | category | flops | bytes accessed | tf_op | source)
XLA Modules:
  0.0 49.3 jit_solution(3701350601951050049)
XLA Ops:
  0.0 2.4 %shard_map.82 = (f32[3,3,32,128]{3,2,1,0:T(8,128)S(1)}, f32[3,32,128]{2,1,0:T(8,128)S(1)}, f32[3,32,128]{2,1,0:T(8,128)S(1)}, bf16[7,32,128]{2,1,0:T(8,128)(2,1)S(1)}, f32[3,32,128]{2,1,0:T(8,128)S(1)}) custom-call(f32[3,4096]{1,0:T(4,128)} %refs_0_.1, s32[32,128]{1,0:T(8,128)} %bitcast.5, f32[3,3,4096]{2,1,0:T(4,128)} %refs_2_.2, f32[4,4096]{1,0:T(4,128)} %refs_2_.3), custom_call_target="tpu_custom_call" | custom-call | flops 2200000000 | bytes 2200000 | tf_op jit(solution)/shard_map/pallas_call | solution.py:74
  2.4 0.0 copy-start.5
  2.4 2.1 %collective-permute-start = (f32[3,32,128]{2,1,0:T(8,128)S(1)}, f32[3,32,128]{2,1,0:T(8,128)S(1)}, u32[]{:S(2)}, u32[]{:S(2)}) collective-permute-start(f32[3,32,128]{2,1,0:T(8,128)S(1)} %get-tuple-element.47), channel_id=1, source_target_pairs={{0,32},{32,0},{64,96},{96,64},{128,160},{160,128},{192,224},{224,1... | collective-permute-start | bytes 147464 | tf_op jit(solution)/shard_map/ppermute | solution.py:660
  4.6 2.6 %shard_map.83 = (s16[32,4096]{1,0:T(8,128)(2,1)S(1)}, s16[16,4096]{1,0:T(8,128)(2,1)S(1)}, s16[16,4096]{1,0:T(8,128)(2,1)S(1)}, s16[32,4096]{1,0:T(8,128)(2,1)S(...) custom-call(s32[32,4096]{1,0:T(8,128)S(1)} %copy-done.1), custom_call_target="tpu_custom_call" | custom-call | flops 2500000000 | bytes 2500000 | tf_op jit(solution)/shard_map/pallas_call | solution.py:74
  7.2 0.0 collective-permute-done
  7.2 1.4 %collective-permute-start.3 = (f32[3,32,128]{2,1,0:T(8,128)S(1)}, f32[3,32,128]{2,1,0:T(8,128)S(1)}, u32[]{:S(2)}, u32[]{:S(2)}) collective-permute-start(f32[3,32,128]{2,1,0:T(8,128)S(1)} %add.6), channel_id=1, source_target_pairs={{0,64},{32,96},{64,0},{96,32},{128,192},{160,224},{192,128},{224,1... | collective-permute-start | bytes 147464 | tf_op jit(solution)/shard_map/ppermute | solution.py:660
  8.6 1.5 %collective-permute-start.2 = (bf16[7,32,128]{2,1,0:T(8,128)(2,1)S(1)}, bf16[7,32,128]{2,1,0:T(8,128)(2,1)S(1)}, u32[]{:S(2)}, u32[]{:S(2)}) collective-permute-start(bf16[7,32,128]{2,1,0:T(8,128)(2,1)S(1)} %get-tuple-element.48.refs_18_), channel_id=1, source_target_pairs={{0,1},{2,3},{4,5},{6,7},{8,9},{10,11},{12,13},{14,15},{16,17},{18,... | collective-permute-start | bytes 172040 | tf_op jit(solution)/shard_map/ppermute | solution.py:614
  10.1 2.4 %collective-permute-start.1 = (bf16[7,32,128]{2,1,0:T(8,128)(2,1)S(1)}, bf16[7,32,128]{2,1,0:T(8,128)(2,1)S(1)}, u32[]{:S(2)}, u32[]{:S(2)}) collective-permute-start(bf16[7,32,128]{2,1,0:T(8,128)(2,1)S(1)} %get-tuple-element.48.refs_18_), channel_id=1, source_target_pairs={{1,2},{3,4},{5,6},{7,8},{9,10},{11,12},{13,14},{15,16},{17,18},{19... | collective-permute-start | bytes 172040 | tf_op jit(solution)/shard_map/ppermute | solution.py:613
  12.5 0.0 collective-permute-done.3
  12.5 2.7 %collective-permute-start.4 = (f32[3,32,128]{2,1,0:T(8,128)S(1)}, f32[3,32,128]{2,1,0:T(8,128)S(1)}, u32[]{:S(2)}, u32[]{:S(2)}) collective-permute-start(f32[3,32,128]{2,1,0:T(8,128)S(1)} %add.7.refs_15_), channel_id=1, source_target_pairs={{0,128},{32,160},{64,192},{96,224},{128,0},{160,32},{192,64},{224,... | collective-permute-start | bytes 147464 | tf_op jit(solution)/shard_map/ppermute | solution.py:660
  15.3 3.8 %shard_map.84.refs_14_ = bf16[3,32,4096]{2,1,0:T(8,128)(2,1)S(1)} custom-call(f32[3,32,128]{2,1,0:T(8,128)S(1)} %get-tuple-element.51.smooth.refs_11_.refs_12_, s16[32,4096]{1,0:T(8,128)(2,1)S(1)} %get-tuple-element.40.picks.refs_2_, s16[16,4096]{1,0:T(8,128)(2,1)S(1)} %get-tuple-element.54.start, s16[32,4096]{1,0:T(8,128)(2,1)S(1)} %get-tuple-element.42.spot.refs_4_, ...), custom_call_target="tpu_custom_call" | custom-call | flops 3500000000 | bytes 3500000 | tf_op jit(solution)/shard_map/pallas_call | solution.py:74
  19.0 0.0 collective-permute-done.2.refs_8_.refs_16_.refs_4_
  19.0 0.0 collective-permute-done.1.refs_7_.refs_15_.refs_3_
  19.0 0.0 collective-permute-done.4.refs_16_
  19.1 2.2 %shard_map.85 = (f32[3,32,128]{2,1,0:T(8,128)S(1)}, f32[3,32,128]{2,1,0:T(8,128)S(1)}, f32[3,32,128]{2,1,0:T(8,128)S(1)}, bf16[10,32,128]{2,1,0:T(8,128)(2,1)S(1)}, bf16[10,32,128]{2,1,0:T(8,128)(2,1)S(1)}) custom-call(s32[8,128]{1,0:T(8,128)S(1)} %broadcast_in_dim.3.refs_0_, s32[48,128]{1,0:T(8,128)S(1)} %get-tuple-element.39.most.refs_1_, ...), custom_call_target="tpu_custom_call" | custom-call | flops 2500000000 | bytes 2500000 | tf_op jit(solution)/shard_map/pallas_call | solution.py:74
  21.3 3.1 %collective-permute-start.5 = (bf16[10,32,128]{2,1,0:T(8,128)(2,1)S(1)}, bf16[10,32,128]{2,1,0:T(8,128)(2,1)S(1)}, u32[]{:S(2)}, u32[]{:S(2)}) collective-permute-start(bf16[10,32,128]{2,1,0:T(8,128)(2,1)S(1)} %get-tuple-element.57), channel_id=1, source_target_pairs={{1,2},{3,4},{5,6},{7,8},{9,10},{11,12},{13,14},{15,16},{17,18},{19... | collective-permute-start | bytes 245768 | tf_op jit(solution)/shard_map/ppermute | solution.py:613
  24.4 3.4 %collective-permute-start.6 = (bf16[10,32,128]{2,1,0:T(8,128)(2,1)S(1)}, bf16[10,32,128]{2,1,0:T(8,128)(2,1)S(1)}, u32[]{:S(2)}, u32[]{:S(2)}) collective-permute-start(bf16[10,32,128]{2,1,0:T(8,128)(2,1)S(1)} %get-tuple-element.58), channel_id=1, source_target_pairs={{0,1},{2,3},{4,5},{6,7},{8,9},{10,11},{12,13},{14,15},{16,17},{18,... | collective-permute-start | bytes 245768 | tf_op jit(solution)/shard_map/ppermute | solution.py:614
  27.8 3.8 %shard_map.86.refs_14_ = bf16[3,32,4096]{2,1,0:T(8,128)(2,1)S(1)} custom-call(f32[3,32,128]{2,1,0:T(8,128)S(1)} %get-tuple-element.59.smooth.refs_11_, s16[32,4096]{1,0:T(8,128)(2,1)S(1)} %get-tuple-element.40.picks.refs_2_, s16[16,4096]{1,0:T(8,128)(2,1)S(1)} %get-tuple-element.54.start, s16[32,4096]{1,0:T(8,128)(2,1)S(1)} %get-tuple-element.42.spot.refs_4_, ...), custom_call_target="tpu_custom_call" | custom-call | flops 3500000000 | bytes 3500000 | tf_op jit(solution)/shard_map/pallas_call | solution.py:74
  31.6 0.0 collective-permute-done.5.refs_7_.refs_5_
  31.6 0.0 collective-permute-done.6.refs_8_.refs_6_
  31.6 2.1 %shard_map.87 = (f32[3,32,128]{2,1,0:T(8,128)S(1)}, f32[3,32,128]{2,1,0:T(8,128)S(1)}, bf16[6,32,128]{2,1,0:T(8,128)(2,1)S(1)}, bf16[6,32,128]{2,1,0:T(8,128)(2,1)S(1)}, bf16[21,32,128]{2,1,0:T(8,128)(2,1)S(1)}) custom-call(s32[8,128]{1,0:T(8,128)S(1)} %broadcast_in_dim.3.refs_0_, s32[48,128]{1,0:T(8,128)S(1)} %get-tuple-element.39.most.refs_1_, ...), custom_call_target="tpu_custom_call" | custom-call | flops 2500000000 | bytes 2500000 | tf_op jit(solution)/shard_map/pallas_call | solution.py:74
  33.7 2.3 %collective-permute-start.10 = (bf16[21,32,128]{2,1,0:T(8,128)(2,1)S(1)}, bf16[21,32,128]{2,1,0:T(8,128)(2,1)S(1)}, u32[]{:S(2)}, u32[]{:S(2)}) collective-permute-start(bf16[21,32,128]{2,1,0:T(8,128)(2,1)S(1)} %get-tuple-element.64), channel_id=1, source_target_pairs={{0,28},{1,29},{2,30},{3,31},{4,0},{5,1},{6,2},{7,3},{8,4},{9,5},{1... | collective-permute-start | bytes 516104 | tf_op jit(solution)/shard_map/ppermute | solution.py:606
  36.0 0.0 collective-permute-start.9
  36.0 3.4 %collective-permute-start.7 = (bf16[6,32,128]{2,1,0:T(8,128)(2,1)S(1)}, bf16[6,32,128]{2,1,0:T(8,128)(2,1)S(1)}, u32[]{:S(2)}, u32[]{:S(2)}) collective-permute-start(bf16[6,32,128]{2,1,0:T(8,128)(2,1)S(1)} %get-tuple-element.61), channel_id=1, source_target_pairs={{1,2},{3,4},{5,6},{7,8},{9,10},{11,12},{13,14},{15,16},{17,18},{19... | collective-permute-start | bytes 147464 | tf_op jit(solution)/shard_map/ppermute | solution.py:613
  39.3 2.1 %collective-permute-start.8 = (bf16[6,32,128]{2,1,0:T(8,128)(2,1)S(1)}, bf16[6,32,128]{2,1,0:T(8,128)(2,1)S(1)}, u32[]{:S(2)}, u32[]{:S(2)}) collective-permute-start(bf16[6,32,128]{2,1,0:T(8,128)(2,1)S(1)} %get-tuple-element.62), channel_id=1, source_target_pairs={{0,1},{2,3},{4,5},{6,7},{8,9},{10,11},{12,13},{14,15},{16,17},{18,... | collective-permute-start | bytes 147464 | tf_op jit(solution)/shard_map/ppermute | solution.py:614
  41.4 3.8 %shard_map.88.refs_14_ = bf16[3,32,4096]{2,1,0:T(8,128)(2,1)S(1)} custom-call(f32[3,32,128]{2,1,0:T(8,128)S(1)} %get-tuple-element.63.smooth.refs_11_, s16[32,4096]{1,0:T(8,128)(2,1)S(1)} %get-tuple-element.40.picks.refs_2_, s16[16,4096]{1,0:T(8,128)(2,1)S(1)} %get-tuple-element.54.start, s16[32,4096]{1,0:T(8,128)(2,1)S(1)} %get-tuple-element.42.spot.refs_4_, ...), custom_call_target="tpu_custom_call" | custom-call | flops 3500000000 | bytes 3500000 | tf_op jit(solution)/shard_map/pallas_call | solution.py:74
  45.2 0.0 collective-permute-done.7.refs_7_
  45.2 0.0 collective-permute-done.8.refs_8_
  45.3 0.0 copy-start.3
  45.3 0.0 copy-start.4
  45.3 2.1 %shard_map.89.refs_12_ = f32[3,32,128]{2,1,0:T(8,128)S(1)} custom-call(s32[8,128]{1,0:T(8,128)S(1)} %broadcast_in_dim.3.refs_0_, s32[48,128]{1,0:T(8,128)S(1)} %get-tuple-element.39.most.refs_1_, s16[32,4096]{1,0:T(8,128)(2,1)S(1)} %get-tuple-element.40.picks.refs_2_, s16[16,4096]{1,0:T(8,128)(2,1)S(1)} %get-tuple-element.41.refs_3_, ...), custom_call_target="tpu_custom_call" | custom-call | flops 2500000000 | bytes 2500000 | tf_op jit(solution)/shard_map/pallas_call | solution.py:74
  47.4 1.9 %shard_map.90 = f32[3,4096]{1,0:T(4,128)} custom-call(s32[8,128]{1,0:T(8,128)S(1)} %broadcast_in_dim.3.refs_0_, f32[3,32,128]{2,1,0:T(8,128)S(1)} %get-tuple-element.56.refs_17_.refs_1_, f32[4,4096]{1,0:T(4,128)S(1)} %copy-done.3, bf16[7,32,128]{2,1,0:T(8,128)(2,1)S(1)} %collective-permute-done.1.refs_7_.refs_15_.refs_3_, ...), custom_call_target="tpu_custom_call" | custom-call | flops 2000000000 | bytes 2000000 | tf_op jit(solution)/shard_map/pallas_call | solution.py:74
  (15 shorter events, 0.1 us)
Async XLA Ops:
  0.0 4.6 %copy-start.1 = (s32[32,4096]{1,0:T(8,128)S(1)}, s32[32,4096]{1,0:T(8,128)}, u32[]{:S(2)}) copy-start(s32[32,4096]{1,0:T(8,128)} %col) | copy-start | bytes 1572868
  2.4 6.2 %copy-start.5 = (s32[1,2,512]{2,1,0:T(2,128)S(1)}, s32[1,2,512]{2,1,0:T(2,128)}, u32[]{:S(2)}) copy-start(s32[1,2,512]{2,1,0:T(2,128)} %param.11) | copy-start | bytes 12292
  2.4 4.8 %collective-permute-start = (f32[3,32,128]{2,1,0:T(8,128)S(1)}, f32[3,32,128]{2,1,0:T(8,128)S(1)}, u32[]{:S(2)}, u32[]{:S(2)}) collective-permute-start(f32[3,32,128]{2,1,0:T(8,128)S(1)} %get-tuple-element.47), channel_id=1, source_target_pairs={{0,32},{32,0},{64,96},{96,64},{128,160},{160,128},{192,224},{224,1... | collective-permute-start | bytes 147464 | tf_op jit(solution)/shard_map/ppermute | solution.py:660
  7.2 5.3 %collective-permute-start.3 = (f32[3,32,128]{2,1,0:T(8,128)S(1)}, f32[3,32,128]{2,1,0:T(8,128)S(1)}, u32[]{:S(2)}, u32[]{:S(2)}) collective-permute-start(f32[3,32,128]{2,1,0:T(8,128)S(1)} %add.6), channel_id=1, source_target_pairs={{0,64},{32,96},{64,0},{96,32},{128,192},{160,224},{192,128},{224,1... | collective-permute-start | bytes 147464 | tf_op jit(solution)/shard_map/ppermute | solution.py:660
  8.6 10.4 %collective-permute-start.2 = (bf16[7,32,128]{2,1,0:T(8,128)(2,1)S(1)}, bf16[7,32,128]{2,1,0:T(8,128)(2,1)S(1)}, u32[]{:S(2)}, u32[]{:S(2)}) collective-permute-start(bf16[7,32,128]{2,1,0:T(8,128)(2,1)S(1)} %get-tuple-element.48.refs_18_), channel_id=1, source_target_pairs={{0,1},{2,3},{4,5},{6,7},{8,9},{10,11},{12,13},{14,15},{16,17},{18,... | collective-permute-start | bytes 172040 | tf_op jit(solution)/shard_map/ppermute | solution.py:614
  10.1 9.0 %collective-permute-start.1 = (bf16[7,32,128]{2,1,0:T(8,128)(2,1)S(1)}, bf16[7,32,128]{2,1,0:T(8,128)(2,1)S(1)}, u32[]{:S(2)}, u32[]{:S(2)}) collective-permute-start(bf16[7,32,128]{2,1,0:T(8,128)(2,1)S(1)} %get-tuple-element.48.refs_18_), channel_id=1, source_target_pairs={{1,2},{3,4},{5,6},{7,8},{9,10},{11,12},{13,14},{15,16},{17,18},{19... | collective-permute-start | bytes 172040 | tf_op jit(solution)/shard_map/ppermute | solution.py:613
  12.5 6.5 %collective-permute-start.4 = (f32[3,32,128]{2,1,0:T(8,128)S(1)}, f32[3,32,128]{2,1,0:T(8,128)S(1)}, u32[]{:S(2)}, u32[]{:S(2)}) collective-permute-start(f32[3,32,128]{2,1,0:T(8,128)S(1)} %add.7.refs_15_), channel_id=1, source_target_pairs={{0,128},{32,160},{64,192},{96,224},{128,0},{160,32},{192,64},{224,... | collective-permute-start | bytes 147464 | tf_op jit(solution)/shard_map/ppermute | solution.py:660
  15.2 3.8 %copy-start = (bf16[32,3,3,4096]{3,0,2,1:T(8,128)(2,1)S(1)}, bf16[32,3,3,4096]{3,0,2,1:T(8,128)(2,1)}, u32[]{:S(2)}) copy-start(bf16[32,3,3,4096]{3,0,2,1:T(8,128)(2,1)} %param.9) | copy-start | bytes 7077892
  15.2 3.8 %copy-start.2 = (f32[3,3,4096]{2,1,0:T(4,128)S(1)}, f32[3,3,4096]{2,1,0:T(4,128)}, u32[]{:S(2)}) copy-start(f32[3,3,4096]{2,1,0:T(4,128)} %refs_17_.1) | copy-start | bytes 442372
  21.3 10.2 %collective-permute-start.5 = (bf16[10,32,128]{2,1,0:T(8,128)(2,1)S(1)}, bf16[10,32,128]{2,1,0:T(8,128)(2,1)S(1)}, u32[]{:S(2)}, u32[]{:S(2)}) collective-permute-start(bf16[10,32,128]{2,1,0:T(8,128)(2,1)S(1)} %get-tuple-element.57), channel_id=1, source_target_pairs={{1,2},{3,4},{5,6},{7,8},{9,10},{11,12},{13,14},{15,16},{17,18},{19... | collective-permute-start | bytes 245768 | tf_op jit(solution)/shard_map/ppermute | solution.py:613
  24.4 7.2 %collective-permute-start.6 = (bf16[10,32,128]{2,1,0:T(8,128)(2,1)S(1)}, bf16[10,32,128]{2,1,0:T(8,128)(2,1)S(1)}, u32[]{:S(2)}, u32[]{:S(2)}) collective-permute-start(bf16[10,32,128]{2,1,0:T(8,128)(2,1)S(1)} %get-tuple-element.58), channel_id=1, source_target_pairs={{0,1},{2,3},{4,5},{6,7},{8,9},{10,11},{12,13},{14,15},{16,17},{18,... | collective-permute-start | bytes 245768 | tf_op jit(solution)/shard_map/ppermute | solution.py:614
  33.7 11.5 %collective-permute-start.10 = (bf16[21,32,128]{2,1,0:T(8,128)(2,1)S(1)}, bf16[21,32,128]{2,1,0:T(8,128)(2,1)S(1)}, u32[]{:S(2)}, u32[]{:S(2)}) collective-permute-start(bf16[21,32,128]{2,1,0:T(8,128)(2,1)S(1)} %get-tuple-element.64), channel_id=1, source_target_pairs={{0,28},{1,29},{2,30},{3,31},{4,0},{5,1},{6,2},{7,3},{8,4},{9,5},{1... | collective-permute-start | bytes 516104 | tf_op jit(solution)/shard_map/ppermute | solution.py:606
  36.0 9.3 %collective-permute-start.9 = (bf16[21,32,128]{2,1,0:T(8,128)(2,1)S(1)}, bf16[21,32,128]{2,1,0:T(8,128)(2,1)S(1)}, u32[]{:S(2)}, u32[]{:S(2)}) collective-permute-start(bf16[21,32,128]{2,1,0:T(8,128)(2,1)S(1)} %get-tuple-element.64), channel_id=1, source_target_pairs={{0,4},{1,5},{2,6},{3,7},{4,8},{5,9},{6,10},{7,11},{8,12},{9,13},{1... | collective-permute-start | bytes 516104 | tf_op jit(solution)/shard_map/ppermute | solution.py:606
  36.0 9.3 %collective-permute-start.7 = (bf16[6,32,128]{2,1,0:T(8,128)(2,1)S(1)}, bf16[6,32,128]{2,1,0:T(8,128)(2,1)S(1)}, u32[]{:S(2)}, u32[]{:S(2)}) collective-permute-start(bf16[6,32,128]{2,1,0:T(8,128)(2,1)S(1)} %get-tuple-element.61), channel_id=1, source_target_pairs={{1,2},{3,4},{5,6},{7,8},{9,10},{11,12},{13,14},{15,16},{17,18},{19... | collective-permute-start | bytes 147464 | tf_op jit(solution)/shard_map/ppermute | solution.py:613
  39.3 5.9 %collective-permute-start.8 = (bf16[6,32,128]{2,1,0:T(8,128)(2,1)S(1)}, bf16[6,32,128]{2,1,0:T(8,128)(2,1)S(1)}, u32[]{:S(2)}, u32[]{:S(2)}) collective-permute-start(bf16[6,32,128]{2,1,0:T(8,128)(2,1)S(1)} %get-tuple-element.62), channel_id=1, source_target_pairs={{0,1},{2,3},{4,5},{6,7},{8,9},{10,11},{12,13},{14,15},{16,17},{18,... | collective-permute-start | bytes 147464 | tf_op jit(solution)/shard_map/ppermute | solution.py:614
  45.3 2.1 %copy-start.3 = (f32[4,4096]{1,0:T(4,128)S(1)}, f32[4,4096]{1,0:T(4,128)}, u32[]{:S(2)}) copy-start(f32[4,4096]{1,0:T(4,128)} %refs_2_.3) | copy-start | bytes 196612
  45.3 2.1 %copy-start.4 = (s32[4096]{0:T(1024)S(1)}, s32[4096]{0:T(1024)}, u32[]{:S(2)}) copy-start(s32[4096]{0:T(1024)} %param.13) | copy-start | bytes 49156

commit v7 on v6

--- a/solution.py
+++ b/solution.py
@@ -92,27 +92,28 @@
     return ref[lead + (slice(group * LANES, (group + 1) * LANES),)]
 
 
-def first_kernel(*refs):
-    sources = refs[:4]
-    dense_dinv, dense_residual, smooth, message, rhs = refs[4:9]
-    residual, aggregate, dinv, couple, semaphores = refs[9:]
+def restrict_kernel(*refs):
+    sources = refs[:2]
+    dense_residual, rhs = refs[2:4]
+    residual, aggregate, semaphores = refs[4:]
     copies = [
         pltpu.make_async_copy(source, target, semaphores.at[i])
-        for i, (source, target) in enumerate(zip(sources, (residual, aggregate, dinv, couple)))
+        for i, (source, target) in enumerate(zip(sources, (residual, aggregate)))
     ]
     for copy in copies:
         copy.start()
-    groups = smooth.shape[1]
     copies[0].wait()
-    for g in range(groups):
+    for g in range(dense_residual.shape[1]):
         for e in range(3):
             dense_residual[e, g : g + 1, :] = residual[
                 e : e + 1, g * LANES : (g + 1) * LANES
             ]
     copies[1].wait()
     restrict(dense_residual, aggregate, rhs)
-    copies[2].wait()
-    copies[3].wait()
+
+
+def first_kernel(dense_residual, dinv, couple, dense_dinv, smooth, message):
+    groups = smooth.shape[1]
     coarse_groups = message.shape[1]
     for g in range(groups):
         lanes = slice(g * LANES, (g + 1) * LANES)
@@ -347,8 +348,10 @@
 
 def halo_kernel(*refs, stage, scale_old, scale_new, unroll=8):
     (place, most, picks, halo_start, spot, rank, ghost, outer, inner) = refs[:9]
-    (residual, dinv, smooth, update, bonds, local_found) = refs[9:15]
-    refs = refs[15:]
+    (residual, dinv, smooth, update, bonds) = refs[9:14]
+    pieces = 2 if stage == SWEEPS - 1 else 1
+    local_found = refs[14 : 14 + pieces]
+    refs = refs[14 + pieces :]
     if stage == 0:
         rhs, arrived, coarse_dinv = refs[:3]
         new_smooth, new_update, base, out_outer, out_inner = refs[3:8]
@@ -426,25 +429,29 @@
             totals.append(total[:8] + total[8:])
         return totals
 
-    def some_tiles(t, carry):
-        for u in range(unroll):
-            tile = t * unroll + u
-            here = pl.ds(pl.multiple_of(tile * LANES, LANES), LANES)
-            chosen = halves_of(picks, here)
-            spots, ranks = halves_of(spot, here), halves_of(rank, here)
-            values = [
-                [local_found[e, h * PACK : (h + 1) * PACK, here] for e in range(3)]
-                for h in range(2)
-            ]
-            for v in range(HALO_LAYERS):
-                row = layer(halo_start[:, here] + jnp.int16(4 * v), chosen, even, odd)
-                put_back(row, jnp.int16(32 + v), spots, ranks, values)
-            totals = apply_tile(tile, values)
-            for c in range(3):
-                partial[c, pl.ds(pl.multiple_of(tile * 8, 8), 8), :] = totals[c]
-        return carry
-
-    lax.fori_loop(0, groups // unroll, some_tiles, 0)
+    for piece, part in enumerate(local_found):
+        first = piece * (groups // pieces)
+
+        def some_tiles(t, carry, part=part, first=first):
+            for u in range(unroll):
+                there = pl.ds(pl.multiple_of((t * unroll + u) * LANES, LANES), LANES)
+                tile = first + t * unroll + u
+                here = pl.ds(pl.multiple_of(tile * LANES, LANES), LANES)
+                chosen = halves_of(picks, here)
+                spots, ranks = halves_of(spot, here), halves_of(rank, here)
+                values = [
+                    [part[e, h * PACK : (h + 1) * PACK, there] for e in range(3)]
+                    for h in range(2)
+                ]
+                for v in range(HALO_LAYERS):
+                    row = layer(halo_start[:, here] + jnp.int16(4 * v), chosen, even, odd)
+                    put_back(row, jnp.int16(32 + v), spots, ranks, values)
+                totals = apply_tile(tile, values)
+                for c in range(3):
+                    partial[c, pl.ds(pl.multiple_of(tile * 8, 8), 8), :] = totals[c]
+            return carry
+
+        lax.fori_loop(0, groups // pieces // unroll, some_tiles, 0)
 
     last_layer = most[groups + 8, 0]
 
@@ -636,22 +643,23 @@
     def message(rows):
         return sds((rows, groups, LANES), BF16)
 
-    dinv, residual, smooth, packed, rhs = call(
-        first_kernel,
-        (sds((3, 3, groups, LANES), F32), field, field, message(7), coarse_field),
-        tuple(
-            pltpu.with_memory_space_constraint(x, pltpu.HBM)
-            for x in (fine_residual, agg, fine_dinv, coarse_couple)
-        ),
+    residual, rhs = call(
+        restrict_kernel,
+        (field, coarse_field),
+        tuple(pltpu.with_memory_space_constraint(x, pltpu.HBM) for x in (fine_residual, agg)),
         scratch=[
             VMEM(fine_residual.shape, F32),
             VMEM(agg.shape, jnp.int32),
-            VMEM(fine_dinv.shape, F32),
-            VMEM(coarse_couple.shape, F32),
-            pltpu.SemaphoreType.DMA((4,)),
+            pltpu.SemaphoreType.DMA((2,)),
         ],
-        us=2.2,
-        spaces={i: pltpu.HBM for i in range(4)},
+        us=1.6,
+        spaces={0: pltpu.HBM, 1: pltpu.HBM},
+    )
+    dinv, smooth, packed = call(
+        first_kernel,
+        (sds((3, 3, groups, LANES), F32), field, message(7)),
+        (residual, fine_dinv, coarse_couple),
+        us=0.8,
     )
     update = smooth
     own_packed = packed
@@ -659,6 +667,7 @@
     def exchanged(value, step):
         return lax.ppermute(value, "dom", [(i, i ^ step) for i in range(doms)])
 
+    assert doms == 8
     arrived = exchanged(rhs, 1)
     columns, rhs = lax.optimization_barrier((bond_col, rhs))
 
@@ -685,24 +694,30 @@
     arrived = exchanged(rhs, 2)
     first = arrived_sides = exchanged_by_pairs(packed, packed)
     rhs = rhs + arrived
-    arrived = exchanged(rhs, 4)
+    arrived = exchanged(rhs, 6)
     start, rhs = lax.optimization_barrier((start, rhs))
 
     factor = HALF / CENTER
     for stage in range(SWEEPS):
         factor_new = 1.0 / (2.0 * CENTER / HALF - factor)
-        found = call(
-            functools.partial(local_kernel, first=0, tiles=groups),
-            sds((3, bonds_of, points), BF16),
-            (smooth, picks, start, spot, rank, most),
-            us=3.5,
-        )
-        if stage == SWEEPS - 1:
-            found, far_after, far_before = lax.optimization_barrier(
-                (found, far_after, far_before)
+        pieces = 2 if stage == SWEEPS - 1 else 1
+        tiles = groups // pieces
+        found = []
+        for piece in range(pieces):
+            found.append(
+                call(
+                    functools.partial(local_kernel, first=piece * tiles, tiles=tiles),
+                    sds((3, bonds_of, tiles * LANES), BF16),
+                    (smooth, picks, start, spot, rank, most),
+                    us=3.7 if pieces == 1 else 0.2,
+                )
             )
+            if stage == SWEEPS - 1 and piece == 0:
+                far, start, found[0] = lax.optimization_barrier((far, start, found[0]))
+                far_after = shifted(far, 4)
+                far_before = shifted(far, -4)
         inputs = [place, most, picks, halo_start, spot, rank, ghost, *arrived_sides]
-        inputs += [residual, dinv, smooth, update, relaid, found]
+        inputs += [residual, dinv, smooth, update, relaid, *found]
         if stage == 0:
             inputs += [rhs, arrived, coarse_dinv]
             outs = (field, field, coarse_field, message(10), message(10))
@@ -730,8 +745,6 @@
         elif stage == 1:
             smooth, update, outer, inner, far = result
             third = arrived_sides = exchanged_by_pairs(outer, inner)
-            far_after = shifted(far, 4)
-            far_before = shifted(far, -4)
         else:
             (smooth,) = result
     return call(

time: 49.4 us -> 48.5 us (0.982)
  starting transfers between devices: 24.3 us -> 21.8 us
  waiting for transfers between devices: 0.03 us -> 1.66 us
    ppermute x3, starting transfers between devices: 8.87 us -> 4.54 us  [exchanged_by_pairs(): outer = lax.ppermute(outer, 'sub', across + [(j, i) for i, j in across])]
    ppermute x3, starting transfers between devices: 6.98 us -> 10 us  [exchanged_by_pairs(): inner = lax.ppermute(inner, 'sub', within + [(j, i) for i, j in within])]
    ppermute x2, waiting for transfers between devices: 0.01 us -> 1.64 us  [shifted(): lax.ppermute(value, 'sub', [(i, (i + steps) % count) for i in range(count)])]
    ppermute x3, starting transfers between devices: 6.22 us -> 5.5 us  [exchanged(): return lax.ppermute(value, 'dom', [(i, i ^ step) for i in range(doms)])]
    ppermute x2, starting transfers between devices: 2.26 us -> 1.72 us  [shifted(): lax.ppermute(value, 'sub', [(i, (i + steps) % count) for i in range(count)])]
    pallas_call x9 -> x11, Pallas kernels: 24.7 us -> 24.7 us  [call(): pl.pallas_call(kernel, out_shape=out, in_specs=[pl.BlockSpec(memory_space...]
  transfers between devices with their start and end apart: 11 -> 11, of which waited for: 0 -> 2; matrix products, arithmetic and copies ran while one was open for 0% -> 0% of each run, Pallas kernels for 28% -> 34%
where the time goes in v7:
time: 48.5 us; the launch traced here: 48.4 us
  Pallas kernels  24.7 us (51%)
  starting transfers between devices  21.8 us (45%)
  waiting for transfers between devices  1.66 us (3%)
    pallas_call x11, Pallas kernels, call(): pl.pallas_call(kernel, out_shape=out, in_specs=[pl.BlockSpec(memory_space...  24.7 us
    ppermute x3, starting transfers between devices, exchanged_by_pairs(): inner = lax.ppermute(inner, 'sub', within + [(j, i) for i, j in within])  10 us
    ppermute x3, starting transfers between devices, exchanged(): return lax.ppermute(value, 'dom', [(i, i ^ step) for i in range(doms)])  5.5 us
    ppermute x3, starting transfers between devices, exchanged_by_pairs(): outer = lax.ppermute(outer, 'sub', across + [(j, i) for i, j in across])  4.54 us
    ppermute x2, starting transfers between devices, shifted(): lax.ppermute(value, 'sub', [(i, (i + steps) % count) for i in range(count)])  1.72 us
    ppermute x2, waiting for transfers between devices, shifted(): lax.ppermute(value, 'sub', [(i, (i + steps) % count) for i in range(count)])  1.64 us
  transfers between devices with their start and end apart: 11, of which 2 were waited for; matrix products, arithmetic and copies ran while one was open for 0% of the time, Pallas kernels for 34%

profile of v7, /device:TPU:1, one launch (start us, length us, event | category | flops | bytes accessed | tf_op | source)
XLA Modules:
  0.0 48.4 jit_solution(2846560611601999292)
XLA Ops:
  0.0 2.2 %shard_map.82 = (f32[3,32,128]{2,1,0:T(8,128)S(1)}, f32[3,32,128]{2,1,0:T(8,128)S(1)}) custom-call(f32[3,4096]{1,0:T(4,128)} %refs_0_.1, s32[32,128]{1,0:T(8,128)} %bitcast.5), custom_call_target="tpu_custom_call" | custom-call | flops 1600000000 | bytes 1600000 | tf_op jit(solution)/shard_map/pallas_call | solution.py:74
  2.2 0.0 copy-start.2
  2.2 0.0 copy-start.4
  2.2 2.1 %collective-permute-start = (f32[3,32,128]{2,1,0:T(8,128)S(1)}, f32[3,32,128]{2,1,0:T(8,128)S(1)}, u32[]{:S(2)}, u32[]{:S(2)}) collective-permute-start(f32[3,32,128]{2,1,0:T(8,128)S(1)} %get-tuple-element.48), channel_id=1, source_target_pairs={{0,32},{32,0},{64,96},{96,64},{128,160},{160,128},{192,224},{224,1... | collective-permute-start | bytes 147464 | tf_op jit(solution)/shard_map/ppermute | solution.py:668
  4.3 2.6 %shard_map.83 = (s16[32,4096]{1,0:T(8,128)(2,1)S(1)}, s16[16,4096]{1,0:T(8,128)(2,1)S(1)}, s16[16,4096]{1,0:T(8,128)(2,1)S(1)}, s16[32,4096]{1,0:T(8,128)(2,1)S(...) custom-call(s32[32,4096]{1,0:T(8,128)S(1)} %copy-done.1), custom_call_target="tpu_custom_call" | custom-call | flops 2500000000 | bytes 2500000 | tf_op jit(solution)/shard_map/pallas_call | solution.py:74
  7.0 0.2 shard_map.84
  7.2 1.4 %collective-permute-start.3 = (f32[3,32,128]{2,1,0:T(8,128)S(1)}, f32[3,32,128]{2,1,0:T(8,128)S(1)}, u32[]{:S(2)}, u32[]{:S(2)}) collective-permute-start(f32[3,32,128]{2,1,0:T(8,128)S(1)} %add.6), channel_id=1, source_target_pairs={{0,64},{32,96},{64,0},{96,32},{128,192},{160,224},{192,128},{224,1... | collective-permute-start | bytes 147464 | tf_op jit(solution)/shard_map/ppermute | solution.py:668
  8.6 3.6 %collective-permute-start.1 = (bf16[7,32,128]{2,1,0:T(8,128)(2,1)S(1)}, bf16[7,32,128]{2,1,0:T(8,128)(2,1)S(1)}, u32[]{:S(2)}, u32[]{:S(2)}) collective-permute-start(bf16[7,32,128]{2,1,0:T(8,128)(2,1)S(1)} %get-tuple-element.49.refs_18_), channel_id=1, source_target_pairs={{1,2},{3,4},{5,6},{7,8},{9,10},{11,12},{13,14},{15,16},{17,18},{19... | collective-permute-start | bytes 172040 | tf_op jit(solution)/shard_map/ppermute | solution.py:620
  12.2 4.6 %collective-permute-start.2 = (bf16[7,32,128]{2,1,0:T(8,128)(2,1)S(1)}, bf16[7,32,128]{2,1,0:T(8,128)(2,1)S(1)}, u32[]{:S(2)}, u32[]{:S(2)}) collective-permute-start(bf16[7,32,128]{2,1,0:T(8,128)(2,1)S(1)} %get-tuple-element.49.refs_18_), channel_id=1, source_target_pairs={{0,1},{2,3},{4,5},{6,7},{8,9},{10,11},{12,13},{14,15},{16,17},{18,... | collective-permute-start | bytes 172040 | tf_op jit(solution)/shard_map/ppermute | solution.py:621
  16.8 0.0 collective-permute-done.3
  16.8 2.0 %collective-permute-start.4 = (f32[3,32,128]{2,1,0:T(8,128)S(1)}, f32[3,32,128]{2,1,0:T(8,128)S(1)}, u32[]{:S(2)}, u32[]{:S(2)}) collective-permute-start(f32[3,32,128]{2,1,0:T(8,128)S(1)} %add.7.refs_15_), channel_id=1, source_target_pairs={{0,192},{32,224},{64,128},{96,160},{128,64},{160,96},{192,0},{224,... | collective-permute-start | bytes 147464 | tf_op jit(solution)/shard_map/ppermute | solution.py:668
  18.8 3.8 %shard_map.85.refs_14_ = bf16[3,32,4096]{2,1,0:T(8,128)(2,1)S(1)} custom-call(f32[3,32,128]{2,1,0:T(8,128)S(1)} %get-tuple-element.51.smooth.refs_11_.refs_12_, s16[32,4096]{1,0:T(8,128)(2,1)S(1)} %get-tuple-element.40.picks.refs_2_, s16[16,4096]{1,0:T(8,128)(2,1)S(1)} %get-tuple-element.68.start, s16[32,4096]{1,0:T(8,128)(2,1)S(1)} %get-tuple-element.42.spot.refs_4_, ...), custom_call_target="tpu_custom_call" | custom-call | flops 3700000000 | bytes 3700000 | tf_op jit(solution)/shard_map/pallas_call | solution.py:74
  22.6 0.0 collective-permute-done.1.refs_7_.refs_15_.refs_3_
  22.6 0.0 collective-permute-done.2.refs_8_.refs_16_.refs_4_
  22.6 2.2 %shard_map.86 = (f32[3,32,128]{2,1,0:T(8,128)S(1)}, f32[3,32,128]{2,1,0:T(8,128)S(1)}, f32[3,32,128]{2,1,0:T(8,128)S(1)}, bf16[10,32,128]{2,1,0:T(8,128)(2,1)S(1)}, bf16[10,32,128]{2,1,0:T(8,128)(2,1)S(1)}) custom-call(s32[8,128]{1,0:T(8,128)S(1)} %broadcast_in_dim.3.refs_0_, s32[48,128]{1,0:T(8,128)S(1)} %get-tuple-element.39.most.refs_1_, ...), custom_call_target="tpu_custom_call" | custom-call | flops 2500000000 | bytes 2500000 | tf_op jit(solution)/shard_map/pallas_call | solution.py:74
  24.8 0.1 collective-permute-start.5
  24.9 2.4 %collective-permute-start.6 = (bf16[10,32,128]{2,1,0:T(8,128)(2,1)S(1)}, bf16[10,32,128]{2,1,0:T(8,128)(2,1)S(1)}, u32[]{:S(2)}, u32[]{:S(2)}) collective-permute-start(bf16[10,32,128]{2,1,0:T(8,128)(2,1)S(1)} %get-tuple-element.58), channel_id=1, source_target_pairs={{0,1},{2,3},{4,5},{6,7},{8,9},{10,11},{12,13},{14,15},{16,17},{18,... | collective-permute-start | bytes 245768 | tf_op jit(solution)/shard_map/ppermute | solution.py:621
  27.4 3.8 %shard_map.87.refs_14_ = bf16[3,32,4096]{2,1,0:T(8,128)(2,1)S(1)} custom-call(f32[3,32,128]{2,1,0:T(8,128)S(1)} %get-tuple-element.59.smooth.refs_11_, s16[32,4096]{1,0:T(8,128)(2,1)S(1)} %get-tuple-element.40.picks.refs_2_, s16[16,4096]{1,0:T(8,128)(2,1)S(1)} %get-tuple-element.68.start, s16[32,4096]{1,0:T(8,128)(2,1)S(1)} %get-tuple-element.42.spot.refs_4_, ...), custom_call_target="tpu_custom_call" | custom-call | flops 3700000000 | bytes 3700000 | tf_op jit(solution)/shard_map/pallas_call | solution.py:74
  31.2 0.0 collective-permute-done.6.refs_8_.refs_6_
  31.2 2.1 %shard_map.88 = (f32[3,32,128]{2,1,0:T(8,128)S(1)}, f32[3,32,128]{2,1,0:T(8,128)S(1)}, bf16[6,32,128]{2,1,0:T(8,128)(2,1)S(1)}, bf16[6,32,128]{2,1,0:T(8,128)(2,1)S(1)}, bf16[21,32,128]{2,1,0:T(8,128)(2,1)S(1)}) custom-call(s32[8,128]{1,0:T(8,128)S(1)} %broadcast_in_dim.3.refs_0_, s32[48,128]{1,0:T(8,128)S(1)} %get-tuple-element.39.most.refs_1_, ...), custom_call_target="tpu_custom_call" | custom-call | flops 2500000000 | bytes 2500000 | tf_op jit(solution)/shard_map/pallas_call | solution.py:74
  33.3 0.9 %collective-permute-start.7 = (bf16[6,32,128]{2,1,0:T(8,128)(2,1)S(1)}, bf16[6,32,128]{2,1,0:T(8,128)(2,1)S(1)}, u32[]{:S(2)}, u32[]{:S(2)}) collective-permute-start(bf16[6,32,128]{2,1,0:T(8,128)(2,1)S(1)} %get-tuple-element.61), channel_id=1, source_target_pairs={{1,2},{3,4},{5,6},{7,8},{9,10},{11,12},{13,14},{15,16},{17,18},{19... | collective-permute-start | bytes 147464 | tf_op jit(solution)/shard_map/ppermute | solution.py:620
  34.2 3.0 %collective-permute-start.8 = (bf16[6,32,128]{2,1,0:T(8,128)(2,1)S(1)}, bf16[6,32,128]{2,1,0:T(8,128)(2,1)S(1)}, u32[]{:S(2)}, u32[]{:S(2)}) collective-permute-start(bf16[6,32,128]{2,1,0:T(8,128)(2,1)S(1)} %get-tuple-element.62), channel_id=1, source_target_pairs={{0,1},{2,3},{4,5},{6,7},{8,9},{10,11},{12,13},{14,15},{16,17},{18,... | collective-permute-start | bytes 147464 | tf_op jit(solution)/shard_map/ppermute | solution.py:621
  37.2 1.9 %shard_map.89.refs_14_ = bf16[3,32,2048]{2,1,0:T(8,128)(2,1)S(1)} custom-call(f32[3,32,128]{2,1,0:T(8,128)S(1)} %get-tuple-element.64.smooth.refs_11_, s16[32,4096]{1,0:T(8,128)(2,1)S(1)} %get-tuple-element.40.picks.refs_2_, s16[16,4096]{1,0:T(8,128)(2,1)S(1)} %get-tuple-element.68.start, s16[32,4096]{1,0:T(8,128)(2,1)S(1)} %get-tuple-element.42.spot.refs_4_, ...), custom_call_target="tpu_custom_call" | custom-call | flops 200000000 | bytes 200000 | tf_op jit(solution)/shard_map/pallas_call | solution.py:74
  39.1 1.1 %collective-permute-start.10 = (bf16[21,32,128]{2,1,0:T(8,128)(2,1)S(1)}, bf16[21,32,128]{2,1,0:T(8,128)(2,1)S(1)}, u32[]{:S(2)}, u32[]{:S(2)}) collective-permute-start(bf16[21,32,128]{2,1,0:T(8,128)(2,1)S(1)} %get-tuple-element.65), channel_id=1, source_target_pairs={{0,28},{1,29},{2,30},{3,31},{4,0},{5,1},{6,2},{7,3},{8,4},{9,5},{1... | collective-permute-start | bytes 516104 | tf_op jit(solution)/shard_map/ppermute | solution.py:613
  40.2 0.6 %collective-permute-start.9 = (bf16[21,32,128]{2,1,0:T(8,128)(2,1)S(1)}, bf16[21,32,128]{2,1,0:T(8,128)(2,1)S(1)}, u32[]{:S(2)}, u32[]{:S(2)}) collective-permute-start(bf16[21,32,128]{2,1,0:T(8,128)(2,1)S(1)} %get-tuple-element.65), channel_id=1, source_target_pairs={{0,4},{1,5},{2,6},{3,7},{4,8},{5,9},{6,10},{7,11},{8,12},{9,13},{1... | collective-permute-start | bytes 516104 | tf_op jit(solution)/shard_map/ppermute | solution.py:613
  40.8 1.9 %shard_map.90.refs_15_ = bf16[3,32,2048]{2,1,0:T(8,128)(2,1)S(1)} custom-call(f32[3,32,128]{2,1,0:T(8,128)S(1)} %get-tuple-element.64.smooth.refs_11_, s16[32,4096]{1,0:T(8,128)(2,1)S(1)} %get-tuple-element.40.picks.refs_2_, s16[16,4096]{1,0:T(8,128)(2,1)S(1)} %get-tuple-element.68.start, s16[32,4096]{1,0:T(8,128)(2,1)S(1)} %get-tuple-element.42.spot.refs_4_, ...), custom_call_target="tpu_custom_call" | custom-call | flops 200000000 | bytes 200000 | tf_op jit(solution)/shard_map/pallas_call | solution.py:74
  42.8 0.0 collective-permute-done.8.refs_8_
  42.8 0.0 copy-start.5
  42.8 2.1 %shard_map.91.refs_12_ = f32[3,32,128]{2,1,0:T(8,128)S(1)} custom-call(s32[8,128]{1,0:T(8,128)S(1)} %broadcast_in_dim.3.refs_0_, s32[48,128]{1,0:T(8,128)S(1)} %get-tuple-element.39.most.refs_1_, s16[32,4096]{1,0:T(8,128)(2,1)S(1)} %get-tuple-element.40.picks.refs_2_, s16[16,4096]{1,0:T(8,128)(2,1)S(1)} %get-tuple-element.41.refs_3_, ...), custom_call_target="tpu_custom_call" | custom-call | flops 2500000000 | bytes 2500000 | tf_op jit(solution)/shard_map/pallas_call | solution.py:74
  44.9 0.5 %collective-permute-done.10.refs_10_ = bf16[21,32,128]{2,1,0:T(8,128)(2,1)S(1)} collective-permute-done((bf16[21,32,128]{2,1,0:T(8,128)(2,1)S(1)}, bf16[21,32,128]{2,1,0:T(8,128)(2,1)S(1)}, u32[]{:S(2)}, u32[]{:S(2)}) %collective-permute-start.10) | collective-permute-done | bytes 172064 | tf_op jit(solution)/shard_map/ppermute | solution.py:613
  45.4 1.1 %collective-permute-done.9.refs_9_ = bf16[21,32,128]{2,1,0:T(8,128)(2,1)S(1)} collective-permute-done((bf16[21,32,128]{2,1,0:T(8,128)(2,1)S(1)}, bf16[21,32,128]{2,1,0:T(8,128)(2,1)S(1)}, u32[]{:S(2)}, u32[]{:S(2)}) %collective-permute-start.9) | collective-permute-done | bytes 172064 | tf_op jit(solution)/shard_map/ppermute | solution.py:613
  46.5 1.9 %shard_map.92 = f32[3,4096]{1,0:T(4,128)} custom-call(s32[8,128]{1,0:T(8,128)S(1)} %broadcast_in_dim.3.refs_0_, f32[3,32,128]{2,1,0:T(8,128)S(1)} %get-tuple-element.56.refs_17_.refs_1_, f32[4,4096]{1,0:T(4,128)S(1)} %copy-done.4, bf16[7,32,128]{2,1,0:T(8,128)(2,1)S(1)} %collective-permute-done.1.refs_7_.refs_15_.refs_3_, ...), custom_call_target="tpu_custom_call" | custom-call | flops 2000000000 | bytes 2000000 | tf_op jit(solution)/shard_map/pallas_call | solution.py:74
  (19 shorter events, 0.1 us)
Async XLA Ops:
  0.0 4.3 %copy-start.1 = (s32[32,4096]{1,0:T(8,128)S(1)}, s32[32,4096]{1,0:T(8,128)}, u32[]{:S(2)}) copy-start(s32[32,4096]{1,0:T(8,128)} %col) | copy-start | bytes 1572868
  2.2 4.8 %copy-start.2 = (f32[3,3,4096]{2,1,0:T(4,128)S(1)}, f32[3,3,4096]{2,1,0:T(4,128)}, u32[]{:S(2)}) copy-start(f32[3,3,4096]{2,1,0:T(4,128)} %dinv.1) | copy-start | bytes 442372
  2.2 4.8 %copy-start.4 = (f32[4,4096]{1,0:T(4,128)S(1)}, f32[4,4096]{1,0:T(4,128)}, u32[]{:S(2)}) copy-start(f32[4,4096]{1,0:T(4,128)} %refs_2_.1) | copy-start | bytes 196612
  2.2 5.0 %collective-permute-start = (f32[3,32,128]{2,1,0:T(8,128)S(1)}, f32[3,32,128]{2,1,0:T(8,128)S(1)}, u32[]{:S(2)}, u32[]{:S(2)}) collective-permute-start(f32[3,32,128]{2,1,0:T(8,128)S(1)} %get-tuple-element.48), channel_id=1, source_target_pairs={{0,32},{32,0},{64,96},{96,64},{128,160},{160,128},{192,224},{224,1... | collective-permute-start | bytes 147464 | tf_op jit(solution)/shard_map/ppermute | solution.py:668
  7.0 1.7 %copy-start.6 = (s32[1,2,512]{2,1,0:T(2,128)S(1)}, s32[1,2,512]{2,1,0:T(2,128)}, u32[]{:S(2)}) copy-start(s32[1,2,512]{2,1,0:T(2,128)} %param.11) | copy-start | bytes 12292
  7.2 9.5 %collective-permute-start.3 = (f32[3,32,128]{2,1,0:T(8,128)S(1)}, f32[3,32,128]{2,1,0:T(8,128)S(1)}, u32[]{:S(2)}, u32[]{:S(2)}) collective-permute-start(f32[3,32,128]{2,1,0:T(8,128)S(1)} %add.6), channel_id=1, source_target_pairs={{0,64},{32,96},{64,0},{96,32},{128,192},{160,224},{192,128},{224,1... | collective-permute-start | bytes 147464 | tf_op jit(solution)/shard_map/ppermute | solution.py:668
  8.6 13.9 %collective-permute-start.1 = (bf16[7,32,128]{2,1,0:T(8,128)(2,1)S(1)}, bf16[7,32,128]{2,1,0:T(8,128)(2,1)S(1)}, u32[]{:S(2)}, u32[]{:S(2)}) collective-permute-start(bf16[7,32,128]{2,1,0:T(8,128)(2,1)S(1)} %get-tuple-element.49.refs_18_), channel_id=1, source_target_pairs={{1,2},{3,4},{5,6},{7,8},{9,10},{11,12},{13,14},{15,16},{17,18},{19... | collective-permute-start | bytes 172040 | tf_op jit(solution)/shard_map/ppermute | solution.py:620
  12.2 10.4 %collective-permute-start.2 = (bf16[7,32,128]{2,1,0:T(8,128)(2,1)S(1)}, bf16[7,32,128]{2,1,0:T(8,128)(2,1)S(1)}, u32[]{:S(2)}, u32[]{:S(2)}) collective-permute-start(bf16[7,32,128]{2,1,0:T(8,128)(2,1)S(1)} %get-tuple-element.49.refs_18_), channel_id=1, source_target_pairs={{0,1},{2,3},{4,5},{6,7},{8,9},{10,11},{12,13},{14,15},{16,17},{18,... | collective-permute-start | bytes 172040 | tf_op jit(solution)/shard_map/ppermute | solution.py:621
  16.8 5.8 %collective-permute-start.4 = (f32[3,32,128]{2,1,0:T(8,128)S(1)}, f32[3,32,128]{2,1,0:T(8,128)S(1)}, u32[]{:S(2)}, u32[]{:S(2)}) collective-permute-start(f32[3,32,128]{2,1,0:T(8,128)S(1)} %add.7.refs_15_), channel_id=1, source_target_pairs={{0,192},{32,224},{64,128},{96,160},{128,64},{160,96},{192,0},{224,... | collective-permute-start | bytes 147464 | tf_op jit(solution)/shard_map/ppermute | solution.py:668
  18.8 3.8 %copy-start = (bf16[32,3,3,4096]{3,0,2,1:T(8,128)(2,1)S(1)}, bf16[32,3,3,4096]{3,0,2,1:T(8,128)(2,1)}, u32[]{:S(2)}) copy-start(bf16[32,3,3,4096]{3,0,2,1:T(8,128)(2,1)} %param.9) | copy-start | bytes 7077892
  18.8 3.8 %copy-start.3 = (f32[3,3,4096]{2,1,0:T(4,128)S(1)}, f32[3,3,4096]{2,1,0:T(4,128)}, u32[]{:S(2)}) copy-start(f32[3,3,4096]{2,1,0:T(4,128)} %refs_17_.1) | copy-start | bytes 442372
  24.8 6.3 %collective-permute-start.5 = (bf16[10,32,128]{2,1,0:T(8,128)(2,1)S(1)}, bf16[10,32,128]{2,1,0:T(8,128)(2,1)S(1)}, u32[]{:S(2)}, u32[]{:S(2)}) collective-permute-start(bf16[10,32,128]{2,1,0:T(8,128)(2,1)S(1)} %get-tuple-element.57), channel_id=1, source_target_pairs={{1,2},{3,4},{5,6},{7,8},{9,10},{11,12},{13,14},{15,16},{17,18},{19... | collective-permute-start | bytes 245768 | tf_op jit(solution)/shard_map/ppermute | solution.py:620
  24.9 6.2 %collective-permute-start.6 = (bf16[10,32,128]{2,1,0:T(8,128)(2,1)S(1)}, bf16[10,32,128]{2,1,0:T(8,128)(2,1)S(1)}, u32[]{:S(2)}, u32[]{:S(2)}) collective-permute-start(bf16[10,32,128]{2,1,0:T(8,128)(2,1)S(1)} %get-tuple-element.58), channel_id=1, source_target_pairs={{0,1},{2,3},{4,5},{6,7},{8,9},{10,11},{12,13},{14,15},{16,17},{18,... | collective-permute-start | bytes 245768 | tf_op jit(solution)/shard_map/ppermute | solution.py:621
  33.3 9.4 %collective-permute-start.7 = (bf16[6,32,128]{2,1,0:T(8,128)(2,1)S(1)}, bf16[6,32,128]{2,1,0:T(8,128)(2,1)S(1)}, u32[]{:S(2)}, u32[]{:S(2)}) collective-permute-start(bf16[6,32,128]{2,1,0:T(8,128)(2,1)S(1)} %get-tuple-element.61), channel_id=1, source_target_pairs={{1,2},{3,4},{5,6},{7,8},{9,10},{11,12},{13,14},{15,16},{17,18},{19... | collective-permute-start | bytes 147464 | tf_op jit(solution)/shard_map/ppermute | solution.py:620
  34.2 8.6 %collective-permute-start.8 = (bf16[6,32,128]{2,1,0:T(8,128)(2,1)S(1)}, bf16[6,32,128]{2,1,0:T(8,128)(2,1)S(1)}, u32[]{:S(2)}, u32[]{:S(2)}) collective-permute-start(bf16[6,32,128]{2,1,0:T(8,128)(2,1)S(1)} %get-tuple-element.62), channel_id=1, source_target_pairs={{0,1},{2,3},{4,5},{6,7},{8,9},{10,11},{12,13},{14,15},{16,17},{18,... | collective-permute-start | bytes 147464 | tf_op jit(solution)/shard_map/ppermute | solution.py:621
  39.1 6.3 %collective-permute-start.10 = (bf16[21,32,128]{2,1,0:T(8,128)(2,1)S(1)}, bf16[21,32,128]{2,1,0:T(8,128)(2,1)S(1)}, u32[]{:S(2)}, u32[]{:S(2)}) collective-permute-start(bf16[21,32,128]{2,1,0:T(8,128)(2,1)S(1)} %get-tuple-element.65), channel_id=1, source_target_pairs={{0,28},{1,29},{2,30},{3,31},{4,0},{5,1},{6,2},{7,3},{8,4},{9,5},{1... | collective-permute-start | bytes 516104 | tf_op jit(solution)/shard_map/ppermute | solution.py:613
  40.2 6.3 %collective-permute-start.9 = (bf16[21,32,128]{2,1,0:T(8,128)(2,1)S(1)}, bf16[21,32,128]{2,1,0:T(8,128)(2,1)S(1)}, u32[]{:S(2)}, u32[]{:S(2)}) collective-permute-start(bf16[21,32,128]{2,1,0:T(8,128)(2,1)S(1)} %get-tuple-element.65), channel_id=1, source_target_pairs={{0,4},{1,5},{2,6},{3,7},{4,8},{5,9},{6,10},{7,11},{8,12},{9,13},{1... | collective-permute-start | bytes 516104 | tf_op jit(solution)/shard_map/ppermute | solution.py:613
  42.8 3.8 %copy-start.5 = (s32[4096]{0:T(1024)S(1)}, s32[4096]{0:T(1024)}, u32[]{:S(2)}) copy-start(s32[4096]{0:T(1024)} %param.13) | copy-start | bytes 49156

commit v8 on v7

--- a/solution.py
+++ b/solution.py
@@ -9,6 +9,7 @@
 
 SWEEPS = 3
 STEPS = 5
+FAR = 4
 LOW_EIG = 0.3
 HIGH_EIG = 2.2
 CENTER = (HIGH_EIG + LOW_EIG) / 2.0
@@ -139,40 +140,46 @@
     agg = aggregate[...] & (bins * LANES - 1)
     low = agg & (LANES - 1)
     high = agg >> 7
-    batch = 4
-    total = [jnp.zeros((2 * bins, LANES), F32) for c in range(3)]
-    lane_ids = lax.broadcasted_iota(jnp.int32, (LANES, LANES), 0)
-    bin_ids = lax.broadcasted_iota(jnp.int32, (bins, LANES), 0)
+    batch = 8
+    row16 = lax.broadcasted_iota(jnp.int32, (PACK, LANES), 0).astype(jnp.int16)
+    one, zero = jnp.ones((PACK, LANES), BF16), jnp.zeros((PACK, LANES), BF16)
+
+    def wide(row, kind):
+        return jnp.broadcast_to(row, (PACK, LANES)).astype(kind)
+
+    total = jnp.zeros((6 * bins, LANES), F32)
     for block in range(groups // batch):
-        onehot = []
-        spread = [[] for c in range(3)]
+        onehot, spread = [], []
         for g in range(block * batch, (block + 1) * batch):
-            same = jnp.broadcast_to(low[g : g + 1], (LANES, LANES)) == lane_ids
-            onehot.append(jnp.where(same, 1.0, 0.0).astype(BF16))
-            chosen = jnp.broadcast_to(high[g : g + 1], (bins, LANES)) == bin_ids
+            lane = wide(low[g : g + 1], jnp.int16)
+            line = wide(high[g : g + 1], jnp.int16)
+            onehot.append(
+                jnp.concatenate(
+                    [
+                        jnp.where(lane == row16 + jnp.int16(first), one, zero)
+                        for first in range(0, LANES, PACK)
+                    ],
+                    axis=0,
+                )
+            )
+            chosen = [line == row16 + jnp.int16(first) for first in range(0, bins, PACK)]
+            column = []
             for c in range(3):
                 value = residual[c, g : g + 1, :]
                 upper = value.astype(BF16).astype(F32)
-                lower = value - upper
-                spread[c].append(
-                    jnp.concatenate(
-                        [
-                            jnp.where(chosen, jnp.broadcast_to(part, (bins, LANES)), 0.0)
-                            for part in (upper, lower)
-                        ],
-                        axis=0,
-                    ).astype(BF16)
-                )
-        onehot = jnp.concatenate(onehot, axis=1)
-        for c in range(3):
-            total[c] = total[c] + lax.dot_general(
-                jnp.concatenate(spread[c], axis=1),
-                onehot,
-                (((1,), (1,)), ((), ())),
-                preferred_element_type=F32,
-            )
+                for part in (upper, value - upper):
+                    part = wide(part, BF16)
+                    column += [jnp.where(mask, part, zero) for mask in chosen]
+            spread.append(jnp.concatenate(column, axis=0))
+        total = total + lax.dot_general(
+            jnp.concatenate(spread, axis=1),
+            jnp.concatenate(onehot, axis=1),
+            (((1,), (1,)), ((), ())),
+            preferred_element_type=F32,
+        )
     for c in range(3):
-        out[c] = total[c][:bins] + total[c][bins:]
+        first = 2 * c * bins
+        out[c] = total[first : first + bins] + total[first + bins : first + 2 * bins]
 
 
 def spread_max(values):
@@ -346,7 +353,26 @@
     return solved
 
 
-def halo_kernel(*refs, stage, scale_old, scale_new, unroll=8):
+def sideways(x):
+    lines = x.shape[0]
+    lane = lax.broadcasted_iota(jnp.int32, x.shape, 1)
+    right = pltpu.roll(x, 1, 1)
+    right = jnp.where(lane == 0, pltpu.roll(right, 1, 0), right)
+    left = pltpu.roll(x, LANES - 1, 1)
+    left = jnp.where(lane == LANES - 1, pltpu.roll(left, lines - 1, 0), left)
+    return right, left
+
+
+def inside_masks(shape):
+    lane = lax.broadcasted_iota(jnp.int32, shape, 1)
+    line = lax.broadcasted_iota(jnp.int32, shape, 0)
+    return (
+        jnp.logical_or(lane > 0, line > 0),
+        jnp.logical_or(lane < LANES - 1, line < shape[0] - 1),
+    )
+
+
+def halo_kernel(*refs, stage, scale_old, scale_new, subs, unroll=8):
     (place, most, picks, halo_start, spot, rank, ghost, outer, inner) = refs[:9]
     (residual, dinv, smooth, update, bonds) = refs[9:14]
     pieces = 2 if stage == SWEEPS - 1 else 1
@@ -358,8 +384,8 @@
         refs = refs[8:]
     elif stage == 1:
         first_outer, first_inner, base, couple_own = refs[:4]
-        new_smooth, new_update, out_outer, out_inner, far = refs[4:9]
-        refs = refs[9:]
+        new_smooth, new_update, out_outer, out_inner, far_next, far_prev = refs[4:10]
+        refs = refs[10:]
     else:
         (new_smooth,) = refs[:1]
         refs = refs[1:]
@@ -384,12 +410,31 @@
     elif stage == 1:
         out_outer[3:6] = inner[3:6]
         out_inner[3:6] = outer[3:6]
-        far[0:3] = outer[3:6]
-        far[3:6] = base[...].astype(BF16)
-        far[6:9] = inner[3:6]
-        far[9:13] = couple_own[3:7]
-        far[13:17] = first_outer[3:7]
-        far[17:21] = first_inner[3:7]
+        me = jnp.concatenate([place[...]] * (base.shape[1] // 8), axis=0)
+        even = (me & 1) == 0
+        links = [couple_own[3 + k].astype(F32) for k in range(4)]
+        links[0] = jnp.where(me > 0, links[0], 0.0)
+        links[1] = jnp.where(me < subs - 1, links[1], 0.0)
+        for k, mask in zip((2, 3), inside_masks(me.shape)):
+            links[k] = jnp.where(mask, links[k], 0.0)
+        for c in range(3):
+            own = base[c]
+            outer_row, inner_row = outer[3 + c].astype(F32), inner[3 + c].astype(F32)
+            below = jnp.where(even, outer_row, inner_row)
+            above = jnp.where(even, inner_row, outer_row)
+            right, left = sideways(own)
+            iterate = own + (
+                links[0] * below + links[1] * above + links[2] * right + links[3] * left
+            )
+            for message, beyond in ((far_next, above), (far_prev, below)):
+                message[c] = own.astype(BF16)
+                message[3 + c] = iterate.astype(BF16)
+                message[6 + c] = beyond.astype(BF16)
+        for k in range(4):
+            outer_row = first_outer[3 + k].astype(F32)
+            inner_row = first_inner[3 + k].astype(F32)
+            far_next[9 + k] = jnp.where(even, inner_row, outer_row).astype(BF16)
+            far_prev[9 + k] = jnp.where(even, outer_row, inner_row).astype(BF16)
     wanted = ghost[...]
     half = wanted.shape[0] // 2
     low = wanted & (LANES - 1)
@@ -518,71 +563,51 @@
     def plain(ref, start):
         return lambda i: ref[start + i].astype(F32)
 
-    def either(ref, when_even, when_odd):
-        return lambda i: jnp.where(
-            even, ref[when_even + i].astype(F32), ref[when_odd + i].astype(F32)
-        )
-
     base_rows = {
-        -5: either(far_after, 0, 6),
-        -4: plain(far_after, 3),
-        -3: either(far_after, 6, 0),
+        -4: plain(far_after, 0),
+        -3: plain(far_after, 6),
         -2: from_after(third, 3),
         -1: from_after(second, 3),
         1: from_before(second, 3),
         2: from_before(third, 3),
-        3: either(far_before, 0, 6),
-        4: plain(far_before, 3),
-        5: either(far_before, 6, 0),
+        3: plain(far_before, 6),
+        4: plain(far_before, 0),
     }
     link_rows = {
-        -4: plain(far_after, 9),
-        -3: either(far_after, 17, 13),
+        -3: plain(far_after, 9),
         -2: from_after(second, 6),
         -1: from_after(first, 3),
         1: from_before(first, 3),
         2: from_before(second, 6),
-        3: either(far_before, 13, 17),
-        4: plain(far_before, 9),
+        3: plain(far_before, 9),
     }
-
-    def base_of(row, c):
-        if row == 0:
-            return base[c]
-        return base_rows[row](c) * valid(row)
-
-    for k in range(4):
-        for g in range(groups):
-            links[STEPS - 1, k, g : g + 1, :] = own_couple[
+    for g in range(groups):
+        for k in range(4):
+            links[FAR - 1, k, g : g + 1, :] = own_couple[
                 k : k + 1, g * LANES : (g + 1) * LANES
             ]
     for row, read in link_rows.items():
         for k in range(4):
-            links[row + STEPS - 1, k] = read(k) * valid(row)
-    lane = lax.broadcasted_iota(jnp.int32, (groups, LANES), 1)
-    line = lax.broadcasted_iota(jnp.int32, (groups, LANES), 0)
-    inner_first = jnp.logical_or(lane > 0, line > 0)
-    inner_last = jnp.logical_or(lane < LANES - 1, line < groups - 1)
-    for row in range(2 * STEPS - 1):
-        links[row, 2] = jnp.where(inner_first, links[row, 2], 0.0)
-        links[row, 3] = jnp.where(inner_last, links[row, 3], 0.0)
-    for row in range(-STEPS, STEPS + 1):
-        for c in range(3):
-            value = base_of(row, c)
-            kept[row + STEPS, c] = value
-            field[0, row + STEPS, c] = value
+            links[row + FAR - 1, k] = read(k) * valid(row)
+    for k, mask in zip((2, 3), inside_masks(me.shape)):
+        for row in range(2 * FAR - 1):
+            links[row, k] = jnp.where(mask, links[row, k], 0.0)
+    for c in range(3):
+        field[0, FAR, c] = base[c]
+        for row, read in base_rows.items():
+            field[0, row + FAR, c] = read(c) * valid(row)
+        field[1, 0, c] = far_after[3 + c].astype(F32) * valid(-FAR)
+        field[1, 2 * FAR, c] = far_before[3 + c].astype(F32) * valid(FAR)
+        for row in range(2 * FAR + 1):
+            kept[row, c] = field[0, row, c]
     for step in range(STEPS):
         old, new = step % 2, (step + 1) % 2
-        reach = STEPS - 1 - step
+        reach = min(STEPS - 1 - step, FAR - 1)
         for row in range(-reach, reach + 1):
-            spot = row + STEPS
-            weights = [links[row + STEPS - 1, k] for k in range(4)]
+            spot = row + FAR
+            weights = [links[spot - 1, k] for k in range(4)]
             for c in range(3):
-                x = field[old, spot, c]
-                right = pltpu.roll(x, 1, 1)
-                right = jnp.where(lane == 0, pltpu.roll(right, 1, 0), right)
-                left = pltpu.roll(x, LANES - 1, 1)
-                left = jnp.where(lane == LANES - 1, pltpu.roll(left, groups - 1, 0), left)
+                right, left = sideways(field[old, spot, c])
                 field[new, spot, c] = kept[spot, c] + (
                     weights[0] * field[old, spot - 1, c]
                     + weights[1] * field[old, spot + 1, c]
@@ -599,7 +624,7 @@
         for g in range(groups):
             chosen = high == g
             for c in range(3):
-                rows = jnp.broadcast_to(field[final, STEPS, c, g : g + 1, :], (8, LANES))
+                rows = jnp.broadcast_to(field[final, FAR, c, g : g + 1, :], (8, LANES))
                 found[c] = jnp.where(chosen, lane_gather(rows, low), found[c])
         for c in range(3):
             result = smooth[c, block * 8 : (block + 1) * 8, :] + found[c]
@@ -713,9 +738,11 @@
                 )
             )
             if stage == SWEEPS - 1 and piece == 0:
-                far, start, found[0] = lax.optimization_barrier((far, start, found[0]))
-                far_after = shifted(far, 4)
-                far_before = shifted(far, -4)
+                far_next, far_prev, start, found[0] = lax.optimization_barrier(
+                    (far_next, far_prev, start, found[0])
+                )
+                far_after = shifted(far_next, 4)
+                far_before = shifted(far_prev, -4)
         inputs = [place, most, picks, halo_start, spot, rank, ghost, *arrived_sides]
         inputs += [residual, dinv, smooth, update, relaid, *found]
         if stage == 0:
@@ -723,7 +750,7 @@
             outs = (field, field, coarse_field, message(10), message(10))
         elif stage == 1:
             inputs += [*first, base, own_packed]
-            outs = (field, field, message(6), message(6), message(21))
+            outs = (field, field, message(6), message(6), message(13), message(13))
         else:
             outs = (field,)
         result = call(
@@ -732,6 +759,7 @@
                 stage=stage,
                 scale_old=factor_new * factor,
                 scale_new=2.0 * factor_new / HALF,
+                subs=lax.axis_size("sub"),
             ),
             outs,
             inputs,
@@ -743,7 +771,7 @@
             smooth, update, base, outer, inner = result
             second = arrived_sides = exchanged_by_pairs(outer, inner)
         elif stage == 1:
-            smooth, update, outer, inner, far = result
+            smooth, update, outer, inner, far_next, far_prev = result
             third = arrived_sides = exchanged_by_pairs(outer, inner)
         else:
             (smooth,) = result
@@ -763,9 +791,9 @@
             smooth,
         ),
         scratch=[
-            VMEM((2, 2 * STEPS + 1, 3, coarse_groups, LANES), F32),
-            VMEM((2 * STEPS - 1, 4, coarse_groups, LANES), F32),
-            VMEM((2 * STEPS + 1, 3, coarse_groups, LANES), F32),
+            VMEM((2, 2 * FAR + 1, 3, coarse_groups, LANES), F32),
+            VMEM((2 * FAR - 1, 4, coarse_groups, LANES), F32),
+            VMEM((2 * FAR + 1, 3, coarse_groups, LANES), F32),
         ],
         us=2.0,
     )

time: 48.5 us -> 48.1 us (level)
  starting transfers between devices: 21.8 us -> 23.6 us
  waiting for transfers between devices: 1.66 us -> 0.03 us
  Pallas kernels: 24.7 us -> 24 us
    ppermute x2, waiting for transfers between devices: 1.64 us -> 0.01 us  [shifted(): lax.ppermute(value, 'sub', [(i, (i + steps) % count) for i in range(count)])]
    ppermute x3, starting transfers between devices: 4.54 us -> 6.08 us  [exchanged_by_pairs(): outer = lax.ppermute(outer, 'sub', across + [(j, i) for i, j in across])]
    ppermute x2, starting transfers between devices: 1.72 us -> 2.93 us  [shifted(): lax.ppermute(value, 'sub', [(i, (i + steps) % count) for i in range(count)])]
    ppermute x3, starting transfers between devices: 10 us -> 9.1 us  [exchanged_by_pairs(): inner = lax.ppermute(inner, 'sub', within + [(j, i) for i, j in within])]
    pallas_call x11, Pallas kernels: 24.7 us -> 24 us  [call(): pl.pallas_call(kernel, out_shape=out, in_specs=[pl.BlockSpec(memory_space...]
  transfers between devices with their start and end apart: 11 -> 11, of which waited for: 2 -> 0; matrix products, arithmetic and copies ran while one was open for 0% -> 0% of each run, Pallas kernels for 34% -> 34%
where the time goes in v8:
time: 48.1 us; the launch traced here: 48 us
  Pallas kernels  24 us (50%)
  starting transfers between devices  23.6 us (49%)
    pallas_call x11, Pallas kernels, call(): pl.pallas_call(kernel, out_shape=out, in_specs=[pl.BlockSpec(memory_space...  24 us
    ppermute x3, starting transfers between devices, exchanged_by_pairs(): inner = lax.ppermute(inner, 'sub', within + [(j, i) for i, j in within])  9.1 us
    ppermute x3, starting transfers between devices, exchanged_by_pairs(): outer = lax.ppermute(outer, 'sub', across + [(j, i) for i, j in across])  6.08 us
    ppermute x3, starting transfers between devices, exchanged(): return lax.ppermute(value, 'dom', [(i, i ^ step) for i in range(doms)])  5.51 us
    ppermute x2, starting transfers between devices, shifted(): lax.ppermute(value, 'sub', [(i, (i + steps) % count) for i in range(count)])  2.93 us
  transfers between devices with their start and end apart: 11, of which 0 were waited for; matrix products, arithmetic and copies ran while one was open for 0% of the time, Pallas kernels for 34%

profile of v8, /device:TPU:1, one launch (start us, length us, event | category | flops | bytes accessed | tf_op | source)
XLA Modules:
  0.0 48.0 jit_solution(15171893513468421483)
XLA Ops:
  0.0 1.5 %shard_map.82 = (f32[3,32,128]{2,1,0:T(8,128)S(1)}, f32[3,32,128]{2,1,0:T(8,128)S(1)}) custom-call(f32[3,4096]{1,0:T(4,128)} %refs_0_.1, s32[32,128]{1,0:T(8,128)} %bitcast.5), custom_call_target="tpu_custom_call" | custom-call | flops 1600000000 | bytes 1600000 | tf_op jit(solution)/shard_map/pallas_call | solution.py:75
  1.5 0.0 copy-start.2
  1.6 0.0 copy-start.4
  1.6 2.1 %collective-permute-start = (f32[3,32,128]{2,1,0:T(8,128)S(1)}, f32[3,32,128]{2,1,0:T(8,128)S(1)}, u32[]{:S(2)}, u32[]{:S(2)}) collective-permute-start(f32[3,32,128]{2,1,0:T(8,128)S(1)} %get-tuple-element.50), channel_id=1, source_target_pairs={{0,32},{32,0},{64,96},{96,64},{128,160},{160,128},{192,224},{224,1... | collective-permute-start | bytes 147464 | tf_op jit(solution)/shard_map/ppermute | solution.py:693
  3.7 2.6 %shard_map.83 = (s16[32,4096]{1,0:T(8,128)(2,1)S(1)}, s16[16,4096]{1,0:T(8,128)(2,1)S(1)}, s16[16,4096]{1,0:T(8,128)(2,1)S(1)}, s16[32,4096]{1,0:T(8,128)(2,1)S(...) custom-call(s32[32,4096]{1,0:T(8,128)S(1)} %copy-done.1), custom_call_target="tpu_custom_call" | custom-call | flops 2500000000 | bytes 2500000 | tf_op jit(solution)/shard_map/pallas_call | solution.py:75
  6.4 0.2 shard_map.84
  6.6 0.0 collective-permute-done
  6.6 1.4 %collective-permute-start.3 = (f32[3,32,128]{2,1,0:T(8,128)S(1)}, f32[3,32,128]{2,1,0:T(8,128)S(1)}, u32[]{:S(2)}, u32[]{:S(2)}) collective-permute-start(f32[3,32,128]{2,1,0:T(8,128)S(1)} %add.6), channel_id=1, source_target_pairs={{0,64},{32,96},{64,0},{96,32},{128,192},{160,224},{192,128},{224,1... | collective-permute-start | bytes 147464 | tf_op jit(solution)/shard_map/ppermute | solution.py:693
  8.0 1.3 %collective-permute-start.2 = (bf16[7,32,128]{2,1,0:T(8,128)(2,1)S(1)}, bf16[7,32,128]{2,1,0:T(8,128)(2,1)S(1)}, u32[]{:S(2)}, u32[]{:S(2)}) collective-permute-start(bf16[7,32,128]{2,1,0:T(8,128)(2,1)S(1)} %get-tuple-element.51.refs_18_), channel_id=1, source_target_pairs={{0,1},{2,3},{4,5},{6,7},{8,9},{10,11},{12,13},{14,15},{16,17},{18,... | collective-permute-start | bytes 172040 | tf_op jit(solution)/shard_map/ppermute | solution.py:646
  9.3 2.4 %collective-permute-start.1 = (bf16[7,32,128]{2,1,0:T(8,128)(2,1)S(1)}, bf16[7,32,128]{2,1,0:T(8,128)(2,1)S(1)}, u32[]{:S(2)}, u32[]{:S(2)}) collective-permute-start(bf16[7,32,128]{2,1,0:T(8,128)(2,1)S(1)} %get-tuple-element.51.refs_18_), channel_id=1, source_target_pairs={{1,2},{3,4},{5,6},{7,8},{9,10},{11,12},{13,14},{15,16},{17,18},{19... | collective-permute-start | bytes 172040 | tf_op jit(solution)/shard_map/ppermute | solution.py:645
  11.7 0.0 collective-permute-done.3
  11.7 2.0 %collective-permute-start.4 = (f32[3,32,128]{2,1,0:T(8,128)S(1)}, f32[3,32,128]{2,1,0:T(8,128)S(1)}, u32[]{:S(2)}, u32[]{:S(2)}) collective-permute-start(f32[3,32,128]{2,1,0:T(8,128)S(1)} %add.7.refs_15_), channel_id=1, source_target_pairs={{0,192},{32,224},{64,128},{96,160},{128,64},{160,96},{192,0},{224,... | collective-permute-start | bytes 147464 | tf_op jit(solution)/shard_map/ppermute | solution.py:693
  13.7 3.8 %shard_map.85.refs_14_ = bf16[3,32,4096]{2,1,0:T(8,128)(2,1)S(1)} custom-call(f32[3,32,128]{2,1,0:T(8,128)S(1)} %get-tuple-element.53.smooth.refs_11_.refs_12_, s16[32,4096]{1,0:T(8,128)(2,1)S(1)} %get-tuple-element.42.picks.refs_2_, s16[16,4096]{1,0:T(8,128)(2,1)S(1)} %get-tuple-element.72.start, s16[32,4096]{1,0:T(8,128)(2,1)S(1)} %get-tuple-element.44.spot.refs_4_, ...), custom_call_target="tpu_custom_call" | custom-call | flops 3700000000 | bytes 3700000 | tf_op jit(solution)/shard_map/pallas_call | solution.py:75
  17.5 0.0 collective-permute-done.2.refs_8_.refs_16_.refs_4_
  17.5 0.0 collective-permute-done.1.refs_7_.refs_15_.refs_3_
  17.5 2.2 %shard_map.86 = (f32[3,32,128]{2,1,0:T(8,128)S(1)}, f32[3,32,128]{2,1,0:T(8,128)S(1)}, f32[3,32,128]{2,1,0:T(8,128)S(1)}, bf16[10,32,128]{2,1,0:T(8,128)(2,1)S(1)}, bf16[10,32,128]{2,1,0:T(8,128)(2,1)S(1)}) custom-call(s32[8,128]{1,0:T(8,128)S(1)} %broadcast_in_dim.3.refs_0_, s32[48,128]{1,0:T(8,128)S(1)} %get-tuple-element.41.most.refs_1_, ...), custom_call_target="tpu_custom_call" | custom-call | flops 2500000000 | bytes 2500000 | tf_op jit(solution)/shard_map/pallas_call | solution.py:75
  19.8 3.6 %collective-permute-start.5 = (bf16[10,32,128]{2,1,0:T(8,128)(2,1)S(1)}, bf16[10,32,128]{2,1,0:T(8,128)(2,1)S(1)}, u32[]{:S(2)}, u32[]{:S(2)}) collective-permute-start(bf16[10,32,128]{2,1,0:T(8,128)(2,1)S(1)} %get-tuple-element.59), channel_id=1, source_target_pairs={{1,2},{3,4},{5,6},{7,8},{9,10},{11,12},{13,14},{15,16},{17,18},{19... | collective-permute-start | bytes 245768 | tf_op jit(solution)/shard_map/ppermute | solution.py:645
  23.4 3.6 %collective-permute-start.6 = (bf16[10,32,128]{2,1,0:T(8,128)(2,1)S(1)}, bf16[10,32,128]{2,1,0:T(8,128)(2,1)S(1)}, u32[]{:S(2)}, u32[]{:S(2)}) collective-permute-start(bf16[10,32,128]{2,1,0:T(8,128)(2,1)S(1)} %get-tuple-element.60), channel_id=1, source_target_pairs={{0,1},{2,3},{4,5},{6,7},{8,9},{10,11},{12,13},{14,15},{16,17},{18,... | collective-permute-start | bytes 245768 | tf_op jit(solution)/shard_map/ppermute | solution.py:646
  26.9 3.8 %shard_map.87.refs_14_ = bf16[3,32,4096]{2,1,0:T(8,128)(2,1)S(1)} custom-call(f32[3,32,128]{2,1,0:T(8,128)S(1)} %get-tuple-element.61.smooth.refs_11_, s16[32,4096]{1,0:T(8,128)(2,1)S(1)} %get-tuple-element.42.picks.refs_2_, s16[16,4096]{1,0:T(8,128)(2,1)S(1)} %get-tuple-element.72.start, s16[32,4096]{1,0:T(8,128)(2,1)S(1)} %get-tuple-element.44.spot.refs_4_, ...), custom_call_target="tpu_custom_call" | custom-call | flops 3700000000 | bytes 3700000 | tf_op jit(solution)/shard_map/pallas_call | solution.py:75
  30.7 0.0 collective-permute-done.5.refs_7_.refs_5_
  30.7 0.0 collective-permute-done.6.refs_8_.refs_6_
  30.7 2.1 %shard_map.88 = (f32[3,32,128]{2,1,0:T(8,128)S(1)}, f32[3,32,128]{2,1,0:T(8,128)S(1)}, bf16[6,32,128]{2,1,0:T(8,128)(2,1)S(1)}, bf16[6,32,128]{2,1,0:T(8,128)(2,...) custom-call(s32[8,128]{1,0:T(8,128)S(1)} %broadcast_in_dim.3.refs_0_, ...), custom_call_target="tpu_custom_call" | custom-call | flops 2500000000 | bytes 2500000 | tf_op jit(solution)/shard_map/pallas_call | solution.py:75
  32.9 0.1 collective-permute-start.7
  33.0 4.2 %collective-permute-start.8 = (bf16[6,32,128]{2,1,0:T(8,128)(2,1)S(1)}, bf16[6,32,128]{2,1,0:T(8,128)(2,1)S(1)}, u32[]{:S(2)}, u32[]{:S(2)}) collective-permute-start(bf16[6,32,128]{2,1,0:T(8,128)(2,1)S(1)} %get-tuple-element.64), channel_id=1, source_target_pairs={{0,1},{2,3},{4,5},{6,7},{8,9},{10,11},{12,13},{14,15},{16,17},{18,... | collective-permute-start | bytes 147464 | tf_op jit(solution)/shard_map/ppermute | solution.py:646
  37.2 1.9 %shard_map.89.refs_14_ = bf16[3,32,2048]{2,1,0:T(8,128)(2,1)S(1)} custom-call(f32[3,32,128]{2,1,0:T(8,128)S(1)} %get-tuple-element.67.smooth.refs_11_, s16[32,4096]{1,0:T(8,128)(2,1)S(1)} %get-tuple-element.42.picks.refs_2_, s16[16,4096]{1,0:T(8,128)(2,1)S(1)} %get-tuple-element.72.start, s16[32,4096]{1,0:T(8,128)(2,1)S(1)} %get-tuple-element.44.spot.refs_4_, ...), custom_call_target="tpu_custom_call" | custom-call | flops 200000000 | bytes 200000 | tf_op jit(solution)/shard_map/pallas_call | solution.py:75
  39.1 0.3 collective-permute-start.9
  39.4 2.7 %collective-permute-start.10 = (bf16[13,32,128]{2,1,0:T(8,128)(2,1)S(1)}, bf16[13,32,128]{2,1,0:T(8,128)(2,1)S(1)}, u32[]{:S(2)}, u32[]{:S(2)}) collective-permute-start(bf16[13,32,128]{2,1,0:T(8,128)(2,1)S(1)} %get-tuple-element.69), channel_id=1, source_target_pairs={{0,28},{1,29},{2,30},{3,31},{4,0},{5,1},{6,2},{7,3},{8,4},{9,5},{1... | collective-permute-start | bytes 319496 | tf_op jit(solution)/shard_map/ppermute | solution.py:638
  42.1 1.9 %shard_map.90.refs_15_ = bf16[3,32,2048]{2,1,0:T(8,128)(2,1)S(1)} custom-call(f32[3,32,128]{2,1,0:T(8,128)S(1)} %get-tuple-element.67.smooth.refs_11_, s16[32,4096]{1,0:T(8,128)(2,1)S(1)} %get-tuple-element.42.picks.refs_2_, s16[16,4096]{1,0:T(8,128)(2,1)S(1)} %get-tuple-element.72.start, s16[32,4096]{1,0:T(8,128)(2,1)S(1)} %get-tuple-element.44.spot.refs_4_, ...), custom_call_target="tpu_custom_call" | custom-call | flops 200000000 | bytes 200000 | tf_op jit(solution)/shard_map/pallas_call | solution.py:75
  44.0 0.0 copy-start.5
  44.0 2.1 %shard_map.91.refs_12_ = f32[3,32,128]{2,1,0:T(8,128)S(1)} custom-call(s32[8,128]{1,0:T(8,128)S(1)} %broadcast_in_dim.3.refs_0_, s32[48,128]{1,0:T(8,128)S(1)} %get-tuple-element.41.most.refs_1_, s16[32,4096]{1,0:T(8,128)(2,1)S(1)} %get-tuple-element.42.picks.refs_2_, s16[16,4096]{1,0:T(8,128)(2,1)S(1)} %get-tuple-element.43.refs_3_, ...), custom_call_target="tpu_custom_call" | custom-call | flops 2500000000 | bytes 2500000 | tf_op jit(solution)/shard_map/pallas_call | solution.py:75
  46.1 0.0 collective-permute-done.9.refs_9_
  46.1 1.9 %shard_map.92 = f32[3,4096]{1,0:T(4,128)} custom-call(s32[8,128]{1,0:T(8,128)S(1)} %broadcast_in_dim.3.refs_0_, f32[3,32,128]{2,1,0:T(8,128)S(1)} %get-tuple-element.58.refs_17_.refs_1_, f32[4,4096]{1,0:T(4,128)S(1)} %copy-done.4, bf16[7,32,128]{2,1,0:T(8,128)(2,1)S(1)} %collective-permute-done.1.refs_7_.refs_15_.refs_3_, ...), custom_call_target="tpu_custom_call" | custom-call | flops 2000000000 | bytes 2000000 | tf_op jit(solution)/shard_map/pallas_call | solution.py:75
  (19 shorter events, 0.1 us)
Async XLA Ops:
  0.0 3.7 %copy-start.1 = (s32[32,4096]{1,0:T(8,128)S(1)}, s32[32,4096]{1,0:T(8,128)}, u32[]{:S(2)}) copy-start(s32[32,4096]{1,0:T(8,128)} %col) | copy-start | bytes 1572868
  1.5 4.8 %copy-start.2 = (f32[3,3,4096]{2,1,0:T(4,128)S(1)}, f32[3,3,4096]{2,1,0:T(4,128)}, u32[]{:S(2)}) copy-start(f32[3,3,4096]{2,1,0:T(4,128)} %dinv.1) | copy-start | bytes 442372
  1.6 4.8 %copy-start.4 = (f32[4,4096]{1,0:T(4,128)S(1)}, f32[4,4096]{1,0:T(4,128)}, u32[]{:S(2)}) copy-start(f32[4,4096]{1,0:T(4,128)} %refs_2_.1) | copy-start | bytes 196612
  1.6 5.0 %collective-permute-start = (f32[3,32,128]{2,1,0:T(8,128)S(1)}, f32[3,32,128]{2,1,0:T(8,128)S(1)}, u32[]{:S(2)}, u32[]{:S(2)}) collective-permute-start(f32[3,32,128]{2,1,0:T(8,128)S(1)} %get-tuple-element.50), channel_id=1, source_target_pairs={{0,32},{32,0},{64,96},{96,64},{128,160},{160,128},{192,224},{224,1... | collective-permute-start | bytes 147464 | tf_op jit(solution)/shard_map/ppermute | solution.py:693
  6.3 1.7 %copy-start.6 = (s32[1,2,512]{2,1,0:T(2,128)S(1)}, s32[1,2,512]{2,1,0:T(2,128)}, u32[]{:S(2)}) copy-start(s32[1,2,512]{2,1,0:T(2,128)} %param.11) | copy-start | bytes 12292
  6.6 5.1 %collective-permute-start.3 = (f32[3,32,128]{2,1,0:T(8,128)S(1)}, f32[3,32,128]{2,1,0:T(8,128)S(1)}, u32[]{:S(2)}, u32[]{:S(2)}) collective-permute-start(f32[3,32,128]{2,1,0:T(8,128)S(1)} %add.6), channel_id=1, source_target_pairs={{0,64},{32,96},{64,0},{96,32},{128,192},{160,224},{192,128},{224,1... | collective-permute-start | bytes 147464 | tf_op jit(solution)/shard_map/ppermute | solution.py:693
  8.0 9.4 %collective-permute-start.2 = (bf16[7,32,128]{2,1,0:T(8,128)(2,1)S(1)}, bf16[7,32,128]{2,1,0:T(8,128)(2,1)S(1)}, u32[]{:S(2)}, u32[]{:S(2)}) collective-permute-start(bf16[7,32,128]{2,1,0:T(8,128)(2,1)S(1)} %get-tuple-element.51.refs_18_), channel_id=1, source_target_pairs={{0,1},{2,3},{4,5},{6,7},{8,9},{10,11},{12,13},{14,15},{16,17},{18,... | collective-permute-start | bytes 172040 | tf_op jit(solution)/shard_map/ppermute | solution.py:646
  9.3 8.2 %collective-permute-start.1 = (bf16[7,32,128]{2,1,0:T(8,128)(2,1)S(1)}, bf16[7,32,128]{2,1,0:T(8,128)(2,1)S(1)}, u32[]{:S(2)}, u32[]{:S(2)}) collective-permute-start(bf16[7,32,128]{2,1,0:T(8,128)(2,1)S(1)} %get-tuple-element.51.refs_18_), channel_id=1, source_target_pairs={{1,2},{3,4},{5,6},{7,8},{9,10},{11,12},{13,14},{15,16},{17,18},{19... | collective-permute-start | bytes 172040 | tf_op jit(solution)/shard_map/ppermute | solution.py:645
  11.7 5.8 %collective-permute-start.4 = (f32[3,32,128]{2,1,0:T(8,128)S(1)}, f32[3,32,128]{2,1,0:T(8,128)S(1)}, u32[]{:S(2)}, u32[]{:S(2)}) collective-permute-start(f32[3,32,128]{2,1,0:T(8,128)S(1)} %add.7.refs_15_), channel_id=1, source_target_pairs={{0,192},{32,224},{64,128},{96,160},{128,64},{160,96},{192,0},{224,... | collective-permute-start | bytes 147464 | tf_op jit(solution)/shard_map/ppermute | solution.py:693
  13.7 3.8 %copy-start = (bf16[32,3,3,4096]{3,0,2,1:T(8,128)(2,1)S(1)}, bf16[32,3,3,4096]{3,0,2,1:T(8,128)(2,1)}, u32[]{:S(2)}) copy-start(bf16[32,3,3,4096]{3,0,2,1:T(8,128)(2,1)} %param.9) | copy-start | bytes 7077892
  13.7 3.8 %copy-start.3 = (f32[3,3,4096]{2,1,0:T(4,128)S(1)}, f32[3,3,4096]{2,1,0:T(4,128)}, u32[]{:S(2)}) copy-start(f32[3,3,4096]{2,1,0:T(4,128)} %refs_17_.1) | copy-start | bytes 442372
  19.8 11.0 %collective-permute-start.5 = (bf16[10,32,128]{2,1,0:T(8,128)(2,1)S(1)}, bf16[10,32,128]{2,1,0:T(8,128)(2,1)S(1)}, u32[]{:S(2)}, u32[]{:S(2)}) collective-permute-start(bf16[10,32,128]{2,1,0:T(8,128)(2,1)S(1)} %get-tuple-element.59), channel_id=1, source_target_pairs={{1,2},{3,4},{5,6},{7,8},{9,10},{11,12},{13,14},{15,16},{17,18},{19... | collective-permute-start | bytes 245768 | tf_op jit(solution)/shard_map/ppermute | solution.py:645
  23.4 7.4 %collective-permute-start.6 = (bf16[10,32,128]{2,1,0:T(8,128)(2,1)S(1)}, bf16[10,32,128]{2,1,0:T(8,128)(2,1)S(1)}, u32[]{:S(2)}, u32[]{:S(2)}) collective-permute-start(bf16[10,32,128]{2,1,0:T(8,128)(2,1)S(1)} %get-tuple-element.60), channel_id=1, source_target_pairs={{0,1},{2,3},{4,5},{6,7},{8,9},{10,11},{12,13},{14,15},{16,17},{18,... | collective-permute-start | bytes 245768 | tf_op jit(solution)/shard_map/ppermute | solution.py:646
  32.9 11.1 %collective-permute-start.7 = (bf16[6,32,128]{2,1,0:T(8,128)(2,1)S(1)}, bf16[6,32,128]{2,1,0:T(8,128)(2,1)S(1)}, u32[]{:S(2)}, u32[]{:S(2)}) collective-permute-start(bf16[6,32,128]{2,1,0:T(8,128)(2,1)S(1)} %get-tuple-element.63), channel_id=1, source_target_pairs={{1,2},{3,4},{5,6},{7,8},{9,10},{11,12},{13,14},{15,16},{17,18},{19... | collective-permute-start | bytes 147464 | tf_op jit(solution)/shard_map/ppermute | solution.py:645
  33.0 11.0 %collective-permute-start.8 = (bf16[6,32,128]{2,1,0:T(8,128)(2,1)S(1)}, bf16[6,32,128]{2,1,0:T(8,128)(2,1)S(1)}, u32[]{:S(2)}, u32[]{:S(2)}) collective-permute-start(bf16[6,32,128]{2,1,0:T(8,128)(2,1)S(1)} %get-tuple-element.64), channel_id=1, source_target_pairs={{0,1},{2,3},{4,5},{6,7},{8,9},{10,11},{12,13},{14,15},{16,17},{18,... | collective-permute-start | bytes 147464 | tf_op jit(solution)/shard_map/ppermute | solution.py:646
  39.1 7.0 %collective-permute-start.9 = (bf16[13,32,128]{2,1,0:T(8,128)(2,1)S(1)}, bf16[13,32,128]{2,1,0:T(8,128)(2,1)S(1)}, u32[]{:S(2)}, u32[]{:S(2)}) collective-permute-start(bf16[13,32,128]{2,1,0:T(8,128)(2,1)S(1)} %get-tuple-element.68), channel_id=1, source_target_pairs={{0,4},{1,5},{2,6},{3,7},{4,8},{5,9},{6,10},{7,11},{8,12},{9,13},{1... | collective-permute-start | bytes 319496 | tf_op jit(solution)/shard_map/ppermute | solution.py:638
  39.4 6.7 %collective-permute-start.10 = (bf16[13,32,128]{2,1,0:T(8,128)(2,1)S(1)}, bf16[13,32,128]{2,1,0:T(8,128)(2,1)S(1)}, u32[]{:S(2)}, u32[]{:S(2)}) collective-permute-start(bf16[13,32,128]{2,1,0:T(8,128)(2,1)S(1)} %get-tuple-element.69), channel_id=1, source_target_pairs={{0,28},{1,29},{2,30},{3,31},{4,0},{5,1},{6,2},{7,3},{8,4},{9,5},{1... | collective-permute-start | bytes 319496 | tf_op jit(solution)/shard_map/ppermute | solution.py:638
  44.0 2.1 %copy-start.5 = (s32[4096]{0:T(1024)S(1)}, s32[4096]{0:T(1024)}, u32[]{:S(2)}) copy-start(s32[4096]{0:T(1024)} %param.13) | copy-start | bytes 49156

commit v9 on v8

--- a/solution.py
+++ b/solution.py
@@ -372,10 +372,10 @@
     )
 
 
-def halo_kernel(*refs, stage, scale_old, scale_new, subs, unroll=8):
+def halo_kernel(*refs, stage, sizes, scale_old, scale_new, subs, unroll=8):
     (place, most, picks, halo_start, spot, rank, ghost, outer, inner) = refs[:9]
     (residual, dinv, smooth, update, bonds) = refs[9:14]
-    pieces = 2 if stage == SWEEPS - 1 else 1
+    pieces = len(sizes)
     local_found = refs[14 : 14 + pieces]
     refs = refs[14 + pieces :]
     if stage == 0:
@@ -475,7 +475,7 @@
         return totals
 
     for piece, part in enumerate(local_found):
-        first = piece * (groups // pieces)
+        first = sum(sizes[:piece])
 
         def some_tiles(t, carry, part=part, first=first):
             for u in range(unroll):
@@ -496,7 +496,7 @@
                     partial[c, pl.ds(pl.multiple_of(tile * 8, 8), 8), :] = totals[c]
             return carry
 
-        lax.fori_loop(0, groups // pieces // unroll, some_tiles, 0)
+        lax.fori_loop(0, sizes[piece] // unroll, some_tiles, 0)
 
     last_layer = most[groups + 8, 0]
 
@@ -638,13 +638,29 @@
     return lax.ppermute(value, "sub", [(i, (i + steps) % count) for i in range(count)])
 
 
+def across_chips(value):
+    count = lax.axis_size("sub")
+    pairs = [(i, (i + 1) % count) for i in range(1, count, 2)]
+    return lax.ppermute(value, "sub", pairs + [(j, i) for i, j in pairs])
+
+
+def within_chip(value):
+    count = lax.axis_size("sub")
+    pairs = [(i, i + 1) for i in range(0, count, 2)]
+    return lax.ppermute(value, "sub", pairs + [(j, i) for i, j in pairs])
+
+
 def exchanged_by_pairs(outer, inner):
-    count = lax.axis_size("sub")
-    across = [(i, (i + 1) % count) for i in range(1, count, 2)]
-    within = [(i, i + 1) for i in range(0, count, 2)]
-    outer = lax.ppermute(outer, "sub", across + [(j, i) for i, j in across])
-    inner = lax.ppermute(inner, "sub", within + [(j, i) for i, j in within])
-    return outer, inner
+    return across_chips(outer), within_chip(inner)
+
+
+def local_pass(smooth, picks, start, spot, rank, most, first, tiles, us=None):
+    return call(
+        functools.partial(local_kernel, first=first, tiles=tiles),
+        jax.ShapeDtypeStruct((3, picks.shape[0], tiles * LANES), BF16),
+        (smooth, picks, start, spot, rank, most),
+        us=us or 0.12 * tiles,
+    )
 
 
 def body(
@@ -715,34 +731,37 @@
     )
     start, rhs = lax.optimization_barrier((start, rhs))
     rhs = rhs + arrived
-    packed, rhs = lax.optimization_barrier((packed, rhs))
+    packed, start, rhs = lax.optimization_barrier((packed, start, rhs))
     arrived = exchanged(rhs, 2)
-    first = arrived_sides = exchanged_by_pairs(packed, packed)
+    first_outer = across_chips(packed)
+    early = local_pass(smooth, picks, start, spot, rank, most, 0, 8)
+    rhs, early = lax.optimization_barrier((rhs, early))
     rhs = rhs + arrived
+    packed_inner, start, rhs = lax.optimization_barrier((packed, start, rhs))
     arrived = exchanged(rhs, 6)
-    start, rhs = lax.optimization_barrier((start, rhs))
+    first = arrived_sides = (first_outer, within_chip(packed_inner))
 
     factor = HALF / CENTER
     for stage in range(SWEEPS):
         factor_new = 1.0 / (2.0 * CENTER / HALF - factor)
-        pieces = 2 if stage == SWEEPS - 1 else 1
-        tiles = groups // pieces
-        found = []
-        for piece in range(pieces):
+        lists = (smooth, picks, start, spot, rank, most)
+        if stage == 0:
+            sizes = (8, groups - 8)
+            found = [early, local_pass(*lists, *sizes)]
+        elif stage == 1:
+            sizes = (groups,)
+            found = [local_pass(*lists, 0, groups)]
+        else:
+            sizes = (groups // 2,) * 2
+            found = [local_pass(*lists, 0, sizes[0], us=0.2)]
+            far_next, far_prev, start, found[0] = lax.optimization_barrier(
+                (far_next, far_prev, start, found[0])
+            )
+            far_after = shifted(far_next, 4)
+            far_before = shifted(far_prev, -4)
             found.append(
-                call(
-                    functools.partial(local_kernel, first=piece * tiles, tiles=tiles),
-                    sds((3, bonds_of, tiles * LANES), BF16),
-                    (smooth, picks, start, spot, rank, most),
-                    us=3.7 if pieces == 1 else 0.2,
-                )
+                local_pass(smooth, picks, start, spot, rank, most, *sizes, us=0.2)
             )
-            if stage == SWEEPS - 1 and piece == 0:
-                far_next, far_prev, start, found[0] = lax.optimization_barrier(
-                    (far_next, far_prev, start, found[0])
-                )
-                far_after = shifted(far_next, 4)
-                far_before = shifted(far_prev, -4)
         inputs = [place, most, picks, halo_start, spot, rank, ghost, *arrived_sides]
         inputs += [residual, dinv, smooth, update, relaid, *found]
         if stage == 0:
@@ -757,6 +776,7 @@
             functools.partial(
                 halo_kernel,
                 stage=stage,
+                sizes=sizes,
                 scale_old=factor_new * factor,
                 scale_new=2.0 * factor_new / HALF,
                 subs=lax.axis_size("sub"),

time: 48.1 us -> 48.6 us (1.010)
  starting transfers between devices: 23.6 us -> 24.1 us
    ppermute x6, starting transfers between devices: 15.2 us -> 15.9 us  [the longest x3 12.1 us: within_chip(): return lax.ppermute(value, 'sub', pairs + [(j, i) for i, j in pairs])]
    pallas_call x11 -> x12, Pallas kernels: 24 us -> 24 us  [call(): pl.pallas_call(kernel, out_shape=out, in_specs=[pl.BlockSpec(memory_space...]
where the time goes in v9:
time: 48.6 us; the launch traced here: 48.5 us
  starting transfers between devices  24.1 us (50%)
  Pallas kernels  24 us (49%)
    pallas_call x12, Pallas kernels, call(): pl.pallas_call(kernel, out_shape=out, in_specs=[pl.BlockSpec(memory_space...  24 us
    ppermute x3, starting transfers between devices, within_chip(): return lax.ppermute(value, 'sub', pairs + [(j, i) for i, j in pairs])  12.1 us
    ppermute x3, starting transfers between devices, exchanged(): return lax.ppermute(value, 'dom', [(i, i ^ step) for i in range(doms)])  5.49 us
    ppermute x3, starting transfers between devices, across_chips(): return lax.ppermute(value, 'sub', pairs + [(j, i) for i, j in pairs])  3.76 us
    ppermute x2, starting transfers between devices, shifted(): lax.ppermute(value, 'sub', [(i, (i + steps) % count) for i in range(count)])  2.75 us
  transfers between devices with their start and end apart: 11, of which 0 were waited for; matrix products, arithmetic and copies ran while one was open for 0% of the time, Pallas kernels for 34%

profile of v9, /device:TPU:1, one launch (start us, length us, event | category | flops | bytes accessed | tf_op | source)
XLA Modules:
  0.0 48.5 jit_solution(7268046734487485011)
XLA Ops:
  0.0 1.5 %shard_map.82 = (f32[3,32,128]{2,1,0:T(8,128)S(1)}, f32[3,32,128]{2,1,0:T(8,128)S(1)}) custom-call(f32[3,4096]{1,0:T(4,128)} %refs_0_.1, s32[32,128]{1,0:T(8,128)} %bitcast.5), custom_call_target="tpu_custom_call" | custom-call | flops 1600000000 | bytes 1600000 | tf_op jit(solution)/shard_map/pallas_call | solution.py:75
  1.6 2.1 %collective-permute-start = (f32[3,32,128]{2,1,0:T(8,128)S(1)}, f32[3,32,128]{2,1,0:T(8,128)S(1)}, u32[]{:S(2)}, u32[]{:S(2)}) collective-permute-start(f32[3,32,128]{2,1,0:T(8,128)S(1)} %get-tuple-element.55), channel_id=1, source_target_pairs={{0,32},{32,0},{64,96},{96,64},{128,160},{160,128},{192,224},{224,1... | collective-permute-start | bytes 147464 | tf_op jit(solution)/shard_map/ppermute | solution.py:709
  3.7 0.0 copy-start.2
  3.7 0.0 copy-start.4
  3.7 2.6 %shard_map.83 = (s16[32,4096]{1,0:T(8,128)(2,1)S(1)}, s16[16,4096]{1,0:T(8,128)(2,1)S(1)}, s16[16,4096]{1,0:T(8,128)(2,1)S(1)}, s16[32,4096]{1,0:T(8,128)(2,1)S(...) custom-call(s32[32,4096]{1,0:T(8,128)S(1)} %copy-done.1), custom_call_target="tpu_custom_call" | custom-call | flops 2500000000 | bytes 2500000 | tf_op jit(solution)/shard_map/pallas_call | solution.py:75
  6.4 0.2 shard_map.84
  6.6 0.0 collective-permute-done
  6.6 1.4 %collective-permute-start.2 = (f32[3,32,128]{2,1,0:T(8,128)S(1)}, f32[3,32,128]{2,1,0:T(8,128)S(1)}, u32[]{:S(2)}, u32[]{:S(2)}) collective-permute-start(f32[3,32,128]{2,1,0:T(8,128)S(1)} %add.6), channel_id=1, source_target_pairs={{0,64},{32,96},{64,0},{96,32},{128,192},{160,224},{192,128},{224,1... | collective-permute-start | bytes 147464 | tf_op jit(solution)/shard_map/ppermute | solution.py:709
  8.0 3.6 %collective-permute-start.1 = (bf16[7,32,128]{2,1,0:T(8,128)(2,1)S(1)}, bf16[7,32,128]{2,1,0:T(8,128)(2,1)S(1)}, u32[]{:S(2)}, u32[]{:S(2)}) collective-permute-start(bf16[7,32,128]{2,1,0:T(8,128)(2,1)S(1)} %get-tuple-element.61.refs_18_), channel_id=1, source_target_pairs={{1,2},{3,4},{5,6},{7,8},{9,10},{11,12},{13,14},{15,16},{17,18},{19... | collective-permute-start | bytes 172040 | tf_op jit(solution)/shard_map/ppermute | solution.py:644
  11.6 0.9 %shard_map.85.refs_14_ = bf16[3,32,1024]{2,1,0:T(8,128)(2,1)S(1)} custom-call(f32[3,32,128]{2,1,0:T(8,128)S(1)} %get-tuple-element.59.smooth.refs_11_.refs_12_, s16[32,4096]{1,0:T(8,128)(2,1)S(1)} %get-tuple-element.46.picks.refs_2_, s16[16,4096]{1,0:T(8,128)(2,1)S(1)} %get-tuple-element.80.start, s16[32,4096]{1,0:T(8,128)(2,1)S(1)} %get-tuple-element.48.spot.refs_4_, ...), custom_call_target="tpu_custom_call" | custom-call | flops 960000000 | bytes 960000 | tf_op jit(solution)/shard_map/pallas_call | solution.py:75
  12.6 0.0 copy-start
  12.6 0.0 copy-start.3
  12.6 2.0 %collective-permute-start.4 = (f32[3,32,128]{2,1,0:T(8,128)S(1)}, f32[3,32,128]{2,1,0:T(8,128)S(1)}, u32[]{:S(2)}, u32[]{:S(2)}) collective-permute-start(f32[3,32,128]{2,1,0:T(8,128)S(1)} %add.7.refs_16_), channel_id=1, source_target_pairs={{0,192},{32,224},{64,128},{96,160},{128,64},{160,96},{192,0},{224,... | collective-permute-start | bytes 147464 | tf_op jit(solution)/shard_map/ppermute | solution.py:709
  14.6 4.8 %collective-permute-start.3 = (bf16[7,32,128]{2,1,0:T(8,128)(2,1)S(1)}, bf16[7,32,128]{2,1,0:T(8,128)(2,1)S(1)}, u32[]{:S(2)}, u32[]{:S(2)}) collective-permute-start(bf16[7,32,128]{2,1,0:T(8,128)(2,1)S(1)} %get-tuple-element.61.refs_18_), channel_id=1, source_target_pairs={{0,1},{2,3},{4,5},{6,7},{8,9},{10,11},{12,13},{14,15},{16,17},{18,... | collective-permute-start | bytes 172040 | tf_op jit(solution)/shard_map/ppermute | solution.py:650
  19.4 2.8 %shard_map.86.refs_15_ = bf16[3,32,3072]{2,1,0:T(8,128)(2,1)S(1)} custom-call(f32[3,32,128]{2,1,0:T(8,128)S(1)} %get-tuple-element.59.smooth.refs_11_.refs_12_, s16[32,4096]{1,0:T(8,128)(2,1)S(1)} %get-tuple-element.46.picks.refs_2_, s16[16,4096]{1,0:T(8,128)(2,1)S(1)} %get-tuple-element.80.start, s16[32,4096]{1,0:T(8,128)(2,1)S(1)} %get-tuple-element.48.spot.refs_4_, ...), custom_call_target="tpu_custom_call" | custom-call | flops 2880000000 | bytes 2880000 | tf_op jit(solution)/shard_map/pallas_call | solution.py:75
  22.3 0.0 collective-permute-done.4.refs_17_
  22.3 0.0 collective-permute-done.3.refs_8_.refs_16_.refs_4_
  22.3 2.2 %shard_map.87 = (f32[3,32,128]{2,1,0:T(8,128)S(1)}, f32[3,32,128]{2,1,0:T(8,128)S(1)}, f32[3,32,128]{2,1,0:T(8,128)S(1)}, bf16[10,32,128]{2,1,0:T(8,128)(2,1)S(1)}, bf16[10,32,128]{2,1,0:T(8,128)(2,1)S(1)}) custom-call(s32[8,128]{1,0:T(8,128)S(1)} %broadcast_in_dim.3.refs_0_, s32[48,128]{1,0:T(8,128)S(1)} %get-tuple-element.45.most.refs_1_, ...), custom_call_target="tpu_custom_call" | custom-call | flops 2500000000 | bytes 2500000 | tf_op jit(solution)/shard_map/pallas_call | solution.py:75
  24.5 0.1 collective-permute-start.5
  24.6 3.6 %collective-permute-start.6 = (bf16[10,32,128]{2,1,0:T(8,128)(2,1)S(1)}, bf16[10,32,128]{2,1,0:T(8,128)(2,1)S(1)}, u32[]{:S(2)}, u32[]{:S(2)}) collective-permute-start(bf16[10,32,128]{2,1,0:T(8,128)(2,1)S(1)} %get-tuple-element.68), channel_id=1, source_target_pairs={{0,1},{2,3},{4,5},{6,7},{8,9},{10,11},{12,13},{14,15},{16,17},{18,... | collective-permute-start | bytes 245768 | tf_op jit(solution)/shard_map/ppermute | solution.py:650
  28.2 3.8 %shard_map.88.refs_14_ = bf16[3,32,4096]{2,1,0:T(8,128)(2,1)S(1)} custom-call(f32[3,32,128]{2,1,0:T(8,128)S(1)} %get-tuple-element.69.smooth.refs_11_, s16[32,4096]{1,0:T(8,128)(2,1)S(1)} %get-tuple-element.46.picks.refs_2_, s16[16,4096]{1,0:T(8,128)(2,1)S(1)} %get-tuple-element.80.start, s16[32,4096]{1,0:T(8,128)(2,1)S(1)} %get-tuple-element.48.spot.refs_4_, ...), custom_call_target="tpu_custom_call" | custom-call | flops 3840000000 | bytes 3840000 | tf_op jit(solution)/shard_map/pallas_call | solution.py:75
  32.0 0.0 collective-permute-done.5.refs_7_.refs_5_
  32.0 2.1 %shard_map.89 = (f32[3,32,128]{2,1,0:T(8,128)S(1)}, f32[3,32,128]{2,1,0:T(8,128)S(1)}, bf16[6,32,128]{2,1,0:T(8,128)(2,1)S(1)}, bf16[6,32,128]{2,1,0:T(8,128)(2,...) custom-call(s32[8,128]{1,0:T(8,128)S(1)} %broadcast_in_dim.3.refs_0_, ...), custom_call_target="tpu_custom_call" | custom-call | flops 2500000000 | bytes 2500000 | tf_op jit(solution)/shard_map/pallas_call | solution.py:75
  34.1 0.1 collective-permute-start.7
  34.2 3.7 %collective-permute-start.8 = (bf16[6,32,128]{2,1,0:T(8,128)(2,1)S(1)}, bf16[6,32,128]{2,1,0:T(8,128)(2,1)S(1)}, u32[]{:S(2)}, u32[]{:S(2)}) collective-permute-start(bf16[6,32,128]{2,1,0:T(8,128)(2,1)S(1)} %get-tuple-element.72), channel_id=1, source_target_pairs={{0,1},{2,3},{4,5},{6,7},{8,9},{10,11},{12,13},{14,15},{16,17},{18,... | collective-permute-start | bytes 147464 | tf_op jit(solution)/shard_map/ppermute | solution.py:650
  37.9 1.9 %shard_map.90.refs_14_ = bf16[3,32,2048]{2,1,0:T(8,128)(2,1)S(1)} custom-call(f32[3,32,128]{2,1,0:T(8,128)S(1)} %get-tuple-element.75.smooth.refs_11_, s16[32,4096]{1,0:T(8,128)(2,1)S(1)} %get-tuple-element.46.picks.refs_2_, s16[16,4096]{1,0:T(8,128)(2,1)S(1)} %get-tuple-element.80.start, s16[32,4096]{1,0:T(8,128)(2,1)S(1)} %get-tuple-element.48.spot.refs_4_, ...), custom_call_target="tpu_custom_call" | custom-call | flops 200000000 | bytes 200000 | tf_op jit(solution)/shard_map/pallas_call | solution.py:75
  39.8 0.1 collective-permute-start.9
  39.9 2.7 %collective-permute-start.10 = (bf16[13,32,128]{2,1,0:T(8,128)(2,1)S(1)}, bf16[13,32,128]{2,1,0:T(8,128)(2,1)S(1)}, u32[]{:S(2)}, u32[]{:S(2)}) collective-permute-start(bf16[13,32,128]{2,1,0:T(8,128)(2,1)S(1)} %get-tuple-element.77), channel_id=1, source_target_pairs={{0,28},{1,29},{2,30},{3,31},{4,0},{5,1},{6,2},{7,3},{8,4},{9,5},{1... | collective-permute-start | bytes 319496 | tf_op jit(solution)/shard_map/ppermute | solution.py:638
  42.6 1.9 %shard_map.91.refs_15_ = bf16[3,32,2048]{2,1,0:T(8,128)(2,1)S(1)} custom-call(f32[3,32,128]{2,1,0:T(8,128)S(1)} %get-tuple-element.75.smooth.refs_11_, s16[32,4096]{1,0:T(8,128)(2,1)S(1)} %get-tuple-element.46.picks.refs_2_, s16[16,4096]{1,0:T(8,128)(2,1)S(1)} %get-tuple-element.80.start, s16[32,4096]{1,0:T(8,128)(2,1)S(1)} %get-tuple-element.48.spot.refs_4_, ...), custom_call_target="tpu_custom_call" | custom-call | flops 200000000 | bytes 200000 | tf_op jit(solution)/shard_map/pallas_call | solution.py:75
  44.5 0.0 copy-start.5
  44.5 2.1 %shard_map.92.refs_12_ = f32[3,32,128]{2,1,0:T(8,128)S(1)} custom-call(s32[8,128]{1,0:T(8,128)S(1)} %broadcast_in_dim.3.refs_0_, s32[48,128]{1,0:T(8,128)S(1)} %get-tuple-element.45.most.refs_1_, s16[32,4096]{1,0:T(8,128)(2,1)S(1)} %get-tuple-element.46.picks.refs_2_, s16[16,4096]{1,0:T(8,128)(2,1)S(1)} %get-tuple-element.47.refs_3_, ...), custom_call_target="tpu_custom_call" | custom-call | flops 2500000000 | bytes 2500000 | tf_op jit(solution)/shard_map/pallas_call | solution.py:75
  46.6 1.8 %shard_map.93 = f32[3,4096]{1,0:T(4,128)} custom-call(s32[8,128]{1,0:T(8,128)S(1)} %broadcast_in_dim.3.refs_0_, f32[3,32,128]{2,1,0:T(8,128)S(1)} %get-tuple-element.66.refs_17_.refs_1_, f32[4,4096]{1,0:T(4,128)S(1)} %copy-done.4, bf16[7,32,128]{2,1,0:T(8,128)(2,1)S(1)} %collective-permute-done.1.refs_7_.refs_15_.refs_3_, ...), custom_call_target="tpu_custom_call" | custom-call | flops 2000000000 | bytes 2000000 | tf_op jit(solution)/shard_map/pallas_call | solution.py:75
  (20 shorter events, 0.1 us)
Async XLA Ops:
  0.0 3.7 %copy-start.6 = (s32[1,2,512]{2,1,0:T(2,128)S(1)}, s32[1,2,512]{2,1,0:T(2,128)}, u32[]{:S(2)}) copy-start(s32[1,2,512]{2,1,0:T(2,128)} %param.11) | copy-start | bytes 12292
  0.0 3.7 %copy-start.1 = (s32[32,4096]{1,0:T(8,128)S(1)}, s32[32,4096]{1,0:T(8,128)}, u32[]{:S(2)}) copy-start(s32[32,4096]{1,0:T(8,128)} %col) | copy-start | bytes 1572868
  1.6 5.0 %collective-permute-start = (f32[3,32,128]{2,1,0:T(8,128)S(1)}, f32[3,32,128]{2,1,0:T(8,128)S(1)}, u32[]{:S(2)}, u32[]{:S(2)}) collective-permute-start(f32[3,32,128]{2,1,0:T(8,128)S(1)} %get-tuple-element.55), channel_id=1, source_target_pairs={{0,32},{32,0},{64,96},{96,64},{128,160},{160,128},{192,224},{224,1... | collective-permute-start | bytes 147464 | tf_op jit(solution)/shard_map/ppermute | solution.py:709
  3.7 2.7 %copy-start.2 = (f32[3,3,4096]{2,1,0:T(4,128)S(1)}, f32[3,3,4096]{2,1,0:T(4,128)}, u32[]{:S(2)}) copy-start(f32[3,3,4096]{2,1,0:T(4,128)} %dinv.1) | copy-start | bytes 442372
  3.7 2.7 %copy-start.4 = (f32[4,4096]{1,0:T(4,128)S(1)}, f32[4,4096]{1,0:T(4,128)}, u32[]{:S(2)}) copy-start(f32[4,4096]{1,0:T(4,128)} %refs_2_.1) | copy-start | bytes 196612
  6.6 5.9 %collective-permute-start.2 = (f32[3,32,128]{2,1,0:T(8,128)S(1)}, f32[3,32,128]{2,1,0:T(8,128)S(1)}, u32[]{:S(2)}, u32[]{:S(2)}) collective-permute-start(f32[3,32,128]{2,1,0:T(8,128)S(1)} %add.6), channel_id=1, source_target_pairs={{0,64},{32,96},{64,0},{96,32},{128,192},{160,224},{192,128},{224,1... | collective-permute-start | bytes 147464 | tf_op jit(solution)/shard_map/ppermute | solution.py:709
  8.0 14.3 %collective-permute-start.1 = (bf16[7,32,128]{2,1,0:T(8,128)(2,1)S(1)}, bf16[7,32,128]{2,1,0:T(8,128)(2,1)S(1)}, u32[]{:S(2)}, u32[]{:S(2)}) collective-permute-start(bf16[7,32,128]{2,1,0:T(8,128)(2,1)S(1)} %get-tuple-element.61.refs_18_), channel_id=1, source_target_pairs={{1,2},{3,4},{5,6},{7,8},{9,10},{11,12},{13,14},{15,16},{17,18},{19... | collective-permute-start | bytes 172040 | tf_op jit(solution)/shard_map/ppermute | solution.py:644
  12.6 9.7 %copy-start = (bf16[32,3,3,4096]{3,0,2,1:T(8,128)(2,1)S(1)}, bf16[32,3,3,4096]{3,0,2,1:T(8,128)(2,1)}, u32[]{:S(2)}) copy-start(bf16[32,3,3,4096]{3,0,2,1:T(8,128)(2,1)} %param.9) | copy-start | bytes 7077892
  12.6 9.7 %copy-start.3 = (f32[3,3,4096]{2,1,0:T(4,128)S(1)}, f32[3,3,4096]{2,1,0:T(4,128)}, u32[]{:S(2)}) copy-start(f32[3,3,4096]{2,1,0:T(4,128)} %refs_18_.1) | copy-start | bytes 442372
  12.6 9.7 %collective-permute-start.4 = (f32[3,32,128]{2,1,0:T(8,128)S(1)}, f32[3,32,128]{2,1,0:T(8,128)S(1)}, u32[]{:S(2)}, u32[]{:S(2)}) collective-permute-start(f32[3,32,128]{2,1,0:T(8,128)S(1)} %add.7.refs_16_), channel_id=1, source_target_pairs={{0,192},{32,224},{64,128},{96,160},{128,64},{160,96},{192,0},{224,... | collective-permute-start | bytes 147464 | tf_op jit(solution)/shard_map/ppermute | solution.py:709
  14.6 7.7 %collective-permute-start.3 = (bf16[7,32,128]{2,1,0:T(8,128)(2,1)S(1)}, bf16[7,32,128]{2,1,0:T(8,128)(2,1)S(1)}, u32[]{:S(2)}, u32[]{:S(2)}) collective-permute-start(bf16[7,32,128]{2,1,0:T(8,128)(2,1)S(1)} %get-tuple-element.61.refs_18_), channel_id=1, source_target_pairs={{0,1},{2,3},{4,5},{6,7},{8,9},{10,11},{12,13},{14,15},{16,17},{18,... | collective-permute-start | bytes 172040 | tf_op jit(solution)/shard_map/ppermute | solution.py:650
  24.5 7.5 %collective-permute-start.5 = (bf16[10,32,128]{2,1,0:T(8,128)(2,1)S(1)}, bf16[10,32,128]{2,1,0:T(8,128)(2,1)S(1)}, u32[]{:S(2)}, u32[]{:S(2)}) collective-permute-start(bf16[10,32,128]{2,1,0:T(8,128)(2,1)S(1)} %get-tuple-element.67), channel_id=1, source_target_pairs={{1,2},{3,4},{5,6},{7,8},{9,10},{11,12},{13,14},{15,16},{17,18},{19... | collective-permute-start | bytes 245768 | tf_op jit(solution)/shard_map/ppermute | solution.py:644
  24.6 7.4 %collective-permute-start.6 = (bf16[10,32,128]{2,1,0:T(8,128)(2,1)S(1)}, bf16[10,32,128]{2,1,0:T(8,128)(2,1)S(1)}, u32[]{:S(2)}, u32[]{:S(2)}) collective-permute-start(bf16[10,32,128]{2,1,0:T(8,128)(2,1)S(1)} %get-tuple-element.68), channel_id=1, source_target_pairs={{0,1},{2,3},{4,5},{6,7},{8,9},{10,11},{12,13},{14,15},{16,17},{18,... | collective-permute-start | bytes 245768 | tf_op jit(solution)/shard_map/ppermute | solution.py:650
  34.1 10.4 %collective-permute-start.7 = (bf16[6,32,128]{2,1,0:T(8,128)(2,1)S(1)}, bf16[6,32,128]{2,1,0:T(8,128)(2,1)S(1)}, u32[]{:S(2)}, u32[]{:S(2)}) collective-permute-start(bf16[6,32,128]{2,1,0:T(8,128)(2,1)S(1)} %get-tuple-element.71), channel_id=1, source_target_pairs={{1,2},{3,4},{5,6},{7,8},{9,10},{11,12},{13,14},{15,16},{17,18},{19... | collective-permute-start | bytes 147464 | tf_op jit(solution)/shard_map/ppermute | solution.py:644
  34.2 10.3 %collective-permute-start.8 = (bf16[6,32,128]{2,1,0:T(8,128)(2,1)S(1)}, bf16[6,32,128]{2,1,0:T(8,128)(2,1)S(1)}, u32[]{:S(2)}, u32[]{:S(2)}) collective-permute-start(bf16[6,32,128]{2,1,0:T(8,128)(2,1)S(1)} %get-tuple-element.72), channel_id=1, source_target_pairs={{0,1},{2,3},{4,5},{6,7},{8,9},{10,11},{12,13},{14,15},{16,17},{18,... | collective-permute-start | bytes 147464 | tf_op jit(solution)/shard_map/ppermute | solution.py:650
  39.8 6.8 %collective-permute-start.9 = (bf16[13,32,128]{2,1,0:T(8,128)(2,1)S(1)}, bf16[13,32,128]{2,1,0:T(8,128)(2,1)S(1)}, u32[]{:S(2)}, u32[]{:S(2)}) collective-permute-start(bf16[13,32,128]{2,1,0:T(8,128)(2,1)S(1)} %get-tuple-element.76), channel_id=1, source_target_pairs={{0,4},{1,5},{2,6},{3,7},{4,8},{5,9},{6,10},{7,11},{8,12},{9,13},{1... | collective-permute-start | bytes 319496 | tf_op jit(solution)/shard_map/ppermute | solution.py:638
  39.9 6.7 %collective-permute-start.10 = (bf16[13,32,128]{2,1,0:T(8,128)(2,1)S(1)}, bf16[13,32,128]{2,1,0:T(8,128)(2,1)S(1)}, u32[]{:S(2)}, u32[]{:S(2)}) collective-permute-start(bf16[13,32,128]{2,1,0:T(8,128)(2,1)S(1)} %get-tuple-element.77), channel_id=1, source_target_pairs={{0,28},{1,29},{2,30},{3,31},{4,0},{5,1},{6,2},{7,3},{8,4},{9,5},{1... | collective-permute-start | bytes 319496 | tf_op jit(solution)/shard_map/ppermute | solution.py:638
  44.5 2.1 %copy-start.5 = (s32[4096]{0:T(1024)S(1)}, s32[4096]{0:T(1024)}, u32[]{:S(2)}) copy-start(s32[4096]{0:T(1024)} %param.13) | copy-start | bytes 49156

commit v10 on v9

--- a/solution.py
+++ b/solution.py
@@ -16,6 +16,8 @@
 HALF = (HIGH_EIG - LOW_EIG) / 2.0
 LANES = 128
 PACK = 16
+LAYERS = 10
+HALO_LAYERS = 3
 F32 = jnp.float32
 BF16 = jnp.bfloat16
 VMEM = pltpu.VMEM
@@ -187,7 +189,9 @@
     return jnp.broadcast_to(top, values.shape)
 
 
-def prepare_kernel(col, picks, start, halo_start, spot, rank, most, flip):
+def prepare_kernel(
+    col, picks, start, halo_start, spot, rank, most, columns, halo_columns, flip
+):
     bonds_of = col.shape[0]
     groups = col.shape[1] // LANES
     stride = bonds_of + 1
@@ -240,7 +244,19 @@
                         probe < PACK, row_gather(first, inner), row_gather(second, inner)
                     )
                     place = jnp.where(value < pair, place + jnp.int16(step), place)
-                target[:, lanes_of(t)] = place if extra is None else place + extra
+                place = place if extra is None else place + extra
+                target[:, lanes_of(t)] = place
+                chosen = [(x & 255).astype(jnp.int16) for x in halves]
+                if extra is None:
+                    for m in range(LAYERS):
+                        columns[m * PACK : (m + 1) * PACK, lanes_of(t)] = picked(
+                            place + jnp.int16(m), chosen
+                        )
+                else:
+                    for v in range(HALO_LAYERS):
+                        halo_columns[v * PACK : (v + 1) * PACK, lanes_of(t)] = picked(
+                            place + jnp.int16(4 * v), chosen
+                        )
         back = sort_planes(back)
         for k in range(bonds_of):
             flip[pl.ds(k, 8, stride=stride), :] = back[k] & 1023
@@ -259,13 +275,14 @@
     most[groups + 8 :, :] = spread_max(halo_best) >> 2
 
 
-def layer(place, picks, even, odd):
+def picked(place, picks):
     inner = place & jnp.int16(PACK - 1)
-    pick = jnp.where(
-        place < PACK, row_gather(picks[0], inner), row_gather(picks[1], inner)
-    )
-    lane = pick & jnp.int16(LANES - 1)
-    second = pick >= LANES
+    return jnp.where(place < PACK, row_gather(picks[0], inner), row_gather(picks[1], inner))
+
+
+def layer(column, even, odd):
+    lane = column & jnp.int16(LANES - 1)
+    second = column >= LANES
     return [
         jnp.where(second, lane_gather(odd[e], lane), lane_gather(even[e], lane))
         for e in range(3)
@@ -287,11 +304,9 @@
     return jnp.full((PACK, LANES), number, jnp.int32).astype(jnp.int16)
 
 
-LAYERS = 10
-HALO_LAYERS = 3
-
-
-def local_kernel(smooth, picks, start, spot, rank, most, out, *, first, tiles, unroll=8):
+def local_kernel(
+    smooth, picks, start, spot, rank, most, columns, out, *, first, tiles, unroll
+):
     even = [smooth[e, pl.ds(0, PACK, stride=2), :].astype(BF16) for e in range(3)]
     odd = [smooth[e, pl.ds(1, PACK, stride=2), :].astype(BF16) for e in range(3)]
 
@@ -299,12 +314,10 @@
         for u in range(unroll):
             source = pl.ds(pl.multiple_of((first + t * unroll + u) * LANES, LANES), LANES)
             target = pl.ds(pl.multiple_of((t * unroll + u) * LANES, LANES), LANES)
-            place = start[:, source]
-            chosen = halves_of(picks, source)
             spots, ranks = halves_of(spot, source), halves_of(rank, source)
             found = [[jnp.zeros((PACK, LANES), BF16)] * 3 for h in range(2)]
             for m in range(LAYERS):
-                values = layer(place + jnp.int16(m), chosen, even, odd)
+                values = layer(columns[m * PACK : (m + 1) * PACK, source], even, odd)
                 put_back(values, jnp.int16(m), spots, ranks, found)
             for h in range(2):
                 for e in range(3):
@@ -326,9 +339,8 @@
                         [out[e, h * PACK : (h + 1) * PACK, target] for e in range(3)]
                         for h in range(2)
                     ]
-                    values = layer(
-                        start[:, source] + number, halves_of(picks, source), even, odd
-                    )
+                    column = picked(start[:, source] + number, halves_of(picks, source))
+                    values = layer(column, even, odd)
                     put_back(
                         values, number, halves_of(spot, source), halves_of(rank, source), found
                     )
@@ -373,11 +385,11 @@
 
 
 def halo_kernel(*refs, stage, sizes, scale_old, scale_new, subs, unroll=8):
-    (place, most, picks, halo_start, spot, rank, ghost, outer, inner) = refs[:9]
-    (residual, dinv, smooth, update, bonds) = refs[9:14]
+    (place, most, picks, halo_start, halo_columns, spot, rank, ghost) = refs[:8]
+    (outer, inner, residual, dinv, smooth, update, bonds) = refs[8:15]
     pieces = len(sizes)
-    local_found = refs[14 : 14 + pieces]
-    refs = refs[14 + pieces :]
+    local_found = refs[15 : 15 + pieces]
+    refs = refs[15 + pieces :]
     if stage == 0:
         rhs, arrived, coarse_dinv = refs[:3]
         new_smooth, new_update, base, out_outer, out_inner = refs[3:8]
@@ -482,14 +494,13 @@
                 there = pl.ds(pl.multiple_of((t * unroll + u) * LANES, LANES), LANES)
                 tile = first + t * unroll + u
                 here = pl.ds(pl.multiple_of(tile * LANES, LANES), LANES)
-                chosen = halves_of(picks, here)
                 spots, ranks = halves_of(spot, here), halves_of(rank, here)
                 values = [
                     [part[e, h * PACK : (h + 1) * PACK, there] for e in range(3)]
                     for h in range(2)
                 ]
                 for v in range(HALO_LAYERS):
-                    row = layer(halo_start[:, here] + jnp.int16(4 * v), chosen, even, odd)
+                    row = layer(halo_columns[v * PACK : (v + 1) * PACK, here], even, odd)
                     put_back(row, jnp.int16(32 + v), spots, ranks, values)
                 totals = apply_tile(tile, values)
                 for c in range(3):
@@ -507,7 +518,8 @@
 
             def more(v, flat):
                 values = [list(flat[:3]), list(flat[3:])]
-                row = layer(halo_start[:, here] + splat(4 * v), halves_of(picks, here), even, odd)
+                column = picked(halo_start[:, here] + splat(4 * v), halves_of(picks, here))
+                row = layer(column, even, odd)
                 put_back(row, splat(32 + v), halves_of(spot, here), halves_of(rank, here), values)
                 return tuple(values[0] + values[1])
 
@@ -654,11 +666,12 @@
     return across_chips(outer), within_chip(inner)
 
 
-def local_pass(smooth, picks, start, spot, rank, most, first, tiles, us=None):
+def local_pass(smooth, lists, first, tiles, us=None):
+    unroll = max(n for n in range(1, 17) if tiles % n == 0)
     return call(
-        functools.partial(local_kernel, first=first, tiles=tiles),
-        jax.ShapeDtypeStruct((3, picks.shape[0], tiles * LANES), BF16),
-        (smooth, picks, start, spot, rank, most),
+        functools.partial(local_kernel, first=first, tiles=tiles, unroll=unroll),
+        jax.ShapeDtypeStruct((3, lists[0].shape[0], tiles * LANES), BF16),
+        (smooth, *lists),
         us=us or 0.12 * tiles,
     )
 
@@ -710,12 +723,12 @@
 
     assert doms == 8
     arrived = exchanged(rhs, 1)
-    columns, rhs = lax.optimization_barrier((bond_col, rhs))
+    later_col, rhs = lax.optimization_barrier((bond_col, rhs))
 
     def shorts(rows):
         return sds((rows, points), jnp.int16)
 
-    picks, start, halo_start, spot, rank, most = call(
+    picks, start, halo_start, spot, rank, most, columns, halo_columns = call(
         prepare_kernel,
         (
             shorts(bonds_of),
@@ -724,8 +737,10 @@
             shorts(bonds_of),
             shorts(bonds_of),
             sds((groups + 16, LANES), jnp.int32),
+            shorts(LAYERS * PACK),
+            shorts(HALO_LAYERS * PACK),
         ),
-        (columns,),
+        (later_col,),
         scratch=[VMEM((8 * (bonds_of + 2), LANES), jnp.int32)],
         us=2.5,
     )
@@ -734,7 +749,7 @@
     packed, start, rhs = lax.optimization_barrier((packed, start, rhs))
     arrived = exchanged(rhs, 2)
     first_outer = across_chips(packed)
-    early = local_pass(smooth, picks, start, spot, rank, most, 0, 8)
+    early = local_pass(smooth, (picks, start, spot, rank, most, columns), 0, 8)
     rhs, early = lax.optimization_barrier((rhs, early))
     rhs = rhs + arrived
     packed_inner, start, rhs = lax.optimization_barrier((packed, start, rhs))
@@ -744,25 +759,25 @@
     factor = HALF / CENTER
     for stage in range(SWEEPS):
         factor_new = 1.0 / (2.0 * CENTER / HALF - factor)
-        lists = (smooth, picks, start, spot, rank, most)
+        lists = (picks, start, spot, rank, most, columns)
         if stage == 0:
             sizes = (8, groups - 8)
-            found = [early, local_pass(*lists, *sizes)]
+            found = [early, local_pass(smooth, lists, *sizes)]
         elif stage == 1:
             sizes = (groups,)
-            found = [local_pass(*lists, 0, groups)]
+            found = [local_pass(smooth, lists, 0, groups)]
         else:
             sizes = (groups // 2,) * 2
-            found = [local_pass(*lists, 0, sizes[0], us=0.2)]
+            found = [local_pass(smooth, lists, 0, sizes[0], us=0.2)]
             far_next, far_prev, start, found[0] = lax.optimization_barrier(
                 (far_next, far_prev, start, found[0])
             )
             far_after = shifted(far_next, 4)
             far_before = shifted(far_prev, -4)
-            found.append(
-                local_pass(smooth, picks, start, spot, rank, most, *sizes, us=0.2)
-            )
-        inputs = [place, most, picks, halo_start, spot, rank, ghost, *arrived_sides]
+            lists = (picks, start, spot, rank, most, columns)
+            found.append(local_pass(smooth, lists, *sizes, us=0.2))
+        inputs = [place, most, picks, halo_start, halo_columns, spot, rank, ghost]
+        inputs += arrived_sides
         inputs += [residual, dinv, smooth, update, relaid, *found]
         if stage == 0:
             inputs += [rhs, arrived, coarse_dinv]

time: 48.6 us -> 48.3 us (level)
  Pallas kernels: 24 us -> 23 us
  starting transfers between devices: 24.1 us -> 24.8 us
    pallas_call x12, Pallas kernels: 24 us -> 23 us  [call(): pl.pallas_call(kernel, out_shape=out, in_specs=[pl.BlockSpec(memory_space...]
  transfers between devices with their start and end apart: 11 -> 11, of which waited for: 0 -> 0; matrix products, arithmetic and copies ran while one was open for 0% -> 0% of each run, Pallas kernels for 34% -> 32%
where the time goes in v10:
time: 48.3 us; the launch traced here: 48.2 us
  starting transfers between devices  24.8 us (51%)
  Pallas kernels  23 us (48%)
    pallas_call x12, Pallas kernels, call(): pl.pallas_call(kernel, out_shape=out, in_specs=[pl.BlockSpec(memory_space...  23 us
    ppermute x3, starting transfers between devices, within_chip(): return lax.ppermute(value, 'sub', pairs + [(j, i) for i, j in pairs])  12.6 us
    ppermute x3, starting transfers between devices, exchanged(): return lax.ppermute(value, 'dom', [(i, i ^ step) for i in range(doms)])  5.49 us
    ppermute x3, starting transfers between devices, across_chips(): return lax.ppermute(value, 'sub', pairs + [(j, i) for i, j in pairs])  3.94 us
    ppermute x2, starting transfers between devices, shifted(): lax.ppermute(value, 'sub', [(i, (i + steps) % count) for i in range(count)])  2.75 us
  transfers between devices with their start and end apart: 11, of which 0 were waited for; matrix products, arithmetic and copies ran while one was open for 0% of the time, Pallas kernels for 32%

profile of v10, /device:TPU:1, one launch (start us, length us, event | category | flops | bytes accessed | tf_op | source)
XLA Modules:
  0.0 48.2 jit_solution(14355603355783326054)
XLA Ops:
  0.0 1.5 %shard_map.82 = (f32[3,32,128]{2,1,0:T(8,128)S(1)}, f32[3,32,128]{2,1,0:T(8,128)S(1)}) custom-call(f32[3,4096]{1,0:T(4,128)} %refs_0_.1, s32[32,128]{1,0:T(8,128)} %bitcast.5), custom_call_target="tpu_custom_call" | custom-call | flops 1600000000 | bytes 1600000 | tf_op jit(solution)/shard_map/pallas_call | solution.py:77
  1.6 2.1 %collective-permute-start = (f32[3,32,128]{2,1,0:T(8,128)S(1)}, f32[3,32,128]{2,1,0:T(8,128)S(1)}, u32[]{:S(2)}, u32[]{:S(2)}) collective-permute-start(f32[3,32,128]{2,1,0:T(8,128)S(1)} %get-tuple-element.58), channel_id=1, source_target_pairs={{0,32},{32,0},{64,96},{96,64},{128,160},{160,128},{192,224},{224,1... | collective-permute-start | bytes 147464 | tf_op jit(solution)/shard_map/ppermute | solution.py:722
  3.7 0.0 copy-start.2
  3.7 0.0 copy-start.4
  3.7 3.3 %shard_map.83 = (s16[32,4096]{1,0:T(8,128)(2,1)S(1)}, s16[16,4096]{1,0:T(8,128)(2,1)S(1)}, s16[16,4096]{1,0:T(8,128)(2,1)S(1)}, s16[32,4096]{1,0:T(8,128)(2,1)S(...) custom-call(s32[32,4096]{1,0:T(8,128)S(1)} %copy-done.1), custom_call_target="tpu_custom_call" | custom-call | flops 2500000000 | bytes 2500000 | tf_op jit(solution)/shard_map/pallas_call | solution.py:77
  7.0 0.2 shard_map.84
  7.2 0.0 collective-permute-done
  7.3 1.4 %collective-permute-start.2 = (f32[3,32,128]{2,1,0:T(8,128)S(1)}, f32[3,32,128]{2,1,0:T(8,128)S(1)}, u32[]{:S(2)}, u32[]{:S(2)}) collective-permute-start(f32[3,32,128]{2,1,0:T(8,128)S(1)} %add.6), channel_id=1, source_target_pairs={{0,64},{32,96},{64,0},{96,32},{128,192},{160,224},{192,128},{224,1... | collective-permute-start | bytes 147464 | tf_op jit(solution)/shard_map/ppermute | solution.py:722
  8.7 3.6 %collective-permute-start.1 = (bf16[7,32,128]{2,1,0:T(8,128)(2,1)S(1)}, bf16[7,32,128]{2,1,0:T(8,128)(2,1)S(1)}, u32[]{:S(2)}, u32[]{:S(2)}) collective-permute-start(bf16[7,32,128]{2,1,0:T(8,128)(2,1)S(1)} %get-tuple-element.65.refs_19_), channel_id=1, source_target_pairs={{1,2},{3,4},{5,6},{7,8},{9,10},{11,12},{13,14},{15,16},{17,18},{19... | collective-permute-start | bytes 172040 | tf_op jit(solution)/shard_map/ppermute | solution.py:656
  12.2 0.9 %shard_map.85.refs_15_ = bf16[3,32,1024]{2,1,0:T(8,128)(2,1)S(1)} custom-call(f32[3,32,128]{2,1,0:T(8,128)S(1)} %get-tuple-element.62.smooth.refs_12_.refs_13_, s16[32,4096]{1,0:T(8,128)(2,1)S(1)} %get-tuple-element.48.picks.refs_2_, s16[16,4096]{1,0:T(8,128)(2,1)S(1)} %get-tuple-element.84.start, s16[32,4096]{1,0:T(8,128)(2,1)S(1)} %get-tuple-element.51.spot.refs_5_, ...), custom_call_target="tpu_custom_call" | custom-call | flops 960000000 | bytes 960000 | tf_op jit(solution)/shard_map/pallas_call | solution.py:77
  13.1 0.0 collective-permute-done.2
  13.1 0.0 copy-start
  13.1 0.0 copy-start.3
  13.2 2.0 %collective-permute-start.4 = (f32[3,32,128]{2,1,0:T(8,128)S(1)}, f32[3,32,128]{2,1,0:T(8,128)S(1)}, u32[]{:S(2)}, u32[]{:S(2)}) collective-permute-start(f32[3,32,128]{2,1,0:T(8,128)S(1)} %add.7.refs_17_), channel_id=1, source_target_pairs={{0,192},{32,224},{64,128},{96,160},{128,64},{160,96},{192,0},{224,... | collective-permute-start | bytes 147464 | tf_op jit(solution)/shard_map/ppermute | solution.py:722
  15.1 4.8 %collective-permute-start.3 = (bf16[7,32,128]{2,1,0:T(8,128)(2,1)S(1)}, bf16[7,32,128]{2,1,0:T(8,128)(2,1)S(1)}, u32[]{:S(2)}, u32[]{:S(2)}) collective-permute-start(bf16[7,32,128]{2,1,0:T(8,128)(2,1)S(1)} %get-tuple-element.65.refs_19_), channel_id=1, source_target_pairs={{0,1},{2,3},{4,5},{6,7},{8,9},{10,11},{12,13},{14,15},{16,17},{18,... | collective-permute-start | bytes 172040 | tf_op jit(solution)/shard_map/ppermute | solution.py:662
  20.0 2.6 %shard_map.86.refs_16_ = bf16[3,32,3072]{2,1,0:T(8,128)(2,1)S(1)} custom-call(f32[3,32,128]{2,1,0:T(8,128)S(1)} %get-tuple-element.62.smooth.refs_12_.refs_13_, s16[32,4096]{1,0:T(8,128)(2,1)S(1)} %get-tuple-element.48.picks.refs_2_, s16[16,4096]{1,0:T(8,128)(2,1)S(1)} %get-tuple-element.84.start, s16[32,4096]{1,0:T(8,128)(2,1)S(1)} %get-tuple-element.51.spot.refs_5_, ...), custom_call_target="tpu_custom_call" | custom-call | flops 2880000000 | bytes 2880000 | tf_op jit(solution)/shard_map/pallas_call | solution.py:77
  22.6 0.0 collective-permute-done.1.refs_8_.refs_16_.refs_3_
  22.6 0.0 collective-permute-done.4.refs_18_
  22.6 2.1 %shard_map.87 = (f32[3,32,128]{2,1,0:T(8,128)S(1)}, f32[3,32,128]{2,1,0:T(8,128)S(1)}, f32[3,32,128]{2,1,0:T(8,128)S(1)}, bf16[10,32,128]{2,1,0:T(8,128)(2,1)S(1)}, bf16[10,32,128]{2,1,0:T(8,128)(2,1)S(1)}) custom-call(s32[8,128]{1,0:T(8,128)S(1)} %broadcast_in_dim.3.refs_0_, s32[48,128]{1,0:T(8,128)S(1)} %get-tuple-element.47.most.refs_1_, ...), custom_call_target="tpu_custom_call" | custom-call | flops 2500000000 | bytes 2500000 | tf_op jit(solution)/shard_map/pallas_call | solution.py:77
  24.7 0.1 collective-permute-start.5
  24.8 3.7 %collective-permute-start.6 = (bf16[10,32,128]{2,1,0:T(8,128)(2,1)S(1)}, bf16[10,32,128]{2,1,0:T(8,128)(2,1)S(1)}, u32[]{:S(2)}, u32[]{:S(2)}) collective-permute-start(bf16[10,32,128]{2,1,0:T(8,128)(2,1)S(1)} %get-tuple-element.72), channel_id=1, source_target_pairs={{0,1},{2,3},{4,5},{6,7},{8,9},{10,11},{12,13},{14,15},{16,17},{18,... | collective-permute-start | bytes 245768 | tf_op jit(solution)/shard_map/ppermute | solution.py:662
  28.5 3.4 %shard_map.88.refs_15_ = bf16[3,32,4096]{2,1,0:T(8,128)(2,1)S(1)} custom-call(f32[3,32,128]{2,1,0:T(8,128)S(1)} %get-tuple-element.73.smooth.refs_12_, s16[32,4096]{1,0:T(8,128)(2,1)S(1)} %get-tuple-element.48.picks.refs_2_, s16[16,4096]{1,0:T(8,128)(2,1)S(1)} %get-tuple-element.84.start, s16[32,4096]{1,0:T(8,128)(2,1)S(1)} %get-tuple-element.51.spot.refs_5_, ...), custom_call_target="tpu_custom_call" | custom-call | flops 3840000000 | bytes 3840000 | tf_op jit(solution)/shard_map/pallas_call | solution.py:77
  31.9 2.0 %shard_map.89 = (f32[3,32,128]{2,1,0:T(8,128)S(1)}, f32[3,32,128]{2,1,0:T(8,128)S(1)}, bf16[6,32,128]{2,1,0:T(8,128)(2,1)S(1)}, bf16[6,32,128]{2,1,0:T(8,128)(2,...) custom-call(s32[8,128]{1,0:T(8,128)S(1)} %broadcast_in_dim.3.refs_0_, ...), custom_call_target="tpu_custom_call" | custom-call | flops 2500000000 | bytes 2500000 | tf_op jit(solution)/shard_map/pallas_call | solution.py:77
  33.9 0.3 collective-permute-start.7
  34.1 4.1 %collective-permute-start.8 = (bf16[6,32,128]{2,1,0:T(8,128)(2,1)S(1)}, bf16[6,32,128]{2,1,0:T(8,128)(2,1)S(1)}, u32[]{:S(2)}, u32[]{:S(2)}) collective-permute-start(bf16[6,32,128]{2,1,0:T(8,128)(2,1)S(1)} %get-tuple-element.76), channel_id=1, source_target_pairs={{0,1},{2,3},{4,5},{6,7},{8,9},{10,11},{12,13},{14,15},{16,17},{18,... | collective-permute-start | bytes 147464 | tf_op jit(solution)/shard_map/ppermute | solution.py:662
  38.2 1.7 %shard_map.90.refs_15_ = bf16[3,32,2048]{2,1,0:T(8,128)(2,1)S(1)} custom-call(f32[3,32,128]{2,1,0:T(8,128)S(1)} %get-tuple-element.79.smooth.refs_12_, s16[32,4096]{1,0:T(8,128)(2,1)S(1)} %get-tuple-element.48.picks.refs_2_, s16[16,4096]{1,0:T(8,128)(2,1)S(1)} %get-tuple-element.84.start, s16[32,4096]{1,0:T(8,128)(2,1)S(1)} %get-tuple-element.51.spot.refs_5_, ...), custom_call_target="tpu_custom_call" | custom-call | flops 200000000 | bytes 200000 | tf_op jit(solution)/shard_map/pallas_call | solution.py:77
  39.9 0.1 collective-permute-start.9
  40.0 2.7 %collective-permute-start.10 = (bf16[13,32,128]{2,1,0:T(8,128)(2,1)S(1)}, bf16[13,32,128]{2,1,0:T(8,128)(2,1)S(1)}, u32[]{:S(2)}, u32[]{:S(2)}) collective-permute-start(bf16[13,32,128]{2,1,0:T(8,128)(2,1)S(1)} %get-tuple-element.81), channel_id=1, source_target_pairs={{0,28},{1,29},{2,30},{3,31},{4,0},{5,1},{6,2},{7,3},{8,4},{9,5},{1... | collective-permute-start | bytes 319496 | tf_op jit(solution)/shard_map/ppermute | solution.py:650
  42.6 1.7 %shard_map.91.refs_16_ = bf16[3,32,2048]{2,1,0:T(8,128)(2,1)S(1)} custom-call(f32[3,32,128]{2,1,0:T(8,128)S(1)} %get-tuple-element.79.smooth.refs_12_, s16[32,4096]{1,0:T(8,128)(2,1)S(1)} %get-tuple-element.48.picks.refs_2_, s16[16,4096]{1,0:T(8,128)(2,1)S(1)} %get-tuple-element.84.start, s16[32,4096]{1,0:T(8,128)(2,1)S(1)} %get-tuple-element.51.spot.refs_5_, ...), custom_call_target="tpu_custom_call" | custom-call | flops 200000000 | bytes 200000 | tf_op jit(solution)/shard_map/pallas_call | solution.py:77
  44.3 0.0 copy-start.5
  44.3 2.0 %shard_map.92.refs_12_ = f32[3,32,128]{2,1,0:T(8,128)S(1)} custom-call(s32[8,128]{1,0:T(8,128)S(1)} %broadcast_in_dim.3.refs_0_, s32[48,128]{1,0:T(8,128)S(1)} %get-tuple-element.47.most.refs_1_, s16[32,4096]{1,0:T(8,128)(2,1)S(1)} %get-tuple-element.48.picks.refs_2_, s16[16,4096]{1,0:T(8,128)(2,1)S(1)} %get-tuple-element.49.refs_3_, ...), custom_call_target="tpu_custom_call" | custom-call | flops 2500000000 | bytes 2500000 | tf_op jit(solution)/shard_map/pallas_call | solution.py:77
  46.3 1.8 %shard_map.93 = f32[3,4096]{1,0:T(4,128)} custom-call(s32[8,128]{1,0:T(8,128)S(1)} %broadcast_in_dim.3.refs_0_, f32[3,32,128]{2,1,0:T(8,128)S(1)} %get-tuple-element.70.refs_18_.refs_1_, f32[4,4096]{1,0:T(4,128)S(1)} %copy-done.4, bf16[7,32,128]{2,1,0:T(8,128)(2,1)S(1)} %collective-permute-done.1.refs_8_.refs_16_.refs_3_, ...), custom_call_target="tpu_custom_call" | custom-call | flops 2000000000 | bytes 2000000 | tf_op jit(solution)/shard_map/pallas_call | solution.py:77
  (20 shorter events, 0.1 us)
Async XLA Ops:
  0.0 3.7 %copy-start.6 = (s32[1,2,512]{2,1,0:T(2,128)S(1)}, s32[1,2,512]{2,1,0:T(2,128)}, u32[]{:S(2)}) copy-start(s32[1,2,512]{2,1,0:T(2,128)} %param.11) | copy-start | bytes 12292
  0.0 3.7 %copy-start.1 = (s32[32,4096]{1,0:T(8,128)S(1)}, s32[32,4096]{1,0:T(8,128)}, u32[]{:S(2)}) copy-start(s32[32,4096]{1,0:T(8,128)} %col) | copy-start | bytes 1572868
  1.6 5.7 %collective-permute-start = (f32[3,32,128]{2,1,0:T(8,128)S(1)}, f32[3,32,128]{2,1,0:T(8,128)S(1)}, u32[]{:S(2)}, u32[]{:S(2)}) collective-permute-start(f32[3,32,128]{2,1,0:T(8,128)S(1)} %get-tuple-element.58), channel_id=1, source_target_pairs={{0,32},{32,0},{64,96},{96,64},{128,160},{160,128},{192,224},{224,1... | collective-permute-start | bytes 147464 | tf_op jit(solution)/shard_map/ppermute | solution.py:722
  3.7 3.3 %copy-start.2 = (f32[3,3,4096]{2,1,0:T(4,128)S(1)}, f32[3,3,4096]{2,1,0:T(4,128)}, u32[]{:S(2)}) copy-start(f32[3,3,4096]{2,1,0:T(4,128)} %dinv.1) | copy-start | bytes 442372
  3.7 3.3 %copy-start.4 = (f32[4,4096]{1,0:T(4,128)S(1)}, f32[4,4096]{1,0:T(4,128)}, u32[]{:S(2)}) copy-start(f32[4,4096]{1,0:T(4,128)} %refs_2_.1) | copy-start | bytes 196612
  7.3 5.8 %collective-permute-start.2 = (f32[3,32,128]{2,1,0:T(8,128)S(1)}, f32[3,32,128]{2,1,0:T(8,128)S(1)}, u32[]{:S(2)}, u32[]{:S(2)}) collective-permute-start(f32[3,32,128]{2,1,0:T(8,128)S(1)} %add.6), channel_id=1, source_target_pairs={{0,64},{32,96},{64,0},{96,32},{128,192},{160,224},{192,128},{224,1... | collective-permute-start | bytes 147464 | tf_op jit(solution)/shard_map/ppermute | solution.py:722
  8.7 13.9 %collective-permute-start.1 = (bf16[7,32,128]{2,1,0:T(8,128)(2,1)S(1)}, bf16[7,32,128]{2,1,0:T(8,128)(2,1)S(1)}, u32[]{:S(2)}, u32[]{:S(2)}) collective-permute-start(bf16[7,32,128]{2,1,0:T(8,128)(2,1)S(1)} %get-tuple-element.65.refs_19_), channel_id=1, source_target_pairs={{1,2},{3,4},{5,6},{7,8},{9,10},{11,12},{13,14},{15,16},{17,18},{19... | collective-permute-start | bytes 172040 | tf_op jit(solution)/shard_map/ppermute | solution.py:656
  13.1 9.5 %copy-start = (bf16[32,3,3,4096]{3,0,2,1:T(8,128)(2,1)S(1)}, bf16[32,3,3,4096]{3,0,2,1:T(8,128)(2,1)}, u32[]{:S(2)}) copy-start(bf16[32,3,3,4096]{3,0,2,1:T(8,128)(2,1)} %param.9) | copy-start | bytes 7077892
  13.1 9.5 %copy-start.3 = (f32[3,3,4096]{2,1,0:T(4,128)S(1)}, f32[3,3,4096]{2,1,0:T(4,128)}, u32[]{:S(2)}) copy-start(f32[3,3,4096]{2,1,0:T(4,128)} %refs_19_.1) | copy-start | bytes 442372
  13.2 9.4 %collective-permute-start.4 = (f32[3,32,128]{2,1,0:T(8,128)S(1)}, f32[3,32,128]{2,1,0:T(8,128)S(1)}, u32[]{:S(2)}, u32[]{:S(2)}) collective-permute-start(f32[3,32,128]{2,1,0:T(8,128)S(1)} %add.7.refs_17_), channel_id=1, source_target_pairs={{0,192},{32,224},{64,128},{96,160},{128,64},{160,96},{192,0},{224,... | collective-permute-start | bytes 147464 | tf_op jit(solution)/shard_map/ppermute | solution.py:722
  15.1 7.5 %collective-permute-start.3 = (bf16[7,32,128]{2,1,0:T(8,128)(2,1)S(1)}, bf16[7,32,128]{2,1,0:T(8,128)(2,1)S(1)}, u32[]{:S(2)}, u32[]{:S(2)}) collective-permute-start(bf16[7,32,128]{2,1,0:T(8,128)(2,1)S(1)} %get-tuple-element.65.refs_19_), channel_id=1, source_target_pairs={{0,1},{2,3},{4,5},{6,7},{8,9},{10,11},{12,13},{14,15},{16,17},{18,... | collective-permute-start | bytes 172040 | tf_op jit(solution)/shard_map/ppermute | solution.py:662
  24.7 7.2 %collective-permute-start.5 = (bf16[10,32,128]{2,1,0:T(8,128)(2,1)S(1)}, bf16[10,32,128]{2,1,0:T(8,128)(2,1)S(1)}, u32[]{:S(2)}, u32[]{:S(2)}) collective-permute-start(bf16[10,32,128]{2,1,0:T(8,128)(2,1)S(1)} %get-tuple-element.71), channel_id=1, source_target_pairs={{1,2},{3,4},{5,6},{7,8},{9,10},{11,12},{13,14},{15,16},{17,18},{19... | collective-permute-start | bytes 245768 | tf_op jit(solution)/shard_map/ppermute | solution.py:656
  24.8 7.1 %collective-permute-start.6 = (bf16[10,32,128]{2,1,0:T(8,128)(2,1)S(1)}, bf16[10,32,128]{2,1,0:T(8,128)(2,1)S(1)}, u32[]{:S(2)}, u32[]{:S(2)}) collective-permute-start(bf16[10,32,128]{2,1,0:T(8,128)(2,1)S(1)} %get-tuple-element.72), channel_id=1, source_target_pairs={{0,1},{2,3},{4,5},{6,7},{8,9},{10,11},{12,13},{14,15},{16,17},{18,... | collective-permute-start | bytes 245768 | tf_op jit(solution)/shard_map/ppermute | solution.py:662
  33.9 10.5 %collective-permute-start.7 = (bf16[6,32,128]{2,1,0:T(8,128)(2,1)S(1)}, bf16[6,32,128]{2,1,0:T(8,128)(2,1)S(1)}, u32[]{:S(2)}, u32[]{:S(2)}) collective-permute-start(bf16[6,32,128]{2,1,0:T(8,128)(2,1)S(1)} %get-tuple-element.75), channel_id=1, source_target_pairs={{1,2},{3,4},{5,6},{7,8},{9,10},{11,12},{13,14},{15,16},{17,18},{19... | collective-permute-start | bytes 147464 | tf_op jit(solution)/shard_map/ppermute | solution.py:656
  34.1 10.2 %collective-permute-start.8 = (bf16[6,32,128]{2,1,0:T(8,128)(2,1)S(1)}, bf16[6,32,128]{2,1,0:T(8,128)(2,1)S(1)}, u32[]{:S(2)}, u32[]{:S(2)}) collective-permute-start(bf16[6,32,128]{2,1,0:T(8,128)(2,1)S(1)} %get-tuple-element.76), channel_id=1, source_target_pairs={{0,1},{2,3},{4,5},{6,7},{8,9},{10,11},{12,13},{14,15},{16,17},{18,... | collective-permute-start | bytes 147464 | tf_op jit(solution)/shard_map/ppermute | solution.py:662
  39.9 6.4 %collective-permute-start.9 = (bf16[13,32,128]{2,1,0:T(8,128)(2,1)S(1)}, bf16[13,32,128]{2,1,0:T(8,128)(2,1)S(1)}, u32[]{:S(2)}, u32[]{:S(2)}) collective-permute-start(bf16[13,32,128]{2,1,0:T(8,128)(2,1)S(1)} %get-tuple-element.80), channel_id=1, source_target_pairs={{0,4},{1,5},{2,6},{3,7},{4,8},{5,9},{6,10},{7,11},{8,12},{9,13},{1... | collective-permute-start | bytes 319496 | tf_op jit(solution)/shard_map/ppermute | solution.py:650
  40.0 6.3 %collective-permute-start.10 = (bf16[13,32,128]{2,1,0:T(8,128)(2,1)S(1)}, bf16[13,32,128]{2,1,0:T(8,128)(2,1)S(1)}, u32[]{:S(2)}, u32[]{:S(2)}) collective-permute-start(bf16[13,32,128]{2,1,0:T(8,128)(2,1)S(1)} %get-tuple-element.81), channel_id=1, source_target_pairs={{0,28},{1,29},{2,30},{3,31},{4,0},{5,1},{6,2},{7,3},{8,4},{9,5},{1... | collective-permute-start | bytes 319496 | tf_op jit(solution)/shard_map/ppermute | solution.py:650
  44.3 2.0 %copy-start.5 = (s32[4096]{0:T(1024)S(1)}, s32[4096]{0:T(1024)}, u32[]{:S(2)}) copy-start(s32[4096]{0:T(1024)} %param.13) | copy-start | bytes 49156

commit v11 on v10

--- a/solution.py
+++ b/solution.py
@@ -17,6 +17,7 @@
 LANES = 128
 PACK = 16
 LAYERS = 10
+FIRST_HALF_LAYERS = 8
 HALO_LAYERS = 3
 F32 = jnp.float32
 BF16 = jnp.bfloat16
@@ -217,7 +218,9 @@
         here = jnp.zeros((8, LANES), jnp.int32)
         for k in range(bonds_of):
             local = pairs[k] < PACK
-            here = jnp.maximum(here, jnp.where(local, ranks[k], 0))
+            early = ((keys[k] >> 8) & 31) < PACK
+            depth = ranks[k] + jnp.where(early, LAYERS - FIRST_HALF_LAYERS, 0)
+            here = jnp.maximum(here, jnp.where(local, depth, 0))
             halo_best = jnp.maximum(halo_best, jnp.where(local, 0, ranks[k]))
             code = jnp.where(
                 local,
@@ -289,8 +292,8 @@
     ]
 
 
-def put_back(values, number, spots, ranks, out):
-    for h in range(2):
+def put_back(values, number, spots, ranks, out, halves=(0, 1)):
+    for h in halves:
         hit = ranks[h] == number
         for e in range(3):
             out[h][e] = jnp.where(hit, row_gather(values[e], spots[h]), out[h][e])
@@ -318,7 +321,8 @@
             found = [[jnp.zeros((PACK, LANES), BF16)] * 3 for h in range(2)]
             for m in range(LAYERS):
                 values = layer(columns[m * PACK : (m + 1) * PACK, source], even, odd)
-                put_back(values, jnp.int16(m), spots, ranks, found)
+                halves = (0, 1) if m < FIRST_HALF_LAYERS else (1,)
+                put_back(values, jnp.int16(m), spots, ranks, found, halves)
             for h in range(2):
                 for e in range(3):
                     out[e, h * PACK : (h + 1) * PACK, target] = found[h][e]
@@ -349,7 +353,9 @@
                             out[e, h * PACK : (h + 1) * PACK, target] = found[h][e]
                 return inner
 
-            lax.fori_loop(LAYERS, most[first + block * 8, 0] + 1, more, 0)
+            deepest = most[first + block * 8, 0]
+            begin = jnp.where(deepest >= LAYERS, FIRST_HALF_LAYERS, deepest + 1)
+            lax.fori_loop(begin, deepest + 1, more, 0)
             return carry
 
         lax.fori_loop(0, tiles // 8, eight_tiles, 0)

time: 48.3 us -> 48.2 us (level)
  no operation moved by 1% of the time
where the time goes in v11:
time: 48.2 us; the launch traced here: 48.1 us
  starting transfers between devices  24.8 us (51%)
  Pallas kernels  22.9 us (48%)
    pallas_call x12, Pallas kernels, call(): pl.pallas_call(kernel, out_shape=out, in_specs=[pl.BlockSpec(memory_space...  22.9 us
    ppermute x3, starting transfers between devices, within_chip(): return lax.ppermute(value, 'sub', pairs + [(j, i) for i, j in pairs])  12.6 us
    ppermute x3, starting transfers between devices, exchanged(): return lax.ppermute(value, 'dom', [(i, i ^ step) for i in range(doms)])  5.49 us
    ppermute x3, starting transfers between devices, across_chips(): return lax.ppermute(value, 'sub', pairs + [(j, i) for i, j in pairs])  3.94 us
    ppermute x2, starting transfers between devices, shifted(): lax.ppermute(value, 'sub', [(i, (i + steps) % count) for i in range(count)])  2.75 us
  transfers between devices with their start and end apart: 11, of which 0 were waited for; matrix products, arithmetic and copies ran while one was open for 0% of the time, Pallas kernels for 32%

profile of v11, /device:TPU:1, one launch (start us, length us, event | category | flops | bytes accessed | tf_op | source)
XLA Modules:
  0.0 48.1 jit_solution(334429660862263342)
XLA Ops:
  0.0 1.5 %shard_map.82 = (f32[3,32,128]{2,1,0:T(8,128)S(1)}, f32[3,32,128]{2,1,0:T(8,128)S(1)}) custom-call(f32[3,4096]{1,0:T(4,128)} %refs_0_.1, s32[32,128]{1,0:T(8,128)} %bitcast.5), custom_call_target="tpu_custom_call" | custom-call | flops 1600000000 | bytes 1600000 | tf_op jit(solution)/shard_map/pallas_call | solution.py:78
  1.6 2.1 %collective-permute-start = (f32[3,32,128]{2,1,0:T(8,128)S(1)}, f32[3,32,128]{2,1,0:T(8,128)S(1)}, u32[]{:S(2)}, u32[]{:S(2)}) collective-permute-start(f32[3,32,128]{2,1,0:T(8,128)S(1)} %get-tuple-element.58), channel_id=1, source_target_pairs={{0,32},{32,0},{64,96},{96,64},{128,160},{160,128},{192,224},{224,1... | collective-permute-start | bytes 147464 | tf_op jit(solution)/shard_map/ppermute | solution.py:728
  3.7 0.0 copy-start.4
  3.7 3.2 %shard_map.83 = (s16[32,4096]{1,0:T(8,128)(2,1)S(1)}, s16[16,4096]{1,0:T(8,128)(2,1)S(1)}, s16[16,4096]{1,0:T(8,128)(2,1)S(1)}, s16[32,4096]{1,0:T(8,128)(2,1)S(...) custom-call(s32[32,4096]{1,0:T(8,128)S(1)} %copy-done.1), custom_call_target="tpu_custom_call" | custom-call | flops 2500000000 | bytes 2500000 | tf_op jit(solution)/shard_map/pallas_call | solution.py:78
  7.0 0.2 shard_map.84
  7.2 1.4 %collective-permute-start.2 = (f32[3,32,128]{2,1,0:T(8,128)S(1)}, f32[3,32,128]{2,1,0:T(8,128)S(1)}, u32[]{:S(2)}, u32[]{:S(2)}) collective-permute-start(f32[3,32,128]{2,1,0:T(8,128)S(1)} %add.6), channel_id=1, source_target_pairs={{0,64},{32,96},{64,0},{96,32},{128,192},{160,224},{192,128},{224,1... | collective-permute-start | bytes 147464 | tf_op jit(solution)/shard_map/ppermute | solution.py:728
  8.6 3.6 %collective-permute-start.1 = (bf16[7,32,128]{2,1,0:T(8,128)(2,1)S(1)}, bf16[7,32,128]{2,1,0:T(8,128)(2,1)S(1)}, u32[]{:S(2)}, u32[]{:S(2)}) collective-permute-start(bf16[7,32,128]{2,1,0:T(8,128)(2,1)S(1)} %get-tuple-element.65.refs_19_), channel_id=1, source_target_pairs={{1,2},{3,4},{5,6},{7,8},{9,10},{11,12},{13,14},{15,16},{17,18},{19... | collective-permute-start | bytes 172040 | tf_op jit(solution)/shard_map/ppermute | solution.py:662
  12.2 0.9 %shard_map.85.refs_15_ = bf16[3,32,1024]{2,1,0:T(8,128)(2,1)S(1)} custom-call(f32[3,32,128]{2,1,0:T(8,128)S(1)} %get-tuple-element.62.smooth.refs_12_.refs_13_, s16[32,4096]{1,0:T(8,128)(2,1)S(1)} %get-tuple-element.48.picks.refs_2_, s16[16,4096]{1,0:T(8,128)(2,1)S(1)} %get-tuple-element.84.start, s16[32,4096]{1,0:T(8,128)(2,1)S(1)} %get-tuple-element.51.spot.refs_5_, ...), custom_call_target="tpu_custom_call" | custom-call | flops 960000000 | bytes 960000 | tf_op jit(solution)/shard_map/pallas_call | solution.py:78
  13.1 0.0 collective-permute-done.2
  13.1 0.0 copy-start
  13.1 0.0 copy-start.3
  13.1 2.0 %collective-permute-start.4 = (f32[3,32,128]{2,1,0:T(8,128)S(1)}, f32[3,32,128]{2,1,0:T(8,128)S(1)}, u32[]{:S(2)}, u32[]{:S(2)}) collective-permute-start(f32[3,32,128]{2,1,0:T(8,128)S(1)} %add.7.refs_17_), channel_id=1, source_target_pairs={{0,192},{32,224},{64,128},{96,160},{128,64},{160,96},{192,0},{224,... | collective-permute-start | bytes 147464 | tf_op jit(solution)/shard_map/ppermute | solution.py:728
  15.1 4.8 %collective-permute-start.3 = (bf16[7,32,128]{2,1,0:T(8,128)(2,1)S(1)}, bf16[7,32,128]{2,1,0:T(8,128)(2,1)S(1)}, u32[]{:S(2)}, u32[]{:S(2)}) collective-permute-start(bf16[7,32,128]{2,1,0:T(8,128)(2,1)S(1)} %get-tuple-element.65.refs_19_), channel_id=1, source_target_pairs={{0,1},{2,3},{4,5},{6,7},{8,9},{10,11},{12,13},{14,15},{16,17},{18,... | collective-permute-start | bytes 172040 | tf_op jit(solution)/shard_map/ppermute | solution.py:668
  20.0 2.5 %shard_map.86.refs_16_ = bf16[3,32,3072]{2,1,0:T(8,128)(2,1)S(1)} custom-call(f32[3,32,128]{2,1,0:T(8,128)S(1)} %get-tuple-element.62.smooth.refs_12_.refs_13_, s16[32,4096]{1,0:T(8,128)(2,1)S(1)} %get-tuple-element.48.picks.refs_2_, s16[16,4096]{1,0:T(8,128)(2,1)S(1)} %get-tuple-element.84.start, s16[32,4096]{1,0:T(8,128)(2,1)S(1)} %get-tuple-element.51.spot.refs_5_, ...), custom_call_target="tpu_custom_call" | custom-call | flops 2880000000 | bytes 2880000 | tf_op jit(solution)/shard_map/pallas_call | solution.py:78
  22.5 0.0 collective-permute-done.4.refs_18_
  22.5 0.0 collective-permute-done.3.refs_9_.refs_17_.refs_4_
  22.6 2.1 %shard_map.87 = (f32[3,32,128]{2,1,0:T(8,128)S(1)}, f32[3,32,128]{2,1,0:T(8,128)S(1)}, f32[3,32,128]{2,1,0:T(8,128)S(1)}, bf16[10,32,128]{2,1,0:T(8,128)(2,1)S(1)}, bf16[10,32,128]{2,1,0:T(8,128)(2,1)S(1)}) custom-call(s32[8,128]{1,0:T(8,128)S(1)} %broadcast_in_dim.3.refs_0_, s32[48,128]{1,0:T(8,128)S(1)} %get-tuple-element.47.most.refs_1_, ...), custom_call_target="tpu_custom_call" | custom-call | flops 2500000000 | bytes 2500000 | tf_op jit(solution)/shard_map/pallas_call | solution.py:78
  24.6 0.1 collective-permute-start.5
  24.7 3.7 %collective-permute-start.6 = (bf16[10,32,128]{2,1,0:T(8,128)(2,1)S(1)}, bf16[10,32,128]{2,1,0:T(8,128)(2,1)S(1)}, u32[]{:S(2)}, u32[]{:S(2)}) collective-permute-start(bf16[10,32,128]{2,1,0:T(8,128)(2,1)S(1)} %get-tuple-element.72), channel_id=1, source_target_pairs={{0,1},{2,3},{4,5},{6,7},{8,9},{10,11},{12,13},{14,15},{16,17},{18,... | collective-permute-start | bytes 245768 | tf_op jit(solution)/shard_map/ppermute | solution.py:668
  28.4 3.3 %shard_map.88.refs_15_ = bf16[3,32,4096]{2,1,0:T(8,128)(2,1)S(1)} custom-call(f32[3,32,128]{2,1,0:T(8,128)S(1)} %get-tuple-element.73.smooth.refs_12_, s16[32,4096]{1,0:T(8,128)(2,1)S(1)} %get-tuple-element.48.picks.refs_2_, s16[16,4096]{1,0:T(8,128)(2,1)S(1)} %get-tuple-element.84.start, s16[32,4096]{1,0:T(8,128)(2,1)S(1)} %get-tuple-element.51.spot.refs_5_, ...), custom_call_target="tpu_custom_call" | custom-call | flops 3840000000 | bytes 3840000 | tf_op jit(solution)/shard_map/pallas_call | solution.py:78
  31.7 0.0 collective-permute-done.5.refs_8_.refs_5_
  31.8 0.0 collective-permute-done.6.refs_9_.refs_6_
  31.8 2.0 %shard_map.89 = (f32[3,32,128]{2,1,0:T(8,128)S(1)}, f32[3,32,128]{2,1,0:T(8,128)S(1)}, bf16[6,32,128]{2,1,0:T(8,128)(2,1)S(1)}, bf16[6,32,128]{2,1,0:T(8,128)(2,...) custom-call(s32[8,128]{1,0:T(8,128)S(1)} %broadcast_in_dim.3.refs_0_, ...), custom_call_target="tpu_custom_call" | custom-call | flops 2500000000 | bytes 2500000 | tf_op jit(solution)/shard_map/pallas_call | solution.py:78
  33.8 0.3 collective-permute-start.7
  34.1 4.1 %collective-permute-start.8 = (bf16[6,32,128]{2,1,0:T(8,128)(2,1)S(1)}, bf16[6,32,128]{2,1,0:T(8,128)(2,1)S(1)}, u32[]{:S(2)}, u32[]{:S(2)}) collective-permute-start(bf16[6,32,128]{2,1,0:T(8,128)(2,1)S(1)} %get-tuple-element.76), channel_id=1, source_target_pairs={{0,1},{2,3},{4,5},{6,7},{8,9},{10,11},{12,13},{14,15},{16,17},{18,... | collective-permute-start | bytes 147464 | tf_op jit(solution)/shard_map/ppermute | solution.py:668
  38.2 1.7 %shard_map.90.refs_15_ = bf16[3,32,2048]{2,1,0:T(8,128)(2,1)S(1)} custom-call(f32[3,32,128]{2,1,0:T(8,128)S(1)} %get-tuple-element.79.smooth.refs_12_, s16[32,4096]{1,0:T(8,128)(2,1)S(1)} %get-tuple-element.48.picks.refs_2_, s16[16,4096]{1,0:T(8,128)(2,1)S(1)} %get-tuple-element.84.start, s16[32,4096]{1,0:T(8,128)(2,1)S(1)} %get-tuple-element.51.spot.refs_5_, ...), custom_call_target="tpu_custom_call" | custom-call | flops 200000000 | bytes 200000 | tf_op jit(solution)/shard_map/pallas_call | solution.py:78
  39.8 0.1 collective-permute-start.9
  39.9 2.7 %collective-permute-start.10 = (bf16[13,32,128]{2,1,0:T(8,128)(2,1)S(1)}, bf16[13,32,128]{2,1,0:T(8,128)(2,1)S(1)}, u32[]{:S(2)}, u32[]{:S(2)}) collective-permute-start(bf16[13,32,128]{2,1,0:T(8,128)(2,1)S(1)} %get-tuple-element.81), channel_id=1, source_target_pairs={{0,28},{1,29},{2,30},{3,31},{4,0},{5,1},{6,2},{7,3},{8,4},{9,5},{1... | collective-permute-start | bytes 319496 | tf_op jit(solution)/shard_map/ppermute | solution.py:656
  42.6 1.7 %shard_map.91.refs_16_ = bf16[3,32,2048]{2,1,0:T(8,128)(2,1)S(1)} custom-call(f32[3,32,128]{2,1,0:T(8,128)S(1)} %get-tuple-element.79.smooth.refs_12_, s16[32,4096]{1,0:T(8,128)(2,1)S(1)} %get-tuple-element.48.picks.refs_2_, s16[16,4096]{1,0:T(8,128)(2,1)S(1)} %get-tuple-element.84.start, s16[32,4096]{1,0:T(8,128)(2,1)S(1)} %get-tuple-element.51.spot.refs_5_, ...), custom_call_target="tpu_custom_call" | custom-call | flops 200000000 | bytes 200000 | tf_op jit(solution)/shard_map/pallas_call | solution.py:78
  44.2 0.0 copy-start.5
  44.3 2.0 %shard_map.92.refs_12_ = f32[3,32,128]{2,1,0:T(8,128)S(1)} custom-call(s32[8,128]{1,0:T(8,128)S(1)} %broadcast_in_dim.3.refs_0_, s32[48,128]{1,0:T(8,128)S(1)} %get-tuple-element.47.most.refs_1_, s16[32,4096]{1,0:T(8,128)(2,1)S(1)} %get-tuple-element.48.picks.refs_2_, s16[16,4096]{1,0:T(8,128)(2,1)S(1)} %get-tuple-element.49.refs_3_, ...), custom_call_target="tpu_custom_call" | custom-call | flops 2500000000 | bytes 2500000 | tf_op jit(solution)/shard_map/pallas_call | solution.py:78
  46.2 1.8 %shard_map.93 = f32[3,4096]{1,0:T(4,128)} custom-call(s32[8,128]{1,0:T(8,128)S(1)} %broadcast_in_dim.3.refs_0_, f32[3,32,128]{2,1,0:T(8,128)S(1)} %get-tuple-element.70.refs_18_.refs_1_, f32[4,4096]{1,0:T(4,128)S(1)} %copy-done.4, bf16[7,32,128]{2,1,0:T(8,128)(2,1)S(1)} %collective-permute-done.1.refs_8_.refs_16_.refs_3_, ...), custom_call_target="tpu_custom_call" | custom-call | flops 2000000000 | bytes 2000000 | tf_op jit(solution)/shard_map/pallas_call | solution.py:78
  (20 shorter events, 0.1 us)
Async XLA Ops:
  0.0 3.7 %copy-start.6 = (s32[1,2,512]{2,1,0:T(2,128)S(1)}, s32[1,2,512]{2,1,0:T(2,128)}, u32[]{:S(2)}) copy-start(s32[1,2,512]{2,1,0:T(2,128)} %param.11) | copy-start | bytes 12292
  0.0 3.7 %copy-start.1 = (s32[32,4096]{1,0:T(8,128)S(1)}, s32[32,4096]{1,0:T(8,128)}, u32[]{:S(2)}) copy-start(s32[32,4096]{1,0:T(8,128)} %col) | copy-start | bytes 1572868
  1.6 5.7 %collective-permute-start = (f32[3,32,128]{2,1,0:T(8,128)S(1)}, f32[3,32,128]{2,1,0:T(8,128)S(1)}, u32[]{:S(2)}, u32[]{:S(2)}) collective-permute-start(f32[3,32,128]{2,1,0:T(8,128)S(1)} %get-tuple-element.58), channel_id=1, source_target_pairs={{0,32},{32,0},{64,96},{96,64},{128,160},{160,128},{192,224},{224,1... | collective-permute-start | bytes 147464 | tf_op jit(solution)/shard_map/ppermute | solution.py:728
  3.7 3.3 %copy-start.2 = (f32[3,3,4096]{2,1,0:T(4,128)S(1)}, f32[3,3,4096]{2,1,0:T(4,128)}, u32[]{:S(2)}) copy-start(f32[3,3,4096]{2,1,0:T(4,128)} %dinv.1) | copy-start | bytes 442372
  3.7 3.3 %copy-start.4 = (f32[4,4096]{1,0:T(4,128)S(1)}, f32[4,4096]{1,0:T(4,128)}, u32[]{:S(2)}) copy-start(f32[4,4096]{1,0:T(4,128)} %refs_2_.1) | copy-start | bytes 196612
  7.2 5.8 %collective-permute-start.2 = (f32[3,32,128]{2,1,0:T(8,128)S(1)}, f32[3,32,128]{2,1,0:T(8,128)S(1)}, u32[]{:S(2)}, u32[]{:S(2)}) collective-permute-start(f32[3,32,128]{2,1,0:T(8,128)S(1)} %add.6), channel_id=1, source_target_pairs={{0,64},{32,96},{64,0},{96,32},{128,192},{160,224},{192,128},{224,1... | collective-permute-start | bytes 147464 | tf_op jit(solution)/shard_map/ppermute | solution.py:728
  8.6 13.9 %collective-permute-start.1 = (bf16[7,32,128]{2,1,0:T(8,128)(2,1)S(1)}, bf16[7,32,128]{2,1,0:T(8,128)(2,1)S(1)}, u32[]{:S(2)}, u32[]{:S(2)}) collective-permute-start(bf16[7,32,128]{2,1,0:T(8,128)(2,1)S(1)} %get-tuple-element.65.refs_19_), channel_id=1, source_target_pairs={{1,2},{3,4},{5,6},{7,8},{9,10},{11,12},{13,14},{15,16},{17,18},{19... | collective-permute-start | bytes 172040 | tf_op jit(solution)/shard_map/ppermute | solution.py:662
  13.1 9.5 %copy-start = (bf16[32,3,3,4096]{3,0,2,1:T(8,128)(2,1)S(1)}, bf16[32,3,3,4096]{3,0,2,1:T(8,128)(2,1)}, u32[]{:S(2)}) copy-start(bf16[32,3,3,4096]{3,0,2,1:T(8,128)(2,1)} %param.9) | copy-start | bytes 7077892
  13.1 9.5 %copy-start.3 = (f32[3,3,4096]{2,1,0:T(4,128)S(1)}, f32[3,3,4096]{2,1,0:T(4,128)}, u32[]{:S(2)}) copy-start(f32[3,3,4096]{2,1,0:T(4,128)} %refs_19_.1) | copy-start | bytes 442372
  13.1 9.4 %collective-permute-start.4 = (f32[3,32,128]{2,1,0:T(8,128)S(1)}, f32[3,32,128]{2,1,0:T(8,128)S(1)}, u32[]{:S(2)}, u32[]{:S(2)}) collective-permute-start(f32[3,32,128]{2,1,0:T(8,128)S(1)} %add.7.refs_17_), channel_id=1, source_target_pairs={{0,192},{32,224},{64,128},{96,160},{128,64},{160,96},{192,0},{224,... | collective-permute-start | bytes 147464 | tf_op jit(solution)/shard_map/ppermute | solution.py:728
  15.1 7.4 %collective-permute-start.3 = (bf16[7,32,128]{2,1,0:T(8,128)(2,1)S(1)}, bf16[7,32,128]{2,1,0:T(8,128)(2,1)S(1)}, u32[]{:S(2)}, u32[]{:S(2)}) collective-permute-start(bf16[7,32,128]{2,1,0:T(8,128)(2,1)S(1)} %get-tuple-element.65.refs_19_), channel_id=1, source_target_pairs={{0,1},{2,3},{4,5},{6,7},{8,9},{10,11},{12,13},{14,15},{16,17},{18,... | collective-permute-start | bytes 172040 | tf_op jit(solution)/shard_map/ppermute | solution.py:668
  24.6 7.1 %collective-permute-start.5 = (bf16[10,32,128]{2,1,0:T(8,128)(2,1)S(1)}, bf16[10,32,128]{2,1,0:T(8,128)(2,1)S(1)}, u32[]{:S(2)}, u32[]{:S(2)}) collective-permute-start(bf16[10,32,128]{2,1,0:T(8,128)(2,1)S(1)} %get-tuple-element.71), channel_id=1, source_target_pairs={{1,2},{3,4},{5,6},{7,8},{9,10},{11,12},{13,14},{15,16},{17,18},{19... | collective-permute-start | bytes 245768 | tf_op jit(solution)/shard_map/ppermute | solution.py:662
  24.7 7.0 %collective-permute-start.6 = (bf16[10,32,128]{2,1,0:T(8,128)(2,1)S(1)}, bf16[10,32,128]{2,1,0:T(8,128)(2,1)S(1)}, u32[]{:S(2)}, u32[]{:S(2)}) collective-permute-start(bf16[10,32,128]{2,1,0:T(8,128)(2,1)S(1)} %get-tuple-element.72), channel_id=1, source_target_pairs={{0,1},{2,3},{4,5},{6,7},{8,9},{10,11},{12,13},{14,15},{16,17},{18,... | collective-permute-start | bytes 245768 | tf_op jit(solution)/shard_map/ppermute | solution.py:668
  33.8 10.5 %collective-permute-start.7 = (bf16[6,32,128]{2,1,0:T(8,128)(2,1)S(1)}, bf16[6,32,128]{2,1,0:T(8,128)(2,1)S(1)}, u32[]{:S(2)}, u32[]{:S(2)}) collective-permute-start(bf16[6,32,128]{2,1,0:T(8,128)(2,1)S(1)} %get-tuple-element.75), channel_id=1, source_target_pairs={{1,2},{3,4},{5,6},{7,8},{9,10},{11,12},{13,14},{15,16},{17,18},{19... | collective-permute-start | bytes 147464 | tf_op jit(solution)/shard_map/ppermute | solution.py:662
  34.1 10.2 %collective-permute-start.8 = (bf16[6,32,128]{2,1,0:T(8,128)(2,1)S(1)}, bf16[6,32,128]{2,1,0:T(8,128)(2,1)S(1)}, u32[]{:S(2)}, u32[]{:S(2)}) collective-permute-start(bf16[6,32,128]{2,1,0:T(8,128)(2,1)S(1)} %get-tuple-element.76), channel_id=1, source_target_pairs={{0,1},{2,3},{4,5},{6,7},{8,9},{10,11},{12,13},{14,15},{16,17},{18,... | collective-permute-start | bytes 147464 | tf_op jit(solution)/shard_map/ppermute | solution.py:668
  39.8 6.4 %collective-permute-start.9 = (bf16[13,32,128]{2,1,0:T(8,128)(2,1)S(1)}, bf16[13,32,128]{2,1,0:T(8,128)(2,1)S(1)}, u32[]{:S(2)}, u32[]{:S(2)}) collective-permute-start(bf16[13,32,128]{2,1,0:T(8,128)(2,1)S(1)} %get-tuple-element.80), channel_id=1, source_target_pairs={{0,4},{1,5},{2,6},{3,7},{4,8},{5,9},{6,10},{7,11},{8,12},{9,13},{1... | collective-permute-start | bytes 319496 | tf_op jit(solution)/shard_map/ppermute | solution.py:656
  39.9 6.3 %collective-permute-start.10 = (bf16[13,32,128]{2,1,0:T(8,128)(2,1)S(1)}, bf16[13,32,128]{2,1,0:T(8,128)(2,1)S(1)}, u32[]{:S(2)}, u32[]{:S(2)}) collective-permute-start(bf16[13,32,128]{2,1,0:T(8,128)(2,1)S(1)} %get-tuple-element.81), channel_id=1, source_target_pairs={{0,28},{1,29},{2,30},{3,31},{4,0},{5,1},{6,2},{7,3},{8,4},{9,5},{1... | collective-permute-start | bytes 319496 | tf_op jit(solution)/shard_map/ppermute | solution.py:656
  44.2 2.0 %copy-start.5 = (s32[4096]{0:T(1024)S(1)}, s32[4096]{0:T(1024)}, u32[]{:S(2)}) copy-start(s32[4096]{0:T(1024)} %param.13) | copy-start | bytes 49156

commit v12 on v10

--- a/solution.py
+++ b/solution.py
@@ -300,6 +300,10 @@
     return [ref[h * PACK : (h + 1) * PACK, lanes] for h in range(2)]
 
 
+def tiles_per_step(tiles):
+    return max(n for n in range(1, 17) if tiles % n == 0)
+
+
 def splat(number):
     return jnp.full((PACK, LANES), number, jnp.int32).astype(jnp.int16)
 
@@ -384,7 +388,7 @@
     )
 
 
-def halo_kernel(*refs, stage, sizes, scale_old, scale_new, subs, unroll=8):
+def halo_kernel(*refs, stage, sizes, scale_old, scale_new, subs):
     (place, most, picks, halo_start, halo_columns, spot, rank, ghost) = refs[:8]
     (outer, inner, residual, dinv, smooth, update, bonds) = refs[8:15]
     pieces = len(sizes)
@@ -488,8 +492,9 @@
 
     for piece, part in enumerate(local_found):
         first = sum(sizes[:piece])
-
-        def some_tiles(t, carry, part=part, first=first):
+        unroll = tiles_per_step(sizes[piece])
+
+        def some_tiles(t, carry, part=part, first=first, unroll=unroll):
             for u in range(unroll):
                 there = pl.ds(pl.multiple_of((t * unroll + u) * LANES, LANES), LANES)
                 tile = first + t * unroll + u
@@ -667,7 +672,7 @@
 
 
 def local_pass(smooth, lists, first, tiles, us=None):
-    unroll = max(n for n in range(1, 17) if tiles % n == 0)
+    unroll = tiles_per_step(tiles)
     return call(
         functools.partial(local_kernel, first=first, tiles=tiles, unroll=unroll),
         jax.ShapeDtypeStruct((3, lists[0].shape[0], tiles * LANES), BF16),

time: 48.3 us -> 47.9 us (level)
  no operation moved by 1% of the time
where the time goes in v12:
time: 47.9 us
  starting transfers between devices  24.6 us (51%)
  Pallas kernels  22.9 us (48%)
    pallas_call x12, Pallas kernels, call(): pl.pallas_call(kernel, out_shape=out, in_specs=[pl.BlockSpec(memory_space...  22.9 us
    ppermute x3, starting transfers between devices, within_chip(): return lax.ppermute(value, 'sub', pairs + [(j, i) for i, j in pairs])  12.6 us
    ppermute x3, starting transfers between devices, exchanged(): return lax.ppermute(value, 'dom', [(i, i ^ step) for i in range(doms)])  5.49 us
    ppermute x3, starting transfers between devices, across_chips(): return lax.ppermute(value, 'sub', pairs + [(j, i) for i, j in pairs])  3.76 us
    ppermute x2, starting transfers between devices, shifted(): lax.ppermute(value, 'sub', [(i, (i + steps) % count) for i in range(count)])  2.75 us
  transfers between devices with their start and end apart: 11, of which 0 were waited for; matrix products, arithmetic and copies ran while one was open for 0% of the time, Pallas kernels for 32%

profile of v12, /device:TPU:1, one launch (start us, length us, event | category | flops | bytes accessed | tf_op | source)
XLA Modules:
  0.0 47.9 jit_solution(13833161091417270327)
XLA Ops:
  0.0 1.5 %shard_map.82 = (f32[3,32,128]{2,1,0:T(8,128)S(1)}, f32[3,32,128]{2,1,0:T(8,128)S(1)}) custom-call(f32[3,4096]{1,0:T(4,128)} %refs_0_.1, s32[32,128]{1,0:T(8,128)} %bitcast.5), custom_call_target="tpu_custom_call" | custom-call | flops 1600000000 | bytes 1600000 | tf_op jit(solution)/shard_map/pallas_call | solution.py:77
  1.6 2.1 %collective-permute-start = (f32[3,32,128]{2,1,0:T(8,128)S(1)}, f32[3,32,128]{2,1,0:T(8,128)S(1)}, u32[]{:S(2)}, u32[]{:S(2)}) collective-permute-start(f32[3,32,128]{2,1,0:T(8,128)S(1)} %get-tuple-element.58), channel_id=1, source_target_pairs={{0,32},{32,0},{64,96},{96,64},{128,160},{160,128},{192,224},{224,1... | collective-permute-start | bytes 147464 | tf_op jit(solution)/shard_map/ppermute | solution.py:727
  3.7 0.0 copy-start.2
  3.7 0.0 copy-start.4
  3.7 3.3 %shard_map.83 = (s16[32,4096]{1,0:T(8,128)(2,1)S(1)}, s16[16,4096]{1,0:T(8,128)(2,1)S(1)}, s16[16,4096]{1,0:T(8,128)(2,1)S(1)}, s16[32,4096]{1,0:T(8,128)(2,1)S(...) custom-call(s32[32,4096]{1,0:T(8,128)S(1)} %copy-done.1), custom_call_target="tpu_custom_call" | custom-call | flops 2500000000 | bytes 2500000 | tf_op jit(solution)/shard_map/pallas_call | solution.py:77
  7.0 0.2 shard_map.84
  7.2 0.0 collective-permute-done
  7.3 1.4 %collective-permute-start.2 = (f32[3,32,128]{2,1,0:T(8,128)S(1)}, f32[3,32,128]{2,1,0:T(8,128)S(1)}, u32[]{:S(2)}, u32[]{:S(2)}) collective-permute-start(f32[3,32,128]{2,1,0:T(8,128)S(1)} %add.6), channel_id=1, source_target_pairs={{0,64},{32,96},{64,0},{96,32},{128,192},{160,224},{192,128},{224,1... | collective-permute-start | bytes 147464 | tf_op jit(solution)/shard_map/ppermute | solution.py:727
  8.7 3.6 %collective-permute-start.1 = (bf16[7,32,128]{2,1,0:T(8,128)(2,1)S(1)}, bf16[7,32,128]{2,1,0:T(8,128)(2,1)S(1)}, u32[]{:S(2)}, u32[]{:S(2)}) collective-permute-start(bf16[7,32,128]{2,1,0:T(8,128)(2,1)S(1)} %get-tuple-element.65.refs_19_), channel_id=1, source_target_pairs={{1,2},{3,4},{5,6},{7,8},{9,10},{11,12},{13,14},{15,16},{17,18},{19... | collective-permute-start | bytes 172040 | tf_op jit(solution)/shard_map/ppermute | solution.py:661
  12.2 0.9 %shard_map.85.refs_15_ = bf16[3,32,1024]{2,1,0:T(8,128)(2,1)S(1)} custom-call(f32[3,32,128]{2,1,0:T(8,128)S(1)} %get-tuple-element.62.smooth.refs_12_.refs_13_, s16[32,4096]{1,0:T(8,128)(2,1)S(1)} %get-tuple-element.48.picks.refs_2_, s16[16,4096]{1,0:T(8,128)(2,1)S(1)} %get-tuple-element.84.start, s16[32,4096]{1,0:T(8,128)(2,1)S(1)} %get-tuple-element.51.spot.refs_5_, ...), custom_call_target="tpu_custom_call" | custom-call | flops 960000000 | bytes 960000 | tf_op jit(solution)/shard_map/pallas_call | solution.py:77
  13.1 0.0 collective-permute-done.2
  13.1 0.0 copy-start
  13.1 0.0 copy-start.3
  13.2 2.0 %collective-permute-start.4 = (f32[3,32,128]{2,1,0:T(8,128)S(1)}, f32[3,32,128]{2,1,0:T(8,128)S(1)}, u32[]{:S(2)}, u32[]{:S(2)}) collective-permute-start(f32[3,32,128]{2,1,0:T(8,128)S(1)} %add.7.refs_17_), channel_id=1, source_target_pairs={{0,192},{32,224},{64,128},{96,160},{128,64},{160,96},{192,0},{224,... | collective-permute-start | bytes 147464 | tf_op jit(solution)/shard_map/ppermute | solution.py:727
  15.1 4.8 %collective-permute-start.3 = (bf16[7,32,128]{2,1,0:T(8,128)(2,1)S(1)}, bf16[7,32,128]{2,1,0:T(8,128)(2,1)S(1)}, u32[]{:S(2)}, u32[]{:S(2)}) collective-permute-start(bf16[7,32,128]{2,1,0:T(8,128)(2,1)S(1)} %get-tuple-element.65.refs_19_), channel_id=1, source_target_pairs={{0,1},{2,3},{4,5},{6,7},{8,9},{10,11},{12,13},{14,15},{16,17},{18,... | collective-permute-start | bytes 172040 | tf_op jit(solution)/shard_map/ppermute | solution.py:667
  20.0 2.6 %shard_map.86.refs_16_ = bf16[3,32,3072]{2,1,0:T(8,128)(2,1)S(1)} custom-call(f32[3,32,128]{2,1,0:T(8,128)S(1)} %get-tuple-element.62.smooth.refs_12_.refs_13_, s16[32,4096]{1,0:T(8,128)(2,1)S(1)} %get-tuple-element.48.picks.refs_2_, s16[16,4096]{1,0:T(8,128)(2,1)S(1)} %get-tuple-element.84.start, s16[32,4096]{1,0:T(8,128)(2,1)S(1)} %get-tuple-element.51.spot.refs_5_, ...), custom_call_target="tpu_custom_call" | custom-call | flops 2880000000 | bytes 2880000 | tf_op jit(solution)/shard_map/pallas_call | solution.py:77
  22.6 0.0 collective-permute-done.1.refs_8_.refs_16_.refs_3_
  22.6 0.0 collective-permute-done.4.refs_18_
  22.6 2.0 %shard_map.87 = (f32[3,32,128]{2,1,0:T(8,128)S(1)}, f32[3,32,128]{2,1,0:T(8,128)S(1)}, f32[3,32,128]{2,1,0:T(8,128)S(1)}, bf16[10,32,128]{2,1,0:T(8,128)(2,1)S(1)}, bf16[10,32,128]{2,1,0:T(8,128)(2,1)S(1)}) custom-call(s32[8,128]{1,0:T(8,128)S(1)} %broadcast_in_dim.3.refs_0_, s32[48,128]{1,0:T(8,128)S(1)} %get-tuple-element.47.most.refs_1_, ...), custom_call_target="tpu_custom_call" | custom-call | flops 2500000000 | bytes 2500000 | tf_op jit(solution)/shard_map/pallas_call | solution.py:77
  24.6 0.1 collective-permute-start.5
  24.7 3.7 %collective-permute-start.6 = (bf16[10,32,128]{2,1,0:T(8,128)(2,1)S(1)}, bf16[10,32,128]{2,1,0:T(8,128)(2,1)S(1)}, u32[]{:S(2)}, u32[]{:S(2)}) collective-permute-start(bf16[10,32,128]{2,1,0:T(8,128)(2,1)S(1)} %get-tuple-element.72), channel_id=1, source_target_pairs={{0,1},{2,3},{4,5},{6,7},{8,9},{10,11},{12,13},{14,15},{16,17},{18,... | collective-permute-start | bytes 245768 | tf_op jit(solution)/shard_map/ppermute | solution.py:667
  28.4 3.4 %shard_map.88.refs_15_ = bf16[3,32,4096]{2,1,0:T(8,128)(2,1)S(1)} custom-call(f32[3,32,128]{2,1,0:T(8,128)S(1)} %get-tuple-element.73.smooth.refs_12_, s16[32,4096]{1,0:T(8,128)(2,1)S(1)} %get-tuple-element.48.picks.refs_2_, s16[16,4096]{1,0:T(8,128)(2,1)S(1)} %get-tuple-element.84.start, s16[32,4096]{1,0:T(8,128)(2,1)S(1)} %get-tuple-element.51.spot.refs_5_, ...), custom_call_target="tpu_custom_call" | custom-call | flops 3840000000 | bytes 3840000 | tf_op jit(solution)/shard_map/pallas_call | solution.py:77
  31.8 2.1 %shard_map.89 = (f32[3,32,128]{2,1,0:T(8,128)S(1)}, f32[3,32,128]{2,1,0:T(8,128)S(1)}, bf16[6,32,128]{2,1,0:T(8,128)(2,1)S(1)}, bf16[6,32,128]{2,1,0:T(8,128)(2,...) custom-call(s32[8,128]{1,0:T(8,128)S(1)} %broadcast_in_dim.3.refs_0_, ...), custom_call_target="tpu_custom_call" | custom-call | flops 2500000000 | bytes 2500000 | tf_op jit(solution)/shard_map/pallas_call | solution.py:77
  33.9 0.1 collective-permute-start.7
  34.0 4.1 %collective-permute-start.8 = (bf16[6,32,128]{2,1,0:T(8,128)(2,1)S(1)}, bf16[6,32,128]{2,1,0:T(8,128)(2,1)S(1)}, u32[]{:S(2)}, u32[]{:S(2)}) collective-permute-start(bf16[6,32,128]{2,1,0:T(8,128)(2,1)S(1)} %get-tuple-element.76), channel_id=1, source_target_pairs={{0,1},{2,3},{4,5},{6,7},{8,9},{10,11},{12,13},{14,15},{16,17},{18,... | collective-permute-start | bytes 147464 | tf_op jit(solution)/shard_map/ppermute | solution.py:667
  38.1 1.7 %shard_map.90.refs_15_ = bf16[3,32,2048]{2,1,0:T(8,128)(2,1)S(1)} custom-call(f32[3,32,128]{2,1,0:T(8,128)S(1)} %get-tuple-element.79.smooth.refs_12_, s16[32,4096]{1,0:T(8,128)(2,1)S(1)} %get-tuple-element.48.picks.refs_2_, s16[16,4096]{1,0:T(8,128)(2,1)S(1)} %get-tuple-element.84.start, s16[32,4096]{1,0:T(8,128)(2,1)S(1)} %get-tuple-element.51.spot.refs_5_, ...), custom_call_target="tpu_custom_call" | custom-call | flops 200000000 | bytes 200000 | tf_op jit(solution)/shard_map/pallas_call | solution.py:77
  39.7 0.1 collective-permute-start.9
  39.8 2.7 %collective-permute-start.10 = (bf16[13,32,128]{2,1,0:T(8,128)(2,1)S(1)}, bf16[13,32,128]{2,1,0:T(8,128)(2,1)S(1)}, u32[]{:S(2)}, u32[]{:S(2)}) collective-permute-start(bf16[13,32,128]{2,1,0:T(8,128)(2,1)S(1)} %get-tuple-element.81), channel_id=1, source_target_pairs={{0,28},{1,29},{2,30},{3,31},{4,0},{5,1},{6,2},{7,3},{8,4},{9,5},{1... | collective-permute-start | bytes 319496 | tf_op jit(solution)/shard_map/ppermute | solution.py:655
  42.5 1.7 %shard_map.91.refs_16_ = bf16[3,32,2048]{2,1,0:T(8,128)(2,1)S(1)} custom-call(f32[3,32,128]{2,1,0:T(8,128)S(1)} %get-tuple-element.79.smooth.refs_12_, s16[32,4096]{1,0:T(8,128)(2,1)S(1)} %get-tuple-element.48.picks.refs_2_, s16[16,4096]{1,0:T(8,128)(2,1)S(1)} %get-tuple-element.84.start, s16[32,4096]{1,0:T(8,128)(2,1)S(1)} %get-tuple-element.51.spot.refs_5_, ...), custom_call_target="tpu_custom_call" | custom-call | flops 200000000 | bytes 200000 | tf_op jit(solution)/shard_map/pallas_call | solution.py:77
  44.2 0.0 copy-start.5
  44.2 1.8 %shard_map.92.refs_12_ = f32[3,32,128]{2,1,0:T(8,128)S(1)} custom-call(s32[8,128]{1,0:T(8,128)S(1)} %broadcast_in_dim.3.refs_0_, s32[48,128]{1,0:T(8,128)S(1)} %get-tuple-element.47.most.refs_1_, s16[32,4096]{1,0:T(8,128)(2,1)S(1)} %get-tuple-element.48.picks.refs_2_, s16[16,4096]{1,0:T(8,128)(2,1)S(1)} %get-tuple-element.49.refs_3_, ...), custom_call_target="tpu_custom_call" | custom-call | flops 2500000000 | bytes 2500000 | tf_op jit(solution)/shard_map/pallas_call | solution.py:77
  46.0 1.8 %shard_map.93 = f32[3,4096]{1,0:T(4,128)} custom-call(s32[8,128]{1,0:T(8,128)S(1)} %broadcast_in_dim.3.refs_0_, f32[3,32,128]{2,1,0:T(8,128)S(1)} %get-tuple-element.70.refs_18_.refs_1_, f32[4,4096]{1,0:T(4,128)S(1)} %copy-done.4, bf16[7,32,128]{2,1,0:T(8,128)(2,1)S(1)} %collective-permute-done.1.refs_8_.refs_16_.refs_3_, ...), custom_call_target="tpu_custom_call" | custom-call | flops 2000000000 | bytes 2000000 | tf_op jit(solution)/shard_map/pallas_call | solution.py:77
  (20 shorter events, 0.1 us)
Async XLA Ops:
  0.0 3.7 %copy-start.6 = (s32[1,2,512]{2,1,0:T(2,128)S(1)}, s32[1,2,512]{2,1,0:T(2,128)}, u32[]{:S(2)}) copy-start(s32[1,2,512]{2,1,0:T(2,128)} %param.11) | copy-start | bytes 12292
  0.0 3.7 %copy-start.1 = (s32[32,4096]{1,0:T(8,128)S(1)}, s32[32,4096]{1,0:T(8,128)}, u32[]{:S(2)}) copy-start(s32[32,4096]{1,0:T(8,128)} %col) | copy-start | bytes 1572868
  1.6 5.7 %collective-permute-start = (f32[3,32,128]{2,1,0:T(8,128)S(1)}, f32[3,32,128]{2,1,0:T(8,128)S(1)}, u32[]{:S(2)}, u32[]{:S(2)}) collective-permute-start(f32[3,32,128]{2,1,0:T(8,128)S(1)} %get-tuple-element.58), channel_id=1, source_target_pairs={{0,32},{32,0},{64,96},{96,64},{128,160},{160,128},{192,224},{224,1... | collective-permute-start | bytes 147464 | tf_op jit(solution)/shard_map/ppermute | solution.py:727
  3.7 3.3 %copy-start.2 = (f32[3,3,4096]{2,1,0:T(4,128)S(1)}, f32[3,3,4096]{2,1,0:T(4,128)}, u32[]{:S(2)}) copy-start(f32[3,3,4096]{2,1,0:T(4,128)} %dinv.1) | copy-start | bytes 442372
  3.7 3.3 %copy-start.4 = (f32[4,4096]{1,0:T(4,128)S(1)}, f32[4,4096]{1,0:T(4,128)}, u32[]{:S(2)}) copy-start(f32[4,4096]{1,0:T(4,128)} %refs_2_.1) | copy-start | bytes 196612
  7.3 5.8 %collective-permute-start.2 = (f32[3,32,128]{2,1,0:T(8,128)S(1)}, f32[3,32,128]{2,1,0:T(8,128)S(1)}, u32[]{:S(2)}, u32[]{:S(2)}) collective-permute-start(f32[3,32,128]{2,1,0:T(8,128)S(1)} %add.6), channel_id=1, source_target_pairs={{0,64},{32,96},{64,0},{96,32},{128,192},{160,224},{192,128},{224,1... | collective-permute-start | bytes 147464 | tf_op jit(solution)/shard_map/ppermute | solution.py:727
  8.7 13.9 %collective-permute-start.1 = (bf16[7,32,128]{2,1,0:T(8,128)(2,1)S(1)}, bf16[7,32,128]{2,1,0:T(8,128)(2,1)S(1)}, u32[]{:S(2)}, u32[]{:S(2)}) collective-permute-start(bf16[7,32,128]{2,1,0:T(8,128)(2,1)S(1)} %get-tuple-element.65.refs_19_), channel_id=1, source_target_pairs={{1,2},{3,4},{5,6},{7,8},{9,10},{11,12},{13,14},{15,16},{17,18},{19... | collective-permute-start | bytes 172040 | tf_op jit(solution)/shard_map/ppermute | solution.py:661
  13.1 9.5 %copy-start = (bf16[32,3,3,4096]{3,0,2,1:T(8,128)(2,1)S(1)}, bf16[32,3,3,4096]{3,0,2,1:T(8,128)(2,1)}, u32[]{:S(2)}) copy-start(bf16[32,3,3,4096]{3,0,2,1:T(8,128)(2,1)} %param.9) | copy-start | bytes 7077892
  13.1 9.5 %copy-start.3 = (f32[3,3,4096]{2,1,0:T(4,128)S(1)}, f32[3,3,4096]{2,1,0:T(4,128)}, u32[]{:S(2)}) copy-start(f32[3,3,4096]{2,1,0:T(4,128)} %refs_19_.1) | copy-start | bytes 442372
  13.2 9.4 %collective-permute-start.4 = (f32[3,32,128]{2,1,0:T(8,128)S(1)}, f32[3,32,128]{2,1,0:T(8,128)S(1)}, u32[]{:S(2)}, u32[]{:S(2)}) collective-permute-start(f32[3,32,128]{2,1,0:T(8,128)S(1)} %add.7.refs_17_), channel_id=1, source_target_pairs={{0,192},{32,224},{64,128},{96,160},{128,64},{160,96},{192,0},{224,... | collective-permute-start | bytes 147464 | tf_op jit(solution)/shard_map/ppermute | solution.py:727
  15.1 7.5 %collective-permute-start.3 = (bf16[7,32,128]{2,1,0:T(8,128)(2,1)S(1)}, bf16[7,32,128]{2,1,0:T(8,128)(2,1)S(1)}, u32[]{:S(2)}, u32[]{:S(2)}) collective-permute-start(bf16[7,32,128]{2,1,0:T(8,128)(2,1)S(1)} %get-tuple-element.65.refs_19_), channel_id=1, source_target_pairs={{0,1},{2,3},{4,5},{6,7},{8,9},{10,11},{12,13},{14,15},{16,17},{18,... | collective-permute-start | bytes 172040 | tf_op jit(solution)/shard_map/ppermute | solution.py:667
  24.6 7.2 %collective-permute-start.5 = (bf16[10,32,128]{2,1,0:T(8,128)(2,1)S(1)}, bf16[10,32,128]{2,1,0:T(8,128)(2,1)S(1)}, u32[]{:S(2)}, u32[]{:S(2)}) collective-permute-start(bf16[10,32,128]{2,1,0:T(8,128)(2,1)S(1)} %get-tuple-element.71), channel_id=1, source_target_pairs={{1,2},{3,4},{5,6},{7,8},{9,10},{11,12},{13,14},{15,16},{17,18},{19... | collective-permute-start | bytes 245768 | tf_op jit(solution)/shard_map/ppermute | solution.py:661
  24.7 7.1 %collective-permute-start.6 = (bf16[10,32,128]{2,1,0:T(8,128)(2,1)S(1)}, bf16[10,32,128]{2,1,0:T(8,128)(2,1)S(1)}, u32[]{:S(2)}, u32[]{:S(2)}) collective-permute-start(bf16[10,32,128]{2,1,0:T(8,128)(2,1)S(1)} %get-tuple-element.72), channel_id=1, source_target_pairs={{0,1},{2,3},{4,5},{6,7},{8,9},{10,11},{12,13},{14,15},{16,17},{18,... | collective-permute-start | bytes 245768 | tf_op jit(solution)/shard_map/ppermute | solution.py:667
  33.9 10.3 %collective-permute-start.7 = (bf16[6,32,128]{2,1,0:T(8,128)(2,1)S(1)}, bf16[6,32,128]{2,1,0:T(8,128)(2,1)S(1)}, u32[]{:S(2)}, u32[]{:S(2)}) collective-permute-start(bf16[6,32,128]{2,1,0:T(8,128)(2,1)S(1)} %get-tuple-element.75), channel_id=1, source_target_pairs={{1,2},{3,4},{5,6},{7,8},{9,10},{11,12},{13,14},{15,16},{17,18},{19... | collective-permute-start | bytes 147464 | tf_op jit(solution)/shard_map/ppermute | solution.py:661
  34.0 10.2 %collective-permute-start.8 = (bf16[6,32,128]{2,1,0:T(8,128)(2,1)S(1)}, bf16[6,32,128]{2,1,0:T(8,128)(2,1)S(1)}, u32[]{:S(2)}, u32[]{:S(2)}) collective-permute-start(bf16[6,32,128]{2,1,0:T(8,128)(2,1)S(1)} %get-tuple-element.76), channel_id=1, source_target_pairs={{0,1},{2,3},{4,5},{6,7},{8,9},{10,11},{12,13},{14,15},{16,17},{18,... | collective-permute-start | bytes 147464 | tf_op jit(solution)/shard_map/ppermute | solution.py:667
  39.7 6.2 %collective-permute-start.9 = (bf16[13,32,128]{2,1,0:T(8,128)(2,1)S(1)}, bf16[13,32,128]{2,1,0:T(8,128)(2,1)S(1)}, u32[]{:S(2)}, u32[]{:S(2)}) collective-permute-start(bf16[13,32,128]{2,1,0:T(8,128)(2,1)S(1)} %get-tuple-element.80), channel_id=1, source_target_pairs={{0,4},{1,5},{2,6},{3,7},{4,8},{5,9},{6,10},{7,11},{8,12},{9,13},{1... | collective-permute-start | bytes 319496 | tf_op jit(solution)/shard_map/ppermute | solution.py:655
  39.8 6.2 %collective-permute-start.10 = (bf16[13,32,128]{2,1,0:T(8,128)(2,1)S(1)}, bf16[13,32,128]{2,1,0:T(8,128)(2,1)S(1)}, u32[]{:S(2)}, u32[]{:S(2)}) collective-permute-start(bf16[13,32,128]{2,1,0:T(8,128)(2,1)S(1)} %get-tuple-element.81), channel_id=1, source_target_pairs={{0,28},{1,29},{2,30},{3,31},{4,0},{5,1},{6,2},{7,3},{8,4},{9,5},{1... | collective-permute-start | bytes 319496 | tf_op jit(solution)/shard_map/ppermute | solution.py:655
  44.2 1.8 %copy-start.5 = (s32[4096]{0:T(1024)S(1)}, s32[4096]{0:T(1024)}, u32[]{:S(2)}) copy-start(s32[4096]{0:T(1024)} %param.13) | copy-start | bytes 49156
